TPU v7x, 32 devices: a whole 2x2x4 slice. The times are simulated.
32 devices in a mesh: expert: 16 (over z, y, x), shard: 2 (over core).
Axes of the slice: x: 2, y: 2, z: 4, core: 2. Of those that a mesh axis runs over, the one named last changes fastest.
Arguments:
- tokens: bfloat16 [2, 2048, 2048], P('shard', 'expert'), may hold values from -6 to 6
- lengths: int32 [2, 2], P('shard'), may hold values from 0 to 2048, as said below
- routes: int32 [2, 2048, 6], P('shard', 'expert'), may hold values from 0 to 15, all different within a row; in each aligned block of 128 rows (0 to 127, 128 to 255, ..., all dimensions but the last counted through in order) at most 54 rows name the same one
- attn_gain: bfloat16 [2048], P('shard'), may hold values from 0.5 to 1.5
- query_weight: bfloat16 [2048, 3072], P('shard'), may hold values from -0.25 to 0.25
- latent_weight: bfloat16 [2048, 576], P('shard'), may hold values from -0.125 to 0.125
- latent_gain: bfloat16 [512], P('shard'), may hold values from 0.5 to 1.5
- expand_weight: bfloat16 [512, 4096], P('shard'), may hold values from -0.25 to 0.25
- output_weight: bfloat16 [2048, 2048], P('shard'), may hold values from -2 to 2
- ffn_gain: bfloat16 [2048], P('shard'), may hold values from 0.5 to 1.5
- router_weight: bfloat16 [2048, 16], P('shard'), may hold values from -0.0625 to 0.0625
- shared_in: bfloat16 [2048, 5632], P('shard'), may hold values from -0.125 to 0.125
- shared_out: bfloat16 [2816, 2048], P('shard'), may hold values from -0.21875 to 0.21875
- expert_in: bfloat16 [16, 2048, 2, 1408], P('expert', None, None, 'shard'), may hold values from -0.125 to 0.125
- expert_out: bfloat16 [16, 1408, 2048], P('expert', 'shard'), may hold values from -2.5 to 2.5
- cotangent: bfloat16 [2, 2048, 2048], P('shard', 'expert'), may hold values from -6 to 6
Outputs:
- block_out: bfloat16 [2, 2048, 2048], P('shard', 'expert')
- tokens_grad: bfloat16 [2, 2048, 2048], P('shard', 'expert')
- grad_attn_gain: float32 [2048], P(('expert', 'shard'))
- grad_query_weight: float32 [2048, 3072], P(('expert', 'shard'))
- grad_latent_weight: float32 [2048, 576], P(('expert', 'shard'))
- grad_latent_gain: float32 [512], P(('expert', 'shard'))
- grad_expand_weight: float32 [512, 4096], P(('expert', 'shard'))
- grad_output_weight: float32 [2048, 2048], P(('expert', 'shard'))
- grad_ffn_gain: float32 [2048], P(('expert', 'shard'))
- grad_router_weight: float32 [2048, 16], P(('expert', 'shard'))
- grad_shared_in: float32 [2048, 5632], P(('expert', 'shard'))
- grad_shared_out: float32 [2816, 2048], P(('expert', 'shard'))
- grad_expert_in: float32 [16, 2048, 2, 1408], P('expert', None, None, 'shard')
- grad_expert_out: float32 [16, 1408, 2048], P('expert', 'shard')
Inputs may be any that keep to these rules, and one draw needn't show every extreme that they name: `lengths`: A slot holds either one sequence of 1024 to 2048 tokens, its second entry 0, or two sequences of 1024 and 1024 tokens; the first slot holds one sequence of 2048 tokens. `routes`: every token names 6 different experts; the 128 tokens of one device name any one expert at most 54 times, and in some devices' tokens one expert exactly 54 times.
All inputs are finite; a program needn't handle non-finite values.
Results may differ from a plain program's by a relative error of at most 0.025.
Values may be sent and summed in bfloat16 or wider, within the bound.
A program may use at most 384 MiB of HBM per device.

v0:
```python
import jax
import jax.numpy as jnp
from jax import lax
from jax.sharding import PartitionSpec as P

HEADS = 16
HEAD = 128
ROPE = 64
VHEAD = 128
RANK = 512
FF_S = 2816
SLOT = 2048


EPS = 1e-06
MASK_FILL = -1e30
EXACT_PRECISION = lax.Precision.HIGHEST


def layout(lengths_slot, slot_index):
    first_len = lengths_slot[0]
    second_end = first_len + lengths_slot[1]
    segment = (slot_index >= first_len).astype(jnp.int32) + (slot_index >= second_end).astype(
        jnp.int32
    )
    seq_start = jnp.where(segment == 0, 0, jnp.where(segment == 1, first_len, second_end))
    return (segment, slot_index - seq_start, slot_index < second_end)


def rope_tables(positions):
    half_width = ROPE // 2
    inverse = 10000.0 ** (-jnp.arange(half_width, dtype=jnp.float32) / half_width)
    angles = positions.astype(jnp.float32)[:, None] * inverse[None, :]
    return (jnp.cos(angles), jnp.sin(angles))


def rotate(values, cosine, sine_table):
    half_width = values.shape[-1] // 2
    first_half = values[..., :half_width]
    second_half = values[..., half_width:]
    return jnp.concatenate(
        [
            first_half * cosine - second_half * sine_table,
            second_half * cosine + first_half * sine_table,
        ],
        -1,
    )


def rotate_back(grads_in, cosine, sine_table):
    half_width = grads_in.shape[-1] // 2
    first_half = grads_in[..., :half_width]
    second_half = grads_in[..., half_width:]
    return jnp.concatenate(
        [
            first_half * cosine + second_half * sine_table,
            second_half * cosine - first_half * sine_table,
        ],
        -1,
    )


def silu_parts(gate_in):
    sigma = jax.nn.sigmoid(gate_in)
    return (gate_in * sigma, sigma * (1.0 + gate_in * (1.0 - sigma)))


def rms_scale(values):
    return lax.rsqrt(jnp.mean(values * values, -1, keepdims=True) + EPS)


def norm_back(grad_in, normed, inverse):
    return inverse * (grad_in - normed * jnp.mean(grad_in * normed, -1, keepdims=True))


def per_device(
    tokens,
    lengths,
    routes,
    attn_gain,
    query_weight,
    latent_weight,
    latent_gain,
    expand_weight,
    output_weight,
    ffn_gain,
    router_weight,
    shared_in,
    shared_out,
    expert_in,
    expert_out,
    cotangent,
):
    gathered = (
        lax.all_gather(attn_gain, "shard", axis=0, tiled=True),
        lax.all_gather(query_weight, "shard", axis=0, tiled=True),
        lax.all_gather(latent_weight, "shard", axis=0, tiled=True),
        lax.all_gather(latent_gain, "shard", axis=0, tiled=True),
        lax.all_gather(expand_weight, "shard", axis=0, tiled=True),
        lax.all_gather(output_weight, "shard", axis=0, tiled=True),
        lax.all_gather(ffn_gain, "shard", axis=0, tiled=True),
        lax.all_gather(router_weight, "shard", axis=0, tiled=True),
        lax.all_gather(shared_in, "shard", axis=0, tiled=True),
        lax.all_gather(shared_out, "shard", axis=0, tiled=True),
    )
    (
        gain_attn_low,
        full_query,
        full_latent,
        gain_latent_low,
        full_expand,
        full_output,
        gain_ffn_low,
        full_router,
        full_shared_in,
        full_shared_out,
    ) = gathered
    gain_attn = gain_attn_low.astype(jnp.float32)
    gain_latent = gain_latent_low.astype(jnp.float32)
    gain_ffn = gain_ffn_low.astype(jnp.float32)
    local_rows = tokens.shape[1]
    model_width = tokens.shape[2]
    owners = lax.axis_size("expert")
    experts_all = router_weight.shape[1]
    expert_local = experts_all // owners
    topk_count = routes.shape[2]
    capacity = max(2, 9 * local_rows * topk_count // (8 * experts_all))
    score_scale = (HEAD + ROPE) ** (-0.5)
    slot_index = jnp.arange(SLOT, dtype=jnp.int32)
    here_index = lax.axis_index("expert") * local_rows + jnp.arange(local_rows, dtype=jnp.int32)
    key_segment = layout(lengths[0], slot_index)[0]
    query_segment, query_position, query_valid = layout(lengths[0], here_index)
    cosine, sine_table = rope_tables(query_position)
    inputs = tokens[0].astype(jnp.float32)
    inverse_attn = rms_scale(inputs)
    normed_attn = inputs * inverse_attn
    attn_in = (normed_attn * gain_attn).astype(jnp.bfloat16)
    query_raw = jnp.dot(attn_in, full_query, preferred_element_type=jnp.float32).reshape(
        local_rows, HEADS, HEAD + ROPE
    )
    queries = jnp.concatenate(
        [
            query_raw[..., :HEAD],
            rotate(query_raw[..., HEAD:], cosine[:, None, :], sine_table[:, None, :]),
        ],
        -1,
    ).astype(jnp.bfloat16)
    query_nope = queries[..., :HEAD]
    query_rope = queries[..., HEAD:]
    latent_raw = jnp.dot(attn_in, full_latent, preferred_element_type=jnp.float32)
    latent = latent_raw[:, :RANK]
    inverse_latent = rms_scale(latent)
    normed_latent = latent * inverse_latent
    latent_in = (normed_latent * gain_latent).astype(jnp.bfloat16)
    key_rope = rotate(latent_raw[:, RANK:], cosine, sine_table).astype(jnp.bfloat16)
    slot_latent, slot_rope = (
        lax.all_gather(latent_in, "expert", axis=0, tiled=True),
        lax.all_gather(key_rope, "expert", axis=0, tiled=True),
    )
    expanded = (
        jnp.dot(slot_latent, full_expand, preferred_element_type=jnp.float32)
        .astype(jnp.bfloat16)
        .reshape(SLOT, HEADS, HEAD + VHEAD)
    )
    key_nope = expanded[..., :HEAD]
    values = expanded[..., HEAD:]
    allowed = (query_segment[:, None] == key_segment[None, :]) & (
        slot_index[None, :] <= here_index[:, None]
    )

    def score_block():
        raw_scores = jnp.einsum(
            "qhc,khc->hqk", query_nope, key_nope, preferred_element_type=jnp.float32
        )
        raw_scores = raw_scores + jnp.einsum(
            "qhr,kr->hqk", query_rope, slot_rope, preferred_element_type=jnp.float32
        )
        return jnp.where(allowed[None], raw_scores * score_scale, MASK_FILL)

    scores = score_block()
    highest = jnp.max(scores, -1, keepdims=True)
    shifted = jnp.exp(scores - highest)
    exp_total = jnp.sum(shifted, -1, keepdims=True)
    attention = shifted / exp_total
    log_total = highest + jnp.log(exp_total)
    mixed_heads = (
        jnp.einsum(
            "hqk,khv->qhv",
            attention.astype(jnp.bfloat16),
            values,
            preferred_element_type=jnp.float32,
        )
        .astype(jnp.bfloat16)
        .reshape(local_rows, HEADS * VHEAD)
    )
    hidden_state = inputs + jnp.dot(mixed_heads, full_output, preferred_element_type=jnp.float32)
    inverse_ffn = rms_scale(hidden_state)
    normed_ffn = hidden_state * inverse_ffn
    ffn_in = (normed_ffn * gain_ffn).astype(jnp.bfloat16)
    logits = jnp.dot(ffn_in, full_router, preferred_element_type=jnp.float32)
    logit_exp = jnp.exp(logits - jnp.max(logits, -1, keepdims=True))
    router_probs = logit_exp / jnp.sum(logit_exp, -1, keepdims=True)
    gate_weights = jnp.take_along_axis(router_probs, routes[0], -1)
    shared_both = jnp.dot(ffn_in, full_shared_in, preferred_element_type=jnp.float32)
    shared_act, shared_slope = silu_parts(shared_both[:, :FF_S])
    shared_up = shared_both[:, FF_S:]
    shared_hidden = (shared_act * shared_up).astype(jnp.bfloat16)
    shared_result = jnp.dot(shared_hidden, full_shared_out, preferred_element_type=jnp.float32)
    route_flat = routes[0].reshape(-1)
    expert_ids = jnp.arange(experts_all, dtype=jnp.int32)
    member = (route_flat[:, None] == expert_ids[None, :]).astype(jnp.int32)
    slot_rank = jnp.sum((jnp.cumsum(member, 0) - 1) * member, -1)
    target_slot = route_flat * capacity + slot_rank
    pair_index = jnp.arange(route_flat.shape[0], dtype=jnp.int32)
    source_pair = jnp.zeros((experts_all * capacity,), jnp.int32).at[target_slot].set(pair_index)
    occupied = jnp.zeros((experts_all * capacity,), jnp.bfloat16).at[target_slot].set(1.0)
    send_rows = ffn_in[source_pair // topk_count] * occupied[:, None]
    received = lax.all_to_all(
        send_rows.reshape(owners, expert_local, capacity, model_width),
        "expert",
        split_axis=0,
        concat_axis=0,
        tiled=True,
    )
    weight_in, weight_out = (
        lax.all_gather(expert_in, "shard", axis=3, tiled=True),
        lax.all_gather(expert_out, "shard", axis=1, tiled=True),
    )
    gate_up = jnp.einsum(
        "sxcd,xdgf->sxcgf", received, weight_in, preferred_element_type=jnp.float32
    )
    expert_act, expert_slope = silu_parts(gate_up[..., 0, :])
    expert_up = gate_up[..., 1, :]
    expert_hidden = (expert_act * expert_up).astype(jnp.bfloat16)
    partial_out = jnp.einsum(
        "sxcf,xfd->sxcd", expert_hidden, weight_out, preferred_element_type=jnp.float32
    )
    returned = lax.all_to_all(
        partial_out.astype(jnp.bfloat16), "expert", split_axis=0, concat_axis=0, tiled=True
    ).reshape(experts_all * capacity, model_width)
    picked = returned[target_slot].reshape(local_rows, topk_count, model_width)
    routed = jnp.sum(gate_weights[:, :, None] * picked, 1)
    block_result = hidden_state + shared_result + routed
    live_rows = query_valid.astype(jnp.float32)[:, None]
    grad_out = cotangent[0].astype(jnp.float32) * live_rows
    grad_out_low = grad_out.astype(jnp.bfloat16)
    grad_shared_out = jnp.einsum(
        "tf,td->fd", shared_hidden, grad_out_low, preferred_element_type=jnp.float32
    )
    grad_shared_hidden = jnp.einsum(
        "td,fd->tf", grad_out_low, full_shared_out, preferred_element_type=jnp.float32
    )
    grad_shared_both = jnp.concatenate(
        [grad_shared_hidden * shared_up * shared_slope, grad_shared_hidden * shared_act], -1
    ).astype(jnp.bfloat16)
    grad_shared_in = jnp.einsum(
        "td,tf->df", ffn_in, grad_shared_both, preferred_element_type=jnp.float32
    )
    grad_ffn_in = jnp.einsum(
        "tf,df->td", grad_shared_both, full_shared_in, preferred_element_type=jnp.float32
    )
    grad_gates = jnp.sum(grad_out[:, None, :] * picked, -1)
    grad_picked = (
        (gate_weights[:, :, None] * grad_out[:, None, :])
        .astype(jnp.bfloat16)
        .reshape(-1, model_width)
    )
    send_grads = grad_picked[source_pair] * occupied[:, None]
    received_grads = lax.all_to_all(
        send_grads.reshape(owners, expert_local, capacity, model_width),
        "expert",
        split_axis=0,
        concat_axis=0,
        tiled=True,
    )
    grad_hidden = jnp.einsum(
        "sxcd,xfd->sxcf", received_grads, weight_out, preferred_element_type=jnp.float32
    )
    grad_gate_up = jnp.stack(
        [grad_hidden * expert_up * expert_slope, grad_hidden * expert_act], -2
    ).astype(jnp.bfloat16)
    grad_weight_out = jnp.einsum(
        "sxcf,sxcd->xfd", expert_hidden, received_grads, preferred_element_type=jnp.float32
    )
    grad_weight_in = jnp.einsum(
        "sxcd,sxcgf->xdgf", received, grad_gate_up, preferred_element_type=jnp.float32
    )
    grad_expert_rows = jnp.einsum(
        "sxcgf,xdgf->sxcd", grad_gate_up, weight_in, preferred_element_type=jnp.float32
    )
    grad_expert_in, grad_expert_out = (
        lax.psum_scatter(
            grad_weight_in.astype(jnp.bfloat16), "shard", scatter_dimension=3, tiled=True
        ).astype(jnp.float32),
        lax.psum_scatter(
            grad_weight_out.astype(jnp.bfloat16), "shard", scatter_dimension=1, tiled=True
        ).astype(jnp.float32),
    )
    grad_returned = (
        lax.all_to_all(
            grad_expert_rows.astype(jnp.bfloat16), "expert", split_axis=0, concat_axis=0, tiled=True
        )
        .astype(grad_expert_rows.dtype)
        .reshape(experts_all * capacity, model_width)
    )
    grad_routed = jnp.sum(
        grad_returned[target_slot].reshape(local_rows, topk_count, model_width), 1
    )
    chosen_onehot = (routes[0][:, :, None] == expert_ids[None, None, :]).astype(jnp.float32)
    spread_grads = jnp.sum(grad_gates[:, :, None] * chosen_onehot, 1)
    gate_total = jnp.sum(gate_weights * grad_gates, -1, keepdims=True)
    grad_logits = (router_probs * (spread_grads - gate_total)).astype(jnp.bfloat16)
    grad_router = jnp.einsum("td,te->de", ffn_in, grad_logits, preferred_element_type=jnp.float32)
    grad_ffn_in = (
        grad_ffn_in
        + jnp.einsum("te,de->td", grad_logits, full_router, preferred_element_type=jnp.float32)
        + grad_routed
    )
    grad_gain_ffn = jnp.sum(grad_ffn_in * normed_ffn, 0)
    grad_hidden_state = grad_out + norm_back(grad_ffn_in * gain_ffn, normed_ffn, inverse_ffn)
    grad_attn_out = grad_hidden_state.astype(jnp.bfloat16)
    grad_output = jnp.einsum(
        "tv,td->vd", mixed_heads, grad_attn_out, preferred_element_type=jnp.float32
    )
    grad_mixed = (
        jnp.einsum("td,vd->tv", grad_attn_out, full_output, preferred_element_type=jnp.float32)
        .astype(jnp.bfloat16)
        .reshape(local_rows, HEADS, VHEAD)
    )
    attention_again = jnp.exp(score_block() - log_total)
    grad_attention = jnp.einsum(
        "qhv,khv->hqk", grad_mixed, values, preferred_element_type=jnp.float32
    )
    grad_values = jnp.einsum(
        "hqk,qhv->khv",
        attention_again.astype(jnp.bfloat16),
        grad_mixed,
        preferred_element_type=jnp.float32,
    )
    grad_scores = (
        attention_again
        * (grad_attention - jnp.sum(attention_again * grad_attention, -1, keepdims=True))
    ).astype(jnp.bfloat16)
    grad_query_nope = (
        jnp.einsum("hqk,khc->qhc", grad_scores, key_nope, preferred_element_type=jnp.float32)
        * score_scale
    )
    grad_query_rope = (
        jnp.einsum("hqk,kr->qhr", grad_scores, slot_rope, preferred_element_type=jnp.float32)
        * score_scale
    )
    grad_key_nope = (
        jnp.einsum("hqk,qhc->khc", grad_scores, query_nope, preferred_element_type=jnp.float32)
        * score_scale
    )
    grad_key_rope = (
        jnp.einsum("hqk,qhr->kr", grad_scores, query_rope, preferred_element_type=jnp.float32)
        * score_scale
    )
    expand_wide = full_expand.astype(jnp.float32)
    own_key_nope, own_values, own_key_rope = (
        lax.psum_scatter(
            grad_key_nope.astype(jnp.bfloat16), "expert", scatter_dimension=0, tiled=True
        ).astype(jnp.float32),
        lax.psum_scatter(
            grad_values.astype(jnp.bfloat16), "expert", scatter_dimension=0, tiled=True
        ).astype(jnp.float32),
        lax.psum_scatter(
            grad_key_rope.astype(jnp.bfloat16), "expert", scatter_dimension=0, tiled=True
        ).astype(jnp.float32),
    )
    grad_expanded = jnp.concatenate([own_key_nope, own_values], -1).reshape(
        local_rows, HEADS * (HEAD + VHEAD)
    )
    grad_expand = jnp.einsum(
        "tr,tc->rc", latent_in.astype(jnp.float32), grad_expanded, precision=EXACT_PRECISION
    )
    grad_latent_in = jnp.einsum("tc,rc->tr", grad_expanded, expand_wide, precision=EXACT_PRECISION)
    grad_gain_latent = jnp.sum(grad_latent_in * normed_latent, 0)
    grad_latent = norm_back(grad_latent_in * gain_latent, normed_latent, inverse_latent)
    grad_latent_raw = jnp.concatenate(
        [grad_latent, rotate_back(own_key_rope, cosine, sine_table)], -1
    ).astype(jnp.bfloat16)
    grad_latent_weight = jnp.einsum(
        "td,tc->dc", attn_in, grad_latent_raw, preferred_element_type=jnp.float32
    )
    grad_query_raw = (
        jnp.concatenate(
            [
                grad_query_nope,
                rotate_back(grad_query_rope, cosine[:, None, :], sine_table[:, None, :]),
            ],
            -1,
        )
        .reshape(local_rows, HEADS * (HEAD + ROPE))
        .astype(jnp.bfloat16)
    )
    grad_query = jnp.einsum(
        "td,tc->dc", attn_in, grad_query_raw, preferred_element_type=jnp.float32
    )
    grad_attn_in = jnp.einsum(
        "tc,dc->td", grad_latent_raw, full_latent, preferred_element_type=jnp.float32
    ) + jnp.einsum("tc,dc->td", grad_query_raw, full_query, preferred_element_type=jnp.float32)
    grad_gain_attn = jnp.sum(grad_attn_in * normed_attn, 0)
    tokens_grad = grad_hidden_state + norm_back(grad_attn_in * gain_attn, normed_attn, inverse_attn)
    reduced = (
        lax.psum_scatter(grad_gain_attn, ("expert", "shard"), scatter_dimension=0, tiled=True),
        lax.psum_scatter(grad_query, ("expert", "shard"), scatter_dimension=0, tiled=True),
        lax.psum_scatter(grad_latent_weight, ("expert", "shard"), scatter_dimension=0, tiled=True),
        lax.psum_scatter(grad_gain_latent, ("expert", "shard"), scatter_dimension=0, tiled=True),
        lax.psum_scatter(grad_expand, ("expert", "shard"), scatter_dimension=0, tiled=True),
        lax.psum_scatter(grad_output, ("expert", "shard"), scatter_dimension=0, tiled=True),
        lax.psum_scatter(grad_gain_ffn, ("expert", "shard"), scatter_dimension=0, tiled=True),
        lax.psum_scatter(grad_router, ("expert", "shard"), scatter_dimension=0, tiled=True),
        lax.psum_scatter(grad_shared_in, ("expert", "shard"), scatter_dimension=0, tiled=True),
        lax.psum_scatter(grad_shared_out, ("expert", "shard"), scatter_dimension=0, tiled=True),
    )
    return (
        block_result.astype(jnp.bfloat16)[None],
        tokens_grad.astype(jnp.bfloat16)[None],
        reduced[0],
        reduced[1],
        reduced[2],
        reduced[3],
        reduced[4],
        reduced[5],
        reduced[6],
        reduced[7],
        reduced[8],
        reduced[9],
        grad_expert_in,
        grad_expert_out,
    )


def solution(mesh):
    return jax.shard_map(
        per_device,
        mesh=mesh,
        in_specs=(
            P("shard", "expert", None),
            P("shard", None),
            P("shard", "expert", None),
            P("shard"),
            P("shard", None),
            P("shard", None),
            P("shard"),
            P("shard", None),
            P("shard", None),
            P("shard"),
            P("shard", None),
            P("shard", None),
            P("shard", None),
            P("expert", None, None, "shard"),
            P("expert", "shard", None),
            P("shard", "expert", None),
        ),
        out_specs=(
            P("shard", "expert", None),
            P("shard", "expert", None),
            P(("expert", "shard")),
            P(("expert", "shard"), None),
            P(("expert", "shard"), None),
            P(("expert", "shard")),
            P(("expert", "shard"), None),
            P(("expert", "shard"), None),
            P(("expert", "shard")),
            P(("expert", "shard"), None),
            P(("expert", "shard"), None),
            P(("expert", "shard"), None),
            P("expert", None, None, "shard"),
            P("expert", "shard", None),
        ),
        check_vma=False,
    )
```

profile of v0, /device:TPU:0, one launch (start us, length us, event | category | flops | bytes accessed | tf_op | source)
XLA Modules:
  0.0 2824.9 jit_solution(14302464881808460398)
XLA Ops:
  14.5 8.8 all-gather.11.cloned.1.call-done
  28.1 11.7 copy.110
  53.0 8.6 scatter_custom_fusion.1
  69.8 8.3 mul.536
  79.4 43.9 %all_gather.48 = bf16[2048,64]{0,1:T(8,128)(2,1)S(1)} all-gather(bf16[128,64]{0,1:T(8,128)(2,1)S(1)} %pad_maximum_fusion.15), channel_id=1, replica_groups=mesh['expert'=16,'shard'=2] {'expert'}, dimensions={0}, use_global_device_ids=true | all-gather | bytes 278528 | tf_op jit(solution)/shard_map/all_gather | solution.py:158
  123.3 15.6 convolution_convert_fusion
  138.9 11.3 copy.153
  150.2 7.3 fusion.161
  157.5 12.7 copy.148
  170.2 16.3 copy.99
  186.5 6.8 fusion.99
  193.9 11.1 fusion.15
  204.9 24.2 fusion.163
  229.2 10.1 fusion.2
  239.3 11.6 fusion.83
  266.9 11.1 gather_fusion.2
  298.3 81.6 %all_to_all.20 = bf16[16,1,54,2048]{3,2,1,0:T(8,128)(2,1)} all-to-all(bf16[16,1,54,2048]{3,2,1,0:T(8,128)(2,1)S(1)} %get-tuple-element.97), channel_id=1, replica_groups=mesh['expert'=16,'shard'=2] {'expert'}, dimensions={0} | all-to-all | bytes 7077888 | tf_op jit(solution)/shard_map/all_to_all | solution.py:218
  385.1 29.2 %copy.111 = bf16[1,2048,2,1408]{3,1,2,0:T(8,128)(2,1)} copy(bf16[1,2048,2,1408]{1,2,0,3:T(2,128)(2,1)} %all-gather.25.cloned.1.call-done) | data formatting | bytes 23068672 | tf_op jit(solution)/shard_map/all_gather | solution.py:226
  414.4 17.7 fusion.18
  432.1 11.7 convert_bitcast_fusion
  443.8 8.6 all-to-all-done.2
  452.4 16.6 all-to-all-start.1
  468.9 12.1 fusion.63
  483.2 14.9 fusion.55
  498.1 40.1 %all-to-all-done.1 = bf16[16,1,54,2048]{3,2,1,0:T(8,128)(2,1)} async-done(((bf16[16,1,54,2048]{3,2,1,0:T(8,128)(2,1)}), bf16[16,1,54,2048]{3,2,1,0:T(8,128)(2,1)}, u32[]{:S(2)}, u32[]{:S(2)}) %all-to-all-start.1) | async-done | bytes 3538976 | tf_op jit(solution)/shard_map/all_to_all | solution.py:238
  538.3 16.2 all-to-all-start.3
  555.3 12.4 fusion.169
  567.6 10.1 multiply_convert_fusion.4
  578.6 13.1 fusion.97
  596.5 9.5 gather_fusion.1
  606.1 6.6 reshape.599
  612.6 7.3 multiply_reduce_fusion.1
  629.7 10.2 gather_fusion.3
  639.9 8.0 reshape.594
  658.0 6.3 convolution_convert_fusion.1
  664.6 15.0 multiply_reduce_fusion
  679.5 11.9 multiply_convert_fusion.1
  697.7 11.6 fusion.25
  709.3 12.3 copy.146
  723.0 9.1 multiply_convert_fusion
  732.1 12.4 copy.144
  746.6 17.3 fusion.8
  763.8 29.1 %copy.125 = bf16[1,2048,2,1408]{1,2,0,3:T(2,128)(2,1)} copy(bf16[1,2048,2,1408]{3,1,2,0:T(8,128)(2,1)} %fusion.8) | data formatting | bytes 23068672 | tf_op jit(solution)/shard_map/convert_element_type | solution.py:293
  793.0 12.6 fusion.17
  807.6 154.1 %reduce-scatter.36.cloned.1.call-done = bf16[128,2048]{1,0:T(8,128)(2,1)} async-done(((bf16[2048,2048]{1,0:T(8,128)(2,1)}), bf16[128,2048]{1,0:T(8,128)(2,1)}) %reduce-scatter.36.cloned.1.call-update) | async-done | bytes 524304
  963.0 181.2 %reduce-scatter.34.cloned.1.call-done = bf16[128,2048]{1,0:T(8,128)(2,1)} async-done(((bf16[2048,2048]{1,0:T(8,128)(2,1)}), bf16[128,2048]{1,0:T(8,128)(2,1)}) %reduce-scatter.34.cloned.1.call-update) | async-done | bytes 524304
  1160.5 8.2 fusion.105
  1176.5 11.6 fusion.74
  1189.2 10.9 fusion.101
  1201.1 10.5 fusion.108
  1212.0 19.2 fusion.96
  1233.1 10.1 fusion.170
  1243.2 7.0 fusion.67
  1250.2 33.6 %reduce-scatter.40.cloned.1.call-done = f32[64,16]{1,0:T(8,128)} async-done(((f32[2048,16]{1,0:T(8,128)}), f32[64,16]{1,0:T(8,128)}) %reduce-scatter.40.cloned.1.call-update) | async-done | bytes 4112
  1285.2 41.4 %all-reduce.7.cloned.1.call-done = bf16[1,2048,2,1408]{1,2,0,3:T(2,128)(2,1)} async-done(((bf16[1,2048,2,1408]{1,2,0,3:T(2,128)(2,1)}), bf16[1,2048,2,1408]{1,2,0,3:T(2,128)(2,1)}) %all-reduce.7.cloned.1.call-update) | async-done | bytes 11534352
  1326.7 9.6 dynamic-slice_convert_fusion
  1336.3 17.2 copy.126
  1360.6 41.4 %all-reduce.4 = (f32[2048]{0:T(1024)S(1)}, f32[512]{0:T(512)S(1)}, f32[2048]{0:T(1024)S(1)}) all-reduce(f32[2048]{0:T(1024)S(1)} %get-tuple-element.74, f32[512]{0:T(512)S(1)} %copy-done.72, f32[2048]{0:T(1024)S(1)} %copy-done.50), channel_id=5, replica_groups=mesh['expert'=16,'shard'=2] {'expert','shard'}, use_global_device_ids=true, to_apply=%region_25.26.clone | all-reduce | flops 4608 | bytes 36864
  1406.1 85.4 %reduce-scatter.22.cloned.1.call-done = f32[64,576]{1,0:T(8,128)} async-done(((f32[2048,576]{1,0:T(8,128)}), f32[64,576]{1,0:T(8,128)}) %reduce-scatter.22.cloned.1.call-update) | async-done | bytes 147472 | tf_op jit(solution)/shard_map/reduce_scatter | solution.py:409
  1491.5 147.5 %reduce-scatter.24.cloned.1.call-done = f32[16,4096]{1,0:T(8,128)} async-done(((f32[512,4096]{1,0:T(8,128)}), f32[16,4096]{1,0:T(8,128)}) %reduce-scatter.24.cloned.1.call-update) | async-done | bytes 262160 | tf_op jit(solution)/shard_map/reduce_scatter | solution.py:411
  1639.1 181.5 %reduce-scatter.26.cloned.1.call-done = f32[64,2048]{1,0:T(8,128)} async-done(((f32[2048,2048]{1,0:T(8,128)}), f32[64,2048]{1,0:T(8,128)}) %reduce-scatter.26.cloned.1.call-update) | async-done | bytes 524304 | tf_op jit(solution)/shard_map/reduce_scatter | solution.py:412
  1820.5 255.3 %reduce-scatter.20.cloned.1.call-done = f32[64,3072]{1,0:T(8,128)} async-done(((f32[2048,3072]{1,0:T(8,128)}), f32[64,3072]{1,0:T(8,128)}) %reduce-scatter.20.cloned.1.call-update) | async-done | bytes 786448 | tf_op jit(solution)/shard_map/reduce_scatter | solution.py:408
  2075.9 248.6 %reduce-scatter.30.cloned.1.call-done = f32[88,2048]{1,0:T(8,128)} async-done(((f32[2816,2048]{1,0:T(8,128)}), f32[88,2048]{1,0:T(8,128)}) %reduce-scatter.30.cloned.1.call-update) | async-done | bytes 720912 | tf_op jit(solution)/shard_map/reduce_scatter | solution.py:416
  2324.4 493.1 %reduce-scatter.28.cloned.1.call-done = f32[64,5632]{1,0:T(8,128)} async-done(((f32[2048,5632]{1,0:T(8,128)}), f32[64,5632]{1,0:T(8,128)}) %reduce-scatter.28.cloned.1.call-update) | async-done | bytes 1441808 | tf_op jit(solution)/shard_map/reduce_scatter | solution.py:415
  (322 shorter events, 156.6 us)
Async XLA Ops:
  7.2 16.1 all-gather.11.cloned.1.call-start
  7.9 115.4 %all-gather.15.cloned.1.call-start = ((), (), s32[]{:S(2)}) async-start(), calls=%async_computation.17 | async-start | bytes 6291456 | tf_op jit(solution)/shard_map/all_gather | solution.py:99
  8.7 114.6 %all-gather.13.cloned.1.call-start = ((), (), s32[]{:S(2)}) async-start(), calls=%async_computation.16 | async-start | bytes 2228224 | tf_op jit(solution)/shard_map/all_gather | solution.py:157
  11.3 16.8 copy-start.54
  13.2 173.3 %copy-start.34 = (f32[2048]{0:T(1024)}, f32[2048]{0:T(1024)S(1)}, u32[]{:S(2)}) copy-start(f32[2048]{0:T(1024)S(1)} %convert_element_type.253) | copy-start | bytes 24580
  14.4 172.1 %copy-start.52 = (f32[128]{0:T(128)}, f32[128]{0:T(128)S(1)}, u32[]{:S(2)}) copy-start(f32[128]{0:T(128)S(1)} %add_rsqrt_fusion.2) | copy-start | bytes 1540
  26.0 53.2 %copy-start.19 = (f32[128,576]{0,1:T(8,128)}, f32[128,576]{0,1:T(8,128)S(1)}, u32[]{:S(2)}) copy-start(f32[128,576]{0,1:T(8,128)S(1)} %fusion.116) | copy-start | bytes 884740
  26.1 13.8 copy-start.69
  26.9 143.3 %all-gather.17.cloned.1.call-start = ((), (), s32[]{:S(2)}) async-start(), calls=%async_computation.18 | async-start | bytes 18874368 | tf_op jit(solution)/shard_map/all_gather | solution.py:96
  27.5 223.4 %all-gather.19.cloned.1.call-start = ((), (), s32[]{:S(2)}) async-start(), calls=%async_computation.19 | async-start | bytes 12582912 | tf_op jit(solution)/shard_map/all_gather | solution.py:100
  28.1 357.1 %all-gather.25.cloned.1.call-start = ((), (), s32[]{:S(2)}) async-start(), calls=%async_computation.22 | async-start | bytes 17301504 | tf_op jit(solution)/shard_map/all_gather | solution.py:226
  39.9 392.2 %all-gather.27.cloned.1.call-start = ((), (), s32[]{:S(2)}) async-start(), calls=%async_computation.23 | async-start | bytes 8650752 | tf_op jit(solution)/shard_map/all_gather | solution.py:227
  40.6 21.7 copy-start.51
  40.7 23.6 copy-start.13
  40.7 514.6 %all-gather.21.cloned.1.call-start = ((), (), s32[]{:S(2)}) async-start(), calls=%async_computation.20 | async-start | bytes 34603008 | tf_op jit(solution)/shard_map/all_gather | solution.py:103
  41.4 37.8 %copy-start.74 = (f32[32]{0:T(128)}, f32[32]{0:T(128)S(1)}, u32[]{:S(2)}) copy-start(f32[32]{0:T(128)S(1)} %multiply_power_fusion) | copy-start | bytes 388
  43.4 26.4 copy-start.61
  44.9 24.9 copy-start.32
  46.9 208.9 %copy-start.42 = (f32[2048]{0:T(1024)}, f32[2048]{0:T(1024)S(1)}, u32[]{:S(2)}) copy-start(f32[2048]{0:T(1024)S(1)} %convert_element_type.269) | copy-start | bytes 24580
  49.6 12.0 copy-start.56
  64.2 191.8 %copy-start.36 = (bf16[2048,16]{0,1:T(8,128)(2,1)}, bf16[2048,16]{0,1:T(8,128)(2,1)S(1)}, u32[]{:S(2)}) copy-start(bf16[2048,16]{0,1:T(8,128)(2,1)S(1)} %all_gather.53) | copy-start | bytes 196612
  78.7 60.2 %copy-start.67 = (f32[128]{0:T(128)}, f32[128]{0:T(128)S(1)}, u32[]{:S(2)}) copy-start(f32[128]{0:T(128)S(1)} %fusion.150) | copy-start | bytes 1540
  79.4 114.0 %copy-start.38 = (f32[128,32]{0,1:T(8,128)}, f32[128,32]{0,1:T(8,128)S(1)}, u32[]{:S(2)}) copy-start(f32[128,32]{0,1:T(8,128)S(1)} %get-tuple-element.100) | copy-start | bytes 49156
  79.4 114.1 %copy-start.40 = (f32[128,32]{0,1:T(8,128)}, f32[128,32]{0,1:T(8,128)S(1)}, u32[]{:S(2)}) copy-start(f32[128,32]{0,1:T(8,128)S(1)} %get-tuple-element.101) | copy-start | bytes 49156
  123.3 81.6 %copy-start.25 = (bf16[2048,64]{0,1:T(8,128)(2,1)}, bf16[2048,64]{0,1:T(8,128)(2,1)S(1)}, u32[]{:S(2)}) copy-start(bf16[2048,64]{0,1:T(8,128)(2,1)S(1)} %all_gather.48) | copy-start | bytes 786436
  170.2 16.4 copy-start.1
  186.5 7.3 slice-start.1
  193.4 11.5 copy-start.8
  193.5 11.4 copy-start.28
  193.5 11.4 copy-start.30
  379.9 72.5 %all-to-all-start.2 = ((bf16[16,1,54,2048]{3,2,1,0:T(8,128)(2,1)}), bf16[16,1,54,2048]{3,2,1,0:T(8,128)(2,1)}, u32[]{:S(2)}, u32[]{:S(2)}) async-start(bf16[16,1,54,2048]{3,2,1,0:T(8,128)(2,1)} %get-tuple-element.96), calls=%async_computation.2 | async-start | bytes 7340032 | tf_op jit(solution)/shard_map/all_to_all | solution.py:269
  384.4 183.3 %all-gather.23.cloned.1.call-start = ((), (), s32[]{:S(2)}) async-start(), calls=%async_computation.21 | async-start | bytes 17301504 | tf_op jit(solution)/shard_map/all_gather | solution.py:104
  452.4 85.9 %all-to-all-start.1 = ((bf16[16,1,54,2048]{3,2,1,0:T(8,128)(2,1)}), bf16[16,1,54,2048]{3,2,1,0:T(8,128)(2,1)}, u32[]{:S(2)}, u32[]{:S(2)}) async-start(bf16[16,1,54,2048]{3,2,1,0:T(8,128)(2,1)} %convert_bitcast_fusion), calls=%async_computation.1 | async-start | bytes 7340032 | tf_op jit(solution)/shard_map/all_to_all | solution.py:238
  498.1 56.9 %copy-start.49 = (s32[1,128,6]{1,0,2:T(1,128)S(1)}, s32[1,128,6]{1,0,2:T(1,128)}, u32[]{:S(2)}) copy-start(s32[1,128,6]{1,0,2:T(1,128)} %param.18) | copy-start | bytes 9220
  498.1 56.9 %copy-start.57 = (s32[768]{0:T(1024)S(1)}, s32[768]{0:T(1024)}, u32[]{:S(2)}) copy-start(s32[768]{0:T(1024)} %copy-done.56) | copy-start | bytes 9220
  498.1 57.1 %copy-start.33 = (s32[1,128,6]{2,1,0:T(8,128)S(1)}, s32[1,128,6]{2,1,0:T(8,128)}, u32[]{:S(2)}) copy-start(s32[1,128,6]{2,1,0:T(8,128)} %copy-done.32) | copy-start | bytes 9220
  538.3 85.9 %all-to-all-start.3 = ((bf16[16,1,54,2048]{3,2,1,0:T(8,128)(2,1)}), bf16[16,1,54,2048]{3,2,1,0:T(8,128)(2,1)}, u32[]{:S(2)}, u32[]{:S(2)}) async-start(bf16[16,1,54,2048]{3,2,1,0:T(8,128)(2,1)} %fusion.55), calls=%async_computation.3 | async-start | bytes 7340032 | tf_op jit(solution)/shard_map/all_to_all | solution.py:300
  554.5 251.4 %reduce-scatter.38.cloned.1.call-start = ((), (), s32[]{:S(2)}) async-start(), calls=%async_computation.33 | async-start | bytes 557056
  555.2 12.4 copy-start.14
  555.2 12.4 copy-start.62
  577.7 14.1 copy-start.23
  679.5 15.2 copy-start.29
  679.5 15.2 copy-start.31
  697.4 264.3 %reduce-scatter.36.cloned.1.call-start = ((), (), s32[]{:S(2)}) async-start(), calls=%async_computation.32 | async-start | bytes 8912896
  721.6 422.6 %reduce-scatter.34.cloned.1.call-start = ((), (), s32[]{:S(2)}) async-start(), calls=%async_computation.31 | async-start | bytes 8912896
  744.5 539.3 %reduce-scatter.40.cloned.1.call-start = ((), (), s32[]{:S(2)}) async-start(), calls=%async_computation.34 | async-start | bytes 1081344
  745.9 580.7 %all-reduce.7.cloned.1.call-start = ((), (), s32[]{:S(2)}) async-start(), calls=%async_computation.35 | async-start | bytes 23068672
  792.9 560.6 %reduce-scatter.32.cloned.1.call-start = ((), (), s32[]{:S(2)}) async-start(), calls=%async_computation.30 | async-start | bytes 8650752 | tf_op jit(solution)/shard_map/reduce_scatter | solution.py:295
  805.6 340.0 %copy-start.20 = (f32[128,576]{0,1:T(8,128)S(1)}, f32[128,576]{0,1:T(8,128)}, u32[]{:S(2)}) copy-start(f32[128,576]{0,1:T(8,128)} %copy-done.19) | copy-start | bytes 884740
  805.6 340.0 %copy-start.55 = (f32[2,1,256]{2,1,0:T(1,128)S(1)}, f32[2,1,256]{2,1,0:T(1,128)}, u32[]{:S(2)}) copy-start(f32[2,1,256]{2,1,0:T(1,128)} %copy-done.54) | copy-start | bytes 6148
  805.6 340.0 %copy-start.70 = (f32[128]{0:T(128)S(1)}, f32[128]{0:T(128)}, u32[]{:S(2)}) copy-start(f32[128]{0:T(128)} %copy-done.69) | copy-start | bytes 1540
  805.7 344.9 %copy-start.2 = (bf16[1,128,2048]{2,1,0:T(8,128)(2,1)S(1)}, bf16[1,128,2048]{2,1,0:T(8,128)(2,1)}, u32[]{:S(2)}) copy-start(bf16[1,128,2048]{2,1,0:T(8,128)(2,1)} %param.16) | copy-start | bytes 1572868
  805.7 344.9 %copy-start.35 = (f32[2048]{0:T(1024)S(1)}, f32[2048]{0:T(1024)}, u32[]{:S(2)}) copy-start(f32[2048]{0:T(1024)} %copy-done.34) | copy-start | bytes 24580
  805.7 685.9 %reduce-scatter.22.cloned.1.call-start = ((), (), s32[]{:S(2)}) async-start(), calls=%async_computation.25 | async-start | bytes 5406720 | tf_op jit(solution)/shard_map/reduce_scatter | solution.py:409
  1154.6 484.4 %reduce-scatter.24.cloned.1.call-start = ((), (), s32[]{:S(2)}) async-start(), calls=%async_computation.26 | async-start | bytes 8650752 | tf_op jit(solution)/shard_map/reduce_scatter | solution.py:411
  1159.2 661.3 %reduce-scatter.26.cloned.1.call-start = ((), (), s32[]{:S(2)}) async-start(), calls=%async_computation.27 | async-start | bytes 17301504 | tf_op jit(solution)/shard_map/reduce_scatter | solution.py:412
  1168.8 907.1 %reduce-scatter.20.cloned.1.call-start = ((), (), s32[]{:S(2)}) async-start(), calls=%async_computation.24 | async-start | bytes 25952256 | tf_op jit(solution)/shard_map/reduce_scatter | solution.py:408
  1200.1 1124.3 %reduce-scatter.30.cloned.1.call-start = ((), (), s32[]{:S(2)}) async-start(), calls=%async_computation.29 | async-start | bytes 23789568 | tf_op jit(solution)/shard_map/reduce_scatter | solution.py:416
  1211.7 1605.9 %reduce-scatter.28.cloned.1.call-start = ((), (), s32[]{:S(2)}) async-start(), calls=%async_computation.28 | async-start | bytes 47579136 | tf_op jit(solution)/shard_map/reduce_scatter | solution.py:415
  1233.1 10.1 copy-start.5
  1233.1 10.1 copy-start.16
  1233.1 10.1 copy-start.22
  1353.5 7.2 copy-start.50
  1353.5 7.2 copy-start.72
  (42 other events, 155.0 us)
Sparse Core Ops, SparseCore 0:
  9.6 13.6 all-gather.10
  24.8 14.8 all-gather.14
  43.0 67.4 all-gather.12
  111.9 23.0 all-gather.16
  136.3 21.0 all-gather.18
  159.3 25.0 all-gather.24
  186.0 17.1 all-gather.26
  204.7 39.0 all-gather.20
  386.8 25.0 all-gather.22
  697.5 87.4 reduce-scatter.37
  787.4 174.2 reduce-scatter.35
  963.9 180.2 reduce-scatter.33
  1146.6 137.2 reduce-scatter.39
  1286.1 40.5 all-reduce.6
  1329.4 15.0 reduce-scatter.31
  1347.3 144.2 reduce-scatter.21
  1494.4 144.6 reduce-scatter.23
  1641.9 178.5 reduce-scatter.25
  1828.7 247.1 reduce-scatter.19
  2078.6 245.7 reduce-scatter.29
  2327.3 490.1 reduce-scatter.27
where the time goes:
time: 2840 us; the launch traced here: 2820 us
  waiting for transfers between devices  1890 us (67%)
  matrix products  344 us (12%)
  local copies, waits for them, and re-layouts  286 us (10%)
  blocking collectives  174 us (6%)
  other arithmetic  74.2 us (3%)
  starting transfers between devices  39.9 us (1%)
    reduce_scatter x1, waiting for transfers between devices, per_device(): lax.psum_scatter(grad_shared_in, ('expert', 'shard'), scatter_dimension=0...  493 us
    unnamed x26, waiting for transfers between devices  415 us
    reduce_scatter x1, waiting for transfers between devices, per_device(): lax.psum_scatter(grad_query, ('expert', 'shard'), scatter_dimension=0, ti...  255 us
    reduce_scatter x1, waiting for transfers between devices, per_device(): lax.psum_scatter(grad_shared_out, ('expert', 'shard'), scatter_dimension=...  249 us
    reduce_scatter x1, waiting for transfers between devices, per_device(): lax.psum_scatter(grad_output, ('expert', 'shard'), scatter_dimension=0, t...  181 us
    reduce_scatter x1, waiting for transfers between devices, per_device(): lax.psum_scatter(grad_expand, ('expert', 'shard'), scatter_dimension=0, t...  148 us
    unnamed x181, local copies, waits for them, and re-layouts  101 us
    reduce_scatter x1, waiting for transfers between devices, per_device(): lax.psum_scatter(grad_latent_weight, ('expert', 'shard'), scatter_dimensi...  85.4 us
  transfers between devices with their start and end apart: 24, of which 14 were waited for; matrix products, arithmetic and copies ran while one was open for 22% of the time, Pallas kernels for 0%

commit v1 on v0

v1 whole, which is shorter than its diff:
```python
import functools

import jax
import jax.numpy as jnp
from jax import lax
from jax.experimental import pallas as pl
from jax.experimental.pallas import tpu as pltpu
from jax.sharding import PartitionSpec as P

HEADS = 16
HEAD = 128
ROPE = 64
VHEAD = 128
RANK = 512
FF_S = 2816
SLOT = 2048

EPS = 1e-06
MASK_FILL = -1e30
BF = jnp.bfloat16
F32 = jnp.float32


def layout(lengths_slot, slot_index):
    first_len = lengths_slot[0]
    second_end = first_len + lengths_slot[1]
    segment = (slot_index >= first_len).astype(jnp.int32) + (slot_index >= second_end).astype(
        jnp.int32
    )
    seq_start = jnp.where(segment == 0, 0, jnp.where(segment == 1, first_len, second_end))
    return (segment, slot_index - seq_start, slot_index < second_end)


def rope_tables(positions):
    half_width = ROPE // 2
    inverse = 10000.0 ** (-jnp.arange(half_width, dtype=F32) / half_width)
    angles = positions.astype(F32)[:, None] * inverse[None, :]
    return (jnp.cos(angles), jnp.sin(angles))


def rotate(values, cosine, sine_table):
    half_width = values.shape[-1] // 2
    first_half = values[..., :half_width]
    second_half = values[..., half_width:]
    return jnp.concatenate(
        [
            first_half * cosine - second_half * sine_table,
            second_half * cosine + first_half * sine_table,
        ],
        -1,
    )


def rotate_back(grads_in, cosine, sine_table):
    return rotate(grads_in, cosine, -sine_table)


def silu_parts(gate_in):
    sigma = jax.nn.sigmoid(gate_in)
    return (gate_in * sigma, sigma * (1.0 + gate_in * (1.0 - sigma)))


def rms_scale(values):
    return lax.rsqrt(jnp.mean(values * values, -1, keepdims=True) + EPS)


def norm_back(grad_in, normed, inverse):
    return inverse * (grad_in - normed * jnp.mean(grad_in * normed, -1, keepdims=True))


def dot(left, right):
    return jnp.dot(left, right, preferred_element_type=F32)


def dot_t(left, right):
    return lax.dot_general(left, right, (((1,), (1,)), ((), ())), preferred_element_type=F32)


def t_dot(left, right):
    return lax.dot_general(left, right, (((0,), (0,)), ((), ())), preferred_element_type=F32)


def cross(values, bit):
    count = lax.axis_size("expert")
    return lax.ppermute(values, "expert", [(i, i ^ bit) for i in range(count)])


def swap(values):
    return lax.ppermute(values, "shard", [(0, 1), (1, 0)])


def whole_rows(weight):
    if lax.axis_size("shard") != 2:
        return lax.all_gather(weight, "shard", axis=0, tiled=True)
    other = swap(weight)
    first = lax.axis_index("shard") == 0
    return jnp.where(
        first, jnp.concatenate([weight, other], 0), jnp.concatenate([other, weight], 0)
    )


def row_blocks(weight):
    count = lax.axis_size("shard")
    if count == 2:
        own = lax.axis_index("shard")
        return [(own, weight), (1 - own, swap(weight))]
    blocks = lax.all_gather(weight, "shard", axis=0)
    return [(j, blocks[j]) for j in range(count)]


def times(values, blocks):
    rows = blocks[0][1].shape[0]
    return sum(
        dot(lax.dynamic_slice_in_dim(values, place * rows, rows, 1), block)
        for place, block in blocks
    )


def times_back(grads, blocks):
    pieces = [dot_t(grads, block) for _, block in blocks]
    if len(pieces) != 2:
        return jnp.concatenate(pieces, 1)
    first = lax.axis_index("shard") == 0
    return jnp.where(first, jnp.concatenate(pieces, 1), jnp.concatenate(pieces[::-1], 1))


def group_rows(values):
    if lax.axis_size("shard") == 2:
        return jnp.concatenate([values, swap(values)], 0)
    return lax.all_gather(values, "shard", axis=0, tiled=True)


def collect(values, bits):
    places = [0]
    for bit in bits:
        values = jnp.concatenate([values, cross(values, bit)], 0)
        places = places + [place ^ bit for place in places]
    return values, places


def fold(pieces, bits, rows):
    count = rows << len(bits)
    for bit in bits:
        count = count // 2
        sent = sum(p[count:].astype(F32) for p in pieces).astype(BF)
        pieces = [p[:count] for p in pieces] + [cross(sent, bit)]
    return sum(p.astype(F32) for p in pieces)


def fold_order(bits):
    places = [0]
    for bit in reversed(bits):
        places = places + [place ^ bit for place in places]
    return places


def differing(blocks, bits):
    count = len(bits)
    here = lax.axis_index("expert")
    blocks = blocks.reshape((2,) * count + blocks.shape[1:])
    for k in range(count):
        odd = (here >> (count - 1 - k)) % 2 == 1
        blocks = jnp.where(odd, jnp.flip(blocks, k), blocks)
    axes = [count - bit.bit_length() for bit in bits]
    blocks = blocks.transpose(axes + list(range(count, blocks.ndim)))
    return blocks.reshape((1 << count,) + blocks.shape[count:])


def gradient_kernel(rows, order_ref, left_ref, right_ref, kept_ref, sent_ref, picked_ref):
    count = picked_ref.shape[0] // rows

    @pl.when(pl.program_id(0) == 0)
    def _():
        for j in range(count):
            start = pl.multiple_of(order_ref[j] * rows, rows)
            picked_ref[j * rows : (j + 1) * rows, :] = left_ref[pl.ds(start, rows), :]

    half = kept_ref.shape[0]
    right = right_ref[...]
    kept_ref[...] = dot(picked_ref[:half, :].astype(BF), right).astype(kept_ref.dtype)
    sent_ref[...] = dot(picked_ref[half:, :].astype(BF), right).astype(sent_ref.dtype)


def gradient_halves(left, right, bits):
    experts, shards = lax.axis_size("expert"), lax.axis_size("shard")
    tokens, rows_all = left.shape
    columns = right.shape[1]
    rows = rows_all // (experts * shards)
    blocks = (
        lax.axis_index("expert") ^ jnp.array(fold_order(bits), jnp.int32)
    ) * shards + lax.axis_index("shard")
    left = left.T
    half = rows * experts // 2
    if rows % 8:
        picked = lax.dynamic_index_in_dim(
            left.reshape(experts, shards, rows, tokens), lax.axis_index("shard"), 1, keepdims=False
        )
        picked = differing(picked, bits).reshape(-1, tokens)
        product = dot(picked, right).astype(BF)
        return product[:half], product[half:]
    if rows % 16:
        left = left.astype(F32)
    tile = next(t for t in (512, 384, 256, 128, columns) if columns % t == 0)
    return pl.pallas_call(
        functools.partial(gradient_kernel, rows),
        grid_spec=pltpu.PrefetchScalarGridSpec(
            num_scalar_prefetch=1,
            grid=(columns // tile,),
            in_specs=[
                pl.BlockSpec((rows_all, tokens), lambda i, order: (0, 0)),
                pl.BlockSpec((tokens, tile), lambda i, order: (0, i)),
            ],
            out_specs=[
                pl.BlockSpec((half, tile), lambda i, order: (0, i)),
                pl.BlockSpec((half, tile), lambda i, order: (0, i)),
            ],
            scratch_shapes=[pltpu.VMEM((rows * experts, tokens), left.dtype)],
        ),
        out_shape=[jax.ShapeDtypeStruct((half, columns), BF)] * 2,
        compiler_params=pltpu.CompilerParams(vmem_limit_bytes=40 << 20),
        cost_estimate=pl.CostEstimate(
            flops=4 * half * tokens * columns,
            bytes_accessed=4 * half * columns + 2 * tokens * (rows_all + columns),
            transcendentals=0,
        ),
    )(blocks, left, right)


def reduce_product(left, right, bits):
    kept, sent = gradient_halves(left, right, bits)
    rows = 2 * kept.shape[0] >> len(bits)
    arrived = cross(sent, bits[0])
    return fold([kept, arrived], bits[1:], rows)


def reduce_partial(partial, bits):
    experts, shards = lax.axis_size("expert"), lax.axis_size("shard")
    rows = partial.shape[0] // (experts * shards)
    if shards != 2:
        return lax.psum_scatter(partial, ("expert", "shard"), scatter_dimension=0, tiled=True)
    own = lax.axis_index("shard")
    blocks = partial.reshape(experts, 2, rows, partial.shape[1])
    kept = lax.dynamic_index_in_dim(blocks, own, 1, keepdims=False)
    sent = lax.dynamic_index_in_dim(blocks, 1 - own, 1, keepdims=False)
    total = (kept.astype(F32) + swap(sent).astype(F32)).astype(partial.dtype)
    return fold([differing(total, bits).reshape(experts * rows, -1)], bits, rows)


def per_device(
    tokens,
    lengths,
    routes,
    attn_gain,
    query_weight,
    latent_weight,
    latent_gain,
    expand_weight,
    output_weight,
    ffn_gain,
    router_weight,
    shared_in,
    shared_out,
    expert_in,
    expert_out,
    cotangent,
):
    local_rows = tokens.shape[1]
    model_width = tokens.shape[2]
    owners, shards = lax.axis_size("expert"), lax.axis_size("shard")
    experts_all = router_weight.shape[1]
    assert experts_all == owners
    topk_count = routes.shape[2]
    capacity = max(2, 9 * local_rows * topk_count // (8 * experts_all))
    capacity = -(-capacity // 8) * 8
    score_scale = (HEAD + ROPE) ** (-0.5)
    here = lax.axis_index("expert")
    bits = [1 << k for k in range(owners.bit_length() - 1)]
    first_x = tuple(bits)
    first_y = tuple(bits[1:2] + bits[:1] + bits[2:])

    query_blocks = row_blocks(query_weight)
    latent_blocks = row_blocks(latent_weight)
    gains = jnp.concatenate([attn_gain, ffn_gain, latent_gain])[None]
    gains = (
        jnp.where(
            lax.axis_index("shard") == 0,
            jnp.concatenate([gains, swap(gains)], 0),
            jnp.concatenate([swap(gains), gains], 0),
        )
        if shards == 2
        else lax.all_gather(gains, "shard", axis=0, tiled=True)
    ).astype(F32)
    cut = attn_gain.shape[0]
    gain_attn = gains[:, :cut].reshape(-1)
    gain_ffn = gains[:, cut : 2 * cut].reshape(-1)
    gain_latent = gains[:, 2 * cut :].reshape(-1)
    expand = whole_rows(expand_weight).reshape(RANK, HEADS, HEAD + VHEAD)
    expand_key, expand_value = expand[..., :HEAD], expand[..., HEAD:]
    output_blocks = row_blocks(output_weight)
    router = whole_rows(router_weight)
    shared_out_blocks = row_blocks(shared_out)
    shared_in_blocks = row_blocks(shared_in)
    expert_out_blocks = row_blocks(expert_out[0])
    gate_blocks = row_blocks(expert_in[0, :, 0, :])
    up_blocks = row_blocks(expert_in[0, :, 1, :])

    here_index = here * local_rows + jnp.arange(local_rows, dtype=jnp.int32)
    query_segment, query_position, query_valid = layout(lengths[0], here_index)
    cosine, sine_table = rope_tables(query_position)
    live_rows = query_valid.astype(F32)[:, None]
    grad_out = cotangent[0].astype(F32) * live_rows
    grad_out_low = grad_out.astype(BF)

    expert_ids = jnp.arange(experts_all, dtype=jnp.int32)
    member = jnp.any(routes[0][:, :, None] == expert_ids[None, None, :], 1)
    token_ids = jnp.arange(local_rows, dtype=jnp.int32)
    earlier = (token_ids[None, :] < token_ids[:, None]).astype(BF)
    rank = dot(earlier, member.astype(BF)).astype(jnp.int32)
    place_ids = jnp.arange(capacity, dtype=jnp.int32)
    spread = (
        member.T[:, None, :] & (rank.T[:, None, :] == place_ids[None, :, None])
    ).reshape(experts_all * capacity, local_rows).astype(BF)

    def exchange(rows):
        return lax.all_to_all(
            rows.reshape(owners, capacity, model_width),
            "expert",
            split_axis=0,
            concat_axis=0,
            tiled=True,
        ).reshape(owners * capacity, model_width)

    inputs = tokens[0].astype(F32)
    inverse_attn = rms_scale(inputs)
    normed_attn = inputs * inverse_attn
    attn_in = (normed_attn * gain_attn).astype(BF)
    latent_raw = times(attn_in, latent_blocks)
    latent = latent_raw[:, :RANK]
    inverse_latent = rms_scale(latent)
    normed_latent = latent * inverse_latent
    latent_in = (normed_latent * gain_latent).astype(BF)
    key_rope = rotate(latent_raw[:, RANK:], cosine, sine_table).astype(BF)
    own_keys = jnp.concatenate([latent_in, key_rope], -1)
    part = local_rows // 2
    collect_bits = (tuple(reversed(first_x)), tuple(reversed(first_y)))
    keys, key_index = [], []
    for k in range(2):
        gathered, places = collect(own_keys[k * part : (k + 1) * part], collect_bits[k])
        keys.append(gathered)
        key_index.append(
            (
                (here ^ jnp.array(places, jnp.int32))[:, None] * local_rows
                + k * part
                + jnp.arange(part, dtype=jnp.int32)[None, :]
            ).reshape(-1)
        )
    keys = jnp.concatenate(keys, 0)
    key_index = jnp.concatenate(key_index)

    received_grads = exchange(dot(spread, grad_out_low).astype(BF))

    query_raw = times(attn_in, query_blocks).reshape(local_rows, HEADS, HEAD + ROPE)
    query_nope = query_raw[..., :HEAD].astype(BF)
    query_rope = rotate(
        query_raw[..., HEAD:], cosine[:, None, :], sine_table[:, None, :]
    ).astype(BF)
    query_latent = jnp.einsum(
        "qhc,rhc->hqr", query_nope, expand_key, preferred_element_type=F32
    ).astype(BF)
    queries = jnp.concatenate([query_latent, query_rope.transpose(1, 0, 2)], -1).reshape(
        HEADS * local_rows, RANK + ROPE
    )
    key_segment = layout(lengths[0], key_index)[0]
    allowed = (query_segment[:, None] == key_segment[None, :]) & (
        key_index[None, :] <= here_index[:, None]
    )
    scores = dot_t(queries, keys).reshape(HEADS, local_rows, SLOT)
    scores = jnp.where(allowed[None], scores * score_scale, MASK_FILL)
    shifted = jnp.exp(scores - jnp.max(scores, -1, keepdims=True))
    attention = (shifted / jnp.sum(shifted, -1, keepdims=True)).reshape(HEADS * local_rows, SLOT)
    attention_low = attention.astype(BF)
    mixed_latent = dot(attention_low, keys[:, :RANK]).astype(BF).reshape(HEADS, local_rows, RANK)
    mixed_heads = (
        jnp.einsum("hqr,rhv->qhv", mixed_latent, expand_value, preferred_element_type=F32)
        .astype(BF)
        .reshape(local_rows, HEADS * VHEAD)
    )
    hidden_state = inputs + times(mixed_heads, output_blocks)
    inverse_ffn = rms_scale(hidden_state)
    normed_ffn = hidden_state * inverse_ffn
    ffn_in = (normed_ffn * gain_ffn).astype(BF)

    received = exchange(dot(spread, ffn_in).astype(BF))
    slopes_in = [dot_t(received_grads, block) for _, block in expert_out_blocks]
    row_logits = dot(received, router)
    row_exp = jnp.exp(row_logits - jnp.max(row_logits, -1, keepdims=True))
    row_probs = row_exp / jnp.sum(row_exp, -1, keepdims=True)
    own_expert = (expert_ids == here).astype(F32)[None, :]
    row_gate = jnp.sum(row_probs * own_expert, -1, keepdims=True)
    row_gate_grad = 0.0
    hidden, grads_gate, grads_up = [], [], []
    for j in range(shards):
        gate = dot(received, gate_blocks[j][1])
        up = dot(received, up_blocks[j][1])
        act, slope = silu_parts(gate)
        units = (act * up).astype(BF)
        row_gate_grad = row_gate_grad + jnp.sum(slopes_in[j] * units.astype(F32), -1, keepdims=True)
        grad_units = row_gate * slopes_in[j]
        hidden.append(units)
        grads_gate.append((grad_units * up * slope).astype(BF))
        grads_up.append((grad_units * act).astype(BF))
    row_grad_logits = (row_probs * (own_expert - row_gate) * row_gate_grad).astype(BF)
    row_grads = dot_t(row_grad_logits, router)
    for j in range(shards):
        row_grads = row_grads + dot_t(grads_gate[j], gate_blocks[j][1])
        row_grads = row_grads + dot_t(grads_up[j], up_blocks[j][1])
    returned_grads = exchange(row_grads.astype(BF))
    row_out = sum(dot(hidden[j], expert_out_blocks[j][1]) for j in range(shards))
    returned = exchange((row_gate * row_out).astype(BF))
    routed = t_dot(spread, returned)
    grad_routed = t_dot(spread, returned_grads)
    weighted_grads = (row_gate * received_grads.astype(F32)).astype(BF)
    grad_expert_parts = [
        (
            t_dot(received, grads_gate[j]),
            t_dot(received, grads_up[j]),
            t_dot(hidden[j], weighted_grads),
        )
        for j in range(shards)
    ]
    if shards == 2:
        own_parts, other_parts = grad_expert_parts
        own_parts = [
            own + swap(other.astype(BF)).astype(F32)
            for own, other in zip(own_parts, other_parts)
        ]
    else:
        own_parts = [
            lax.psum_scatter(
                jnp.stack([p[k].astype(BF) for p in grad_expert_parts]), "shard", tiled=True
            )[0].astype(F32)
            for k in range(3)
        ]
    grad_expert_in = jnp.stack(own_parts[:2], 1)[None]
    grad_expert_out = own_parts[2][None]
    grad_router = t_dot(received, row_grad_logits)

    shared_both = times(ffn_in, shared_in_blocks)
    shared_act, shared_slope = silu_parts(shared_both[:, :FF_S])
    shared_up = shared_both[:, FF_S:]
    shared_hidden = (shared_act * shared_up).astype(BF)
    shared_result = times(shared_hidden, shared_out_blocks)
    block_result = hidden_state + shared_result + routed
    grad_shared_hidden = times_back(grad_out_low, shared_out_blocks)
    grad_shared_gate = (grad_shared_hidden * shared_up * shared_slope).astype(BF)
    grad_shared_up = (grad_shared_hidden * shared_act).astype(BF)
    grad_shared_both = jnp.concatenate([grad_shared_gate, grad_shared_up], -1)
    group_ffn_in = group_rows(ffn_in)
    grad_shared_out = reduce_product(
        group_rows(shared_hidden), group_rows(grad_out_low), first_x
    )
    grad_shared_in = jnp.concatenate(
        [
            reduce_product(group_ffn_in, group_rows(grad_shared_gate), first_y),
            reduce_product(group_ffn_in, group_rows(grad_shared_up), first_x),
        ],
        -1,
    )
    grad_ffn_in = times_back(grad_shared_both, shared_in_blocks) + grad_routed
    grad_gain_ffn = jnp.sum(grad_ffn_in * normed_ffn, 0)
    grad_hidden_state = grad_out + norm_back(grad_ffn_in * gain_ffn, normed_ffn, inverse_ffn)

    grad_attn_out = grad_hidden_state.astype(BF)
    grad_output = reduce_product(group_rows(mixed_heads), group_rows(grad_attn_out), first_y)
    grad_mixed = times_back(grad_attn_out, output_blocks).astype(BF).reshape(
        local_rows, HEADS, VHEAD
    )
    grad_mixed_latent = (
        jnp.einsum("qhv,rhv->hqr", grad_mixed, expand_value, preferred_element_type=F32)
        .astype(BF)
        .reshape(HEADS * local_rows, RANK)
    )
    grad_attention = dot_t(grad_mixed_latent, keys[:, :RANK])
    grad_scores = (
        attention
        * (grad_attention - jnp.sum(attention * grad_attention, -1, keepdims=True))
        * score_scale
    ).astype(BF)
    grad_queries = dot(grad_scores, keys).reshape(HEADS, local_rows, RANK + ROPE)
    grad_query_latent = grad_queries[..., :RANK].astype(BF)
    grad_query_rope = grad_queries[..., RANK:].transpose(1, 0, 2)
    grad_keys = t_dot(grad_scores, queries)
    grad_keys = jnp.concatenate(
        [
            grad_keys[:, :RANK] + t_dot(attention_low, grad_mixed_latent),
            grad_keys[:, RANK:],
        ],
        -1,
    ).astype(BF)
    slot_half = SLOT // 2
    grad_own_keys = jnp.concatenate(
        [
            fold(
                [grad_keys[k * slot_half : (k + 1) * slot_half]],
                tuple(reversed(collect_bits[k])),
                part,
            )
            for k in range(2)
        ],
        0,
    )
    grad_expand = jnp.concatenate(
        [
            jnp.einsum("hqr,qhc->rhc", grad_query_latent, query_nope, preferred_element_type=F32),
            jnp.einsum("hqr,qhv->rhv", mixed_latent, grad_mixed, preferred_element_type=F32),
        ],
        -1,
    ).reshape(RANK, HEADS * (HEAD + VHEAD))
    grad_expand = reduce_partial(grad_expand.astype(BF), first_x).astype(F32)
    grad_latent_in = grad_own_keys[:, :RANK]
    grad_gain_latent = jnp.sum(grad_latent_in * normed_latent, 0)
    grad_latent = norm_back(grad_latent_in * gain_latent, normed_latent, inverse_latent)
    grad_latent_raw = jnp.concatenate(
        [grad_latent, rotate_back(grad_own_keys[:, RANK:], cosine, sine_table)], -1
    ).astype(BF)
    grad_query_nope = jnp.einsum(
        "hqr,rhc->qhc", grad_query_latent, expand_key, preferred_element_type=F32
    )
    grad_query_raw = (
        jnp.concatenate(
            [
                grad_query_nope,
                rotate_back(grad_query_rope, cosine[:, None, :], sine_table[:, None, :]),
            ],
            -1,
        )
        .reshape(local_rows, HEADS * (HEAD + ROPE))
        .astype(BF)
    )
    group_attn_in = group_rows(attn_in)
    group_grad_query = group_rows(grad_query_raw)
    query_half = group_grad_query.shape[1] // 2
    grad_query = jnp.concatenate(
        [
            reduce_product(group_attn_in, group_grad_query[:, :query_half], first_x),
            reduce_product(group_attn_in, group_grad_query[:, query_half:], first_y),
        ],
        -1,
    )
    grad_latent_weight = reduce_product(group_attn_in, group_rows(grad_latent_raw), first_y)
    grad_attn_in = times_back(grad_latent_raw, latent_blocks) + times_back(
        grad_query_raw, query_blocks
    )
    grad_gain_attn = jnp.sum(grad_attn_in * normed_attn, 0)
    tokens_grad = grad_hidden_state + norm_back(grad_attn_in * gain_attn, normed_attn, inverse_attn)

    devices = owners * shards
    rows = model_width // devices
    latent_column = jnp.pad(
        grad_gain_latent.reshape(devices, -1), ((0, 0), (0, rows - RANK // devices))
    ).reshape(-1, 1)
    small = jnp.concatenate(
        [grad_router, grad_gain_attn[:, None], grad_gain_ffn[:, None], latent_column], 1
    )
    small = reduce_partial(small, first_x).astype(F32)
    return (
        block_result.astype(BF)[None],
        tokens_grad.astype(BF)[None],
        small[:, experts_all],
        grad_query,
        grad_latent_weight,
        small[: RANK // devices, experts_all + 2],
        grad_expand,
        grad_output,
        small[:, experts_all + 1],
        small[:, :experts_all],
        grad_shared_in,
        grad_shared_out,
        grad_expert_in,
        grad_expert_out,
    )


def solution(mesh):
    return jax.shard_map(
        per_device,
        mesh=mesh,
        in_specs=(
            P("shard", "expert", None),
            P("shard", None),
            P("shard", "expert", None),
            P("shard"),
            P("shard", None),
            P("shard", None),
            P("shard"),
            P("shard", None),
            P("shard", None),
            P("shard"),
            P("shard", None),
            P("shard", None),
            P("shard", None),
            P("expert", None, None, "shard"),
            P("expert", "shard", None),
            P("shard", "expert", None),
        ),
        out_specs=(
            P("shard", "expert", None),
            P("shard", "expert", None),
            P(("expert", "shard")),
            P(("expert", "shard"), None),
            P(("expert", "shard"), None),
            P(("expert", "shard")),
            P(("expert", "shard"), None),
            P(("expert", "shard"), None),
            P(("expert", "shard")),
            P(("expert", "shard"), None),
            P(("expert", "shard"), None),
            P(("expert", "shard"), None),
            P("expert", None, None, "shard"),
            P("expert", "shard", None),
        ),
        check_vma=False,
    )
```

time: 2840 us -> 1020 us (0.36)
  waiting for transfers between devices: 1890 us -> 223 us
  blocking collectives: 174 us -> 0 us
  local copies, waits for them, and re-layouts: 286 us -> 168 us
  other arithmetic: 74.2 us -> 156 us
  starting transfers between devices: 39.9 us -> 111 us
    reduce_scatter x7 -> x0, waiting for transfers between devices: 1410 us -> none  [the longest x1 493 us: per_device(): lax.psum_scatter(grad_shared_in, ('expert', 'shard'), scatter_dimension=0...]
    unnamed x26 -> x0, waiting for transfers between devices: 415 us -> none
    ppermute x0 -> x78, waiting for transfers between devices: none -> 223 us  [the longest x52 223 us: cross(): return lax.ppermute(values, 'expert', [(i, i ^ bit) for i in range(count)])]
    all_to_all x1 -> x0, blocking collectives: 81.6 us -> none  [per_device(): lax.all_to_all(send_rows.reshape(owners, expert_local, capacity, model_wi...]
    ppermute x0 -> x78, starting transfers between devices: none -> 80.3 us  [the longest x52 74.2 us: cross(): return lax.ppermute(values, 'expert', [(i, i ^ bit) for i in range(count)])]
    unnamed x181 -> x264, local copies, waits for them, and re-layouts: 101 us -> 46.1 us
    all_to_all x3 -> x4, waiting for transfers between devices: 52.7 us -> 0.01 us  [exchange(): lax.all_to_all(rows.reshape(owners, capacity, model_width), 'expert', spl...]
    all_gather x5 -> x0, blocking collectives: 51.4 us -> none  [the longest x1 43.9 us: per_device(): lax.all_gather(key_rope, 'expert', axis=0, tiled=True)]
  transfers between devices with their start and end apart: 24 -> 82, of which waited for: 14 -> 28; matrix products, arithmetic and copies ran while one was open for 22% -> 62% of each run, Pallas kernels for 0% -> 2%
where the time goes in v1:
time: 1020 us; the launch traced here: 1010 us
  matrix products  321 us (31%)
  waiting for transfers between devices  223 us (22%)
  local copies, waits for them, and re-layouts  168 us (16%)
  other arithmetic  156 us (15%)
  starting transfers between devices  111 us (11%)
  Pallas kernels  25.2 us (2%)
    ppermute x52, waiting for transfers between devices, cross(): return lax.ppermute(values, 'expert', [(i, i ^ bit) for i in range(count)])  223 us
    dot_general x22, matrix products, dot(): return jnp.dot(left, right, preferred_element_type=F32)  116 us
    dot_general x17, matrix products, dot_t(): lax.dot_general(left, right, (((1,), (1,)), ((), ())), preferred_element_...  116 us
    ppermute x52, starting transfers between devices, cross(): return lax.ppermute(values, 'expert', [(i, i ^ bit) for i in range(count)])  74.2 us
    dot_general x11, matrix products, t_dot(): lax.dot_general(left, right, (((0,), (0,)), ((), ())), preferred_element_...  68.7 us
    unnamed x264, local copies, waits for them, and re-layouts  46.1 us
    convert_element_type x31, other arithmetic, fold(): sent = sum((p[count:].astype(F32) for p in pieces)).astype(BF)  31.8 us
    all_to_all x4, starting transfers between devices, exchange(): lax.all_to_all(rows.reshape(owners, capacity, model_width), 'expert', spl...  30.2 us
  transfers between devices with their start and end apart: 82, of which 28 were waited for; matrix products, arithmetic and copies ran while one was open for 62% of the time, Pallas kernels for 2%

profile of v1, /device:TPU:0, one launch (start us, length us, event | category | flops | bytes accessed | tf_op | source)
XLA Modules:
  0.0 1009.5 jit_solution(3684807675163882092)
XLA Ops:
  62.4 5.9 maximum_select_fusion
  73.8 5.4 convolution_add_fusion.1
  90.2 10.2 %fusion.23 = f32[16,128,2048]{2,1,0:T(8,128)} fusion(bf16[2048,576]{0,1:T(8,128)(2,1)S(1)} %copy-done.33, bf16[16,128,64]{2,1,0:T(8,128)(2,1)S(1)} %maximum_bitcast_fusion.4, bf16[16,128,512]{2,1,0:T(8,128)(2,1)S(1)} %convolution_convert_fusion.6), kind=kOutput, calls=%fused_computation.76 | convolution fusion | flops 4836556800 | bytes 21495808 | tf_op jit(solution)/shard_map/dot_general | solution.py:76
  100.4 21.0 %fusion.182 = (f32[16,128]{1,0:T(8,128)S(1)}, f32[16,128,2048]{2,1,0:T(8,128)}) fusion(f32[16,128,2048]{2,1,0:T(8,128)} %fusion.23, pred[128,2048]{1,0:T(8,128)(4,1)S(1)} %copy-done.78), kind=kOutput, calls=%fused_computation.397 | output fusion | flops 25167872 | bytes 33824768 | tf_op jit(solution)/shard_map/sub | solution.py:379
  121.4 6.8 broadcast_divide_fusion
  128.3 8.9 fusion.13
  149.2 6.1 all-to-all-start
  156.1 5.2 fusion.186
  161.3 6.2 slice_bitcast_fusion.1
  175.7 5.3 fusion.187
  181.6 10.5 %fusion.92 = f32[128,5632]{0,1:T(8,128)} fusion(bf16[1024,5632]{1,0:T(8,128)(2,1)} %param.36, bf16[128,2048]{1,0:T(8,128)(2,1)S(1)} %multiply_convert_fusion.16, s32[]{:T(128)S(6)} %select_n.187), kind=kOutput, calls=%fused_computation.240 | convolution fusion | flops 1476395008 | bytes 14680068 | tf_op jit(solution)/shard_map/dot_general | solution.py:72
  192.0 17.7 %copy.391 = f32[2048,2048]{0,1:T(8,128)} copy(f32[2048,2048]{1,0:T(8,128)} %bitcast.272) | data formatting | bytes 33554432 | tf_op jit(solution)/shard_map/reshape | solution.py:380
  220.1 9.7 convolution_add_fusion
  232.1 11.6 %all-to-all-start.2 = ((bf16[16,56,2048]{2,1,0:T(8,128)(2,1)}), bf16[16,56,2048]{2,1,0:T(8,128)(2,1)}, u32[]{:S(2)}, u32[]{:S(2)}) async-start(bf16[16,56,2048]{2,1,0:T(8,128)(2,1)} %bitcast.280), calls=%async_computation.2 | async-start | bytes 7340032 | tf_op jit(solution)/shard_map/all_to_all | solution.py:325
  243.7 9.1 fusion.67
  252.8 9.1 fusion.66
  291.7 6.8 shard_map.348
  300.1 6.4 copy.410
  310.2 7.7 fusion.171
  317.8 6.7 fusion.169
  326.4 7.6 fusion.185
  334.0 7.6 fusion.184
  341.6 8.7 multiply_reduce_fusion.1
  350.3 7.7 convolution_convert_fusion.4
  358.0 6.7 convolution_convert_fusion.2
  365.2 8.3 multiply_reduce_fusion.2
  373.5 5.2 fusion.168
  378.7 5.4 fusion.170
  384.1 7.9 fusion.188
  394.1 14.4 %add_convert_fusion = bf16[896,2048]{1,0:T(8,128)(2,1)} fusion(f32[896,2048]{1,0:T(8,128)} %fusion.188, f32[896,2048]{1,0:T(8,128)} %fusion.170, f32[896,2048]{1,0:T(8,128)S(1)} %fusion.135, f32[896,2048]{1,0:T(8,128)} %fusion.168, bf16[896,704]{0,1:T(8,128)(2,1)S(1)} %get-tuple-element.62, bf16[2048,704]{0,1:T(8,128)(2,1)} %collective-permute-done.17), kind=kOutput, calls=%fused_computation.24 | convolution fusion | flops 2592866304 | bytes 37175296 | tf_op jit(solution)/shard_map/dot_general | solution.py:76
  408.6 6.2 all-to-all-start.3
  414.7 5.0 fusion.160
  419.7 7.0 multiply_convert_fusion.2
  429.3 5.6 convolution_convert_fusion.3
  448.1 7.6 add_bitcast_fusion
  455.8 7.6 add_bitcast_fusion.1
  463.3 7.3 add_bitcast_fusion.2
  470.6 10.7 %maximum_bitcast_fusion = f32[1,2048,2,704]{1,3,2,0:T(8,128)} fusion(f32[2048,1,704]{0,2,1:T(8,128)} %add_bitcast_fusion.1, f32[2048,1,704]{0,2,1:T(8,128)} %add_bitcast_fusion.2), kind=kLoop, calls=%fused_computation.6 | loop fusion | flops 2883584 | bytes 23068672 | tf_op jit(solution)/shard_map/broadcast_in_dim | solution.py:444
  481.3 10.7 %collective-permute-done.72 = bf16[352,2048]{1,0:T(8,128)(2,1)S(1)} collective-permute-done((bf16[352,2048]{1,0:T(8,128)(2,1)}, bf16[352,2048]{1,0:T(8,128)(2,1)S(1)}, u32[]{:S(2)}, u32[]{:S(2)}) %collective-permute-start.72) | collective-permute-done | bytes 1441824 | tf_op jit(solution)/shard_map/ppermute | solution.py:85
  493.4 6.5 collective-permute-start.73
  500.0 22.7 %collective-permute-done.66 = bf16[256,2816]{1,0:T(8,128)(2,1)} collective-permute-done((bf16[256,2816]{1,0:T(8,128)(2,1)}, bf16[256,2816]{1,0:T(8,128)(2,1)}, u32[]{:S(2)}, u32[]{:S(2)}) %collective-permute-start.66) | collective-permute-done | bytes 1441824 | tf_op jit(solution)/shard_map/ppermute | solution.py:85
  524.2 6.9 collective-permute-start.67
  533.9 21.9 %collective-permute-done.67 = bf16[128,2816]{1,0:T(8,128)(2,1)S(1)} collective-permute-done((bf16[128,2816]{1,0:T(8,128)(2,1)S(1)}, bf16[128,2816]{1,0:T(8,128)(2,1)S(1)}, u32[]{:S(2)}, u32[]{:S(2)}) %collective-permute-start.67) | collective-permute-done | bytes 720928 | tf_op jit(solution)/shard_map/ppermute | solution.py:85
  557.2 15.0 %collective-permute-done.62 = bf16[128,2816]{1,0:T(8,128)(2,1)S(1)} collective-permute-done((bf16[128,2816]{1,0:T(8,128)(2,1)S(1)}, bf16[128,2816]{1,0:T(8,128)(2,1)S(1)}, u32[]{:S(2)}, u32[]{:S(2)}) %collective-permute-start.62) | collective-permute-done | bytes 720928 | tf_op jit(solution)/shard_map/ppermute | solution.py:85
  577.0 14.9 %collective-permute-done.68 = bf16[64,2816]{1,0:T(8,128)(2,1)S(1)} collective-permute-done((bf16[64,2816]{1,0:T(8,128)(2,1)S(1)}, bf16[64,2816]{1,0:T(8,128)(2,1)S(1)}, u32[]{:S(2)}, u32[]{:S(2)}) %collective-permute-start.68) | collective-permute-done | bytes 360480 | tf_op jit(solution)/shard_map/ppermute | solution.py:85
  600.7 6.4 all-to-all-start.1
  621.0 11.7 %multiply_reduce_fusion = (f32[2048]{0:T(1024)S(1)}, f32[2048,2048]{0,1:T(8,128)}) fusion(f32[2048,2048]{0,1:T(8,128)} %copy.391, bf16[2048,512]{1,0:T(8,128)(2,1)S(1)} %bitcast.282, bf16[2048,576]{0,1:T(8,128)(2,1)S(1)} %copy-done.34), kind=kOutput, calls=%fused_computation.2 | convolution fusion | flops 4303353856 | bytes 37756928 | tf_op jit(solution)/shard_map/dot_general | solution.py:76
  632.7 12.5 %multiply_convert_fusion = bf16[2048,2048]{0,1:T(8,128)(2,1)S(1)} fusion(f32[2048,2048]{0,1:T(8,128)} %copy.391, f32[2048,2048]{0,1:T(8,128)} %get-tuple-element.122, f32[2048]{0:T(1024)S(1)} %get-tuple-element.121), kind=kLoop, calls=%fused_computation.1 | loop fusion | flops 16777216 | bytes 41951232 | tf_op jit(solution)/shard_map/convert_element_type | solution.py:488
  645.2 5.4 fusion.191
  654.6 5.4 copy.456
  664.5 9.4 fusion.194
  679.2 8.0 copy.426
  687.2 7.8 convert_element_type.959
  695.0 12.2 %fusion.10 = bf16[2048,512]{1,0:T(8,128)(2,1)S(1)} fusion(f32[2048,512]{1,0:T(8,128)} %copy.456, bf16[16,128,512]{2,1,0:T(8,128)(2,1)} %copy-done.28, f32[16,128,2048]{2,1,0:T(8,128)} %copy-done.15), kind=kOutput, calls=%fused_computation.36 | convolution fusion | flops 4301258752 | bytes 25165824 | tf_op jit(solution)/shard_map/dot_general | solution.py:80
  793.1 5.3 fusion.195
  798.5 5.1 fusion.196
  846.8 10.2 %collective-permute-done.43 = bf16[512,576]{0,1:T(8,128)(2,1)S(1)} collective-permute-done((bf16[512,576]{0,1:T(8,128)(2,1)}, bf16[512,576]{0,1:T(8,128)(2,1)S(1)}, u32[]{:S(2)}, u32[]{:S(2)}) %collective-permute-start.43) | collective-permute-done | bytes 589856 | tf_op jit(solution)/shard_map/ppermute | solution.py:85
  886.7 5.9 collective-permute-done.46
  895.3 38.1 %collective-permute-done.48 = bf16[128,4096]{1,0:T(8,128)(2,1)S(1)} collective-permute-done((bf16[128,4096]{1,0:T(8,128)(2,1)S(1)}, bf16[128,4096]{1,0:T(8,128)(2,1)S(1)}, u32[]{:S(2)}, u32[]{:S(2)}) %collective-permute-start.48) | collective-permute-done | bytes 1048608 | tf_op jit(solution)/shard_map/ppermute | solution.py:85
  935.9 12.4 %collective-permute-done.49 = bf16[64,4096]{1,0:T(8,128)(2,1)S(1)} collective-permute-done((bf16[64,4096]{1,0:T(8,128)(2,1)S(1)}, bf16[64,4096]{1,0:T(8,128)(2,1)S(1)}, u32[]{:S(2)}, u32[]{:S(2)}) %collective-permute-start.49) | collective-permute-done | bytes 524320 | tf_op jit(solution)/shard_map/ppermute | solution.py:85
  950.3 7.2 collective-permute-done.50
  965.8 10.2 %collective-permute-done.56 = bf16[128,2048]{1,0:T(8,128)(2,1)S(1)} collective-permute-done((bf16[128,2048]{1,0:T(8,128)(2,1)S(1)}, bf16[128,2048]{1,0:T(8,128)(2,1)S(1)}, u32[]{:S(2)}, u32[]{:S(2)}) %collective-permute-start.56) | collective-permute-done | bytes 524320 | tf_op jit(solution)/shard_map/ppermute | solution.py:85
  981.3 12.7 %collective-permute-done.57 = bf16[64,2048]{1,0:T(8,128)(2,1)S(1)} collective-permute-done((bf16[64,2048]{1,0:T(8,128)(2,1)S(1)}, bf16[64,2048]{1,0:T(8,128)(2,1)S(1)}, u32[]{:S(2)}, u32[]{:S(2)}) %collective-permute-start.57) | collective-permute-done | bytes 262176 | tf_op jit(solution)/shard_map/ppermute | solution.py:85
  999.2 6.9 collective-permute-done.37
  (630 shorter events, 401.0 us)
Async XLA Ops:
  1.5 10.0 collective-permute-start.1
  2.0 11.7 %collective-permute-start.3 = (bf16[1024,576]{0,1:T(8,128)(2,1)}, bf16[1024,576]{0,1:T(8,128)(2,1)}, u32[]{:S(2)}, u32[]{:S(2)}) collective-permute-start(bf16[1024,576]{0,1:T(8,128)(2,1)} %param.30), channel_id=1, source_target_pairs={{0,1},{1,0},{2,3},{3,2},{4,5},{5,4},{6,7},{7,6},{8,9},{9,8},{10,11... | collective-permute-start | bytes 3538952 | tf_op jit(solution)/shard_map/ppermute | solution.py:89
  6.1 52.3 %collective-permute-start = (bf16[256,4096]{0,1:T(8,128)(2,1)}, bf16[256,4096]{0,1:T(8,128)(2,1)}, u32[]{:S(2)}, u32[]{:S(2)}) collective-permute-start(bf16[256,4096]{0,1:T(8,128)(2,1)} %copy.354), channel_id=1, source_target_pairs={{0,1},{1,0},{2,3},{3,2},{4,5},{5,4},{6,7},{7,6},{8,9},{9,8},{10,11... | collective-permute-start | bytes 6291464 | tf_op jit(solution)/shard_map/ppermute | solution.py:89
  6.6 136.3 %collective-permute-start.12 = (bf16[1024,2048]{1,0:T(8,128)(2,1)}, bf16[1024,2048]{1,0:T(8,128)(2,1)}, u32[]{:S(2)}, u32[]{:S(2)}) collective-permute-start(bf16[1024,2048]{1,0:T(8,128)(2,1)} %param.33), channel_id=1, source_target_pairs={{0,1},{1,0},{2,3},{3,2},{4,5},{5,4},{6,7},{7,6},{8,9},{9,8},{10,11... | collective-permute-start | bytes 12582920 | tf_op jit(solution)/shard_map/ppermute | solution.py:89
  6.7 67.2 %collective-permute-start.2 = (bf16[1024,3072]{1,0:T(8,128)(2,1)}, bf16[1024,3072]{1,0:T(8,128)(2,1)}, u32[]{:S(2)}, u32[]{:S(2)}) collective-permute-start(bf16[1024,3072]{1,0:T(8,128)(2,1)} %param.29), channel_id=1, source_target_pairs={{0,1},{1,0},{2,3},{3,2},{4,5},{5,4},{6,7},{7,6},{8,9},{9,8},{10,11... | collective-permute-start | bytes 18874376 | tf_op jit(solution)/shard_map/ppermute | solution.py:89
  47.2 21.2 %collective-permute-start.7 = (bf16[512,576]{0,1:T(8,128)(2,1)}, bf16[512,576]{0,1:T(8,128)(2,1)S(1)}, u32[]{:S(2)}, u32[]{:S(2)}) collective-permute-start(bf16[512,576]{0,1:T(8,128)(2,1)} %copy.367), channel_id=1, source_target_pairs={{0,2},{2,0},{4,6},{6,4},{8,10},{10,8},{12,14},{14,12},{16,18},{18,... | collective-permute-start | bytes 1769480 | tf_op jit(solution)/shard_map/ppermute | solution.py:85
  48.8 20.1 %collective-permute-start.11 = (bf16[512,576]{0,1:T(8,128)(2,1)}, bf16[512,576]{0,1:T(8,128)(2,1)}, u32[]{:S(2)}, u32[]{:S(2)}) collective-permute-start(bf16[512,576]{0,1:T(8,128)(2,1)} %copy.368), channel_id=1, source_target_pairs={{0,4},{2,6},{4,0},{6,2},{8,12},{10,14},{12,8},{14,10},{16,20},{18,... | collective-permute-start | bytes 1769480 | tf_op jit(solution)/shard_map/ppermute | solution.py:85
  58.4 117.3 %collective-permute-start.14 = (bf16[1408,2048]{1,0:T(8,128)(2,1)}, bf16[1408,2048]{1,0:T(8,128)(2,1)}, u32[]{:S(2)}, u32[]{:S(2)}) collective-permute-start(bf16[1408,2048]{1,0:T(8,128)(2,1)} %param.37), channel_id=1, source_target_pairs={{0,1},{1,0},{2,3},{3,2},{4,5},{5,4},{6,7},{7,6},{8,9},{9,8},{10,11... | collective-permute-start | bytes 17301512 | tf_op jit(solution)/shard_map/ppermute | solution.py:89
  68.4 151.8 %collective-permute-start.13 = (bf16[1024,5632]{1,0:T(8,128)(2,1)}, bf16[1024,5632]{1,0:T(8,128)(2,1)}, u32[]{:S(2)}, u32[]{:S(2)}) collective-permute-start(bf16[1024,5632]{1,0:T(8,128)(2,1)} %param.36), channel_id=1, source_target_pairs={{0,1},{1,0},{2,3},{3,2},{4,5},{5,4},{6,7},{7,6},{8,9},{9,8},{10,11... | collective-permute-start | bytes 34603016 | tf_op jit(solution)/shard_map/ppermute | solution.py:89
  149.2 82.8 %all-to-all-start = ((bf16[16,56,2048]{2,1,0:T(8,128)(2,1)}), bf16[16,56,2048]{2,1,0:T(8,128)(2,1)}, u32[]{:S(2)}, u32[]{:S(2)}) async-start(bf16[16,56,2048]{2,1,0:T(8,128)(2,1)} %bitcast.273), calls=%async_computation | async-start | bytes 7340032 | tf_op jit(solution)/shard_map/all_to_all | solution.py:325
  155.3 151.3 %collective-permute-start.15 = (bf16[1024,16]{0,1:T(8,128)(2,1)}, bf16[1024,16]{0,1:T(8,128)(2,1)}, u32[]{:S(2)}, u32[]{:S(2)}) collective-permute-start(bf16[1024,16]{0,1:T(8,128)(2,1)} %param.35), channel_id=1, source_target_pairs={{0,1},{1,0},{2,3},{3,2},{4,5},{5,4},{6,7},{7,6},{8,9},{9,8},{10,11... | collective-permute-start | bytes 98312 | tf_op jit(solution)/shard_map/ppermute | solution.py:89
  155.6 15.2 %collective-permute-start.70 = (bf16[128,2048]{1,0:T(8,128)(2,1)S(1)}, bf16[128,2048]{1,0:T(8,128)(2,1)S(1)}, u32[]{:S(2)}, u32[]{:S(2)}) collective-permute-start(bf16[128,2048]{1,0:T(8,128)(2,1)S(1)} %fusion.53), channel_id=1, source_target_pairs={{0,1},{1,0},{2,3},{3,2},{4,5},{5,4},{6,7},{7,6},{8,9},{9,8},{10,11... | collective-permute-start | bytes 1572872 | tf_op jit(solution)/shard_map/ppermute | solution.py:89
  171.6 170.0 %collective-permute-start.18 = (bf16[704,2048]{1,0:T(8,128)(2,1)}, bf16[704,2048]{1,0:T(8,128)(2,1)}, u32[]{:S(2)}, u32[]{:S(2)}) collective-permute-start(bf16[704,2048]{1,0:T(8,128)(2,1)} %bitcast.21), channel_id=1, source_target_pairs={{0,1},{1,0},{2,3},{3,2},{4,5},{5,4},{6,7},{7,6},{8,9},{9,8},{10,11... | collective-permute-start | bytes 8650760 | tf_op jit(solution)/shard_map/ppermute | solution.py:89
  181.0 36.8 %collective-permute-start.52 = (bf16[128,2048]{0,1:T(8,128)(2,1)}, bf16[128,2048]{0,1:T(8,128)(2,1)}, u32[]{:S(2)}, u32[]{:S(2)}) collective-permute-start(bf16[128,2048]{0,1:T(8,128)(2,1)} %bitcast.12), channel_id=1, source_target_pairs={{0,1},{1,0},{2,3},{3,2},{4,5},{5,4},{6,7},{7,6},{8,9},{9,8},{10,11... | collective-permute-start | bytes 1572872 | tf_op jit(solution)/shard_map/ppermute | solution.py:89
  181.2 31.9 %collective-permute-start.58 = (bf16[128,2048]{1,0:T(8,128)(2,1)S(1)}, bf16[128,2048]{1,0:T(8,128)(2,1)}, u32[]{:S(2)}, u32[]{:S(2)}) collective-permute-start(bf16[128,2048]{1,0:T(8,128)(2,1)S(1)} %multiply_convert_fusion.16), channel_id=1, source_target_pairs={{0,1},{1,0},{2,3},{3,2},{4,5},{5,4},{6,7},{7,6},{8,9},{9,8},{10,11... | collective-permute-start | bytes 1572872 | tf_op jit(solution)/shard_map/ppermute | solution.py:89
  213.1 120.9 %collective-permute-start.16 = (bf16[2048,704]{0,1:T(8,128)(2,1)}, bf16[2048,704]{0,1:T(8,128)(2,1)}, u32[]{:S(2)}, u32[]{:S(2)}) collective-permute-start(bf16[2048,704]{0,1:T(8,128)(2,1)} %get-tuple-element.59), channel_id=1, source_target_pairs={{0,1},{1,0},{2,3},{3,2},{4,5},{5,4},{6,7},{7,6},{8,9},{9,8},{10,11... | collective-permute-start | bytes 8650760 | tf_op jit(solution)/shard_map/ppermute | solution.py:89
  231.5 33.3 %collective-permute-start.59 = (bf16[128,2816]{0,1:T(8,128)(2,1)S(1)}, bf16[128,2816]{0,1:T(8,128)(2,1)}, u32[]{:S(2)}, u32[]{:S(2)}) collective-permute-start(bf16[128,2816]{0,1:T(8,128)(2,1)S(1)} %get-tuple-element.63), channel_id=1, source_target_pairs={{0,1},{1,0},{2,3},{3,2},{4,5},{5,4},{6,7},{7,6},{8,9},{9,8},{10,11... | collective-permute-start | bytes 2162696 | tf_op jit(solution)/shard_map/ppermute | solution.py:89
  231.9 35.4 %collective-permute-start.64 = (bf16[128,2816]{0,1:T(8,128)(2,1)S(1)}, bf16[128,2816]{0,1:T(8,128)(2,1)}, u32[]{:S(2)}, u32[]{:S(2)}) collective-permute-start(bf16[128,2816]{0,1:T(8,128)(2,1)S(1)} %get-tuple-element.64), channel_id=1, source_target_pairs={{0,1},{1,0},{2,3},{3,2},{4,5},{5,4},{6,7},{7,6},{8,9},{9,8},{10,11... | collective-permute-start | bytes 2162696 | tf_op jit(solution)/shard_map/ppermute | solution.py:89
  232.1 109.5 %all-to-all-start.2 = ((bf16[16,56,2048]{2,1,0:T(8,128)(2,1)}), bf16[16,56,2048]{2,1,0:T(8,128)(2,1)}, u32[]{:S(2)}, u32[]{:S(2)}) async-start(bf16[16,56,2048]{2,1,0:T(8,128)(2,1)} %bitcast.280), calls=%async_computation.2 | async-start | bytes 7340032 | tf_op jit(solution)/shard_map/all_to_all | solution.py:325
  264.8 9.7 collective-permute-start.69
  267.3 57.2 %collective-permute-start.17 = (bf16[2048,704]{0,1:T(8,128)(2,1)}, bf16[2048,704]{0,1:T(8,128)(2,1)}, u32[]{:S(2)}, u32[]{:S(2)}) collective-permute-start(bf16[2048,704]{0,1:T(8,128)(2,1)} %get-tuple-element.60), channel_id=1, source_target_pairs={{0,1},{1,0},{2,3},{3,2},{4,5},{5,4},{6,7},{7,6},{8,9},{9,8},{10,11... | collective-permute-start | bytes 8650760 | tf_op jit(solution)/shard_map/ppermute | solution.py:89
  282.0 152.9 %collective-permute-start.71 = (bf16[704,2048]{1,0:T(8,128)(2,1)}, bf16[704,2048]{1,0:T(8,128)(2,1)}, u32[]{:S(2)}, u32[]{:S(2)}) collective-permute-start(bf16[704,2048]{1,0:T(8,128)(2,1)} %get-tuple-element.41), channel_id=1, source_target_pairs={{0,2},{2,0},{4,6},{6,4},{8,10},{10,8},{12,14},{14,12},{16,18},{18,... | collective-permute-start | bytes 8650760 | tf_op jit(solution)/shard_map/ppermute | solution.py:85
  306.5 131.6 %collective-permute-start.65 = (bf16[512,2816]{1,0:T(8,128)(2,1)}, bf16[512,2816]{1,0:T(8,128)(2,1)}, u32[]{:S(2)}, u32[]{:S(2)}) collective-permute-start(bf16[512,2816]{1,0:T(8,128)(2,1)} %copy-done.14), channel_id=1, source_target_pairs={{0,2},{2,0},{4,6},{6,4},{8,10},{10,8},{12,14},{14,12},{16,18},{18,... | collective-permute-start | bytes 8650760 | tf_op jit(solution)/shard_map/ppermute | solution.py:85
  324.6 118.4 %collective-permute-start.60 = (bf16[512,2816]{1,0:T(8,128)(2,1)}, bf16[512,2816]{1,0:T(8,128)(2,1)}, u32[]{:S(2)}, u32[]{:S(2)}) collective-permute-start(bf16[512,2816]{1,0:T(8,128)(2,1)} %get-tuple-element.37), channel_id=1, source_target_pairs={{0,4},{2,6},{4,0},{6,2},{8,12},{10,14},{12,8},{14,10},{16,20},{18,... | collective-permute-start | bytes 8650760 | tf_op jit(solution)/shard_map/ppermute | solution.py:85
  364.7 91.0 %collective-permute-start.76 = (bf16[2048,704]{0,1:T(8,128)(2,1)}, bf16[2048,704]{0,1:T(8,128)(2,1)}, u32[]{:S(2)}, u32[]{:S(2)}) collective-permute-start(bf16[2048,704]{0,1:T(8,128)(2,1)} %convolution_convert_fusion.2), channel_id=1, source_target_pairs={{0,1},{1,0},{2,3},{3,2},{4,5},{5,4},{6,7},{7,6},{8,9},{9,8},{10,11... | collective-permute-start | bytes 8650760 | tf_op jit(solution)/shard_map/ppermute | solution.py:89
  364.7 81.3 %collective-permute-start.77 = (bf16[704,2048]{1,0:T(8,128)(2,1)}, bf16[704,2048]{1,0:T(8,128)(2,1)}, u32[]{:S(2)}, u32[]{:S(2)}) collective-permute-start(bf16[704,2048]{1,0:T(8,128)(2,1)} %convolution_convert_fusion.4), channel_id=1, source_target_pairs={{0,1},{1,0},{2,3},{3,2},{4,5},{5,4},{6,7},{7,6},{8,9},{9,8},{10,11... | collective-permute-start | bytes 8650760 | tf_op jit(solution)/shard_map/ppermute | solution.py:89
  408.6 192.1 %all-to-all-start.3 = ((bf16[16,56,2048]{2,1,0:T(8,128)(2,1)}), bf16[16,56,2048]{2,1,0:T(8,128)(2,1)}, u32[]{:S(2)}, u32[]{:S(2)}) async-start(bf16[16,56,2048]{2,1,0:T(8,128)(2,1)} %bitcast.279), calls=%async_computation.3 | async-start | bytes 7340032 | tf_op jit(solution)/shard_map/all_to_all | solution.py:325
  434.9 28.4 %collective-permute-start.75 = (bf16[2048,704]{0,1:T(8,128)(2,1)S(1)}, bf16[2048,704]{0,1:T(8,128)(2,1)S(1)}, u32[]{:S(2)}, u32[]{:S(2)}) collective-permute-start(bf16[2048,704]{0,1:T(8,128)(2,1)S(1)} %convolution_convert_fusion.3), channel_id=1, source_target_pairs={{0,1},{1,0},{2,3},{3,2},{4,5},{5,4},{6,7},{7,6},{8,9},{9,8},{10,11... | collective-permute-start | bytes 8650760 | tf_op jit(solution)/shard_map/ppermute | solution.py:89
  438.2 53.9 %collective-permute-start.72 = (bf16[352,2048]{1,0:T(8,128)(2,1)}, bf16[352,2048]{1,0:T(8,128)(2,1)S(1)}, u32[]{:S(2)}, u32[]{:S(2)}) collective-permute-start(bf16[352,2048]{1,0:T(8,128)(2,1)} %add_convert_fusion.1), channel_id=1, source_target_pairs={{0,4},{2,6},{4,0},{6,2},{8,12},{10,14},{12,8},{14,10},{16,20},{18,... | collective-permute-start | bytes 4325384 | tf_op jit(solution)/shard_map/ppermute | solution.py:85
  443.0 79.7 %collective-permute-start.66 = (bf16[256,2816]{1,0:T(8,128)(2,1)}, bf16[256,2816]{1,0:T(8,128)(2,1)}, u32[]{:S(2)}, u32[]{:S(2)}) collective-permute-start(bf16[256,2816]{1,0:T(8,128)(2,1)} %add_convert_fusion.2), channel_id=1, source_target_pairs={{0,4},{2,6},{4,0},{6,2},{8,12},{10,14},{12,8},{14,10},{16,20},{18,... | collective-permute-start | bytes 4325384 | tf_op jit(solution)/shard_map/ppermute | solution.py:85
  446.1 85.1 %collective-permute-start.61 = (bf16[256,2816]{1,0:T(8,128)(2,1)}, bf16[256,2816]{1,0:T(8,128)(2,1)S(1)}, u32[]{:S(2)}, u32[]{:S(2)}) collective-permute-start(bf16[256,2816]{1,0:T(8,128)(2,1)} %add_convert_fusion.3), channel_id=1, source_target_pairs={{0,2},{2,0},{4,6},{6,4},{8,10},{10,8},{12,14},{14,12},{16,18},{18,... | collective-permute-start | bytes 4325384 | tf_op jit(solution)/shard_map/ppermute | solution.py:85
  493.4 39.2 %collective-permute-start.73 = (bf16[176,2048]{1,0:T(8,128)(2,1)S(1)}, bf16[176,2048]{1,0:T(8,128)(2,1)S(1)}, u32[]{:S(2)}, u32[]{:S(2)}) collective-permute-start(bf16[176,2048]{1,0:T(8,128)(2,1)S(1)} %add_convert_fusion.7), channel_id=1, source_target_pairs={{0,8},{2,10},{4,12},{6,14},{8,0},{10,2},{12,4},{14,6},{16,24},{18,... | collective-permute-start | bytes 2162696 | tf_op jit(solution)/shard_map/ppermute | solution.py:85
  524.2 31.6 %collective-permute-start.67 = (bf16[128,2816]{1,0:T(8,128)(2,1)S(1)}, bf16[128,2816]{1,0:T(8,128)(2,1)S(1)}, u32[]{:S(2)}, u32[]{:S(2)}) collective-permute-start(bf16[128,2816]{1,0:T(8,128)(2,1)S(1)} %add_convert_fusion.8), channel_id=1, source_target_pairs={{0,8},{2,10},{4,12},{6,14},{8,0},{10,2},{12,4},{14,6},{16,24},{18,... | collective-permute-start | bytes 2162696 | tf_op jit(solution)/shard_map/ppermute | solution.py:85
  532.5 39.7 %collective-permute-start.62 = (bf16[128,2816]{1,0:T(8,128)(2,1)S(1)}, bf16[128,2816]{1,0:T(8,128)(2,1)S(1)}, u32[]{:S(2)}, u32[]{:S(2)}) collective-permute-start(bf16[128,2816]{1,0:T(8,128)(2,1)S(1)} %add_convert_fusion.9), channel_id=1, source_target_pairs={{0,8},{2,10},{4,12},{6,14},{8,0},{10,2},{12,4},{14,6},{16,24},{18,... | collective-permute-start | bytes 2162696 | tf_op jit(solution)/shard_map/ppermute | solution.py:85
  533.8 59.4 %collective-permute-start.74 = (bf16[88,2048]{1,0:T(8,128)(2,1)S(1)}, bf16[88,2048]{1,0:T(8,128)(2,1)S(1)}, u32[]{:S(2)}, u32[]{:S(2)}) collective-permute-start(bf16[88,2048]{1,0:T(8,128)(2,1)S(1)} %add_convert_fusion.15), channel_id=1, source_target_pairs={{0,16},{2,18},{4,20},{6,22},{8,24},{10,26},{12,28},{14,30},{16,0},... | collective-permute-start | bytes 1081352 | tf_op jit(solution)/shard_map/ppermute | solution.py:85
  557.1 34.8 %collective-permute-start.68 = (bf16[64,2816]{1,0:T(8,128)(2,1)S(1)}, bf16[64,2816]{1,0:T(8,128)(2,1)S(1)}, u32[]{:S(2)}, u32[]{:S(2)}) collective-permute-start(bf16[64,2816]{1,0:T(8,128)(2,1)S(1)} %add_convert_fusion.16), channel_id=1, source_target_pairs={{0,16},{2,18},{4,20},{6,22},{8,24},{10,26},{12,28},{14,30},{16,0},... | collective-permute-start | bytes 1081352 | tf_op jit(solution)/shard_map/ppermute | solution.py:85
  573.4 24.8 %collective-permute-start.63 = (bf16[64,2816]{1,0:T(8,128)(2,1)S(1)}, bf16[64,2816]{1,0:T(8,128)(2,1)S(1)}, u32[]{:S(2)}, u32[]{:S(2)}) collective-permute-start(bf16[64,2816]{1,0:T(8,128)(2,1)S(1)} %add_convert_fusion.17), channel_id=1, source_target_pairs={{0,16},{2,18},{4,20},{6,22},{8,24},{10,26},{12,28},{14,30},{16,0},... | collective-permute-start | bytes 1081352 | tf_op jit(solution)/shard_map/ppermute | solution.py:85
  600.7 118.8 %all-to-all-start.1 = ((bf16[16,56,2048]{2,1,0:T(8,128)(2,1)}), bf16[16,56,2048]{2,1,0:T(8,128)(2,1)}, u32[]{:S(2)}, u32[]{:S(2)}) async-start(bf16[16,56,2048]{2,1,0:T(8,128)(2,1)} %bitcast.295), calls=%async_computation.1 | async-start | bytes 7340032 | tf_op jit(solution)/shard_map/all_to_all | solution.py:325
  615.4 127.3 %collective-permute-start.53 = (bf16[128,2048]{1,0:T(8,128)(2,1)}, bf16[128,2048]{1,0:T(8,128)(2,1)}, u32[]{:S(2)}, u32[]{:S(2)}) collective-permute-start(bf16[128,2048]{1,0:T(8,128)(2,1)} %get-tuple-element.51), channel_id=1, source_target_pairs={{0,1},{1,0},{2,3},{3,2},{4,5},{5,4},{6,7},{7,6},{8,9},{9,8},{10,11... | collective-permute-start | bytes 1572872 | tf_op jit(solution)/shard_map/ppermute | solution.py:89
  712.9 20.5 %collective-permute-start.23 = (bf16[512,576]{0,1:T(8,128)(2,1)}, bf16[512,576]{0,1:T(8,128)(2,1)}, u32[]{:S(2)}, u32[]{:S(2)}) collective-permute-start(bf16[512,576]{0,1:T(8,128)(2,1)} %copy.401), channel_id=1, source_target_pairs={{0,4},{2,6},{4,0},{6,2},{8,12},{10,14},{12,8},{14,10},{16,20},{18,... | collective-permute-start | bytes 1769480 | tf_op jit(solution)/shard_map/ppermute | solution.py:85
  714.8 21.5 %collective-permute-start.19 = (bf16[512,576]{0,1:T(8,128)(2,1)}, bf16[512,576]{0,1:T(8,128)(2,1)}, u32[]{:S(2)}, u32[]{:S(2)}) collective-permute-start(bf16[512,576]{0,1:T(8,128)(2,1)} %copy.396), channel_id=1, source_target_pairs={{0,2},{2,0},{4,6},{6,4},{8,10},{10,8},{12,14},{14,12},{16,18},{18,... | collective-permute-start | bytes 1769480 | tf_op jit(solution)/shard_map/ppermute | solution.py:85
  719.5 156.1 %collective-permute-start.47 = (bf16[16,16,4096]{2,1,0:T(8,128)(2,1)}, bf16[16,16,4096]{2,1,0:T(8,128)(2,1)}, u32[]{:S(2)}, u32[]{:S(2)}) collective-permute-start(bf16[16,16,4096]{2,1,0:T(8,128)(2,1)} %dynamic-slice_bitcast_fusion), channel_id=1, source_target_pairs={{0,1},{1,0},{2,3},{3,2},{4,5},{5,4},{6,7},{7,6},{8,9},{9,8},{10,11... | collective-permute-start | bytes 6291464 | tf_op jit(solution)/shard_map/ppermute | solution.py:89
  742.0 10.4 %collective-permute-start.20 = (bf16[256,576]{1,0:T(8,128)(2,1)}, bf16[256,576]{1,0:T(8,128)(2,1)}, u32[]{:S(2)}, u32[]{:S(2)}) collective-permute-start(bf16[256,576]{1,0:T(8,128)(2,1)} %get-tuple-element.72), channel_id=1, source_target_pairs={{0,4},{2,6},{4,0},{6,2},{8,12},{10,14},{12,8},{14,10},{16,20},{18,... | collective-permute-start | bytes 884744 | tf_op jit(solution)/shard_map/ppermute | solution.py:85
  742.5 10.1 %collective-permute-start.24 = (bf16[256,576]{1,0:T(8,128)(2,1)}, bf16[256,576]{1,0:T(8,128)(2,1)}, u32[]{:S(2)}, u32[]{:S(2)}) collective-permute-start(bf16[256,576]{1,0:T(8,128)(2,1)} %get-tuple-element.73), channel_id=1, source_target_pairs={{0,2},{2,0},{4,6},{6,4},{8,10},{10,8},{12,14},{14,12},{16,18},{18,... | collective-permute-start | bytes 884744 | tf_op jit(solution)/shard_map/ppermute | solution.py:85
  765.8 14.1 %collective-permute-start.22 = (bf16[64,576]{1,0:T(8,128)(2,1)}, bf16[64,576]{1,0:T(8,128)(2,1)}, u32[]{:S(2)}, u32[]{:S(2)}) collective-permute-start(bf16[64,576]{1,0:T(8,128)(2,1)} %get-tuple-element.68), channel_id=1, source_target_pairs={{0,16},{2,18},{4,20},{6,22},{8,24},{10,26},{12,28},{14,30},{16,0},... | collective-permute-start | bytes 221192 | tf_op jit(solution)/shard_map/ppermute | solution.py:85
  768.1 11.8 %collective-permute-start.26 = (bf16[64,576]{1,0:T(8,128)(2,1)}, bf16[64,576]{1,0:T(8,128)(2,1)}, u32[]{:S(2)}, u32[]{:S(2)}) collective-permute-start(bf16[64,576]{1,0:T(8,128)(2,1)} %get-tuple-element.69), channel_id=1, source_target_pairs={{0,16},{2,18},{4,20},{6,22},{8,24},{10,26},{12,28},{14,30},{16,0},... | collective-permute-start | bytes 221192 | tf_op jit(solution)/shard_map/ppermute | solution.py:85
  775.1 118.3 %collective-permute-start.54 = (bf16[512,2048]{1,0:T(8,128)(2,1)}, bf16[512,2048]{1,0:T(8,128)(2,1)}, u32[]{:S(2)}, u32[]{:S(2)}) collective-permute-start(bf16[512,2048]{1,0:T(8,128)(2,1)} %get-tuple-element.35), channel_id=1, source_target_pairs={{0,4},{2,6},{4,0},{6,2},{8,12},{10,14},{12,8},{14,10},{16,20},{18,... | collective-permute-start | bytes 6291464 | tf_op jit(solution)/shard_map/ppermute | solution.py:85
  784.4 53.5 %collective-permute-start.42 = (bf16[128,576]{1,0:T(8,128)(2,1)S(1)}, bf16[128,576]{1,0:T(8,128)(2,1)}, u32[]{:S(2)}, u32[]{:S(2)}) collective-permute-start(bf16[128,576]{1,0:T(8,128)(2,1)S(1)} %pad_maximum_fusion.22), channel_id=1, source_target_pairs={{0,1},{1,0},{2,3},{3,2},{4,5},{5,4},{6,7},{7,6},{8,9},{9,8},{10,11... | collective-permute-start | bytes 442376 | tf_op jit(solution)/shard_map/ppermute | solution.py:89
  811.2 55.8 %collective-permute-start.33 = (bf16[128,3072]{1,0:T(8,128)(2,1)}, bf16[128,3072]{1,0:T(8,128)(2,1)}, u32[]{:S(2)}, u32[]{:S(2)}) collective-permute-start(bf16[128,3072]{1,0:T(8,128)(2,1)} %copy.417), channel_id=1, source_target_pairs={{0,1},{1,0},{2,3},{3,2},{4,5},{5,4},{6,7},{7,6},{8,9},{9,8},{10,11... | collective-permute-start | bytes 2359304 | tf_op jit(solution)/shard_map/ppermute | solution.py:89
  843.9 13.1 %collective-permute-start.43 = (bf16[512,576]{0,1:T(8,128)(2,1)}, bf16[512,576]{0,1:T(8,128)(2,1)S(1)}, u32[]{:S(2)}, u32[]{:S(2)}) collective-permute-start(bf16[512,576]{0,1:T(8,128)(2,1)} %copy.421), channel_id=1, source_target_pairs={{0,4},{2,6},{4,0},{6,2},{8,12},{10,14},{12,8},{14,10},{16,20},{18,... | collective-permute-start | bytes 1769480 | tf_op jit(solution)/shard_map/ppermute | solution.py:85
  866.7 12.6 %collective-permute-start.44 = (bf16[256,576]{1,0:T(8,128)(2,1)S(1)}, bf16[256,576]{1,0:T(8,128)(2,1)S(1)}, u32[]{:S(2)}, u32[]{:S(2)}) collective-permute-start(bf16[256,576]{1,0:T(8,128)(2,1)S(1)} %add_convert_fusion.18), channel_id=1, source_target_pairs={{0,2},{2,0},{4,6},{6,4},{8,10},{10,8},{12,14},{14,12},{16,18},{18,... | collective-permute-start | bytes 884744 | tf_op jit(solution)/shard_map/ppermute | solution.py:85
  870.7 63.5 %collective-permute-start.34 = (bf16[512,1536]{1,0:T(8,128)(2,1)S(1)}, bf16[512,1536]{1,0:T(8,128)(2,1)S(1)}, u32[]{:S(2)}, u32[]{:S(2)}) collective-permute-start(bf16[512,1536]{1,0:T(8,128)(2,1)S(1)} %get-tuple-element.29), channel_id=1, source_target_pairs={{0,2},{2,0},{4,6},{6,4},{8,10},{10,8},{12,14},{14,12},{16,18},{18,... | collective-permute-start | bytes 4718600 | tf_op jit(solution)/shard_map/ppermute | solution.py:85
  874.9 75.1 %collective-permute-start.38 = (bf16[512,1536]{1,0:T(8,128)(2,1)S(1)}, bf16[512,1536]{1,0:T(8,128)(2,1)S(1)}, u32[]{:S(2)}, u32[]{:S(2)}) collective-permute-start(bf16[512,1536]{1,0:T(8,128)(2,1)S(1)} %get-tuple-element.31), channel_id=1, source_target_pairs={{0,4},{2,6},{4,0},{6,2},{8,12},{10,14},{12,8},{14,10},{16,20},{18,... | collective-permute-start | bytes 4718600 | tf_op jit(solution)/shard_map/ppermute | solution.py:85
  882.3 51.2 %collective-permute-start.48 = (bf16[128,4096]{1,0:T(8,128)(2,1)S(1)}, bf16[128,4096]{1,0:T(8,128)(2,1)S(1)}, u32[]{:S(2)}, u32[]{:S(2)}) collective-permute-start(bf16[128,4096]{1,0:T(8,128)(2,1)S(1)} %bitcast.303), channel_id=1, source_target_pairs={{0,2},{2,0},{4,6},{6,4},{8,10},{10,8},{12,14},{14,12},{16,18},{18,... | collective-permute-start | bytes 3145736 | tf_op jit(solution)/shard_map/ppermute | solution.py:85
  895.0 63.2 %collective-permute-start.55 = (bf16[256,2048]{1,0:T(8,128)(2,1)S(1)}, bf16[256,2048]{1,0:T(8,128)(2,1)S(1)}, u32[]{:S(2)}, u32[]{:S(2)}) collective-permute-start(bf16[256,2048]{1,0:T(8,128)(2,1)S(1)} %add_convert_fusion.4), channel_id=1, source_target_pairs={{0,2},{2,0},{4,6},{6,4},{8,10},{10,8},{12,14},{14,12},{16,18},{18,... | collective-permute-start | bytes 3145736 | tf_op jit(solution)/shard_map/ppermute | solution.py:85
  933.5 14.8 %collective-permute-start.49 = (bf16[64,4096]{1,0:T(8,128)(2,1)S(1)}, bf16[64,4096]{1,0:T(8,128)(2,1)S(1)}, u32[]{:S(2)}, u32[]{:S(2)}) collective-permute-start(bf16[64,4096]{1,0:T(8,128)(2,1)S(1)} %fusion.65), channel_id=1, source_target_pairs={{0,4},{2,6},{4,0},{6,2},{8,12},{10,14},{12,8},{14,10},{16,20},{18,... | collective-permute-start | bytes 1572872 | tf_op jit(solution)/shard_map/ppermute | solution.py:85
  934.4 44.1 %collective-permute-start.35 = (bf16[256,1536]{1,0:T(8,128)(2,1)S(1)}, bf16[256,1536]{1,0:T(8,128)(2,1)S(1)}, u32[]{:S(2)}, u32[]{:S(2)}) collective-permute-start(bf16[256,1536]{1,0:T(8,128)(2,1)S(1)} %add_convert_fusion.6), channel_id=1, source_target_pairs={{0,4},{2,6},{4,0},{6,2},{8,12},{10,14},{12,8},{14,10},{16,20},{18,... | collective-permute-start | bytes 2359304 | tf_op jit(solution)/shard_map/ppermute | solution.py:85
  950.2 30.9 %collective-permute-start.39 = (bf16[256,1536]{1,0:T(8,128)(2,1)S(1)}, bf16[256,1536]{1,0:T(8,128)(2,1)S(1)}, u32[]{:S(2)}, u32[]{:S(2)}) collective-permute-start(bf16[256,1536]{1,0:T(8,128)(2,1)S(1)} %add_convert_fusion.5), channel_id=1, source_target_pairs={{0,2},{2,0},{4,6},{6,4},{8,10},{10,8},{12,14},{14,12},{16,18},{18,... | collective-permute-start | bytes 2359304 | tf_op jit(solution)/shard_map/ppermute | solution.py:85
  959.5 16.5 %collective-permute-start.56 = (bf16[128,2048]{1,0:T(8,128)(2,1)S(1)}, bf16[128,2048]{1,0:T(8,128)(2,1)S(1)}, u32[]{:S(2)}, u32[]{:S(2)}) collective-permute-start(bf16[128,2048]{1,0:T(8,128)(2,1)S(1)} %add_convert_fusion.10), channel_id=1, source_target_pairs={{0,8},{2,10},{4,12},{6,14},{8,0},{10,2},{12,4},{14,6},{16,24},{18,... | collective-permute-start | bytes 1572872 | tf_op jit(solution)/shard_map/ppermute | solution.py:85
  977.1 16.9 %collective-permute-start.57 = (bf16[64,2048]{1,0:T(8,128)(2,1)S(1)}, bf16[64,2048]{1,0:T(8,128)(2,1)S(1)}, u32[]{:S(2)}, u32[]{:S(2)}) collective-permute-start(bf16[64,2048]{1,0:T(8,128)(2,1)S(1)} %add_convert_fusion.21), channel_id=1, source_target_pairs={{0,16},{2,18},{4,20},{6,22},{8,24},{10,26},{12,28},{14,30},{16,0},... | collective-permute-start | bytes 786440 | tf_op jit(solution)/shard_map/ppermute | solution.py:85
  978.6 17.4 %collective-permute-start.36 = (bf16[128,1536]{1,0:T(8,128)(2,1)S(1)}, bf16[128,1536]{1,0:T(8,128)(2,1)S(1)}, u32[]{:S(2)}, u32[]{:S(2)}) collective-permute-start(bf16[128,1536]{1,0:T(8,128)(2,1)S(1)} %add_convert_fusion.14), channel_id=1, source_target_pairs={{0,8},{2,10},{4,12},{6,14},{8,0},{10,2},{12,4},{14,6},{16,24},{18,... | collective-permute-start | bytes 1179656 | tf_op jit(solution)/shard_map/ppermute | solution.py:85
  981.3 14.9 %collective-permute-start.40 = (bf16[128,1536]{1,0:T(8,128)(2,1)S(1)}, bf16[128,1536]{1,0:T(8,128)(2,1)S(1)}, u32[]{:S(2)}, u32[]{:S(2)}) collective-permute-start(bf16[128,1536]{1,0:T(8,128)(2,1)S(1)} %add_convert_fusion.13), channel_id=1, source_target_pairs={{0,8},{2,10},{4,12},{6,14},{8,0},{10,2},{12,4},{14,6},{16,24},{18,... | collective-permute-start | bytes 1179656 | tf_op jit(solution)/shard_map/ppermute | solution.py:85
  996.0 10.1 collective-permute-start.37
  996.2 12.0 %collective-permute-start.41 = (bf16[64,1536]{1,0:T(8,128)(2,1)S(1)}, bf16[64,1536]{1,0:T(8,128)(2,1)S(1)}, u32[]{:S(2)}, u32[]{:S(2)}) collective-permute-start(bf16[64,1536]{1,0:T(8,128)(2,1)S(1)} %add_convert_fusion.22), channel_id=1, source_target_pairs={{0,16},{2,18},{4,20},{6,22},{8,24},{10,26},{12,28},{14,30},{16,0},... | collective-permute-start | bytes 589832 | tf_op jit(solution)/shard_map/ppermute | solution.py:85
  (138 other events, 1446.0 us)

commit v2 on v1

--- a/solution.py
+++ b/solution.py
@@ -124,12 +124,6 @@
     return jnp.where(first, jnp.concatenate(pieces, 1), jnp.concatenate(pieces[::-1], 1))
 
 
-def group_rows(values):
-    if lax.axis_size("shard") == 2:
-        return jnp.concatenate([values, swap(values)], 0)
-    return lax.all_gather(values, "shard", axis=0, tiled=True)
-
-
 def collect(values, bits):
     places = [0]
     for bit in bits:
@@ -154,14 +148,13 @@
     return places
 
 
-def differing(blocks, bits):
+def differing(blocks, bits, here):
     count = len(bits)
-    here = lax.axis_index("expert")
     blocks = blocks.reshape((2,) * count + blocks.shape[1:])
-    for k in range(count):
-        odd = (here >> (count - 1 - k)) % 2 == 1
-        blocks = jnp.where(odd, jnp.flip(blocks, k), blocks)
-    axes = [count - bit.bit_length() for bit in bits]
+    ranked = sorted(bits, reverse=True)
+    for k, bit in enumerate(ranked):
+        blocks = jnp.where(here // bit % 2 == 1, jnp.flip(blocks, k), blocks)
+    axes = [ranked.index(bit) for bit in bits]
     blocks = blocks.transpose(axes + list(range(count, blocks.ndim)))
     return blocks.reshape((1 << count,) + blocks.shape[count:])
 
@@ -181,23 +174,23 @@
     sent_ref[...] = dot(picked_ref[half:, :].astype(BF), right).astype(sent_ref.dtype)
 
 
-def gradient_halves(left, right, bits):
-    experts, shards = lax.axis_size("expert"), lax.axis_size("shard")
-    tokens, rows_all = left.shape
+def gradient_halves(left, right, blocks, bits):
+    count = 1 << len(bits)
+    rows_all, tokens = left.shape
     columns = right.shape[1]
-    rows = rows_all // (experts * shards)
-    blocks = (
-        lax.axis_index("expert") ^ jnp.array(fold_order(bits), jnp.int32)
-    ) * shards + lax.axis_index("shard")
-    left = left.T
-    half = rows * experts // 2
+    rows = rows_all // count
+    half = rows_all // 2
     if rows % 8:
-        picked = lax.dynamic_index_in_dim(
-            left.reshape(experts, shards, rows, tokens), lax.axis_index("shard"), 1, keepdims=False
-        )
-        picked = differing(picked, bits).reshape(-1, tokens)
+        picked = differing(left.reshape(count, rows, tokens), bits, blocks).reshape(-1, tokens)
         product = dot(picked, right).astype(BF)
         return product[:half], product[half:]
+    order = []
+    for place in fold_order(bits):
+        block = 0
+        for k, bit in enumerate(sorted(bits)):
+            flipped = (blocks >> bit.bit_length() - 1) & 1
+            block = block + ((flipped ^ (place // bit & 1)) << k)
+        order.append(block)
     if rows % 16:
         left = left.astype(F32)
     tile = next(t for t in (512, 384, 256, 128, columns) if columns % t == 0)
@@ -214,7 +207,7 @@
                 pl.BlockSpec((half, tile), lambda i, order: (0, i)),
                 pl.BlockSpec((half, tile), lambda i, order: (0, i)),
             ],
-            scratch_shapes=[pltpu.VMEM((rows * experts, tokens), left.dtype)],
+            scratch_shapes=[pltpu.VMEM((rows_all, tokens), left.dtype)],
         ),
         out_shape=[jax.ShapeDtypeStruct((half, columns), BF)] * 2,
         compiler_params=pltpu.CompilerParams(vmem_limit_bytes=40 << 20),
@@ -223,14 +216,40 @@
             bytes_accessed=4 * half * columns + 2 * tokens * (rows_all + columns),
             transcendentals=0,
         ),
-    )(blocks, left, right)
+    )(jnp.stack(order).astype(jnp.int32), left, right)
+
+
+def group_left(left, bit):
+    experts, shards = lax.axis_size("expert"), lax.axis_size("shard")
+    tokens, columns = left.shape
+    own = lax.axis_index("expert") // bit % 2
+    blocks = left.T.reshape(experts // (2 * bit), 2, bit, shards, -1, tokens)
+    kept = lax.dynamic_index_in_dim(blocks, own, 1, keepdims=False)
+    sent = lax.dynamic_index_in_dim(blocks, 1 - own, 1, keepdims=False)
+    blocks = jnp.concatenate([kept, cross(sent, bit)], -1).reshape(
+        experts // 2, shards, -1, 2 * tokens
+    )
+    if shards != 2:
+        blocks = lax.all_to_all(blocks, "shard", split_axis=1, concat_axis=3, tiled=True)
+        return blocks.reshape(columns // (2 * shards), -1)
+    own = lax.axis_index("shard")
+    kept = lax.dynamic_index_in_dim(blocks, own, 1, keepdims=False)
+    sent = lax.dynamic_index_in_dim(blocks, 1 - own, 1, keepdims=False)
+    return jnp.concatenate([kept, swap(sent)], -1).reshape(columns // 4, -1)
+
+
+def group_right(right, bit):
+    right = jnp.concatenate([right, cross(right, bit)], 0)
+    if lax.axis_size("shard") != 2:
+        return lax.all_gather(right, "shard", axis=0, tiled=True)
+    return jnp.concatenate([right, swap(right)], 0)
 
 
 def reduce_product(left, right, bits):
-    kept, sent = gradient_halves(left, right, bits)
-    rows = 2 * kept.shape[0] >> len(bits)
-    arrived = cross(sent, bits[0])
-    return fold([kept, arrived], bits[1:], rows)
+    kept, sent = gradient_halves(left, right, lax.axis_index("expert"), bits[1:])
+    rows = 2 * kept.shape[0] >> len(bits) - 1
+    arrived = cross(sent, bits[1])
+    return fold([kept, arrived], bits[2:], rows)
 
 
 def reduce_partial(partial, bits):
@@ -243,7 +262,267 @@
     kept = lax.dynamic_index_in_dim(blocks, own, 1, keepdims=False)
     sent = lax.dynamic_index_in_dim(blocks, 1 - own, 1, keepdims=False)
     total = (kept.astype(F32) + swap(sent).astype(F32)).astype(partial.dtype)
-    return fold([differing(total, bits).reshape(experts * rows, -1)], bits, rows)
+    return fold([differing(total, bits, lax.axis_index("expert")).reshape(experts * rows, -1)], bits, rows)
+
+
+def attend_kernel(
+    raw_ref, cosine_ref, sine_ref, expand_ref, keys_ref, bias_ref,
+    nope_ref, queries_ref, weights_ref, mixed_ref, out_ref,
+):
+    rows = raw_ref.shape[0]
+    width = HEAD + ROPE
+    cosine, sine = cosine_ref[...], sine_ref[...]
+    for h in range(2):
+        raw = raw_ref[:, h * width : (h + 1) * width]
+        nope = raw[:, :HEAD].astype(BF)
+        first = raw[:, HEAD : HEAD + ROPE // 2]
+        second = raw[:, HEAD + ROPE // 2 :]
+        turned = jnp.concatenate(
+            [first * cosine - second * sine, second * cosine + first * sine], -1
+        )
+        nope_ref[:, h * HEAD : (h + 1) * HEAD] = nope
+        latent = dot_t(nope, expand_ref[:, 2 * h * HEAD : (2 * h + 1) * HEAD])
+        queries_ref[h * rows : (h + 1) * rows, :RANK] = latent.astype(BF)
+        queries_ref[h * rows : (h + 1) * rows, RANK:] = turned.astype(BF)
+    bias = bias_ref[...]
+    for h in range(2):
+        part = slice(h * rows, (h + 1) * rows)
+        scores = dot_t(queries_ref[part, :], keys_ref[...]) * (HEAD + ROPE) ** -0.5 + bias
+        shifted = jnp.exp(scores - jnp.max(scores, -1, keepdims=True))
+        total = jnp.sum(shifted, -1, keepdims=True)
+        weights_ref[part, :] = (shifted * (1.0 / total)).astype(BF)
+    mixed_ref[...] = dot(weights_ref[...], keys_ref[:, :RANK]).astype(BF)
+    for h in range(2):
+        out_ref[:, h * VHEAD : (h + 1) * VHEAD] = dot(
+            mixed_ref[h * rows : (h + 1) * rows, :],
+            expand_ref[:, (2 * h + 1) * HEAD : (2 * h + 2) * HEAD],
+        ).astype(BF)
+
+
+def attend(query_raw, cosine, sine, expand, keys, bias):
+    rows, slot = bias.shape
+    steps = HEADS // 2
+    whole = lambda *shape: pl.BlockSpec(shape, lambda i: (0,) * len(shape))
+    return pl.pallas_call(
+        attend_kernel,
+        grid=(steps,),
+        in_specs=[
+            pl.BlockSpec((rows, 2 * (HEAD + ROPE)), lambda i: (0, i)),
+            whole(rows, ROPE // 2),
+            whole(rows, ROPE // 2),
+            pl.BlockSpec((RANK, 4 * HEAD), lambda i: (0, i)),
+            whole(slot, RANK + ROPE),
+            whole(rows, slot),
+        ],
+        out_specs=[
+            pl.BlockSpec((rows, 2 * HEAD), lambda i: (0, i)),
+            pl.BlockSpec((2 * rows, RANK + ROPE), lambda i: (i, 0)),
+            pl.BlockSpec((2 * rows, slot), lambda i: (i, 0)),
+            pl.BlockSpec((2 * rows, RANK), lambda i: (i, 0)),
+            pl.BlockSpec((rows, 2 * VHEAD), lambda i: (0, i)),
+        ],
+        out_shape=[
+            jax.ShapeDtypeStruct((rows, HEADS * HEAD), BF),
+            jax.ShapeDtypeStruct((HEADS * rows, RANK + ROPE), BF),
+            jax.ShapeDtypeStruct((HEADS * rows, slot), BF),
+            jax.ShapeDtypeStruct((HEADS * rows, RANK), BF),
+            jax.ShapeDtypeStruct((rows, HEADS * VHEAD), BF),
+        ],
+        compiler_params=pltpu.CompilerParams(vmem_limit_bytes=40 << 20),
+        cost_estimate=pl.CostEstimate(
+            flops=2 * HEADS * rows * slot * (2 * RANK + ROPE),
+            bytes_accessed=2 * HEADS * rows * slot,
+            transcendentals=HEADS * rows * slot,
+        ),
+    )(query_raw, cosine, sine, expand, keys, bias)
+
+
+def attend_back_kernel(
+    grad_ref, expand_ref, keys_ref, weights_ref, queries_ref, mixed_ref, nope_ref, cosine_ref,
+    sine_ref, query_grad_ref, expand_grad_ref, key_grad_ref, latent_ref, scores_ref,
+):
+    rows = grad_ref.shape[0]
+    width = HEAD + ROPE
+    scale = (HEAD + ROPE) ** -0.5
+
+    @pl.when(pl.program_id(0) == 0)
+    def _():
+        key_grad_ref[...] = jnp.zeros_like(key_grad_ref)
+
+    for h in range(2):
+        part = slice(h * rows, (h + 1) * rows)
+        grad = grad_ref[:, h * VHEAD : (h + 1) * VHEAD]
+        latent_ref[part, :] = dot_t(
+            grad, expand_ref[:, (2 * h + 1) * HEAD : (2 * h + 2) * HEAD]
+        ).astype(BF)
+        arrived = dot_t(latent_ref[part, :], keys_ref[:, :RANK])
+        weights = weights_ref[part, :].astype(F32)
+        mean = jnp.sum(weights * arrived, -1, keepdims=True)
+        scores_ref[part, :] = (weights * (arrived - mean) * scale).astype(BF)
+    key_grad_ref[...] += t_dot(queries_ref[...], scores_ref[...])
+    key_grad_ref[:RANK, :] += t_dot(latent_ref[...], weights_ref[...])
+    cosine, sine = cosine_ref[...], sine_ref[...]
+    for h in range(2):
+        part = slice(h * rows, (h + 1) * rows)
+        query_grad = dot(scores_ref[part, :], keys_ref[...])
+        latent = query_grad[:, :RANK].astype(BF)
+        key_part = slice(2 * h * HEAD, (2 * h + 1) * HEAD)
+        value_part = slice((2 * h + 1) * HEAD, (2 * h + 2) * HEAD)
+        nope = dot(latent, expand_ref[:, key_part])
+        first = query_grad[:, RANK : RANK + ROPE // 2]
+        second = query_grad[:, RANK + ROPE // 2 :]
+        query_grad_ref[:, h * width : (h + 1) * width] = jnp.concatenate(
+            [nope, first * cosine + second * sine, second * cosine - first * sine], -1
+        ).astype(BF)
+        expand_grad_ref[:, key_part] = t_dot(
+            latent, nope_ref[:, h * HEAD : (h + 1) * HEAD]
+        ).astype(BF)
+        expand_grad_ref[:, value_part] = t_dot(
+            mixed_ref[part, :], grad_ref[:, h * VHEAD : (h + 1) * VHEAD]
+        ).astype(BF)
+
+
+def attend_back(grad_out, expand, keys, weights, queries, mixed, nope, cosine, sine):
+    rows = grad_out.shape[0]
+    slot = keys.shape[0]
+    whole = lambda *shape: pl.BlockSpec(shape, lambda i: (0,) * len(shape))
+    return pl.pallas_call(
+        attend_back_kernel,
+        grid=(HEADS // 2,),
+        in_specs=[
+            pl.BlockSpec((rows, 2 * VHEAD), lambda i: (0, i)),
+            pl.BlockSpec((RANK, 4 * HEAD), lambda i: (0, i)),
+            whole(slot, RANK + ROPE),
+            pl.BlockSpec((2 * rows, slot), lambda i: (i, 0)),
+            pl.BlockSpec((2 * rows, RANK + ROPE), lambda i: (i, 0)),
+            pl.BlockSpec((2 * rows, RANK), lambda i: (i, 0)),
+            pl.BlockSpec((rows, 2 * HEAD), lambda i: (0, i)),
+            whole(rows, ROPE // 2),
+            whole(rows, ROPE // 2),
+        ],
+        out_specs=[
+            pl.BlockSpec((rows, 2 * (HEAD + ROPE)), lambda i: (0, i)),
+            pl.BlockSpec((RANK, 4 * HEAD), lambda i: (0, i)),
+            whole(RANK + ROPE, slot),
+        ],
+        out_shape=[
+            jax.ShapeDtypeStruct((rows, HEADS * (HEAD + ROPE)), BF),
+            jax.ShapeDtypeStruct((RANK, 2 * HEADS * HEAD), BF),
+            jax.ShapeDtypeStruct((RANK + ROPE, slot), F32),
+        ],
+        scratch_shapes=[pltpu.VMEM((2 * rows, RANK), BF), pltpu.VMEM((2 * rows, slot), BF)],
+        compiler_params=pltpu.CompilerParams(vmem_limit_bytes=48 << 20),
+        cost_estimate=pl.CostEstimate(
+            flops=2 * HEADS * rows * slot * (3 * RANK + 2 * (RANK + ROPE)),
+            bytes_accessed=2 * HEADS * rows * slot,
+            transcendentals=0,
+        ),
+    )(grad_out, expand, keys, weights, queries, mixed, nope, cosine, sine)
+
+
+def expert_kernel(sources, here_ref, rows_ref, grads_ref, router_ref, *refs):
+    weights = refs[: 2 * sources]
+    (
+        row_grad_ref, units_ref, back_ref, gate_ref, logit_grad_ref, total_ref, probs_ref, share_ref,
+    ) = refs[2 * sources :]
+    step = pl.program_id(0)
+    chunks = pl.num_programs(0) // sources
+
+    @pl.when(step == 0)
+    def _():
+        logits = dot_t(router_ref[...], rows_ref[...])
+        powers = jnp.exp(logits - jnp.max(logits, 0, keepdims=True))
+        probs = powers / jnp.sum(powers, 0, keepdims=True)
+        own = lax.broadcasted_iota(jnp.int32, probs.shape, 0) == here_ref[0]
+        probs_ref[...] = probs
+        gate_ref[...] = jnp.sum(jnp.where(own, probs, 0.0), 0, keepdims=True)
+        share_ref[...] = jnp.zeros_like(share_ref)
+        total_ref[...] = jnp.zeros_like(total_ref)
+
+    def work(in_ref, out_ref):
+        gate = dot_t(in_ref[0], rows_ref[...])
+        up = dot_t(in_ref[1], rows_ref[...])
+        back = dot_t(out_ref[...], grads_ref[...])
+        sigma = 1.0 / (1.0 + jnp.exp(-gate))
+        act = gate * sigma
+        units = (act * up).astype(BF)
+        units_ref[...] = units
+        share_ref[...] += jnp.sum(back * units.astype(F32), 0, keepdims=True)
+        back = back * gate_ref[...]
+        back_ref[0] = (back * up * (sigma * (1.0 + gate * (1.0 - sigma)))).astype(BF)
+        back_ref[1] = (back * act).astype(BF)
+        total_ref[...] += t_dot(back_ref[0], in_ref[0])
+        total_ref[...] += t_dot(back_ref[1], in_ref[1])
+
+    for k in range(sources):
+
+        @pl.when(step // chunks == k)
+        def _(k=k):
+            work(weights[2 * k], weights[2 * k + 1])
+
+    @pl.when(step == pl.num_programs(0) - 1)
+    def _():
+        probs = probs_ref[...]
+        own = lax.broadcasted_iota(jnp.int32, probs.shape, 0) == here_ref[0]
+        grad = probs * (own.astype(F32) - gate_ref[...]) * share_ref[...]
+        logit_grad_ref[...] = grad.astype(BF)
+        row_grad_ref[...] = (
+            total_ref[...] + t_dot(logit_grad_ref[...], router_ref[...])
+        ).astype(BF)
+
+
+def expert_pass(here, rows, grads, router, weights):
+    count, width = rows.shape
+    experts = router.shape[0]
+    sources = len(weights)
+    units = weights[0][1].shape[0]
+    tile = next(t for t in (352, 176, 88, 64, 32, 16, units) if units % t == 0)
+    chunks = units // tile
+    once = pl.Buffered(1)
+    in_specs = [
+        pl.BlockSpec((count, width), lambda i, h: (0, 0), pipeline_mode=once),
+        pl.BlockSpec((count, width), lambda i, h: (0, 0), pipeline_mode=once),
+        pl.BlockSpec((experts, width), lambda i, h: (0, 0)),
+    ]
+    for k in range(sources):
+        at = lambda i, k=k: jnp.clip(i - k * chunks, 0, chunks - 1)
+        in_specs.append(pl.BlockSpec((2, tile, width), lambda i, h, at=at: (0, at(i), 0)))
+        in_specs.append(pl.BlockSpec((tile, width), lambda i, h, at=at: (at(i), 0)))
+    return pl.pallas_call(
+        functools.partial(expert_kernel, sources),
+        grid_spec=pltpu.PrefetchScalarGridSpec(
+            num_scalar_prefetch=1,
+            grid=(sources * chunks,),
+            in_specs=in_specs,
+            out_specs=[
+                pl.BlockSpec((count, width), lambda i, h: (0, 0), pipeline_mode=once),
+                pl.BlockSpec((tile, count), lambda i, h: (i, 0)),
+                pl.BlockSpec(
+                    (None, 2, tile, count), lambda i, h: (i // chunks, 0, i % chunks, 0)
+                ),
+                pl.BlockSpec((1, count), lambda i, h: (0, 0)),
+                pl.BlockSpec((experts, count), lambda i, h: (0, 0)),
+            ],
+            scratch_shapes=[
+                pltpu.VMEM((count, width), F32),
+                pltpu.VMEM((experts, count), F32),
+                pltpu.VMEM((1, count), F32),
+            ],
+        ),
+        out_shape=[
+            jax.ShapeDtypeStruct((count, width), BF),
+            jax.ShapeDtypeStruct((sources * units, count), BF),
+            jax.ShapeDtypeStruct((sources, 2, units, count), BF),
+            jax.ShapeDtypeStruct((1, count), F32),
+            jax.ShapeDtypeStruct((experts, count), BF),
+        ],
+        compiler_params=pltpu.CompilerParams(vmem_limit_bytes=58 << 20),
+        cost_estimate=pl.CostEstimate(
+            flops=10 * count * width * sources * units,
+            bytes_accessed=6 * (count + sources * units) * width,
+            transcendentals=count * sources * units,
+        ),
+    )(here, rows, grads, router, *[piece for pair in weights for piece in pair])
 
 
 def per_device(
@@ -272,7 +551,6 @@
     topk_count = routes.shape[2]
     capacity = max(2, 9 * local_rows * topk_count // (8 * experts_all))
     capacity = -(-capacity // 8) * 8
-    score_scale = (HEAD + ROPE) ** (-0.5)
     here = lax.axis_index("expert")
     bits = [1 << k for k in range(owners.bit_length() - 1)]
     first_x = tuple(bits)
@@ -294,15 +572,24 @@
     gain_attn = gains[:, :cut].reshape(-1)
     gain_ffn = gains[:, cut : 2 * cut].reshape(-1)
     gain_latent = gains[:, 2 * cut :].reshape(-1)
-    expand = whole_rows(expand_weight).reshape(RANK, HEADS, HEAD + VHEAD)
-    expand_key, expand_value = expand[..., :HEAD], expand[..., HEAD:]
+    expand = whole_rows(expand_weight)
     output_blocks = row_blocks(output_weight)
     router = whole_rows(router_weight)
     shared_out_blocks = row_blocks(shared_out)
     shared_in_blocks = row_blocks(shared_in)
-    expert_out_blocks = row_blocks(expert_out[0])
-    gate_blocks = row_blocks(expert_in[0, :, 0, :])
-    up_blocks = row_blocks(expert_in[0, :, 1, :])
+    expert_in_rows = expert_in[0].transpose(1, 2, 0)
+    if shards == 2:
+        expert_weights = [
+            (expert_in_rows, expert_out[0]),
+            (swap(expert_in_rows), swap(expert_out[0])),
+        ]
+    else:
+        expert_weights = [
+            (
+                lax.all_gather(expert_in_rows, "shard", axis=1, tiled=True),
+                lax.all_gather(expert_out[0], "shard", axis=0, tiled=True),
+            )
+        ]
 
     here_index = here * local_rows + jnp.arange(local_rows, dtype=jnp.int32)
     query_segment, query_position, query_valid = layout(lengths[0], here_index)
@@ -357,93 +644,59 @@
     keys = jnp.concatenate(keys, 0)
     key_index = jnp.concatenate(key_index)
 
-    received_grads = exchange(dot(spread, grad_out_low).astype(BF))
-
-    query_raw = times(attn_in, query_blocks).reshape(local_rows, HEADS, HEAD + ROPE)
-    query_nope = query_raw[..., :HEAD].astype(BF)
-    query_rope = rotate(
-        query_raw[..., HEAD:], cosine[:, None, :], sine_table[:, None, :]
-    ).astype(BF)
-    query_latent = jnp.einsum(
-        "qhc,rhc->hqr", query_nope, expand_key, preferred_element_type=F32
-    ).astype(BF)
-    queries = jnp.concatenate([query_latent, query_rope.transpose(1, 0, 2)], -1).reshape(
-        HEADS * local_rows, RANK + ROPE
-    )
+    sent_grads, keys = lax.optimization_barrier((dot(spread, grad_out_low).astype(BF), keys))
+    received_grads = exchange(sent_grads)
+
+    query_raw = times(attn_in, query_blocks)
     key_segment = layout(lengths[0], key_index)[0]
     allowed = (query_segment[:, None] == key_segment[None, :]) & (
         key_index[None, :] <= here_index[:, None]
     )
-    scores = dot_t(queries, keys).reshape(HEADS, local_rows, SLOT)
-    scores = jnp.where(allowed[None], scores * score_scale, MASK_FILL)
-    shifted = jnp.exp(scores - jnp.max(scores, -1, keepdims=True))
-    attention = (shifted / jnp.sum(shifted, -1, keepdims=True)).reshape(HEADS * local_rows, SLOT)
-    attention_low = attention.astype(BF)
-    mixed_latent = dot(attention_low, keys[:, :RANK]).astype(BF).reshape(HEADS, local_rows, RANK)
-    mixed_heads = (
-        jnp.einsum("hqr,rhv->qhv", mixed_latent, expand_value, preferred_element_type=F32)
-        .astype(BF)
-        .reshape(local_rows, HEADS * VHEAD)
-    )
+    bias = jnp.where(allowed, 0.0, MASK_FILL).astype(F32)
+    query_nope, queries, attention, mixed_latent, mixed_heads = attend(
+        query_raw, cosine, sine_table, expand, keys, bias
+    )
+    mixed_heads, received_grads = lax.optimization_barrier((mixed_heads, received_grads))
     hidden_state = inputs + times(mixed_heads, output_blocks)
     inverse_ffn = rms_scale(hidden_state)
     normed_ffn = hidden_state * inverse_ffn
     ffn_in = (normed_ffn * gain_ffn).astype(BF)
 
     received = exchange(dot(spread, ffn_in).astype(BF))
-    slopes_in = [dot_t(received_grads, block) for _, block in expert_out_blocks]
-    row_logits = dot(received, router)
-    row_exp = jnp.exp(row_logits - jnp.max(row_logits, -1, keepdims=True))
-    row_probs = row_exp / jnp.sum(row_exp, -1, keepdims=True)
-    own_expert = (expert_ids == here).astype(F32)[None, :]
-    row_gate = jnp.sum(row_probs * own_expert, -1, keepdims=True)
-    row_gate_grad = 0.0
-    hidden, grads_gate, grads_up = [], [], []
-    for j in range(shards):
-        gate = dot(received, gate_blocks[j][1])
-        up = dot(received, up_blocks[j][1])
-        act, slope = silu_parts(gate)
-        units = (act * up).astype(BF)
-        row_gate_grad = row_gate_grad + jnp.sum(slopes_in[j] * units.astype(F32), -1, keepdims=True)
-        grad_units = row_gate * slopes_in[j]
-        hidden.append(units)
-        grads_gate.append((grad_units * up * slope).astype(BF))
-        grads_up.append((grad_units * act).astype(BF))
-    row_grad_logits = (row_probs * (own_expert - row_gate) * row_gate_grad).astype(BF)
-    row_grads = dot_t(row_grad_logits, router)
-    for j in range(shards):
-        row_grads = row_grads + dot_t(grads_gate[j], gate_blocks[j][1])
-        row_grads = row_grads + dot_t(grads_up[j], up_blocks[j][1])
-    returned_grads = exchange(row_grads.astype(BF))
-    row_out = sum(dot(hidden[j], expert_out_blocks[j][1]) for j in range(shards))
+    row_grads, hidden, hidden_grads, row_gate, row_grad_logits = expert_pass(
+        here[None], received, received_grads, router.T, expert_weights
+    )
+    returned_grads = exchange(row_grads)
+    row_gate = row_gate.reshape(-1, 1)
+    row_out = 0.0
+    units = expert_weights[0][1].shape[0]
+    for j, (_, weight) in enumerate(expert_weights):
+        row_out = row_out + t_dot(hidden[j * units : (j + 1) * units], weight)
     returned = exchange((row_gate * row_out).astype(BF))
     routed = t_dot(spread, returned)
     grad_routed = t_dot(spread, returned_grads)
     weighted_grads = (row_gate * received_grads.astype(F32)).astype(BF)
     grad_expert_parts = [
         (
-            t_dot(received, grads_gate[j]),
-            t_dot(received, grads_up[j]),
-            t_dot(hidden[j], weighted_grads),
+            dot(hidden_grads[j].reshape(2 * units, -1), received).reshape(2, units, -1),
+            dot(hidden[j * units : (j + 1) * units], weighted_grads),
         )
-        for j in range(shards)
+        for j in range(len(expert_weights))
     ]
     if shards == 2:
-        own_parts, other_parts = grad_expert_parts
-        own_parts = [
-            own + swap(other.astype(BF)).astype(F32)
-            for own, other in zip(own_parts, other_parts)
+        grad_expert_in, grad_expert_out = [
+            own + swap(other.astype(BF)).astype(F32) for own, other in zip(*grad_expert_parts)
         ]
     else:
-        own_parts = [
+        grad_expert_in, grad_expert_out = [
             lax.psum_scatter(
-                jnp.stack([p[k].astype(BF) for p in grad_expert_parts]), "shard", tiled=True
-            )[0].astype(F32)
-            for k in range(3)
+                part.astype(BF), "shard", scatter_dimension=part.ndim - 2, tiled=True
+            ).astype(F32)
+            for part in grad_expert_parts[0]
         ]
-    grad_expert_in = jnp.stack(own_parts[:2], 1)[None]
-    grad_expert_out = own_parts[2][None]
-    grad_router = t_dot(received, row_grad_logits)
+    grad_expert_in = grad_expert_in.transpose(2, 0, 1)[None]
+    grad_expert_out = grad_expert_out[None]
+    grad_router = dot(row_grad_logits, received).T
 
     shared_both = times(ffn_in, shared_in_blocks)
     shared_act, shared_slope = silu_parts(shared_both[:, :FF_S])
@@ -455,14 +708,15 @@
     grad_shared_gate = (grad_shared_hidden * shared_up * shared_slope).astype(BF)
     grad_shared_up = (grad_shared_hidden * shared_act).astype(BF)
     grad_shared_both = jnp.concatenate([grad_shared_gate, grad_shared_up], -1)
-    group_ffn_in = group_rows(ffn_in)
     grad_shared_out = reduce_product(
-        group_rows(shared_hidden), group_rows(grad_out_low), first_x
+        group_left(shared_hidden, first_x[0]), group_right(grad_out_low, first_x[0]), first_x
     )
     grad_shared_in = jnp.concatenate(
         [
-            reduce_product(group_ffn_in, group_rows(grad_shared_gate), first_y),
-            reduce_product(group_ffn_in, group_rows(grad_shared_up), first_x),
+            reduce_product(
+                group_left(ffn_in, order[0]), group_right(grads_in, order[0]), order
+            )
+            for order, grads_in in ((first_y, grad_shared_gate), (first_x, grad_shared_up))
         ],
         -1,
     )
@@ -471,32 +725,22 @@
     grad_hidden_state = grad_out + norm_back(grad_ffn_in * gain_ffn, normed_ffn, inverse_ffn)
 
     grad_attn_out = grad_hidden_state.astype(BF)
-    grad_output = reduce_product(group_rows(mixed_heads), group_rows(grad_attn_out), first_y)
-    grad_mixed = times_back(grad_attn_out, output_blocks).astype(BF).reshape(
-        local_rows, HEADS, VHEAD
-    )
-    grad_mixed_latent = (
-        jnp.einsum("qhv,rhv->hqr", grad_mixed, expand_value, preferred_element_type=F32)
-        .astype(BF)
-        .reshape(HEADS * local_rows, RANK)
-    )
-    grad_attention = dot_t(grad_mixed_latent, keys[:, :RANK])
-    grad_scores = (
-        attention
-        * (grad_attention - jnp.sum(attention * grad_attention, -1, keepdims=True))
-        * score_scale
-    ).astype(BF)
-    grad_queries = dot(grad_scores, keys).reshape(HEADS, local_rows, RANK + ROPE)
-    grad_query_latent = grad_queries[..., :RANK].astype(BF)
-    grad_query_rope = grad_queries[..., RANK:].transpose(1, 0, 2)
-    grad_keys = t_dot(grad_scores, queries)
-    grad_keys = jnp.concatenate(
-        [
-            grad_keys[:, :RANK] + t_dot(attention_low, grad_mixed_latent),
-            grad_keys[:, RANK:],
-        ],
-        -1,
-    ).astype(BF)
+    grad_output = reduce_product(
+        group_left(mixed_heads, first_y[0]), group_right(grad_attn_out, first_y[0]), first_y
+    )
+    grad_mixed = times_back(grad_attn_out, output_blocks).astype(BF)
+    grad_query_raw, grad_expand, grad_keys = attend_back(
+        grad_mixed,
+        expand,
+        keys,
+        attention,
+        queries,
+        mixed_latent,
+        query_nope,
+        cosine,
+        sine_table,
+    )
+    grad_keys = grad_keys.T.astype(BF)
     slot_half = SLOT // 2
     grad_own_keys = jnp.concatenate(
         [
@@ -509,45 +753,29 @@
         ],
         0,
     )
-    grad_expand = jnp.concatenate(
-        [
-            jnp.einsum("hqr,qhc->rhc", grad_query_latent, query_nope, preferred_element_type=F32),
-            jnp.einsum("hqr,qhv->rhv", mixed_latent, grad_mixed, preferred_element_type=F32),
-        ],
-        -1,
-    ).reshape(RANK, HEADS * (HEAD + VHEAD))
-    grad_expand = reduce_partial(grad_expand.astype(BF), first_x).astype(F32)
+    grad_expand = reduce_partial(grad_expand, first_x).astype(F32)
     grad_latent_in = grad_own_keys[:, :RANK]
     grad_gain_latent = jnp.sum(grad_latent_in * normed_latent, 0)
     grad_latent = norm_back(grad_latent_in * gain_latent, normed_latent, inverse_latent)
     grad_latent_raw = jnp.concatenate(
         [grad_latent, rotate_back(grad_own_keys[:, RANK:], cosine, sine_table)], -1
     ).astype(BF)
-    grad_query_nope = jnp.einsum(
-        "hqr,rhc->qhc", grad_query_latent, expand_key, preferred_element_type=F32
-    )
-    grad_query_raw = (
-        jnp.concatenate(
-            [
-                grad_query_nope,
-                rotate_back(grad_query_rope, cosine[:, None, :], sine_table[:, None, :]),
-            ],
-            -1,
-        )
-        .reshape(local_rows, HEADS * (HEAD + ROPE))
-        .astype(BF)
-    )
-    group_attn_in = group_rows(attn_in)
-    group_grad_query = group_rows(grad_query_raw)
-    query_half = group_grad_query.shape[1] // 2
+    left_x, left_y = group_left(attn_in, first_x[0]), group_left(attn_in, first_y[0])
+    query_half = grad_query_raw.shape[1] // 2
     grad_query = jnp.concatenate(
         [
-            reduce_product(group_attn_in, group_grad_query[:, :query_half], first_x),
-            reduce_product(group_attn_in, group_grad_query[:, query_half:], first_y),
+            reduce_product(
+                left_x, group_right(grad_query_raw[:, :query_half], first_x[0]), first_x
+            ),
+            reduce_product(
+                left_y, group_right(grad_query_raw[:, query_half:], first_y[0]), first_y
+            ),
         ],
         -1,
     )
-    grad_latent_weight = reduce_product(group_attn_in, group_rows(grad_latent_raw), first_y)
+    grad_latent_weight = reduce_product(
+        left_y, group_right(grad_latent_raw, first_y[0]), first_y
+    )
     grad_attn_in = times_back(grad_latent_raw, latent_blocks) + times_back(
         grad_query_raw, query_blocks
     )

time: 1020 us -> 860 us (0.84)
  matrix products: 321 us -> 153 us
  Pallas kernels: 25.2 us -> 135 us
  local copies, waits for them, and re-layouts: 168 us -> 71 us
  other arithmetic: 156 us -> 98.5 us
  waiting for transfers between devices: 223 us -> 277 us
    pallas_call x0 -> x3, Pallas kernels: none -> 113 us  [the longest x1 46.6 us: expert_pass(): pl.pallas_call(functools.partial(expert_kernel, sources), grid_spec=pltpu...]
    dot_general x17 -> x10, matrix products: 116 us -> 49.5 us  [dot_t(): lax.dot_general(left, right, (((1,), (1,)), ((), ())), preferred_element_...]
    ppermute x52 -> x58, waiting for transfers between devices: 223 us -> 275 us  [cross(): return lax.ppermute(values, 'expert', [(i, i ^ bit) for i in range(count)])]
    dot_general x11 -> x4, matrix products: 68.7 us -> 18 us  [t_dot(): lax.dot_general(left, right, (((0,), (0,)), ((), ())), preferred_element_...]
    unnamed x264 -> x217, local copies, waits for them, and re-layouts: 46.1 us -> 16.2 us
    dot_general x22 -> x18, matrix products: 116 us -> 85.9 us  [dot(): return jnp.dot(left, right, preferred_element_type=F32)]
    reshape x2 -> x0, local copies, waits for them, and re-layouts: 24.1 us -> none  [the longest x1 17.7 us: per_device(): (shifted / jnp.sum(shifted, -1, keepdims=True)).reshape(HEADS * local_row...]
    sub x1 -> x0, other arithmetic: 21 us -> none  [per_device(): shifted = jnp.exp(scores - jnp.max(scores, -1, keepdims=True))]
  transfers between devices with their start and end apart: 82 -> 89, of which waited for: 28 -> 38; matrix products, arithmetic and copies ran while one was open for 62% -> 37% of each run, Pallas kernels for 2% -> 16%
where the time goes in v2:
time: 860 us; the launch traced here: 852 us
  waiting for transfers between devices  277 us (32%)
  matrix products  153 us (18%)
  Pallas kernels  135 us (16%)
  starting transfers between devices  112 us (13%)
  other arithmetic  98.5 us (11%)
  local copies, waits for them, and re-layouts  71 us (8%)
    ppermute x58, waiting for transfers between devices, cross(): return lax.ppermute(values, 'expert', [(i, i ^ bit) for i in range(count)])  275 us
    dot_general x18, matrix products, dot(): return jnp.dot(left, right, preferred_element_type=F32)  85.9 us
    ppermute x58, starting transfers between devices, cross(): return lax.ppermute(values, 'expert', [(i, i ^ bit) for i in range(count)])  84.4 us
    dot_general x10, matrix products, dot_t(): lax.dot_general(left, right, (((1,), (1,)), ((), ())), preferred_element_...  49.5 us
    pallas_call x1, Pallas kernels, expert_pass(): pl.pallas_call(functools.partial(expert_kernel, sources), grid_spec=pltpu...  46.6 us
    pallas_call x1, Pallas kernels, attend_back(): pl.pallas_call(attend_back_kernel, grid=(HEADS // 2,), in_specs=[pl.Block...  39.3 us
    pallas_call x1, Pallas kernels, attend(): pl.pallas_call(attend_kernel, grid=(steps,), in_specs=[pl.BlockSpec((rows...  27.5 us
    all_to_all x4, starting transfers between devices, exchange(): lax.all_to_all(rows.reshape(owners, capacity, model_width), 'expert', spl...  22.9 us
  transfers between devices with their start and end apart: 89, of which 38 were waited for; matrix products, arithmetic and copies ran while one was open for 37% of the time, Pallas kernels for 16%

profile of v2, /device:TPU:0, one launch (start us, length us, event | category | flops | bytes accessed | tf_op | source)
XLA Modules:
  0.0 851.6 jit_solution(3697894035982726234)
XLA Ops:
  13.6 3.7 collective-permute-start.4
  17.4 6.7 collective-permute-done.4
  26.5 4.5 collective-permute-done.5
  44.0 3.9 convolution_convert_fusion.2
  65.2 8.9 %all-to-all-start = ((bf16[16,56,2048]{2,1,0:T(8,128)(2,1)}), bf16[16,56,2048]{2,1,0:T(8,128)(2,1)}, u32[]{:S(2)}, u32[]{:S(2)}) async-start(bf16[16,56,2048]{2,1,0:T(8,128)(2,1)} %bitcast.284), calls=%async_computation | async-start | bytes 7340032 | tf_op jit(solution)/shard_map/all_to_all | solution.py:612
  79.8 22.1 %collective-permute-done.38 = bf16[4,2,2,64,128]{4,3,2,1,0:T(8,128)(2,1)S(1)} collective-permute-done((bf16[4,2,2,64,128]{4,3,2,1,0:T(8,128)(2,1)S(1)}, bf16[4,2,2,64,128]{4,3,2,1,0:T(8,128)(2,1)S(1)}, u32[]{:S(2)}, u32[]{:S(2)}) %collective-permute-start.38) | collective-permute-done | bytes 262176 | tf_op jit(solution)/shard_map/ppermute | solution.py:85
  102.7 24.2 %collective-permute-done.31 = bf16[8,1,2,64,128]{4,3,2,0,1:T(8,128)(2,1)S(1)} collective-permute-done((bf16[8,1,2,64,128]{4,3,2,0,1:T(8,128)(2,1)S(1)}, bf16[8,1,2,64,128]{4,3,2,0,1:T(8,128)(2,1)S(1)}, u32[]{:S(2)}, u32[]{:S(2)}) %collective-permute-start.31) | collective-permute-done | bytes 262176 | tf_op jit(solution)/shard_map/ppermute | solution.py:85
  133.4 5.5 fusion.145
  138.9 3.9 fusion.85
  145.9 5.9 maximum_select_fusion.expand_ref
  151.8 5.5 fusion.146
  157.3 4.0 convolution_add_fusion.1.raw_ref
  161.4 27.5 %shard_map.281 = (bf16[128,2048]{1,0:T(8,128)(2,1)S(1)}, bf16[2048,576]{1,0:T(8,128)(2,1)S(1)}, bf16[2048,2048]{1,0:T(8,128)(2,1)}, bf16[2048,512]{1,0:T(8,128)(2,1)S(1)}, bf16[128,2048]{1,0:T(8,128)(2,1)S(1)}) custom-call(f32[128,3072]{1,0:T(8,128)S(1)} %convolution_add_fusion.1.raw_ref, f32[128,32]{1,0:T(8,128)S(1)} %get-tuple-element.142.cosine_ref, ...), custom_call_target="tpu_custom_call" | custom-call | flops 9126805504 | bytes 8388608 | tf_op jit(solution)/shard_map/pallas_call | solution.py:306
  198.2 3.2 multiply_reduce_fusion.2
  210.1 7.6 fusion.76
  220.6 4.5 all-to-all-start.1
  232.1 6.2 convolution_add_fusion
  251.5 5.4 collective-permute-done.76
  257.1 8.8 %fusion.38 = f32[128,1024]{1,0:T(8,128)} fusion(bf16[1024,5632]{1,0:T(8,128)(2,1)} %param.29, bf16[128,2816]{1,0:T(8,128)(2,1)S(1)} %copy-done.18, bf16[128,2816]{1,0:T(8,128)(2,1)S(1)} %get-tuple-element.87), kind=kOutput, calls=%fused_computation.96 | convolution fusion | flops 1479278592 | bytes 13500416 | tf_op jit(solution)/shard_map/dot_general | solution.py:76
  266.1 3.2 shard_map.290
  269.3 19.5 %collective-permute-start.80 = (bf16[352,2048]{1,0:T(8,128)(2,1)S(1)}, bf16[352,2048]{1,0:T(8,128)(2,1)S(1)}, u32[]{:S(2)}, u32[]{:S(2)}) collective-permute-start(bf16[352,2048]{1,0:T(8,128)(2,1)S(1)} %get-tuple-element.74), channel_id=1, source_target_pairs={{0,4},{2,6},{4,0},{6,2},{8,12},{10,14},{12,8},{14,10},{16,20},{18,... | collective-permute-start | bytes 4325384 | tf_op jit(solution)/shard_map/ppermute | solution.py:85
  288.8 10.0 %collective-permute-done.71 = bf16[128,2816]{1,0:T(8,128)(2,1)S(1)} collective-permute-done((bf16[128,2816]{1,0:T(8,128)(2,1)S(1)}, bf16[128,2816]{1,0:T(8,128)(2,1)S(1)}, u32[]{:S(2)}, u32[]{:S(2)}) %collective-permute-start.71) | collective-permute-done | bytes 720928 | tf_op jit(solution)/shard_map/ppermute | solution.py:85
  299.6 8.8 %fusion.37 = f32[128,1024]{1,0:T(8,128)} fusion(bf16[1024,5632]{1,0:T(8,128)(2,1)} %collective-permute-done.13, bf16[128,2816]{1,0:T(8,128)(2,1)S(1)} %copy-done.18, bf16[128,2816]{1,0:T(8,128)(2,1)S(1)} %get-tuple-element.87), kind=kOutput, calls=%fused_computation.95 | convolution fusion | flops 1479278592 | bytes 13500416 | tf_op jit(solution)/shard_map/dot_general | solution.py:76
  308.5 16.8 %collective-permute-done.80 = bf16[352,2048]{1,0:T(8,128)(2,1)S(1)} collective-permute-done((bf16[352,2048]{1,0:T(8,128)(2,1)S(1)}, bf16[352,2048]{1,0:T(8,128)(2,1)S(1)}, u32[]{:S(2)}, u32[]{:S(2)}) %collective-permute-start.80) | collective-permute-done | bytes 1441824 | tf_op jit(solution)/shard_map/ppermute | solution.py:85
  326.8 4.5 shard_map.289
  334.8 4.5 shard_map.288
  346.6 15.7 %collective-permute-done.82 = bf16[88,2048]{1,0:T(8,128)(2,1)S(1)} collective-permute-done((bf16[88,2048]{1,0:T(8,128)(2,1)S(1)}, bf16[88,2048]{1,0:T(8,128)(2,1)S(1)}, u32[]{:S(2)}, u32[]{:S(2)}) %collective-permute-start.82) | collective-permute-done | bytes 360480 | tf_op jit(solution)/shard_map/ppermute | solution.py:85
  367.3 5.6 collective-permute-done.66
  374.9 46.6 %shard_map.282 = (bf16[896,2048]{1,0:T(8,128)(2,1)}, bf16[1408,896]{1,0:T(8,128)(2,1)}, bf16[2,2,704,896]{3,2,1,0:T(8,128)(2,1)}, f32[1,896]{1,0:T(1,128)}, bf16[16,896]{1,0:T(8,128)(2,1)}) custom-call(s32[1]{0:T(128)} %bitcast.9.here_ref, bf16[896,2048]{1,0:T(8,128)(2,1)} %bitcast.13.rows_ref, bf16[896,2048]{1,0:T(8,128)(2,1)} %bitcast.8.grads_ref, ...), custom_call_target="tpu_custom_call" | custom-call | flops 25836912640 | bytes 28311552 | tf_op jit(solution)/shard_map/pallas_call | solution.py:491
  421.5 4.6 all-to-all-start.3
  430.7 10.2 %convolution_convert_fusion = bf16[2,704,2048]{2,1,0:T(8,128)(2,1)} fusion(bf16[896,2048,1]{1,0,2:T(8,128)(2,1)} %bitcast.110, bf16[2,2,704,896]{3,2,1,0:T(8,128)(2,1)} %get-tuple-element.75), kind=kOutput, calls=%fused_computation.5 | convolution fusion | flops 5170266112 | bytes 11960320 | tf_op jit(solution)/shard_map/dot_general | solution.py:72
  443.9 7.4 convolution_convert_fusion.3
  451.6 4.9 fusion.18
  456.6 7.0 multiply_convert_fusion.1
  463.6 6.0 copy.166
  469.6 4.5 fusion.107
  474.1 56.7 %collective-permute-done.75 = bf16[64,2816]{1,0:T(8,128)(2,1)} collective-permute-done((bf16[64,2816]{1,0:T(8,128)(2,1)}, bf16[64,2816]{1,0:T(8,128)(2,1)}, u32[]{:S(2)}, u32[]{:S(2)}) %collective-permute-start.75) | collective-permute-done | bytes 360480 | tf_op jit(solution)/shard_map/ppermute | solution.py:85
  532.1 5.4 collective-permute-done.68
  540.1 4.9 all-to-all-start.2
  545.0 7.7 add_bitcast_fusion.1
  552.7 12.2 %add_bitcast_fusion = f32[1,2048,2,704]{1,3,2,0:T(8,128)} fusion(bf16[2,704,2048]{2,1,0:T(8,128)(2,1)} %collective-permute-done.83, bf16[896,2048,1]{1,0,2:T(8,128)(2,1)} %bitcast.110, bf16[2,2,704,896]{3,2,1,0:T(8,128)(2,1)} %get-tuple-element.75), kind=kOutput, calls=%fused_computation | convolution fusion | flops 5173149696 | bytes 23494656 | tf_op jit(solution)/shard_map/dot_general | solution.py:72
  565.0 3.2 multiply_reduce_fusion
  573.5 3.9 fusion.148
  577.5 39.3 %shard_map.283 = (bf16[128,3072]{1,0:T(8,128)(2,1)S(1)}, bf16[512,4096]{1,0:T(8,128)(2,1)}, f32[576,2048]{1,0:T(8,128)}) custom-call(bf16[128,2048]{1,0:T(8,128)(2,1)S(1)} %fusion.34.grad_ref, bf16[512,4096]{1,0:T(8,128)(2,1)} %maximum_select_fusion.expand_ref, bf16[2048,576]{1,0:T(8,128)(2,1)} %copy-done.3, ...), custom_call_target="tpu_custom_call" | custom-call | flops 22548578304 | bytes 8388608 | tf_op jit(solution)/shard_map/pallas_call | solution.py:389
  616.8 4.1 convert_element_type.636
  621.0 4.5 copy.155
  637.2 3.2 dynamic-slice_bitcast_fusion
  643.3 4.7 fusion.10
  648.0 5.8 fusion.151
  653.9 5.8 fusion.152
  680.5 3.5 collective-permute-done.20
  688.3 3.1 collective-permute-done.21
  695.6 3.1 collective-permute-done.25
  706.9 3.1 fusion.32
  715.7 3.2 shard_map.285
  727.2 12.5 %collective-permute-done.27 = bf16[512,19]{0,1:T(8,128)(2,1)} collective-permute-done((bf16[512,19]{0,1:T(8,128)(2,1)}, bf16[512,19]{0,1:T(8,128)(2,1)}, u32[]{:S(2)}, u32[]{:S(2)}) %collective-permute-start.27) | collective-permute-done | bytes 19488 | tf_op jit(solution)/shard_map/ppermute | solution.py:85
  767.2 4.1 collective-permute-done.47
  774.8 3.8 collective-permute-done.48
  784.6 8.7 %collective-permute-done.49 = bf16[64,576]{1,0:T(8,128)(2,1)S(1)} collective-permute-done((bf16[64,576]{1,0:T(8,128)(2,1)S(1)}, bf16[64,576]{1,0:T(8,128)(2,1)S(1)}, u32[]{:S(2)}, u32[]{:S(2)}) %collective-permute-start.49) | collective-permute-done | bytes 73760 | tf_op jit(solution)/shard_map/ppermute | solution.py:85
  795.0 3.4 collective-permute-start.44
  798.6 13.8 %collective-permute-done.44 = bf16[64,1536]{1,0:T(8,128)(2,1)S(1)} collective-permute-done((bf16[64,1536]{1,0:T(8,128)(2,1)S(1)}, bf16[64,1536]{1,0:T(8,128)(2,1)S(1)}, u32[]{:S(2)}, u32[]{:S(2)}) %collective-permute-start.44) | collective-permute-done | bytes 196640 | tf_op jit(solution)/shard_map/ppermute | solution.py:85
  818.0 11.6 %collective-permute-done.52 = bf16[64,4096]{1,0:T(8,128)(2,1)S(1)} collective-permute-done((bf16[64,4096]{1,0:T(8,128)(2,1)S(1)}, bf16[64,4096]{1,0:T(8,128)(2,1)S(1)}, u32[]{:S(2)}, u32[]{:S(2)}) %collective-permute-start.52) | collective-permute-done | bytes 524320 | tf_op jit(solution)/shard_map/ppermute | solution.py:85
  832.3 8.2 collective-permute-done.53
  840.7 8.3 collective-permute-done.61
  (559 shorter events, 253.3 us)
Async XLA Ops:
  1.9 155.4 %collective-permute-start.1 = (bf16[1024,3072]{1,0:T(8,128)(2,1)}, bf16[1024,3072]{1,0:T(8,128)(2,1)}, u32[]{:S(2)}, u32[]{:S(2)}) collective-permute-start(bf16[1024,3072]{1,0:T(8,128)(2,1)} %param.22), channel_id=1, source_target_pairs={{0,1},{1,0},{2,3},{3,2},{4,5},{5,4},{6,7},{7,6},{8,9},{9,8},{10,11... | collective-permute-start | bytes 18874376 | tf_op jit(solution)/shard_map/ppermute | solution.py:89
  2.4 75.6 %collective-permute-start.15 = (bf16[1024,16]{0,1:T(8,128)(2,1)}, bf16[1024,16]{0,1:T(8,128)(2,1)S(1)}, u32[]{:S(2)}, u32[]{:S(2)}) collective-permute-start(bf16[1024,16]{0,1:T(8,128)(2,1)} %param.28), channel_id=1, source_target_pairs={{0,1},{1,0},{2,3},{3,2},{4,5},{5,4},{6,7},{7,6},{8,9},{9,8},{10,11... | collective-permute-start | bytes 98312 | tf_op jit(solution)/shard_map/ppermute | solution.py:89
  2.5 229.2 %collective-permute-start.13 = (bf16[1024,5632]{1,0:T(8,128)(2,1)}, bf16[1024,5632]{1,0:T(8,128)(2,1)}, u32[]{:S(2)}, u32[]{:S(2)}) collective-permute-start(bf16[1024,5632]{1,0:T(8,128)(2,1)} %param.29), channel_id=1, source_target_pairs={{0,1},{1,0},{2,3},{3,2},{4,5},{5,4},{6,7},{7,6},{8,9},{9,8},{10,11... | collective-permute-start | bytes 34603016 | tf_op jit(solution)/shard_map/ppermute | solution.py:89
  35.3 12.6 %collective-permute-start.10 = (bf16[256,576]{1,0:T(8,128)(2,1)}, bf16[256,576]{1,0:T(8,128)(2,1)}, u32[]{:S(2)}, u32[]{:S(2)}) collective-permute-start(bf16[256,576]{1,0:T(8,128)(2,1)} %pad_maximum_fusion.27), channel_id=1, source_target_pairs={{0,2},{2,0},{4,6},{6,4},{8,10},{10,8},{12,14},{14,12},{16,18},{18,... | collective-permute-start | bytes 884744 | tf_op jit(solution)/shard_map/ppermute | solution.py:85
  42.0 13.7 %collective-permute-start.7 = (bf16[512,576]{0,1:T(8,128)(2,1)}, bf16[512,576]{0,1:T(8,128)(2,1)}, u32[]{:S(2)}, u32[]{:S(2)}) collective-permute-start(bf16[512,576]{0,1:T(8,128)(2,1)} %copy.151), channel_id=1, source_target_pairs={{0,2},{2,0},{4,6},{6,4},{8,10},{10,8},{12,14},{14,12},{16,18},{18,... | collective-permute-start | bytes 1769480 | tf_op jit(solution)/shard_map/ppermute | solution.py:85
  55.7 96.2 %collective-permute-start.14 = (bf16[1408,2048]{1,0:T(8,128)(2,1)}, bf16[1408,2048]{1,0:T(8,128)(2,1)}, u32[]{:S(2)}, u32[]{:S(2)}) collective-permute-start(bf16[1408,2048]{1,0:T(8,128)(2,1)} %param.30), channel_id=1, source_target_pairs={{0,1},{1,0},{2,3},{3,2},{4,5},{5,4},{6,7},{7,6},{8,9},{9,8},{10,11... | collective-permute-start | bytes 17301512 | tf_op jit(solution)/shard_map/ppermute | solution.py:89
  65.2 127.3 %all-to-all-start = ((bf16[16,56,2048]{2,1,0:T(8,128)(2,1)}), bf16[16,56,2048]{2,1,0:T(8,128)(2,1)}, u32[]{:S(2)}, u32[]{:S(2)}) async-start(bf16[16,56,2048]{2,1,0:T(8,128)(2,1)} %bitcast.284), calls=%async_computation | async-start | bytes 7340032 | tf_op jit(solution)/shard_map/all_to_all | solution.py:612
  75.3 27.2 %collective-permute-start.78 = (bf16[128,2048]{1,0:T(8,128)(2,1)S(1)}, bf16[128,2048]{1,0:T(8,128)(2,1)S(1)}, u32[]{:S(2)}, u32[]{:S(2)}) collective-permute-start(bf16[128,2048]{1,0:T(8,128)(2,1)S(1)} %fusion.25), channel_id=1, source_target_pairs={{0,2},{2,0},{4,6},{6,4},{8,10},{10,8},{12,14},{14,12},{16,18},{18,... | collective-permute-start | bytes 1572872 | tf_op jit(solution)/shard_map/ppermute | solution.py:85
  78.0 23.9 %collective-permute-start.38 = (bf16[4,2,2,64,128]{4,3,2,1,0:T(8,128)(2,1)S(1)}, bf16[4,2,2,64,128]{4,3,2,1,0:T(8,128)(2,1)S(1)}, u32[]{:S(2)}, u32[]{:S(2)}) collective-permute-start(bf16[4,2,2,64,128]{4,3,2,1,0:T(8,128)(2,1)S(1)} %get-tuple-element.126), channel_id=1, source_target_pairs={{0,4},{2,6},{4,0},{6,2},{8,12},{10,14},{12,8},{14,10},{16,20},{18,... | collective-permute-start | bytes 786440 | tf_op jit(solution)/shard_map/ppermute | solution.py:85
  101.9 25.0 %collective-permute-start.31 = (bf16[8,1,2,64,128]{4,3,2,0,1:T(8,128)(2,1)S(1)}, bf16[8,1,2,64,128]{4,3,2,0,1:T(8,128)(2,1)S(1)}, u32[]{:S(2)}, u32[]{:S(2)}) collective-permute-start(bf16[8,1,2,64,128]{4,3,2,0,1:T(8,128)(2,1)S(1)} %get-tuple-element.122), channel_id=1, source_target_pairs={{0,2},{2,0},{4,6},{6,4},{8,10},{10,8},{12,14},{14,12},{16,18},{18,... | collective-permute-start | bytes 786440 | tf_op jit(solution)/shard_map/ppermute | solution.py:85
  102.5 24.4 %collective-permute-start.39 = (bf16[8,64,256]{2,1,0:T(8,128)(2,1)S(1)}, bf16[8,64,256]{2,1,0:T(8,128)(2,1)S(1)}, u32[]{:S(2)}, u32[]{:S(2)}) collective-permute-start(bf16[8,64,256]{2,1,0:T(8,128)(2,1)S(1)} %get-tuple-element.125), channel_id=1, source_target_pairs={{0,1},{1,0},{2,3},{3,2},{4,5},{5,4},{6,7},{7,6},{8,9},{9,8},{10,11... | collective-permute-start | bytes 786440 | tf_op jit(solution)/shard_map/ppermute | solution.py:89
  129.9 15.7 %collective-permute-start.2 = (bf16[256,4096]{1,0:T(8,128)(2,1)}, bf16[256,4096]{1,0:T(8,128)(2,1)}, u32[]{:S(2)}, u32[]{:S(2)}) collective-permute-start(bf16[256,4096]{1,0:T(8,128)(2,1)} %param.25), channel_id=1, source_target_pairs={{0,1},{1,0},{2,3},{3,2},{4,5},{5,4},{6,7},{7,6},{8,9},{9,8},{10,11... | collective-permute-start | bytes 6291464 | tf_op jit(solution)/shard_map/ppermute | solution.py:89
  132.9 65.3 %collective-permute-start.12 = (bf16[1024,2048]{1,0:T(8,128)(2,1)}, bf16[1024,2048]{1,0:T(8,128)(2,1)}, u32[]{:S(2)}, u32[]{:S(2)}) collective-permute-start(bf16[1024,2048]{1,0:T(8,128)(2,1)} %param.26), channel_id=1, source_target_pairs={{0,1},{1,0},{2,3},{3,2},{4,5},{5,4},{6,7},{7,6},{8,9},{9,8},{10,11... | collective-permute-start | bytes 12582920 | tf_op jit(solution)/shard_map/ppermute | solution.py:89
  145.7 229.2 %collective-permute-start.17 = (bf16[704,2048]{1,0:T(8,128)(2,1)}, bf16[704,2048]{1,0:T(8,128)(2,1)}, u32[]{:S(2)}, u32[]{:S(2)}) collective-permute-start(bf16[704,2048]{1,0:T(8,128)(2,1)} %bitcast.17.refs_1_), channel_id=1, source_target_pairs={{0,1},{1,0},{2,3},{3,2},{4,5},{5,4},{6,7},{7,6},{8,9},{9,8},{10,11... | collective-permute-start | bytes 8650760 | tf_op jit(solution)/shard_map/ppermute | solution.py:89
  195.2 29.9 %collective-permute-start.55 = (bf16[4,2,2,64,128]{4,3,2,1,0:T(8,128)(2,1)}, bf16[4,2,2,64,128]{4,3,2,1,0:T(8,128)(2,1)}, u32[]{:S(2)}, u32[]{:S(2)}) collective-permute-start(bf16[4,2,2,64,128]{4,3,2,1,0:T(8,128)(2,1)} %get-tuple-element.118), channel_id=1, source_target_pairs={{0,4},{2,6},{4,0},{6,2},{8,12},{10,14},{12,8},{14,10},{16,20},{18,... | collective-permute-start | bytes 786440 | tf_op jit(solution)/shard_map/ppermute | solution.py:85
  205.6 21.7 %collective-permute-start.69 = (bf16[8,1,2,64,128]{4,3,2,0,1:T(8,128)(2,1)}, bf16[8,1,2,64,128]{4,3,2,0,1:T(8,128)(2,1)}, u32[]{:S(2)}, u32[]{:S(2)}) collective-permute-start(bf16[8,1,2,64,128]{4,3,2,0,1:T(8,128)(2,1)} %get-tuple-element.114), channel_id=1, source_target_pairs={{0,2},{2,0},{4,6},{6,4},{8,10},{10,8},{12,14},{14,12},{16,18},{18,... | collective-permute-start | bytes 786440 | tf_op jit(solution)/shard_map/ppermute | solution.py:85
  207.3 22.2 %collective-permute-start.62 = (bf16[4,2,2,64,128]{4,3,2,1,0:T(8,128)(2,1)}, bf16[4,2,2,64,128]{4,3,2,1,0:T(8,128)(2,1)}, u32[]{:S(2)}, u32[]{:S(2)}) collective-permute-start(bf16[4,2,2,64,128]{4,3,2,1,0:T(8,128)(2,1)} %get-tuple-element.110), channel_id=1, source_target_pairs={{0,4},{2,6},{4,0},{6,2},{8,12},{10,14},{12,8},{14,10},{16,20},{18,... | collective-permute-start | bytes 786440 | tf_op jit(solution)/shard_map/ppermute | solution.py:85
  220.6 154.3 %all-to-all-start.1 = ((bf16[16,56,2048]{2,1,0:T(8,128)(2,1)}), bf16[16,56,2048]{2,1,0:T(8,128)(2,1)}, u32[]{:S(2)}, u32[]{:S(2)}) async-start(bf16[16,56,2048]{2,1,0:T(8,128)(2,1)} %bitcast.281), calls=%async_computation.1 | async-start | bytes 7340032 | tf_op jit(solution)/shard_map/all_to_all | solution.py:612
  225.1 149.7 %collective-permute-start.16 = (bf16[2,704,2048]{2,1,0:T(8,128)(2,1)}, bf16[2,704,2048]{2,1,0:T(8,128)(2,1)}, u32[]{:S(2)}, u32[]{:S(2)}) collective-permute-start(bf16[2,704,2048]{2,1,0:T(8,128)(2,1)} %bitcast.338), channel_id=1, source_target_pairs={{0,1},{1,0},{2,3},{3,2},{4,5},{5,4},{6,7},{7,6},{8,9},{9,8},{10,11... | collective-permute-start | bytes 17301512 | tf_op jit(solution)/shard_map/ppermute | solution.py:89
  227.2 16.5 %collective-permute-start.56 = (bf16[8,64,256]{2,1,0:T(8,128)(2,1)}, bf16[8,64,256]{2,1,0:T(8,128)(2,1)}, u32[]{:S(2)}, u32[]{:S(2)}) collective-permute-start(bf16[8,64,256]{2,1,0:T(8,128)(2,1)} %get-tuple-element.117), channel_id=1, source_target_pairs={{0,1},{1,0},{2,3},{3,2},{4,5},{5,4},{6,7},{7,6},{8,9},{9,8},{10,11... | collective-permute-start | bytes 786440 | tf_op jit(solution)/shard_map/ppermute | solution.py:89
  229.5 17.9 %collective-permute-start.70 = (bf16[8,64,256]{2,1,0:T(8,128)(2,1)}, bf16[8,64,256]{2,1,0:T(8,128)(2,1)}, u32[]{:S(2)}, u32[]{:S(2)}) collective-permute-start(bf16[8,64,256]{2,1,0:T(8,128)(2,1)} %get-tuple-element.113), channel_id=1, source_target_pairs={{0,1},{1,0},{2,3},{3,2},{4,5},{5,4},{6,7},{7,6},{8,9},{9,8},{10,11... | collective-permute-start | bytes 786440 | tf_op jit(solution)/shard_map/ppermute | solution.py:89
  231.7 16.7 %collective-permute-start.63 = (bf16[8,64,256]{2,1,0:T(8,128)(2,1)}, bf16[8,64,256]{2,1,0:T(8,128)(2,1)}, u32[]{:S(2)}, u32[]{:S(2)}) collective-permute-start(bf16[8,64,256]{2,1,0:T(8,128)(2,1)} %get-tuple-element.109), channel_id=1, source_target_pairs={{0,1},{1,0},{2,3},{3,2},{4,5},{5,4},{6,7},{7,6},{8,9},{9,8},{10,11... | collective-permute-start | bytes 786440 | tf_op jit(solution)/shard_map/ppermute | solution.py:89
  243.7 13.2 %collective-permute-start.76 = (bf16[8,1,2,88,128]{4,3,2,0,1:T(8,128)(2,1)S(1)}, bf16[8,1,2,88,128]{4,3,2,0,1:T(8,128)(2,1)S(1)}, u32[]{:S(2)}, u32[]{:S(2)}) collective-permute-start(bf16[8,1,2,88,128]{4,3,2,0,1:T(8,128)(2,1)S(1)} %get-tuple-element.102), channel_id=1, source_target_pairs={{0,2},{2,0},{4,6},{6,4},{8,10},{10,8},{12,14},{14,12},{16,18},{18,... | collective-permute-start | bytes 1081352 | tf_op jit(solution)/shard_map/ppermute | solution.py:85
  249.4 49.4 %collective-permute-start.71 = (bf16[128,2816]{1,0:T(8,128)(2,1)S(1)}, bf16[128,2816]{1,0:T(8,128)(2,1)S(1)}, u32[]{:S(2)}, u32[]{:S(2)}) collective-permute-start(bf16[128,2816]{1,0:T(8,128)(2,1)S(1)} %copy-done.18), channel_id=1, source_target_pairs={{0,2},{2,0},{4,6},{6,4},{8,10},{10,8},{12,14},{14,12},{16,18},{18,... | collective-permute-start | bytes 2162696 | tf_op jit(solution)/shard_map/ppermute | solution.py:85
  249.7 49.3 %collective-permute-start.64 = (bf16[128,2816]{1,0:T(8,128)(2,1)S(1)}, bf16[128,2816]{1,0:T(8,128)(2,1)S(1)}, u32[]{:S(2)}, u32[]{:S(2)}) collective-permute-start(bf16[128,2816]{1,0:T(8,128)(2,1)S(1)} %get-tuple-element.87), channel_id=1, source_target_pairs={{0,4},{2,6},{4,0},{6,2},{8,12},{10,14},{12,8},{14,10},{16,20},{18,... | collective-permute-start | bytes 2162696 | tf_op jit(solution)/shard_map/ppermute | solution.py:85
  269.3 55.9 %collective-permute-start.80 = (bf16[352,2048]{1,0:T(8,128)(2,1)S(1)}, bf16[352,2048]{1,0:T(8,128)(2,1)S(1)}, u32[]{:S(2)}, u32[]{:S(2)}) collective-permute-start(bf16[352,2048]{1,0:T(8,128)(2,1)S(1)} %get-tuple-element.74), channel_id=1, source_target_pairs={{0,4},{2,6},{4,0},{6,2},{8,12},{10,14},{12,8},{14,10},{16,20},{18,... | collective-permute-start | bytes 4325384 | tf_op jit(solution)/shard_map/ppermute | solution.py:85
  298.9 27.7 %collective-permute-start.72 = (bf16[256,2816]{1,0:T(8,128)(2,1)S(1)}, bf16[256,2816]{1,0:T(8,128)(2,1)S(1)}, u32[]{:S(2)}, u32[]{:S(2)}) collective-permute-start(bf16[256,2816]{1,0:T(8,128)(2,1)S(1)} %pad_maximum_fusion.8), channel_id=1, source_target_pairs={{0,1},{1,0},{2,3},{3,2},{4,5},{5,4},{6,7},{7,6},{8,9},{9,8},{10,11... | collective-permute-start | bytes 4325384 | tf_op jit(solution)/shard_map/ppermute | solution.py:89
  299.1 34.1 %collective-permute-start.65 = (bf16[256,2816]{1,0:T(8,128)(2,1)S(1)}, bf16[256,2816]{1,0:T(8,128)(2,1)}, u32[]{:S(2)}, u32[]{:S(2)}) collective-permute-start(bf16[256,2816]{1,0:T(8,128)(2,1)S(1)} %pad_maximum_fusion.7), channel_id=1, source_target_pairs={{0,1},{1,0},{2,3},{3,2},{4,5},{5,4},{6,7},{7,6},{8,9},{9,8},{10,11... | collective-permute-start | bytes 4325384 | tf_op jit(solution)/shard_map/ppermute | solution.py:89
  325.5 17.9 %collective-permute-start.81 = (bf16[176,2048]{1,0:T(8,128)(2,1)S(1)}, bf16[176,2048]{1,0:T(8,128)(2,1)}, u32[]{:S(2)}, u32[]{:S(2)}) collective-permute-start(bf16[176,2048]{1,0:T(8,128)(2,1)S(1)} %add_convert_fusion), channel_id=1, source_target_pairs={{0,8},{2,10},{4,12},{6,14},{8,0},{10,2},{12,4},{14,6},{16,24},{18,... | collective-permute-start | bytes 2162696 | tf_op jit(solution)/shard_map/ppermute | solution.py:85
  331.4 33.2 %collective-permute-start.73 = (bf16[256,2816]{1,0:T(8,128)(2,1)S(1)}, bf16[256,2816]{1,0:T(8,128)(2,1)S(1)}, u32[]{:S(2)}, u32[]{:S(2)}) collective-permute-start(bf16[256,2816]{1,0:T(8,128)(2,1)S(1)} %get-tuple-element.72), channel_id=1, source_target_pairs={{0,4},{2,6},{4,0},{6,2},{8,12},{10,14},{12,8},{14,10},{16,20},{18,... | collective-permute-start | bytes 4325384 | tf_op jit(solution)/shard_map/ppermute | solution.py:85
  339.3 33.7 %collective-permute-start.66 = (bf16[256,2816]{1,0:T(8,128)(2,1)S(1)}, bf16[256,2816]{1,0:T(8,128)(2,1)S(1)}, u32[]{:S(2)}, u32[]{:S(2)}) collective-permute-start(bf16[256,2816]{1,0:T(8,128)(2,1)S(1)} %get-tuple-element.70), channel_id=1, source_target_pairs={{0,2},{2,0},{4,6},{6,4},{8,10},{10,8},{12,14},{14,12},{16,18},{18,... | collective-permute-start | bytes 4325384 | tf_op jit(solution)/shard_map/ppermute | solution.py:85
  344.5 17.8 %collective-permute-start.82 = (bf16[88,2048]{1,0:T(8,128)(2,1)S(1)}, bf16[88,2048]{1,0:T(8,128)(2,1)S(1)}, u32[]{:S(2)}, u32[]{:S(2)}) collective-permute-start(bf16[88,2048]{1,0:T(8,128)(2,1)S(1)} %add_convert_fusion.6), channel_id=1, source_target_pairs={{0,16},{2,18},{4,20},{6,22},{8,24},{10,26},{12,28},{14,30},{16,0},... | collective-permute-start | bytes 1081352 | tf_op jit(solution)/shard_map/ppermute | solution.py:85
  365.9 60.3 %collective-permute-start.74 = (bf16[128,2816]{1,0:T(8,128)(2,1)}, bf16[128,2816]{1,0:T(8,128)(2,1)}, u32[]{:S(2)}, u32[]{:S(2)}) collective-permute-start(bf16[128,2816]{1,0:T(8,128)(2,1)} %add_convert_fusion.1), channel_id=1, source_target_pairs={{0,8},{2,10},{4,12},{6,14},{8,0},{10,2},{12,4},{14,6},{16,24},{18,... | collective-permute-start | bytes 2162696 | tf_op jit(solution)/shard_map/ppermute | solution.py:85
  374.1 66.8 %collective-permute-start.67 = (bf16[128,2816]{1,0:T(8,128)(2,1)}, bf16[128,2816]{1,0:T(8,128)(2,1)}, u32[]{:S(2)}, u32[]{:S(2)}) collective-permute-start(bf16[128,2816]{1,0:T(8,128)(2,1)} %add_convert_fusion.2), channel_id=1, source_target_pairs={{0,8},{2,10},{4,12},{6,14},{8,0},{10,2},{12,4},{14,6},{16,24},{18,... | collective-permute-start | bytes 2162696 | tf_op jit(solution)/shard_map/ppermute | solution.py:85
  421.5 118.6 %all-to-all-start.3 = ((bf16[16,56,2048]{2,1,0:T(8,128)(2,1)}), bf16[16,56,2048]{2,1,0:T(8,128)(2,1)}, u32[]{:S(2)}, u32[]{:S(2)}) async-start(bf16[16,56,2048]{2,1,0:T(8,128)(2,1)} %bitcast.301), calls=%async_computation.3 | async-start | bytes 7340032 | tf_op jit(solution)/shard_map/all_to_all | solution.py:612
  428.0 102.7 %collective-permute-start.75 = (bf16[64,2816]{1,0:T(8,128)(2,1)}, bf16[64,2816]{1,0:T(8,128)(2,1)}, u32[]{:S(2)}, u32[]{:S(2)}) collective-permute-start(bf16[64,2816]{1,0:T(8,128)(2,1)} %add_convert_fusion.7), channel_id=1, source_target_pairs={{0,16},{2,18},{4,20},{6,22},{8,24},{10,26},{12,28},{14,30},{16,0},... | collective-permute-start | bytes 1081352 | tf_op jit(solution)/shard_map/ppermute | solution.py:85
  440.9 111.8 %collective-permute-start.83 = (bf16[2,704,2048]{2,1,0:T(8,128)(2,1)}, bf16[2,704,2048]{2,1,0:T(8,128)(2,1)}, u32[]{:S(2)}, u32[]{:S(2)}) collective-permute-start(bf16[2,704,2048]{2,1,0:T(8,128)(2,1)} %convolution_convert_fusion), channel_id=1, source_target_pairs={{0,1},{1,0},{2,3},{3,2},{4,5},{5,4},{6,7},{7,6},{8,9},{9,8},{10,11... | collective-permute-start | bytes 17301512 | tf_op jit(solution)/shard_map/ppermute | solution.py:89
  443.0 94.4 %collective-permute-start.68 = (bf16[64,2816]{1,0:T(8,128)(2,1)}, bf16[64,2816]{1,0:T(8,128)(2,1)}, u32[]{:S(2)}, u32[]{:S(2)}) collective-permute-start(bf16[64,2816]{1,0:T(8,128)(2,1)} %add_convert_fusion.8), channel_id=1, source_target_pairs={{0,16},{2,18},{4,20},{6,22},{8,24},{10,26},{12,28},{14,30},{16,0},... | collective-permute-start | bytes 1081352 | tf_op jit(solution)/shard_map/ppermute | solution.py:85
  451.3 93.7 %collective-permute-start.84 = (bf16[704,2048]{1,0:T(8,128)(2,1)}, bf16[704,2048]{1,0:T(8,128)(2,1)}, u32[]{:S(2)}, u32[]{:S(2)}) collective-permute-start(bf16[704,2048]{1,0:T(8,128)(2,1)} %convolution_convert_fusion.3), channel_id=1, source_target_pairs={{0,1},{1,0},{2,3},{3,2},{4,5},{5,4},{6,7},{7,6},{8,9},{9,8},{10,11... | collective-permute-start | bytes 8650760 | tf_op jit(solution)/shard_map/ppermute | solution.py:89
  540.1 100.2 %all-to-all-start.2 = ((bf16[16,56,2048]{2,1,0:T(8,128)(2,1)}), bf16[16,56,2048]{2,1,0:T(8,128)(2,1)}, u32[]{:S(2)}, u32[]{:S(2)}) async-start(bf16[16,56,2048]{2,1,0:T(8,128)(2,1)} %bitcast.300), calls=%async_computation.2 | async-start | bytes 7340032 | tf_op jit(solution)/shard_map/all_to_all | solution.py:612
  569.6 123.7 %collective-permute-start.57 = (bf16[128,2048]{1,0:T(8,128)(2,1)S(1)}, bf16[128,2048]{1,0:T(8,128)(2,1)}, u32[]{:S(2)}, u32[]{:S(2)}) collective-permute-start(bf16[128,2048]{1,0:T(8,128)(2,1)S(1)} %get-tuple-element.85), channel_id=1, source_target_pairs={{0,4},{2,6},{4,0},{6,2},{8,12},{10,14},{12,8},{14,10},{16,20},{18,... | collective-permute-start | bytes 1572872 | tf_op jit(solution)/shard_map/ppermute | solution.py:85
  630.2 30.2 %collective-permute-start.18 = (bf16[512,576]{0,1:T(8,128)(2,1)}, bf16[512,576]{0,1:T(8,128)(2,1)}, u32[]{:S(2)}, u32[]{:S(2)}) collective-permute-start(bf16[512,576]{0,1:T(8,128)(2,1)} %copy.156), channel_id=1, source_target_pairs={{0,2},{2,0},{4,6},{6,4},{8,10},{10,8},{12,14},{14,12},{16,18},{18,... | collective-permute-start | bytes 1769480 | tf_op jit(solution)/shard_map/ppermute | solution.py:85
  633.4 28.1 %collective-permute-start.22 = (bf16[512,576]{0,1:T(8,128)(2,1)}, bf16[512,576]{0,1:T(8,128)(2,1)}, u32[]{:S(2)}, u32[]{:S(2)}) collective-permute-start(bf16[512,576]{0,1:T(8,128)(2,1)} %copy.161), channel_id=1, source_target_pairs={{0,4},{2,6},{4,0},{6,2},{8,12},{10,14},{12,8},{14,10},{16,20},{18,... | collective-permute-start | bytes 1769480 | tf_op jit(solution)/shard_map/ppermute | solution.py:85
  635.5 30.5 %collective-permute-start.40 = (bf16[128,1536]{1,0:T(8,128)(2,1)}, bf16[128,1536]{1,0:T(8,128)(2,1)}, u32[]{:S(2)}, u32[]{:S(2)}) collective-permute-start(bf16[128,1536]{1,0:T(8,128)(2,1)} %get-tuple-element.99), channel_id=1, source_target_pairs={{0,4},{2,6},{4,0},{6,2},{8,12},{10,14},{12,8},{14,10},{16,20},{18,... | collective-permute-start | bytes 1179656 | tf_op jit(solution)/shard_map/ppermute | solution.py:85
  636.3 33.0 %collective-permute-start.33 = (bf16[128,1536]{1,0:T(8,128)(2,1)S(1)}, bf16[128,1536]{1,0:T(8,128)(2,1)}, u32[]{:S(2)}, u32[]{:S(2)}) collective-permute-start(bf16[128,1536]{1,0:T(8,128)(2,1)S(1)} %get-tuple-element.98), channel_id=1, source_target_pairs={{0,2},{2,0},{4,6},{6,4},{8,10},{10,8},{12,14},{14,12},{16,18},{18,... | collective-permute-start | bytes 1179656 | tf_op jit(solution)/shard_map/ppermute | solution.py:85
  660.4 118.4 %collective-permute-start.50 = (bf16[16,16,4096]{2,1,0:T(8,128)(2,1)}, bf16[16,16,4096]{2,1,0:T(8,128)(2,1)}, u32[]{:S(2)}, u32[]{:S(2)}) collective-permute-start(bf16[16,16,4096]{2,1,0:T(8,128)(2,1)} %dynamic-slice_bitcast_fusion), channel_id=1, source_target_pairs={{0,1},{1,0},{2,3},{3,2},{4,5},{5,4},{6,7},{7,6},{8,9},{9,8},{10,11... | collective-permute-start | bytes 6291464 | tf_op jit(solution)/shard_map/ppermute | solution.py:89
  669.2 45.0 %collective-permute-start.41 = (bf16[256,1536]{1,0:T(8,128)(2,1)}, bf16[256,1536]{1,0:T(8,128)(2,1)}, u32[]{:S(2)}, u32[]{:S(2)}) collective-permute-start(bf16[256,1536]{1,0:T(8,128)(2,1)} %pad_maximum_fusion.15), channel_id=1, source_target_pairs={{0,1},{1,0},{2,3},{3,2},{4,5},{5,4},{6,7},{7,6},{8,9},{9,8},{10,11... | collective-permute-start | bytes 2359304 | tf_op jit(solution)/shard_map/ppermute | solution.py:89
  688.2 33.1 %collective-permute-start.34 = (bf16[256,1536]{1,0:T(8,128)(2,1)}, bf16[256,1536]{1,0:T(8,128)(2,1)}, u32[]{:S(2)}, u32[]{:S(2)}) collective-permute-start(bf16[256,1536]{1,0:T(8,128)(2,1)} %pad_maximum_fusion.14), channel_id=1, source_target_pairs={{0,1},{1,0},{2,3},{3,2},{4,5},{5,4},{6,7},{7,6},{8,9},{9,8},{10,11... | collective-permute-start | bytes 2359304 | tf_op jit(solution)/shard_map/ppermute | solution.py:89
  695.4 65.7 %collective-permute-start.58 = (bf16[256,2048]{1,0:T(8,128)(2,1)}, bf16[256,2048]{1,0:T(8,128)(2,1)}, u32[]{:S(2)}, u32[]{:S(2)}) collective-permute-start(bf16[256,2048]{1,0:T(8,128)(2,1)} %pad_maximum_fusion.10), channel_id=1, source_target_pairs={{0,1},{1,0},{2,3},{3,2},{4,5},{5,4},{6,7},{7,6},{8,9},{9,8},{10,11... | collective-permute-start | bytes 3145736 | tf_op jit(solution)/shard_map/ppermute | solution.py:89
  704.0 51.7 %collective-permute-start.45 = (bf16[128,576]{1,0:T(8,128)(2,1)}, bf16[128,576]{1,0:T(8,128)(2,1)}, u32[]{:S(2)}, u32[]{:S(2)}) collective-permute-start(bf16[128,576]{1,0:T(8,128)(2,1)} %pad_maximum_fusion.32), channel_id=1, source_target_pairs={{0,4},{2,6},{4,0},{6,2},{8,12},{10,14},{12,8},{14,10},{16,20},{18,... | collective-permute-start | bytes 442376 | tf_op jit(solution)/shard_map/ppermute | solution.py:85
  718.9 52.6 %collective-permute-start.42 = (bf16[256,1536]{1,0:T(8,128)(2,1)}, bf16[256,1536]{1,0:T(8,128)(2,1)}, u32[]{:S(2)}, u32[]{:S(2)}) collective-permute-start(bf16[256,1536]{1,0:T(8,128)(2,1)} %get-tuple-element.63), channel_id=1, source_target_pairs={{0,2},{2,0},{4,6},{6,4},{8,10},{10,8},{12,14},{14,12},{16,18},{18,... | collective-permute-start | bytes 2359304 | tf_op jit(solution)/shard_map/ppermute | solution.py:85
  721.3 18.4 %collective-permute-start.27 = (bf16[512,19]{0,1:T(8,128)(2,1)}, bf16[512,19]{0,1:T(8,128)(2,1)}, u32[]{:S(2)}, u32[]{:S(2)}) collective-permute-start(bf16[512,19]{0,1:T(8,128)(2,1)} %convert_element_type.673), channel_id=1, source_target_pairs={{0,2},{2,0},{4,6},{6,4},{8,10},{10,8},{12,14},{14,12},{16,18},{18,... | collective-permute-start | bytes 58376 | tf_op jit(solution)/shard_map/ppermute | solution.py:85
  753.8 20.8 %collective-permute-start.35 = (bf16[256,1536]{1,0:T(8,128)(2,1)S(1)}, bf16[256,1536]{1,0:T(8,128)(2,1)S(1)}, u32[]{:S(2)}, u32[]{:S(2)}) collective-permute-start(bf16[256,1536]{1,0:T(8,128)(2,1)S(1)} %get-tuple-element.61), channel_id=1, source_target_pairs={{0,4},{2,6},{4,0},{6,2},{8,12},{10,14},{12,8},{14,10},{16,20},{18,... | collective-permute-start | bytes 2359304 | tf_op jit(solution)/shard_map/ppermute | solution.py:85
  765.4 52.4 %collective-permute-start.59 = (bf16[256,2048]{1,0:T(8,128)(2,1)S(1)}, bf16[256,2048]{1,0:T(8,128)(2,1)S(1)}, u32[]{:S(2)}, u32[]{:S(2)}) collective-permute-start(bf16[256,2048]{1,0:T(8,128)(2,1)S(1)} %get-tuple-element.68), channel_id=1, source_target_pairs={{0,2},{2,0},{4,6},{6,4},{8,10},{10,8},{12,14},{14,12},{16,18},{18,... | collective-permute-start | bytes 3145736 | tf_op jit(solution)/shard_map/ppermute | solution.py:85
  772.6 21.4 %collective-permute-start.43 = (bf16[128,1536]{1,0:T(8,128)(2,1)S(1)}, bf16[128,1536]{1,0:T(8,128)(2,1)S(1)}, u32[]{:S(2)}, u32[]{:S(2)}) collective-permute-start(bf16[128,1536]{1,0:T(8,128)(2,1)S(1)} %add_convert_fusion.4), channel_id=1, source_target_pairs={{0,8},{2,10},{4,12},{6,14},{8,0},{10,2},{12,4},{14,6},{16,24},{18,... | collective-permute-start | bytes 1179656 | tf_op jit(solution)/shard_map/ppermute | solution.py:85
  774.8 23.7 %collective-permute-start.36 = (bf16[128,1536]{1,0:T(8,128)(2,1)S(1)}, bf16[128,1536]{1,0:T(8,128)(2,1)S(1)}, u32[]{:S(2)}, u32[]{:S(2)}) collective-permute-start(bf16[128,1536]{1,0:T(8,128)(2,1)S(1)} %add_convert_fusion.5), channel_id=1, source_target_pairs={{0,8},{2,10},{4,12},{6,14},{8,0},{10,2},{12,4},{14,6},{16,24},{18,... | collective-permute-start | bytes 1179656 | tf_op jit(solution)/shard_map/ppermute | solution.py:85
  778.6 14.7 %collective-permute-start.49 = (bf16[64,576]{1,0:T(8,128)(2,1)S(1)}, bf16[64,576]{1,0:T(8,128)(2,1)S(1)}, u32[]{:S(2)}, u32[]{:S(2)}) collective-permute-start(bf16[64,576]{1,0:T(8,128)(2,1)S(1)} %add_convert_fusion.17), channel_id=1, source_target_pairs={{0,16},{2,18},{4,20},{6,22},{8,24},{10,26},{12,28},{14,30},{16,0},... | collective-permute-start | bytes 221192 | tf_op jit(solution)/shard_map/ppermute | solution.py:85
  783.4 32.5 %collective-permute-start.51 = (bf16[128,4096]{1,0:T(8,128)(2,1)S(1)}, bf16[128,4096]{1,0:T(8,128)(2,1)S(1)}, u32[]{:S(2)}, u32[]{:S(2)}) collective-permute-start(bf16[128,4096]{1,0:T(8,128)(2,1)S(1)} %bitcast.308), channel_id=1, source_target_pairs={{0,2},{2,0},{4,6},{6,4},{8,10},{10,8},{12,14},{14,12},{16,18},{18,... | collective-permute-start | bytes 3145736 | tf_op jit(solution)/shard_map/ppermute | solution.py:85
  795.0 17.5 %collective-permute-start.44 = (bf16[64,1536]{1,0:T(8,128)(2,1)S(1)}, bf16[64,1536]{1,0:T(8,128)(2,1)S(1)}, u32[]{:S(2)}, u32[]{:S(2)}) collective-permute-start(bf16[64,1536]{1,0:T(8,128)(2,1)S(1)} %add_convert_fusion.12), channel_id=1, source_target_pairs={{0,16},{2,18},{4,20},{6,22},{8,24},{10,26},{12,28},{14,30},{16,0},... | collective-permute-start | bytes 589832 | tf_op jit(solution)/shard_map/ppermute | solution.py:85
  798.5 16.3 %collective-permute-start.37 = (bf16[64,1536]{1,0:T(8,128)(2,1)S(1)}, bf16[64,1536]{1,0:T(8,128)(2,1)S(1)}, u32[]{:S(2)}, u32[]{:S(2)}) collective-permute-start(bf16[64,1536]{1,0:T(8,128)(2,1)S(1)} %add_convert_fusion.13), channel_id=1, source_target_pairs={{0,16},{2,18},{4,20},{6,22},{8,24},{10,26},{12,28},{14,30},{16,0},... | collective-permute-start | bytes 589832 | tf_op jit(solution)/shard_map/ppermute | solution.py:85
  816.0 13.6 %collective-permute-start.52 = (bf16[64,4096]{1,0:T(8,128)(2,1)S(1)}, bf16[64,4096]{1,0:T(8,128)(2,1)S(1)}, u32[]{:S(2)}, u32[]{:S(2)}) collective-permute-start(bf16[64,4096]{1,0:T(8,128)(2,1)S(1)} %fusion.36), channel_id=1, source_target_pairs={{0,4},{2,6},{4,0},{6,2},{8,12},{10,14},{12,8},{14,10},{16,20},{18,... | collective-permute-start | bytes 1572872 | tf_op jit(solution)/shard_map/ppermute | solution.py:85
  817.9 13.3 %collective-permute-start.60 = (bf16[128,2048]{1,0:T(8,128)(2,1)S(1)}, bf16[128,2048]{1,0:T(8,128)(2,1)S(1)}, u32[]{:S(2)}, u32[]{:S(2)}) collective-permute-start(bf16[128,2048]{1,0:T(8,128)(2,1)S(1)} %add_convert_fusion.3), channel_id=1, source_target_pairs={{0,8},{2,10},{4,12},{6,14},{8,0},{10,2},{12,4},{14,6},{16,24},{18,... | collective-permute-start | bytes 1572872 | tf_op jit(solution)/shard_map/ppermute | solution.py:85
  829.7 10.7 %collective-permute-start.53 = (bf16[32,4096]{1,0:T(8,128)(2,1)S(1)}, bf16[32,4096]{1,0:T(8,128)(2,1)S(1)}, u32[]{:S(2)}, u32[]{:S(2)}) collective-permute-start(bf16[32,4096]{1,0:T(8,128)(2,1)S(1)} %fusion.43), channel_id=1, source_target_pairs={{0,8},{2,10},{4,12},{6,14},{8,0},{10,2},{12,4},{14,6},{16,24},{18,... | collective-permute-start | bytes 786440 | tf_op jit(solution)/shard_map/ppermute | solution.py:85
  831.4 17.6 %collective-permute-start.61 = (bf16[64,2048]{1,0:T(8,128)(2,1)S(1)}, bf16[64,2048]{1,0:T(8,128)(2,1)S(1)}, u32[]{:S(2)}, u32[]{:S(2)}) collective-permute-start(bf16[64,2048]{1,0:T(8,128)(2,1)S(1)} %add_convert_fusion.11), channel_id=1, source_target_pairs={{0,16},{2,18},{4,20},{6,22},{8,24},{10,26},{12,28},{14,30},{16,0},... | collective-permute-start | bytes 786440 | tf_op jit(solution)/shard_map/ppermute | solution.py:85
  (122 other events, 1816.6 us)

commit v3 on v2

--- a/solution.py
+++ b/solution.py
@@ -132,13 +132,26 @@
     return values, places
 
 
-def fold(pieces, bits, rows):
-    count = rows << len(bits)
+def after(value, *gates):
+    leaves, tree = jax.tree.flatten(value)
+    fenced = lax.optimization_barrier((*leaves, *jax.tree.leaves(gates)))
+    return jax.tree.unflatten(tree, fenced[: len(leaves)])
+
+
+def fold_step(pieces, bit, *gates):
+    count = pieces[0].shape[0] // 2
+    sent = sum(p[count:].astype(F32) for p in pieces).astype(BF)
+    return [p[:count] for p in pieces] + [cross(after(sent, *gates), bit)]
+
+
+def fold_end(pieces):
+    return sum(p.astype(F32) for p in pieces)
+
+
+def fold(pieces, bits):
     for bit in bits:
-        count = count // 2
-        sent = sum(p[count:].astype(F32) for p in pieces).astype(BF)
-        pieces = [p[:count] for p in pieces] + [cross(sent, bit)]
-    return sum(p.astype(F32) for p in pieces)
+        pieces = fold_step(pieces, bit)
+    return fold_end(pieces)
 
 
 def fold_order(bits):
@@ -245,11 +258,17 @@
     return jnp.concatenate([right, swap(right)], 0)
 
 
-def reduce_product(left, right, bits):
-    kept, sent = gradient_halves(left, right, lax.axis_index("expert"), bits[1:])
-    rows = 2 * kept.shape[0] >> len(bits) - 1
-    arrived = cross(sent, bits[1])
-    return fold([kept, arrived], bits[2:], rows)
+def product_group(left, right, bit):
+    return group_left(left, bit), group_right(right, bit)
+
+
+def product_halves(group, bits):
+    return gradient_halves(*group, lax.axis_index("expert"), bits)
+
+
+def product_sum(group, bits):
+    kept, sent = product_halves(group, bits[1:])
+    return fold([kept, cross(sent, bits[1])], bits[2:])
 
 
 def reduce_partial(partial, bits):
@@ -262,7 +281,7 @@
     kept = lax.dynamic_index_in_dim(blocks, own, 1, keepdims=False)
     sent = lax.dynamic_index_in_dim(blocks, 1 - own, 1, keepdims=False)
     total = (kept.astype(F32) + swap(sent).astype(F32)).astype(partial.dtype)
-    return fold([differing(total, bits, lax.axis_index("expert")).reshape(experts * rows, -1)], bits, rows)
+    return fold([differing(total, bits, lax.axis_index("expert")).reshape(experts * rows, -1)], bits)
 
 
 def attend_kernel(
@@ -420,11 +439,60 @@
     )(grad_out, expand, keys, weights, queries, mixed, nope, cosine, sine)
 
 
+def pick_kernel(spread_ref, tokens_ref, *out_refs):
+    for m, out_ref in enumerate(out_refs):
+        out_ref[...] = dot(spread_ref[m], tokens_ref[...]).astype(BF)
+
+
+def pick_rows(spread, tokens):
+    planes, lines, capacity, count = spread.shape
+    width = tokens.shape[-1]
+    return pl.pallas_call(
+        pick_kernel,
+        grid=(lines,),
+        in_specs=[
+            pl.BlockSpec((planes, None, capacity, count), lambda j: (0, j, 0, 0)),
+            pl.BlockSpec((None, count, width), lambda j: (j, 0, 0)),
+        ],
+        out_specs=[pl.BlockSpec((None, capacity, width), lambda j: (j, 0, 0))] * planes,
+        out_shape=[jax.ShapeDtypeStruct((lines, capacity, width), BF)] * planes,
+        compiler_params=pltpu.CompilerParams(vmem_limit_bytes=24 << 20),
+        cost_estimate=pl.CostEstimate(
+            flops=2 * planes * lines * capacity * count * width,
+            bytes_accessed=2 * lines * (count + planes * capacity) * width,
+            transcendentals=0,
+        ),
+    )(spread, tokens)
+
+
+def put_kernel(spread_ref, *refs):
+    refs[-1][...] = sum(t_dot(spread_ref[m], ref[...]) for m, ref in enumerate(refs[:-1]))
+
+
+def put_rows(spread, rows):
+    planes, lines, capacity, count = spread.shape
+    width = rows[0].shape[-1]
+    return pl.pallas_call(
+        put_kernel,
+        grid=(lines,),
+        in_specs=[pl.BlockSpec((planes, None, capacity, count), lambda j: (0, j, 0, 0))]
+        + [pl.BlockSpec((None, capacity, width), lambda j: (j, 0, 0))] * planes,
+        out_specs=pl.BlockSpec((None, count, width), lambda j: (j, 0, 0)),
+        out_shape=jax.ShapeDtypeStruct((lines, count, width), F32),
+        compiler_params=pltpu.CompilerParams(vmem_limit_bytes=24 << 20),
+        cost_estimate=pl.CostEstimate(
+            flops=2 * planes * lines * capacity * count * width,
+            bytes_accessed=2 * lines * (2 * count + planes * capacity) * width,
+            transcendentals=0,
+        ),
+    )(spread, *rows)
+
+
 def expert_kernel(sources, here_ref, rows_ref, grads_ref, router_ref, *refs):
     weights = refs[: 2 * sources]
     (
-        row_grad_ref, units_ref, back_ref, gate_ref, logit_grad_ref, total_ref, probs_ref, share_ref,
-    ) = refs[2 * sources :]
+        row_grad_refs, units_ref, back_ref, gate_ref, logit_grad_ref, total_ref, probs_ref, share_ref,
+    ) = (refs[2 * sources : 2 * sources + 2], *refs[2 * sources + 2 :])
     step = pl.program_id(0)
     chunks = pl.num_programs(0) // sources
 
@@ -466,9 +534,12 @@
         own = lax.broadcasted_iota(jnp.int32, probs.shape, 0) == here_ref[0]
         grad = probs * (own.astype(F32) - gate_ref[...]) * share_ref[...]
         logit_grad_ref[...] = grad.astype(BF)
-        row_grad_ref[...] = (
-            total_ref[...] + t_dot(logit_grad_ref[...], router_ref[...])
-        ).astype(BF)
+        half = row_grad_refs[0].shape[1]
+        for k, row_grad_ref in enumerate(row_grad_refs):
+            part = slice(k * half, (k + 1) * half)
+            row_grad_ref[...] = (
+                total_ref[:, part] + t_dot(logit_grad_ref[...], router_ref[:, part])
+            ).astype(BF)
 
 
 def expert_pass(here, rows, grads, router, weights):
@@ -495,7 +566,8 @@
             grid=(sources * chunks,),
             in_specs=in_specs,
             out_specs=[
-                pl.BlockSpec((count, width), lambda i, h: (0, 0), pipeline_mode=once),
+                pl.BlockSpec((count, width // 2), lambda i, h: (0, 0), pipeline_mode=once),
+                pl.BlockSpec((count, width // 2), lambda i, h: (0, 0), pipeline_mode=once),
                 pl.BlockSpec((tile, count), lambda i, h: (i, 0)),
                 pl.BlockSpec(
                     (None, 2, tile, count), lambda i, h: (i // chunks, 0, i % chunks, 0)
@@ -510,7 +582,8 @@
             ],
         ),
         out_shape=[
-            jax.ShapeDtypeStruct((count, width), BF),
+            jax.ShapeDtypeStruct((count, width // 2), BF),
+            jax.ShapeDtypeStruct((count, width // 2), BF),
             jax.ShapeDtypeStruct((sources * units, count), BF),
             jax.ShapeDtypeStruct((sources, 2, units, count), BF),
             jax.ShapeDtypeStruct((1, count), F32),
@@ -598,24 +671,36 @@
     grad_out = cotangent[0].astype(F32) * live_rows
     grad_out_low = grad_out.astype(BF)
 
-    expert_ids = jnp.arange(experts_all, dtype=jnp.int32)
-    member = jnp.any(routes[0][:, :, None] == expert_ids[None, None, :], 1)
+    plane = range(4)
+    line_bits = tuple(reversed(bits[2:]))
+    line_routes, line_places = collect(routes[0].T, line_bits)
+    lines = len(line_places)
+    line_routes = line_routes.reshape(lines, 1, topk_count, local_rows)
+    expert_ids = (here ^ jnp.arange(len(plane), dtype=jnp.int32))[:, None, None, None]
+    member = jnp.any(line_routes[None, :, 0] == expert_ids, 2).reshape(-1, local_rows)
     token_ids = jnp.arange(local_rows, dtype=jnp.int32)
-    earlier = (token_ids[None, :] < token_ids[:, None]).astype(BF)
-    rank = dot(earlier, member.astype(BF)).astype(jnp.int32)
+    earlier = (token_ids[:, None] < token_ids[None, :]).astype(BF)
+    rank = dot(member.astype(BF), earlier).astype(jnp.int32)
     place_ids = jnp.arange(capacity, dtype=jnp.int32)
     spread = (
-        member.T[:, None, :] & (rank.T[:, None, :] == place_ids[None, :, None])
-    ).reshape(experts_all * capacity, local_rows).astype(BF)
-
-    def exchange(rows):
-        return lax.all_to_all(
-            rows.reshape(owners, capacity, model_width),
-            "expert",
-            split_axis=0,
-            concat_axis=0,
-            tiled=True,
-        ).reshape(owners * capacity, model_width)
+        (member[:, None, :] & (rank[:, None, :] == place_ids[None, :, None]))
+        .reshape(len(plane), lines, capacity, local_rows)
+        .astype(BF)
+    )
+
+    def dispatch(values):
+        gathered, _ = collect(values, line_bits)
+        rows = pick_rows(spread, gathered.reshape(lines, local_rows, -1))
+        rows = [rows[0]] + [cross(rows[m], m) for m in plane[1:]]
+        return jnp.stack(rows).reshape(-1, values.shape[1])
+
+    def in_plane(values):
+        rows = values.reshape(len(plane), lines, capacity, -1)
+        return [rows[0]] + [cross(rows[m], m) for m in plane[1:]]
+
+    def along_line(rows):
+        sums = put_rows(spread, rows).reshape(lines * local_rows, -1)
+        return fold([sums], tuple(reversed(line_bits)))
 
     inputs = tokens[0].astype(F32)
     inverse_attn = rms_scale(inputs)
@@ -630,10 +715,14 @@
     own_keys = jnp.concatenate([latent_in, key_rope], -1)
     part = local_rows // 2
     collect_bits = (tuple(reversed(first_x)), tuple(reversed(first_y)))
+    own_parts = [collect(own_keys[k * part : (k + 1) * part], line_bits)[0] for k in range(2)]
+    grads_sent, *own_parts = lax.optimization_barrier((grad_out_low, *own_parts))
     keys, key_index = [], []
     for k in range(2):
-        gathered, places = collect(own_keys[k * part : (k + 1) * part], collect_bits[k])
-        keys.append(gathered)
+        keys.append(collect(own_parts[k], collect_bits[k][len(line_bits) :])[0])
+        places = [0]
+        for bit in collect_bits[k]:
+            places = places + [place ^ bit for place in places]
         key_index.append(
             (
                 (here ^ jnp.array(places, jnp.int32))[:, None] * local_rows
@@ -643,9 +732,7 @@
         )
     keys = jnp.concatenate(keys, 0)
     key_index = jnp.concatenate(key_index)
-
-    sent_grads, keys = lax.optimization_barrier((dot(spread, grad_out_low).astype(BF), keys))
-    received_grads = exchange(sent_grads)
+    received_grads = dispatch(grads_sent)
 
     query_raw = times(attn_in, query_blocks)
     key_segment = layout(lengths[0], key_index)[0]
@@ -656,25 +743,96 @@
     query_nope, queries, attention, mixed_latent, mixed_heads = attend(
         query_raw, cosine, sine_table, expand, keys, bias
     )
-    mixed_heads, received_grads = lax.optimization_barrier((mixed_heads, received_grads))
+    mixed_heads = after(
+        mixed_heads, received_grads, output_blocks, shared_in_blocks, shared_out_blocks, expert_weights
+    )
     hidden_state = inputs + times(mixed_heads, output_blocks)
     inverse_ffn = rms_scale(hidden_state)
     normed_ffn = hidden_state * inverse_ffn
     ffn_in = (normed_ffn * gain_ffn).astype(BF)
 
-    received = exchange(dot(spread, ffn_in).astype(BF))
-    row_grads, hidden, hidden_grads, row_gate, row_grad_logits = expert_pass(
+    half_width = model_width // 2
+    received = jnp.concatenate(
+        [dispatch(ffn_in[:, k * half_width : (k + 1) * half_width]) for k in range(2)], 1
+    )
+    shared_both = times(ffn_in, shared_in_blocks)
+    shared_act, shared_slope = silu_parts(shared_both[:, :FF_S])
+    shared_up = shared_both[:, FF_S:]
+    shared_hidden = (shared_act * shared_up).astype(BF)
+    shared_result = times(shared_hidden, shared_out_blocks)
+    grad_shared_hidden = times_back(grad_out_low, shared_out_blocks)
+    grad_shared_gate = (grad_shared_hidden * shared_up * shared_slope).astype(BF)
+    grad_shared_up = (grad_shared_hidden * shared_act).astype(BF)
+    grad_ffn_in = times_back(
+        jnp.concatenate([grad_shared_gate, grad_shared_up], -1), shared_in_blocks
+    )
+    shared_hidden, grad_shared_gate, grad_shared_up, received, shared_result, grad_ffn_in = after(
+        (shared_hidden, grad_shared_gate, grad_shared_up, received, shared_result, grad_ffn_in)
+    )
+
+    shared_orders = (first_x, first_y, first_x)
+    shared_groups = [
+        product_group(shared_hidden, grad_out_low, shared_orders[0][0]),
+        product_group(ffn_in, grad_shared_gate, shared_orders[1][0]),
+        product_group(ffn_in, grad_shared_up, shared_orders[2][0]),
+    ]
+    expert_results = expert_pass(
         here[None], received, received_grads, router.T, expert_weights
     )
-    returned_grads = exchange(row_grads)
+    *row_grads, hidden, hidden_grads, row_gate, row_grad_logits = after(
+        expert_results, shared_groups
+    )
+
+    halves = [
+        product_halves(group, order[1:]) for group, order in zip(shared_groups, shared_orders)
+    ]
+    row_grads = after([in_plane(part) for part in row_grads], halves)
+    grad_routed = jnp.concatenate([along_line(part) for part in row_grads], 1)
+    shared_sums = [
+        [kept, cross(after(sent, row_grads), order[1])]
+        for (kept, sent), order in zip(halves, shared_orders)
+    ]
+    grad_ffn_in = grad_ffn_in + grad_routed
+    grad_gain_ffn = jnp.sum(grad_ffn_in * normed_ffn, 0)
+    grad_hidden_state = grad_out + norm_back(grad_ffn_in * gain_ffn, normed_ffn, inverse_ffn)
+    grad_attn_out = grad_hidden_state.astype(BF)
+    grad_mixed = times_back(grad_attn_out, output_blocks).astype(BF)
     row_gate = row_gate.reshape(-1, 1)
     row_out = 0.0
     units = expert_weights[0][1].shape[0]
     for j, (_, weight) in enumerate(expert_weights):
         row_out = row_out + t_dot(hidden[j * units : (j + 1) * units], weight)
-    returned = exchange((row_gate * row_out).astype(BF))
-    routed = t_dot(spread, returned)
-    grad_routed = t_dot(spread, returned_grads)
+    row_out = (row_gate * row_out).astype(BF)
+
+    grad_mixed, shared_sums, row_out = after((grad_mixed, shared_sums, row_out))
+    shared_sums = [
+        fold_step(pieces, order[2]) for pieces, order in zip(shared_sums, shared_orders)
+    ]
+    row_out = in_plane(row_out)
+    attention_grads = attend_back(
+        grad_mixed,
+        expand,
+        keys,
+        attention,
+        queries,
+        mixed_latent,
+        query_nope,
+        cosine,
+        sine_table,
+    )
+    (grad_query_raw, grad_expand, grad_keys), shared_sums, row_out = after(
+        (attention_grads, shared_sums, row_out)
+    )
+    routed = along_line(row_out)
+    block_result = hidden_state + shared_result + routed
+    grad_shared_out, *grad_shared_in = [
+        fold_end(fold_step(pieces, order[3])) for pieces, order in zip(shared_sums, shared_orders)
+    ]
+    grad_shared_in = jnp.concatenate(grad_shared_in, -1)
+    grad_output = product_sum(
+        product_group(after(mixed_heads, grad_attn_out), grad_attn_out, first_y[0]), first_y
+    )
+
     weighted_grads = (row_gate * received_grads.astype(F32)).astype(BF)
     grad_expert_parts = [
         (
@@ -698,48 +856,6 @@
     grad_expert_out = grad_expert_out[None]
     grad_router = dot(row_grad_logits, received).T
 
-    shared_both = times(ffn_in, shared_in_blocks)
-    shared_act, shared_slope = silu_parts(shared_both[:, :FF_S])
-    shared_up = shared_both[:, FF_S:]
-    shared_hidden = (shared_act * shared_up).astype(BF)
-    shared_result = times(shared_hidden, shared_out_blocks)
-    block_result = hidden_state + shared_result + routed
-    grad_shared_hidden = times_back(grad_out_low, shared_out_blocks)
-    grad_shared_gate = (grad_shared_hidden * shared_up * shared_slope).astype(BF)
-    grad_shared_up = (grad_shared_hidden * shared_act).astype(BF)
-    grad_shared_both = jnp.concatenate([grad_shared_gate, grad_shared_up], -1)
-    grad_shared_out = reduce_product(
-        group_left(shared_hidden, first_x[0]), group_right(grad_out_low, first_x[0]), first_x
-    )
-    grad_shared_in = jnp.concatenate(
-        [
-            reduce_product(
-                group_left(ffn_in, order[0]), group_right(grads_in, order[0]), order
-            )
-            for order, grads_in in ((first_y, grad_shared_gate), (first_x, grad_shared_up))
-        ],
-        -1,
-    )
-    grad_ffn_in = times_back(grad_shared_both, shared_in_blocks) + grad_routed
-    grad_gain_ffn = jnp.sum(grad_ffn_in * normed_ffn, 0)
-    grad_hidden_state = grad_out + norm_back(grad_ffn_in * gain_ffn, normed_ffn, inverse_ffn)
-
-    grad_attn_out = grad_hidden_state.astype(BF)
-    grad_output = reduce_product(
-        group_left(mixed_heads, first_y[0]), group_right(grad_attn_out, first_y[0]), first_y
-    )
-    grad_mixed = times_back(grad_attn_out, output_blocks).astype(BF)
-    grad_query_raw, grad_expand, grad_keys = attend_back(
-        grad_mixed,
-        expand,
-        keys,
-        attention,
-        queries,
-        mixed_latent,
-        query_nope,
-        cosine,
-        sine_table,
-    )
     grad_keys = grad_keys.T.astype(BF)
     slot_half = SLOT // 2
     grad_own_keys = jnp.concatenate(
@@ -747,7 +863,6 @@
             fold(
                 [grad_keys[k * slot_half : (k + 1) * slot_half]],
                 tuple(reversed(collect_bits[k])),
-                part,
             )
             for k in range(2)
         ],
@@ -760,21 +875,22 @@
     grad_latent_raw = jnp.concatenate(
         [grad_latent, rotate_back(grad_own_keys[:, RANK:], cosine, sine_table)], -1
     ).astype(BF)
-    left_x, left_y = group_left(attn_in, first_x[0]), group_left(attn_in, first_y[0])
+    late_attn_in = after(attn_in, grad_attn_out)
+    left_x, left_y = [group_left(late_attn_in, order[0]) for order in (first_x, first_y)]
     query_half = grad_query_raw.shape[1] // 2
     grad_query = jnp.concatenate(
         [
-            reduce_product(
-                left_x, group_right(grad_query_raw[:, :query_half], first_x[0]), first_x
+            product_sum(
+                (left_x, group_right(grad_query_raw[:, :query_half], first_x[0])), first_x
             ),
-            reduce_product(
-                left_y, group_right(grad_query_raw[:, query_half:], first_y[0]), first_y
+            product_sum(
+                (left_y, group_right(grad_query_raw[:, query_half:], first_y[0])), first_y
             ),
         ],
         -1,
     )
-    grad_latent_weight = reduce_product(
-        left_y, group_right(grad_latent_raw, first_y[0]), first_y
+    grad_latent_weight = product_sum(
+        (left_y, group_right(grad_latent_raw, first_y[0])), first_y
     )
     grad_attn_in = times_back(grad_latent_raw, latent_blocks) + times_back(
         grad_query_raw, query_blocks

time: 860 us -> 954 us (1.11)
  waiting for transfers between devices: 277 us -> 339 us
  local copies, waits for them, and re-layouts: 71 us -> 98.2 us
  matrix products: 153 us -> 129 us
  other arithmetic: 98.5 us -> 119 us
  Pallas kernels: 135 us -> 151 us
  starting transfers between devices: 112 us -> 101 us
    ppermute x58 -> x90, waiting for transfers between devices: 275 us -> 337 us  [cross(): return lax.ppermute(values, 'expert', [(i, i ^ bit) for i in range(count)])]
    all_to_all x4 -> x0, starting transfers between devices: 22.9 us -> none  [exchange(): lax.all_to_all(rows.reshape(owners, capacity, model_width), 'expert', spl...]
    dot_general x18 -> x16, matrix products: 85.9 us -> 69.4 us  [dot(): return jnp.dot(left, right, preferred_element_type=F32)]
    unnamed x217 -> x308, local copies, waits for them, and re-layouts: 16.2 us -> 32.7 us
    pallas_call x0 -> x6, Pallas kernels: none -> 13.5 us  [the longest x3 8.61 us: put_rows(): pl.pallas_call(put_kernel, grid=(lines,), in_specs=[pl.BlockSpec((planes,...]
    ppermute x58 -> x90, starting transfers between devices: 84.4 us -> 96.5 us  [cross(): return lax.ppermute(values, 'expert', [(i, i ^ bit) for i in range(count)])]
    convert_element_type x25 -> x29, other arithmetic: 18.9 us -> 29.7 us  [the longest x27 27.6 us: fold_step(): sent = sum((p[count:].astype(F32) for p in pieces)).astype(BF)]
    slice x20 -> x31, local copies, waits for them, and re-layouts: 17.2 us -> 27.3 us  [the longest x19 12 us: fold_step(): sent = sum((p[count:].astype(F32) for p in pieces)).astype(BF)]
  transfers between devices with their start and end apart: 89 -> 117, of which waited for: 38 -> 49; matrix products, arithmetic and copies ran while one was open for 37% -> 33% of each run, Pallas kernels for 16% -> 16%
where the time goes in v3:
time: 954 us; the launch traced here: 942 us
  waiting for transfers between devices  339 us (36%)
  Pallas kernels  151 us (16%)
  matrix products  129 us (14%)
  other arithmetic  119 us (12%)
  starting transfers between devices  101 us (11%)
  local copies, waits for them, and re-layouts  98.2 us (10%)
    ppermute x90, waiting for transfers between devices, cross(): return lax.ppermute(values, 'expert', [(i, i ^ bit) for i in range(count)])  337 us
    ppermute x90, starting transfers between devices, cross(): return lax.ppermute(values, 'expert', [(i, i ^ bit) for i in range(count)])  96.5 us
    dot_general x16, matrix products, dot(): return jnp.dot(left, right, preferred_element_type=F32)  69.4 us
    dot_general x10, matrix products, dot_t(): lax.dot_general(left, right, (((1,), (1,)), ((), ())), preferred_element_...  46.9 us
    pallas_call x1, Pallas kernels, expert_pass(): pl.pallas_call(functools.partial(expert_kernel, sources), grid_spec=pltpu...  46.7 us
    pallas_call x1, Pallas kernels, attend_back(): pl.pallas_call(attend_back_kernel, grid=(HEADS // 2,), in_specs=[pl.Block...  39.8 us
    unnamed x308, local copies, waits for them, and re-layouts  32.7 us
    pallas_call x1, Pallas kernels, attend(): pl.pallas_call(attend_kernel, grid=(steps,), in_specs=[pl.BlockSpec((rows...  28.2 us
  transfers between devices with their start and end apart: 117, of which 49 were waited for; matrix products, arithmetic and copies ran while one was open for 33% of the time, Pallas kernels for 16%

profile of v3, /device:TPU:0, one launch (start us, length us, event | category | flops | bytes accessed | tf_op | source)
XLA Modules:
  0.0 941.6 jit_solution(9593186961795529481)
XLA Ops:
  17.8 6.6 collective-permute-done.4
  36.3 22.9 %collective-permute-done.12 = s32[6,128]{1,0:T(8,128)S(1)} collective-permute-done((s32[6,128]{1,0:T(8,128)S(1)}, s32[6,128]{1,0:T(8,128)S(1)}, u32[]{:S(2)}, u32[]{:S(2)}) %collective-permute-start.12) | collective-permute-done | bytes 3104 | tf_op jit(solution)/shard_map/ppermute | solution.py:85
  59.6 3.3 collective-permute-done.13
  67.2 7.1 collective-permute-done.8
  74.9 8.6 collective-permute-done.10
  86.5 5.8 collective-permute-done.15
  102.3 24.3 %collective-permute-done.11 = bf16[512,576]{0,1:T(8,128)(2,1)S(1)} collective-permute-done((bf16[512,576]{0,1:T(8,128)(2,1)}, bf16[512,576]{0,1:T(8,128)(2,1)S(1)}, u32[]{:S(2)}, u32[]{:S(2)}) %collective-permute-start.11) | collective-permute-done | bytes 589856 | tf_op jit(solution)/shard_map/ppermute | solution.py:85
  128.4 18.8 %collective-permute-done.17 = bf16[4,56,2048]{2,1,0:T(8,128)(2,1)} collective-permute-done((bf16[4,56,2048]{2,1,0:T(8,128)(2,1)S(1)}, bf16[4,56,2048]{2,1,0:T(8,128)(2,1)}, u32[]{:S(2)}, u32[]{:S(2)}) %collective-permute-start.17) | collective-permute-done | bytes 917536 | tf_op jit(solution)/shard_map/ppermute | solution.py:85
  148.8 5.7 fusion.156
  155.7 11.3 %collective-permute-done.16 = bf16[4,56,2048]{2,1,0:T(8,128)(2,1)} collective-permute-done((bf16[4,56,2048]{2,1,0:T(8,128)(2,1)S(1)}, bf16[4,56,2048]{2,1,0:T(8,128)(2,1)}, u32[]{:S(2)}, u32[]{:S(2)}) %collective-permute-start.16) | collective-permute-done | bytes 917536 | tf_op jit(solution)/shard_map/ppermute | solution.py:85
  167.0 4.9 fusion.96
  175.9 6.2 maximum_select_fusion.expand_ref
  191.9 3.3 pad_maximum_fusion
  195.2 5.6 fusion.157
  200.8 3.9 convolution_add_fusion.1.raw_ref
  204.8 28.2 %shard_map.281 = (bf16[128,2048]{1,0:T(8,128)(2,1)S(1)}, bf16[2048,576]{1,0:T(8,128)(2,1)S(1)}, bf16[2048,2048]{1,0:T(8,128)(2,1)}, bf16[2048,512]{1,0:T(8,128)(2,1)S(1)}, bf16[128,2048]{1,0:T(8,128)(2,1)S(1)}) custom-call(f32[128,3072]{1,0:T(8,128)S(1)} %convolution_add_fusion.1.raw_ref, f32[128,32]{1,0:T(8,128)S(1)} %get-tuple-element.279.cosine_ref, ...), custom_call_target="tpu_custom_call" | custom-call | flops 9126805504 | bytes 8388608 | tf_op jit(solution)/shard_map/pallas_call | solution.py:325
  233.2 4.7 fusion.89
  237.9 3.2 multiply_reduce_fusion.2
  241.4 3.3 fusion.87
  256.3 7.1 convolution_add_fusion
  265.4 5.3 fusion.43
  270.8 8.5 fusion.42
  280.7 3.6 fusion.62
  289.9 5.3 collective-permute-done.30
  300.6 4.7 convolution_add_fusion.2
  314.4 12.7 %collective-permute-done.32 = bf16[4,56,1024]{2,1,0:T(8,128)(2,1)S(1)} collective-permute-done((bf16[4,56,1024]{2,1,0:T(8,128)(2,1)S(1)}, bf16[4,56,1024]{2,1,0:T(8,128)(2,1)S(1)}, u32[]{:S(2)}, u32[]{:S(2)}) %collective-permute-start.32) | collective-permute-done | bytes 458784 | tf_op jit(solution)/shard_map/ppermute | solution.py:85
  330.1 6.8 collective-permute-done.27
  345.9 46.7 %shard_map.285 = (bf16[896,1024]{1,0:T(8,128)(2,1)}, bf16[896,1024]{1,0:T(8,128)(2,1)}, bf16[1408,896]{1,0:T(8,128)(2,1)}, bf16[2,2,704,896]{3,2,1,0:T(8,128)(2,...) custom-call(s32[1]{0:T(128)} %bitcast.30.here_ref, bf16[896,2048]{1,0:T(8,128)(2,1)} %pad_maximum_fusion.1.rows_ref, ...), custom_call_target="tpu_custom_call" | custom-call | flops 25836912640 | bytes 28311552 | tf_op jit(solution)/shard_map/pallas_call | solution.py:562
  417.0 9.7 %convolution_convert_fusion = bf16[2,704,2048]{2,1,0:T(8,128)(2,1)} fusion(bf16[896,2048]{1,0:T(8,128)(2,1)S(1)} %copy-done.43, bf16[2,2,704,896]{3,2,1,0:T(8,128)(2,1)} %get-tuple-element.199), kind=kOutput, calls=%fused_computation.5 | convolution fusion | flops 5170266112 | bytes 11960320 | tf_op jit(solution)/shard_map/dot_general | solution.py:72
  426.8 5.4 fusion.21
  433.3 7.2 multiply_convert_fusion.1
  440.5 6.5 shard_map.288
  448.2 4.5 shard_map.287
  455.4 3.7 shard_map.290
  460.1 4.9 convolution_convert_fusion.1
  480.6 8.2 collective-permute-done.53
  492.2 11.2 %collective-permute-done.54 = bf16[128,1024]{1,0:T(8,128)(2,1)S(1)} collective-permute-done((bf16[128,1024]{1,0:T(8,128)(2,1)S(1)}, bf16[128,1024]{1,0:T(8,128)(2,1)S(1)}, u32[]{:S(2)}, u32[]{:S(2)}) %collective-permute-start.54) | collective-permute-done | bytes 262176 | tf_op jit(solution)/shard_map/ppermute | solution.py:85
  511.8 3.7 fusion.158
  519.0 3.6 collective-permute-done.105
  522.6 3.7 fusion.159
  533.1 30.3 %collective-permute-done.107 = bf16[128,2048]{1,0:T(8,128)(2,1)S(1)} collective-permute-done((bf16[128,2048]{1,0:T(8,128)(2,1)S(1)}, bf16[128,2048]{1,0:T(8,128)(2,1)S(1)}, u32[]{:S(2)}, u32[]{:S(2)}) %collective-permute-start.107) | collective-permute-done | bytes 524320 | tf_op jit(solution)/shard_map/ppermute | solution.py:85
  576.8 8.4 collective-permute-done.60
  588.0 39.8 %shard_map.291 = (bf16[128,3072]{1,0:T(8,128)(2,1)S(1)}, bf16[512,4096]{1,0:T(8,128)(2,1)}, f32[576,2048]{1,0:T(8,128)}) custom-call(bf16[128,2048]{1,0:T(8,128)(2,1)S(1)} %fusion.37.grad_ref, bf16[512,4096]{1,0:T(8,128)(2,1)} %maximum_select_fusion.expand_ref, bf16[2048,576]{1,0:T(8,128)(2,1)} %constant_dynamic-update-slice_fusion.keys_ref, ...), custom_call_target="tpu_custom_call" | custom-call | flops 22548578304 | bytes 8388608 | tf_op jit(solution)/shard_map/pallas_call | solution.py:408
  644.5 4.3 copy.143
  666.8 6.2 fusion.162
  673.0 5.9 fusion.163
  683.3 6.6 add_bitcast_fusion.1
  690.0 9.4 collective-permute-done.113
  700.6 16.4 %collective-permute-done.112 = bf16[64,2816]{1,0:T(8,128)(2,1)S(1)} collective-permute-done((bf16[64,2816]{1,0:T(8,128)(2,1)S(1)}, bf16[64,2816]{1,0:T(8,128)(2,1)S(1)}, u32[]{:S(2)}, u32[]{:S(2)}) %collective-permute-start.112) | collective-permute-done | bytes 360480 | tf_op jit(solution)/shard_map/ppermute | solution.py:85
  719.3 15.5 %collective-permute-done.114 = bf16[88,2048]{1,0:T(8,128)(2,1)S(1)} collective-permute-done((bf16[88,2048]{1,0:T(8,128)(2,1)S(1)}, bf16[88,2048]{1,0:T(8,128)(2,1)S(1)}, u32[]{:S(2)}, u32[]{:S(2)}) %collective-permute-start.114) | collective-permute-done | bytes 360480 | tf_op jit(solution)/shard_map/ppermute | solution.py:85
  736.7 9.2 collective-permute-done.90
  769.2 4.0 collective-permute-done.70
  781.2 8.5 collective-permute-done.109
  791.7 3.4 collective-permute-done.75
  800.3 3.3 fusion.29
  859.0 8.4 collective-permute-done.111
  870.5 6.2 collective-permute-done.97
  879.2 5.6 collective-permute-done.98
  890.8 7.3 collective-permute-done.99
  898.9 3.4 collective-permute-start.94
  902.6 7.7 collective-permute-done.101
  911.5 4.2 collective-permute-done.94
  922.5 4.6 collective-permute-done.103
  929.8 10.8 %add_bitcast_fusion = f32[1,2048,2,704]{1,3,2,0:T(8,128)} fusion(bf16[2,704,2048]{2,1,0:T(8,128)(2,1)} %collective-permute-done.115, bf16[896,2048]{1,0:T(8,128)(2,1)S(1)} %copy-done.45, bf16[2,2,704,896]{3,2,1,0:T(8,128)(2,1)S(1)} %bitcast.404), kind=kOutput, calls=%fused_computation | convolution fusion | flops 5173149696 | bytes 23494656 | tf_op jit(solution)/shard_map/dot_general | solution.py:72
  (742 shorter events, 356.2 us)
Async XLA Ops:
  2.1 231.1 %collective-permute-start.20 = (bf16[1024,5632]{1,0:T(8,128)(2,1)}, bf16[1024,5632]{1,0:T(8,128)(2,1)}, u32[]{:S(2)}, u32[]{:S(2)}) collective-permute-start(bf16[1024,5632]{1,0:T(8,128)(2,1)} %param.29), channel_id=1, source_target_pairs={{0,1},{1,0},{2,3},{3,2},{4,5},{5,4},{6,7},{7,6},{8,9},{9,8},{10,11... | collective-permute-start | bytes 34603016 | tf_op jit(solution)/shard_map/ppermute | solution.py:89
  17.4 67.3 %collective-permute-start.2 = (bf16[256,4096]{1,0:T(8,128)(2,1)}, bf16[256,4096]{1,0:T(8,128)(2,1)}, u32[]{:S(2)}, u32[]{:S(2)}) collective-permute-start(bf16[256,4096]{1,0:T(8,128)(2,1)} %param.25), channel_id=1, source_target_pairs={{0,1},{1,0},{2,3},{3,2},{4,5},{5,4},{6,7},{7,6},{8,9},{9,8},{10,11... | collective-permute-start | bytes 6291464 | tf_op jit(solution)/shard_map/ppermute | solution.py:89
  25.7 41.1 %collective-permute-start.38 = (bf16[256,2048]{1,0:T(8,128)(2,1)S(1)}, bf16[256,2048]{1,0:T(8,128)(2,1)S(1)}, u32[]{:S(2)}, u32[]{:S(2)}) collective-permute-start(bf16[256,2048]{1,0:T(8,128)(2,1)S(1)} %pad_maximum_fusion.16), channel_id=1, source_target_pairs={{0,1},{1,0},{2,3},{3,2},{4,5},{5,4},{6,7},{7,6},{8,9},{9,8},{10,11... | collective-permute-start | bytes 3145736 | tf_op jit(solution)/shard_map/ppermute | solution.py:89
  33.3 31.0 %collective-permute-start.14 = (bf16[128,2048]{1,0:T(8,128)(2,1)S(1)}, bf16[128,2048]{1,0:T(8,128)(2,1)S(1)}, u32[]{:S(2)}, u32[]{:S(2)}) collective-permute-start(bf16[128,2048]{1,0:T(8,128)(2,1)S(1)} %fusion.40), channel_id=1, source_target_pairs={{0,16},{2,18},{4,20},{6,22},{8,24},{10,26},{12,28},{14,30},{16,0},... | collective-permute-start | bytes 1572872 | tf_op jit(solution)/shard_map/ppermute | solution.py:85
  36.0 23.2 %collective-permute-start.12 = (s32[6,128]{1,0:T(8,128)S(1)}, s32[6,128]{1,0:T(8,128)S(1)}, u32[]{:S(2)}, u32[]{:S(2)}) collective-permute-start(s32[6,128]{1,0:T(8,128)S(1)} %bitcast.393), channel_id=1, source_target_pairs={{0,16},{2,18},{4,20},{6,22},{8,24},{10,26},{12,28},{14,30},{16,0},... | collective-permute-start | bytes 9224 | tf_op jit(solution)/shard_map/ppermute | solution.py:85
  64.1 111.3 %collective-permute-start.21 = (bf16[1408,2048]{1,0:T(8,128)(2,1)}, bf16[1408,2048]{1,0:T(8,128)(2,1)}, u32[]{:S(2)}, u32[]{:S(2)}) collective-permute-start(bf16[1408,2048]{1,0:T(8,128)(2,1)} %param.30), channel_id=1, source_target_pairs={{0,1},{1,0},{2,3},{3,2},{4,5},{5,4},{6,7},{7,6},{8,9},{9,8},{10,11... | collective-permute-start | bytes 17301512 | tf_op jit(solution)/shard_map/ppermute | solution.py:89
  66.8 25.4 %collective-permute-start.15 = (bf16[256,2048]{1,0:T(8,128)(2,1)}, bf16[256,2048]{1,0:T(8,128)(2,1)}, u32[]{:S(2)}, u32[]{:S(2)}) collective-permute-start(bf16[256,2048]{1,0:T(8,128)(2,1)} %pad_maximum_fusion.13), channel_id=1, source_target_pairs={{0,8},{2,10},{4,12},{6,14},{8,0},{10,2},{12,4},{14,6},{16,24},{18,... | collective-permute-start | bytes 3145736 | tf_op jit(solution)/shard_map/ppermute | solution.py:85
  83.5 117.3 %collective-permute-start.1 = (bf16[1024,3072]{1,0:T(8,128)(2,1)}, bf16[1024,3072]{1,0:T(8,128)(2,1)}, u32[]{:S(2)}, u32[]{:S(2)}) collective-permute-start(bf16[1024,3072]{1,0:T(8,128)(2,1)} %param.22), channel_id=1, source_target_pairs={{0,1},{1,0},{2,3},{3,2},{4,5},{5,4},{6,7},{7,6},{8,9},{9,8},{10,11... | collective-permute-start | bytes 18874376 | tf_op jit(solution)/shard_map/ppermute | solution.py:89
  92.3 34.3 %collective-permute-start.11 = (bf16[512,576]{0,1:T(8,128)(2,1)}, bf16[512,576]{0,1:T(8,128)(2,1)S(1)}, u32[]{:S(2)}, u32[]{:S(2)}) collective-permute-start(bf16[512,576]{0,1:T(8,128)(2,1)} %copy.136), channel_id=1, source_target_pairs={{0,4},{2,6},{4,0},{6,2},{8,12},{10,14},{12,8},{14,10},{16,20},{18,... | collective-permute-start | bytes 1769480 | tf_op jit(solution)/shard_map/ppermute | solution.py:85
  100.8 26.9 %collective-permute-start.18 = (bf16[4,56,2048]{2,1,0:T(8,128)(2,1)S(1)}, bf16[4,56,2048]{2,1,0:T(8,128)(2,1)}, u32[]{:S(2)}, u32[]{:S(2)}) collective-permute-start(bf16[4,56,2048]{2,1,0:T(8,128)(2,1)S(1)} %get-tuple-element.114), channel_id=1, source_target_pairs={{0,6},{2,4},{4,2},{6,0},{8,14},{10,12},{12,10},{14,8},{16,22},{18,... | collective-permute-start | bytes 2752520 | tf_op jit(solution)/shard_map/ppermute | solution.py:85
  126.6 20.7 %collective-permute-start.17 = (bf16[4,56,2048]{2,1,0:T(8,128)(2,1)S(1)}, bf16[4,56,2048]{2,1,0:T(8,128)(2,1)}, u32[]{:S(2)}, u32[]{:S(2)}) collective-permute-start(bf16[4,56,2048]{2,1,0:T(8,128)(2,1)S(1)} %get-tuple-element.113), channel_id=1, source_target_pairs={{0,4},{2,6},{4,0},{6,2},{8,12},{10,14},{12,8},{14,10},{16,20},{18,... | collective-permute-start | bytes 2752520 | tf_op jit(solution)/shard_map/ppermute | solution.py:85
  127.7 105.4 %collective-permute-start.22 = (bf16[2,704,2048]{2,1,0:T(8,128)(2,1)}, bf16[2,704,2048]{2,1,0:T(8,128)(2,1)}, u32[]{:S(2)}, u32[]{:S(2)}) collective-permute-start(bf16[2,704,2048]{2,1,0:T(8,128)(2,1)} %bitcast.401), channel_id=1, source_target_pairs={{0,1},{1,0},{2,3},{3,2},{4,5},{5,4},{6,7},{7,6},{8,9},{9,8},{10,11... | collective-permute-start | bytes 17301512 | tf_op jit(solution)/shard_map/ppermute | solution.py:89
  147.3 19.7 %collective-permute-start.16 = (bf16[4,56,2048]{2,1,0:T(8,128)(2,1)S(1)}, bf16[4,56,2048]{2,1,0:T(8,128)(2,1)}, u32[]{:S(2)}, u32[]{:S(2)}) collective-permute-start(bf16[4,56,2048]{2,1,0:T(8,128)(2,1)S(1)} %get-tuple-element.112), channel_id=1, source_target_pairs={{0,2},{2,0},{4,6},{6,4},{8,10},{10,8},{12,14},{14,12},{16,18},{18,... | collective-permute-start | bytes 2752520 | tf_op jit(solution)/shard_map/ppermute | solution.py:85
  167.0 66.1 %collective-permute-start.19 = (bf16[1024,2048]{1,0:T(8,128)(2,1)}, bf16[1024,2048]{1,0:T(8,128)(2,1)}, u32[]{:S(2)}, u32[]{:S(2)}) collective-permute-start(bf16[1024,2048]{1,0:T(8,128)(2,1)} %param.26), channel_id=1, source_target_pairs={{0,1},{1,0},{2,3},{3,2},{4,5},{5,4},{6,7},{7,6},{8,9},{9,8},{10,11... | collective-permute-start | bytes 12582920 | tf_op jit(solution)/shard_map/ppermute | solution.py:89
  175.4 57.8 %collective-permute-start.23 = (bf16[704,2048]{1,0:T(8,128)(2,1)}, bf16[704,2048]{1,0:T(8,128)(2,1)}, u32[]{:S(2)}, u32[]{:S(2)}) collective-permute-start(bf16[704,2048]{1,0:T(8,128)(2,1)} %bitcast.16.refs_1_), channel_id=1, source_target_pairs={{0,1},{1,0},{2,3},{3,2},{4,5},{5,4},{6,7},{7,6},{8,9},{9,8},{10,11... | collective-permute-start | bytes 8650760 | tf_op jit(solution)/shard_map/ppermute | solution.py:89
  246.4 32.8 %collective-permute-start.29 = (bf16[128,1024]{1,0:T(8,128)(2,1)}, bf16[128,1024]{1,0:T(8,128)(2,1)}, u32[]{:S(2)}, u32[]{:S(2)}) collective-permute-start(bf16[128,1024]{1,0:T(8,128)(2,1)} %get-tuple-element.265), channel_id=1, source_target_pairs={{0,16},{2,18},{4,20},{6,22},{8,24},{10,26},{12,28},{14,30},{16,0},... | collective-permute-start | bytes 786440 | tf_op jit(solution)/shard_map/ppermute | solution.py:85
  249.4 35.0 %collective-permute-start.24 = (bf16[128,1024]{1,0:T(8,128)(2,1)}, bf16[128,1024]{1,0:T(8,128)(2,1)}, u32[]{:S(2)}, u32[]{:S(2)}) collective-permute-start(bf16[128,1024]{1,0:T(8,128)(2,1)} %get-tuple-element.264), channel_id=1, source_target_pairs={{0,16},{2,18},{4,20},{6,22},{8,24},{10,26},{12,28},{14,30},{16,0},... | collective-permute-start | bytes 786440 | tf_op jit(solution)/shard_map/ppermute | solution.py:85
  253.4 33.8 %collective-permute-start.39 = (bf16[4,2,2,64,128]{4,3,2,1,0:T(8,128)(2,1)}, bf16[4,2,2,64,128]{4,3,2,1,0:T(8,128)(2,1)}, u32[]{:S(2)}, u32[]{:S(2)}) collective-permute-start(bf16[4,2,2,64,128]{4,3,2,1,0:T(8,128)(2,1)} %get-tuple-element.262), channel_id=1, source_target_pairs={{0,4},{2,6},{4,0},{6,2},{8,12},{10,14},{12,8},{14,10},{16,20},{18,... | collective-permute-start | bytes 786440 | tf_op jit(solution)/shard_map/ppermute | solution.py:85
  255.7 32.7 %collective-permute-start.43 = (bf16[8,1,2,64,128]{4,3,2,0,1:T(8,128)(2,1)}, bf16[8,1,2,64,128]{4,3,2,0,1:T(8,128)(2,1)}, u32[]{:S(2)}, u32[]{:S(2)}) collective-permute-start(bf16[8,1,2,64,128]{4,3,2,0,1:T(8,128)(2,1)} %get-tuple-element.258), channel_id=1, source_target_pairs={{0,2},{2,0},{4,6},{6,4},{8,10},{10,8},{12,14},{14,12},{16,18},{18,... | collective-permute-start | bytes 786440 | tf_op jit(solution)/shard_map/ppermute | solution.py:85
  285.4 20.4 %collective-permute-start.25 = (bf16[256,1024]{1,0:T(8,128)(2,1)S(1)}, bf16[256,1024]{1,0:T(8,128)(2,1)S(1)}, u32[]{:S(2)}, u32[]{:S(2)}) collective-permute-start(bf16[256,1024]{1,0:T(8,128)(2,1)S(1)} %pad_maximum_fusion.27), channel_id=1, source_target_pairs={{0,8},{2,10},{4,12},{6,14},{8,0},{10,2},{12,4},{14,6},{16,24},{18,... | collective-permute-start | bytes 1572872 | tf_op jit(solution)/shard_map/ppermute | solution.py:85
  288.3 20.5 %collective-permute-start.40 = (bf16[8,64,256]{2,1,0:T(8,128)(2,1)S(1)}, bf16[8,64,256]{2,1,0:T(8,128)(2,1)S(1)}, u32[]{:S(2)}, u32[]{:S(2)}) collective-permute-start(bf16[8,64,256]{2,1,0:T(8,128)(2,1)S(1)} %get-tuple-element.261), channel_id=1, source_target_pairs={{0,1},{1,0},{2,3},{3,2},{4,5},{5,4},{6,7},{7,6},{8,9},{9,8},{10,11... | collective-permute-start | bytes 786440 | tf_op jit(solution)/shard_map/ppermute | solution.py:89
  289.4 21.8 %collective-permute-start.44 = (bf16[8,64,256]{2,1,0:T(8,128)(2,1)S(1)}, bf16[8,64,256]{2,1,0:T(8,128)(2,1)S(1)}, u32[]{:S(2)}, u32[]{:S(2)}) collective-permute-start(bf16[8,64,256]{2,1,0:T(8,128)(2,1)S(1)} %get-tuple-element.257), channel_id=1, source_target_pairs={{0,1},{1,0},{2,3},{3,2},{4,5},{5,4},{6,7},{7,6},{8,9},{9,8},{10,11... | collective-permute-start | bytes 786440 | tf_op jit(solution)/shard_map/ppermute | solution.py:89
  305.3 21.8 %collective-permute-start.32 = (bf16[4,56,1024]{2,1,0:T(8,128)(2,1)S(1)}, bf16[4,56,1024]{2,1,0:T(8,128)(2,1)S(1)}, u32[]{:S(2)}, u32[]{:S(2)}) collective-permute-start(bf16[4,56,1024]{2,1,0:T(8,128)(2,1)S(1)} %get-tuple-element.122), channel_id=1, source_target_pairs={{0,4},{2,6},{4,0},{6,2},{8,12},{10,14},{12,8},{14,10},{16,20},{18,... | collective-permute-start | bytes 1376264 | tf_op jit(solution)/shard_map/ppermute | solution.py:85
  305.8 21.3 %collective-permute-start.31 = (bf16[4,56,1024]{2,1,0:T(8,128)(2,1)S(1)}, bf16[4,56,1024]{2,1,0:T(8,128)(2,1)S(1)}, u32[]{:S(2)}, u32[]{:S(2)}) collective-permute-start(bf16[4,56,1024]{2,1,0:T(8,128)(2,1)S(1)} %get-tuple-element.121), channel_id=1, source_target_pairs={{0,2},{2,0},{4,6},{6,4},{8,10},{10,8},{12,14},{14,12},{16,18},{18,... | collective-permute-start | bytes 1376264 | tf_op jit(solution)/shard_map/ppermute | solution.py:85
  308.8 21.3 %collective-permute-start.28 = (bf16[4,56,1024]{2,1,0:T(8,128)(2,1)S(1)}, bf16[4,56,1024]{2,1,0:T(8,128)(2,1)S(1)}, u32[]{:S(2)}, u32[]{:S(2)}) collective-permute-start(bf16[4,56,1024]{2,1,0:T(8,128)(2,1)S(1)} %get-tuple-element.119), channel_id=1, source_target_pairs={{0,6},{2,4},{4,2},{6,0},{8,14},{10,12},{12,10},{14,8},{16,22},{18,... | collective-permute-start | bytes 1376264 | tf_op jit(solution)/shard_map/ppermute | solution.py:85
  311.2 25.7 %collective-permute-start.27 = (bf16[4,56,1024]{2,1,0:T(8,128)(2,1)S(1)}, bf16[4,56,1024]{2,1,0:T(8,128)(2,1)S(1)}, u32[]{:S(2)}, u32[]{:S(2)}) collective-permute-start(bf16[4,56,1024]{2,1,0:T(8,128)(2,1)S(1)} %get-tuple-element.118), channel_id=1, source_target_pairs={{0,4},{2,6},{4,0},{6,2},{8,12},{10,14},{12,8},{14,10},{16,20},{18,... | collective-permute-start | bytes 1376264 | tf_op jit(solution)/shard_map/ppermute | solution.py:85
  311.8 25.2 %collective-permute-start.26 = (bf16[4,56,1024]{2,1,0:T(8,128)(2,1)S(1)}, bf16[4,56,1024]{2,1,0:T(8,128)(2,1)S(1)}, u32[]{:S(2)}, u32[]{:S(2)}) collective-permute-start(bf16[4,56,1024]{2,1,0:T(8,128)(2,1)S(1)} %get-tuple-element.117), channel_id=1, source_target_pairs={{0,2},{2,0},{4,6},{6,4},{8,10},{10,8},{12,14},{14,12},{16,18},{18,... | collective-permute-start | bytes 1376264 | tf_op jit(solution)/shard_map/ppermute | solution.py:85
  339.3 55.7 %collective-permute-start.41 = (bf16[128,2816]{1,0:T(8,128)(2,1)}, bf16[128,2816]{1,0:T(8,128)(2,1)}, u32[]{:S(2)}, u32[]{:S(2)}) collective-permute-start(bf16[128,2816]{1,0:T(8,128)(2,1)} %get-tuple-element.134), channel_id=1, source_target_pairs={{0,4},{2,6},{4,0},{6,2},{8,12},{10,14},{12,8},{14,10},{16,20},{18,... | collective-permute-start | bytes 2162696 | tf_op jit(solution)/shard_map/ppermute | solution.py:85
  340.5 56.0 %collective-permute-start.45 = (bf16[128,2816]{1,0:T(8,128)(2,1)}, bf16[128,2816]{1,0:T(8,128)(2,1)}, u32[]{:S(2)}, u32[]{:S(2)}) collective-permute-start(bf16[128,2816]{1,0:T(8,128)(2,1)} %get-tuple-element.135), channel_id=1, source_target_pairs={{0,2},{2,0},{4,6},{6,4},{8,10},{10,8},{12,14},{14,12},{16,18},{18,... | collective-permute-start | bytes 2162696 | tf_op jit(solution)/shard_map/ppermute | solution.py:85
  345.8 52.6 %collective-permute-start.35 = (bf16[8,1,2,88,128]{4,3,2,0,1:T(8,128)(2,1)S(1)}, bf16[8,1,2,88,128]{4,3,2,0,1:T(8,128)(2,1)S(1)}, u32[]{:S(2)}, u32[]{:S(2)}) collective-permute-start(bf16[8,1,2,88,128]{4,3,2,0,1:T(8,128)(2,1)S(1)} %get-tuple-element.238), channel_id=1, source_target_pairs={{0,2},{2,0},{4,6},{6,4},{8,10},{10,8},{12,14},{14,12},{16,18},{18,... | collective-permute-start | bytes 1081352 | tf_op jit(solution)/shard_map/ppermute | solution.py:85
  409.6 22.6 %collective-permute-start.47 = (bf16[4,56,1024]{2,1,0:T(8,128)(2,1)}, bf16[4,56,1024]{2,1,0:T(8,128)(2,1)S(1)}, u32[]{:S(2)}, u32[]{:S(2)}) collective-permute-start(bf16[4,56,1024]{2,1,0:T(8,128)(2,1)} %bitcast.54), channel_id=1, source_target_pairs={{0,2},{2,0},{4,6},{6,4},{8,10},{10,8},{12,14},{14,12},{16,18},{18,... | collective-permute-start | bytes 1376264 | tf_op jit(solution)/shard_map/ppermute | solution.py:85
  411.6 42.2 %collective-permute-start.48 = (bf16[4,56,1024]{2,1,0:T(8,128)(2,1)}, bf16[4,56,1024]{2,1,0:T(8,128)(2,1)S(1)}, u32[]{:S(2)}, u32[]{:S(2)}) collective-permute-start(bf16[4,56,1024]{2,1,0:T(8,128)(2,1)} %bitcast.55), channel_id=1, source_target_pairs={{0,4},{2,6},{4,0},{6,2},{8,12},{10,14},{12,8},{14,10},{16,20},{18,... | collective-permute-start | bytes 1376264 | tf_op jit(solution)/shard_map/ppermute | solution.py:85
  412.3 42.3 %collective-permute-start.49 = (bf16[4,56,1024]{2,1,0:T(8,128)(2,1)}, bf16[4,56,1024]{2,1,0:T(8,128)(2,1)S(1)}, u32[]{:S(2)}, u32[]{:S(2)}) collective-permute-start(bf16[4,56,1024]{2,1,0:T(8,128)(2,1)} %bitcast.56), channel_id=1, source_target_pairs={{0,6},{2,4},{4,2},{6,0},{8,14},{10,12},{12,10},{14,8},{16,22},{18,... | collective-permute-start | bytes 1376264 | tf_op jit(solution)/shard_map/ppermute | solution.py:85
  414.4 41.0 %collective-permute-start.50 = (bf16[4,56,1024]{2,1,0:T(8,128)(2,1)}, bf16[4,56,1024]{2,1,0:T(8,128)(2,1)}, u32[]{:S(2)}, u32[]{:S(2)}) collective-permute-start(bf16[4,56,1024]{2,1,0:T(8,128)(2,1)} %bitcast.58), channel_id=1, source_target_pairs={{0,2},{2,0},{4,6},{6,4},{8,10},{10,8},{12,14},{14,12},{16,18},{18,... | collective-permute-start | bytes 1376264 | tf_op jit(solution)/shard_map/ppermute | solution.py:85
  416.4 39.0 %collective-permute-start.51 = (bf16[4,56,1024]{2,1,0:T(8,128)(2,1)}, bf16[4,56,1024]{2,1,0:T(8,128)(2,1)}, u32[]{:S(2)}, u32[]{:S(2)}) collective-permute-start(bf16[4,56,1024]{2,1,0:T(8,128)(2,1)} %bitcast.59), channel_id=1, source_target_pairs={{0,4},{2,6},{4,0},{6,2},{8,12},{10,14},{12,8},{14,10},{16,20},{18,... | collective-permute-start | bytes 1376264 | tf_op jit(solution)/shard_map/ppermute | solution.py:85
  432.3 23.1 %collective-permute-start.52 = (bf16[4,56,1024]{2,1,0:T(8,128)(2,1)S(1)}, bf16[4,56,1024]{2,1,0:T(8,128)(2,1)S(1)}, u32[]{:S(2)}, u32[]{:S(2)}) collective-permute-start(bf16[4,56,1024]{2,1,0:T(8,128)(2,1)S(1)} %bitcast.375), channel_id=1, source_target_pairs={{0,6},{2,4},{4,2},{6,0},{8,14},{10,12},{12,10},{14,8},{16,22},{18,... | collective-permute-start | bytes 1376264 | tf_op jit(solution)/shard_map/ppermute | solution.py:85
  469.0 19.8 %collective-permute-start.53 = (bf16[256,1024]{1,0:T(8,128)(2,1)}, bf16[256,1024]{1,0:T(8,128)(2,1)}, u32[]{:S(2)}, u32[]{:S(2)}) collective-permute-start(bf16[256,1024]{1,0:T(8,128)(2,1)} %bitcast.78), channel_id=1, source_target_pairs={{0,8},{2,10},{4,12},{6,14},{8,0},{10,2},{12,4},{14,6},{16,24},{18,... | collective-permute-start | bytes 1572872 | tf_op jit(solution)/shard_map/ppermute | solution.py:85
  478.5 86.0 %collective-permute-start.57 = (bf16[352,2048]{1,0:T(8,128)(2,1)}, bf16[352,2048]{1,0:T(8,128)(2,1)}, u32[]{:S(2)}, u32[]{:S(2)}) collective-permute-start(bf16[352,2048]{1,0:T(8,128)(2,1)} %copy-done.27), channel_id=1, source_target_pairs={{0,4},{2,6},{4,0},{6,2},{8,12},{10,14},{12,8},{14,10},{16,20},{18,... | collective-permute-start | bytes 4325384 | tf_op jit(solution)/shard_map/ppermute | solution.py:85
  479.4 85.1 %collective-permute-start.58 = (bf16[256,2816]{1,0:T(8,128)(2,1)}, bf16[256,2816]{1,0:T(8,128)(2,1)}, u32[]{:S(2)}, u32[]{:S(2)}) collective-permute-start(bf16[256,2816]{1,0:T(8,128)(2,1)} %copy-done.28), channel_id=1, source_target_pairs={{0,2},{2,0},{4,6},{6,4},{8,10},{10,8},{12,14},{14,12},{16,18},{18,... | collective-permute-start | bytes 4325384 | tf_op jit(solution)/shard_map/ppermute | solution.py:85
  517.0 47.5 %collective-permute-start.59 = (bf16[256,2816]{1,0:T(8,128)(2,1)}, bf16[256,2816]{1,0:T(8,128)(2,1)}, u32[]{:S(2)}, u32[]{:S(2)}) collective-permute-start(bf16[256,2816]{1,0:T(8,128)(2,1)} %get-tuple-element.154), channel_id=1, source_target_pairs={{0,4},{2,6},{4,0},{6,2},{8,12},{10,14},{12,8},{14,10},{16,20},{18,... | collective-permute-start | bytes 4325384 | tf_op jit(solution)/shard_map/ppermute | solution.py:85
  527.1 36.3 %collective-permute-start.107 = (bf16[128,2048]{1,0:T(8,128)(2,1)S(1)}, bf16[128,2048]{1,0:T(8,128)(2,1)S(1)}, u32[]{:S(2)}, u32[]{:S(2)}) collective-permute-start(bf16[128,2048]{1,0:T(8,128)(2,1)S(1)} %get-tuple-element.209), channel_id=1, source_target_pairs={{0,4},{2,6},{4,0},{6,2},{8,12},{10,14},{12,8},{14,10},{16,20},{18,... | collective-permute-start | bytes 1572872 | tf_op jit(solution)/shard_map/ppermute | solution.py:85
  566.0 19.1 %collective-permute-start.60 = (bf16[176,2048]{1,0:T(8,128)(2,1)S(1)}, bf16[176,2048]{1,0:T(8,128)(2,1)S(1)}, u32[]{:S(2)}, u32[]{:S(2)}) collective-permute-start(bf16[176,2048]{1,0:T(8,128)(2,1)S(1)} %add_convert_fusion.2), channel_id=1, source_target_pairs={{0,8},{2,10},{4,12},{6,14},{8,0},{10,2},{12,4},{14,6},{16,24},{18,... | collective-permute-start | bytes 2162696 | tf_op jit(solution)/shard_map/ppermute | solution.py:85
  568.4 67.5 %collective-permute-start.61 = (bf16[128,2816]{1,0:T(8,128)(2,1)}, bf16[128,2816]{1,0:T(8,128)(2,1)}, u32[]{:S(2)}, u32[]{:S(2)}) collective-permute-start(bf16[128,2816]{1,0:T(8,128)(2,1)} %add_convert_fusion.1), channel_id=1, source_target_pairs={{0,8},{2,10},{4,12},{6,14},{8,0},{10,2},{12,4},{14,6},{16,24},{18,... | collective-permute-start | bytes 2162696 | tf_op jit(solution)/shard_map/ppermute | solution.py:85
  572.4 63.5 %collective-permute-start.62 = (bf16[128,2816]{1,0:T(8,128)(2,1)}, bf16[128,2816]{1,0:T(8,128)(2,1)}, u32[]{:S(2)}, u32[]{:S(2)}) collective-permute-start(bf16[128,2816]{1,0:T(8,128)(2,1)} %add_convert_fusion), channel_id=1, source_target_pairs={{0,8},{2,10},{4,12},{6,14},{8,0},{10,2},{12,4},{14,6},{16,24},{18,... | collective-permute-start | bytes 2162696 | tf_op jit(solution)/shard_map/ppermute | solution.py:85
  574.3 62.1 %collective-permute-start.63 = (bf16[4,56,2048]{2,1,0:T(8,128)(2,1)}, bf16[4,56,2048]{2,1,0:T(8,128)(2,1)S(1)}, u32[]{:S(2)}, u32[]{:S(2)}) collective-permute-start(bf16[4,56,2048]{2,1,0:T(8,128)(2,1)} %bitcast.84), channel_id=1, source_target_pairs={{0,2},{2,0},{4,6},{6,4},{8,10},{10,8},{12,14},{14,12},{16,18},{18,... | collective-permute-start | bytes 2752520 | tf_op jit(solution)/shard_map/ppermute | solution.py:85
  575.7 60.8 %collective-permute-start.64 = (bf16[4,56,2048]{2,1,0:T(8,128)(2,1)}, bf16[4,56,2048]{2,1,0:T(8,128)(2,1)S(1)}, u32[]{:S(2)}, u32[]{:S(2)}) collective-permute-start(bf16[4,56,2048]{2,1,0:T(8,128)(2,1)} %bitcast.85), channel_id=1, source_target_pairs={{0,4},{2,6},{4,0},{6,2},{8,12},{10,14},{12,8},{14,10},{16,20},{18,... | collective-permute-start | bytes 2752520 | tf_op jit(solution)/shard_map/ppermute | solution.py:85
  586.1 50.5 %collective-permute-start.65 = (bf16[4,56,2048]{2,1,0:T(8,128)(2,1)S(1)}, bf16[4,56,2048]{2,1,0:T(8,128)(2,1)S(1)}, u32[]{:S(2)}, u32[]{:S(2)}) collective-permute-start(bf16[4,56,2048]{2,1,0:T(8,128)(2,1)S(1)} %bitcast.367), channel_id=1, source_target_pairs={{0,6},{2,4},{4,2},{6,0},{8,14},{10,12},{12,10},{14,8},{16,22},{18,... | collective-permute-start | bytes 2752520 | tf_op jit(solution)/shard_map/ppermute | solution.py:85
  635.9 293.9 %collective-permute-start.115 = (bf16[2,704,2048]{2,1,0:T(8,128)(2,1)}, bf16[2,704,2048]{2,1,0:T(8,128)(2,1)}, u32[]{:S(2)}, u32[]{:S(2)}) collective-permute-start(bf16[2,704,2048]{2,1,0:T(8,128)(2,1)} %convolution_convert_fusion), channel_id=1, source_target_pairs={{0,1},{1,0},{2,3},{3,2},{4,5},{5,4},{6,7},{7,6},{8,9},{9,8},{10,11... | collective-permute-start | bytes 17301512 | tf_op jit(solution)/shard_map/ppermute | solution.py:89
  635.9 44.5 %collective-permute-start.116 = (bf16[704,2048]{1,0:T(8,128)(2,1)}, bf16[704,2048]{1,0:T(8,128)(2,1)}, u32[]{:S(2)}, u32[]{:S(2)}) collective-permute-start(bf16[704,2048]{1,0:T(8,128)(2,1)} %convolution_convert_fusion.1), channel_id=1, source_target_pairs={{0,1},{1,0},{2,3},{3,2},{4,5},{5,4},{6,7},{7,6},{8,9},{9,8},{10,11... | collective-permute-start | bytes 8650760 | tf_op jit(solution)/shard_map/ppermute | solution.py:89
  636.4 24.6 %collective-permute-start.108 = (bf16[256,2048]{1,0:T(8,128)(2,1)}, bf16[256,2048]{1,0:T(8,128)(2,1)}, u32[]{:S(2)}, u32[]{:S(2)}) collective-permute-start(bf16[256,2048]{1,0:T(8,128)(2,1)} %pad_maximum_fusion.17), channel_id=1, source_target_pairs={{0,1},{1,0},{2,3},{3,2},{4,5},{5,4},{6,7},{7,6},{8,9},{9,8},{10,11... | collective-permute-start | bytes 3145736 | tf_op jit(solution)/shard_map/ppermute | solution.py:89
  642.7 132.0 %collective-permute-start.66 = (bf16[256,2048]{1,0:T(8,128)(2,1)}, bf16[256,2048]{1,0:T(8,128)(2,1)}, u32[]{:S(2)}, u32[]{:S(2)}) collective-permute-start(bf16[256,2048]{1,0:T(8,128)(2,1)} %bitcast.88), channel_id=1, source_target_pairs={{0,8},{2,10},{4,12},{6,14},{8,0},{10,2},{12,4},{14,6},{16,24},{18,... | collective-permute-start | bytes 3145736 | tf_op jit(solution)/shard_map/ppermute | solution.py:85
  653.4 94.8 %collective-permute-start.68 = (bf16[512,576]{0,1:T(8,128)(2,1)}, bf16[512,576]{0,1:T(8,128)(2,1)}, u32[]{:S(2)}, u32[]{:S(2)}) collective-permute-start(bf16[512,576]{0,1:T(8,128)(2,1)} %copy.144), channel_id=1, source_target_pairs={{0,2},{2,0},{4,6},{6,4},{8,10},{10,8},{12,14},{14,12},{16,18},{18,... | collective-permute-start | bytes 1769480 | tf_op jit(solution)/shard_map/ppermute | solution.py:85
  661.1 89.1 %collective-permute-start.72 = (bf16[512,576]{0,1:T(8,128)(2,1)}, bf16[512,576]{0,1:T(8,128)(2,1)}, u32[]{:S(2)}, u32[]{:S(2)}) collective-permute-start(bf16[512,576]{0,1:T(8,128)(2,1)} %copy.149), channel_id=1, source_target_pairs={{0,4},{2,6},{4,0},{6,2},{8,12},{10,14},{12,8},{14,10},{16,20},{18,... | collective-permute-start | bytes 1769480 | tf_op jit(solution)/shard_map/ppermute | solution.py:85
  748.2 136.7 %collective-permute-start.100 = (bf16[16,16,4096]{2,1,0:T(8,128)(2,1)}, bf16[16,16,4096]{2,1,0:T(8,128)(2,1)}, u32[]{:S(2)}, u32[]{:S(2)}) collective-permute-start(bf16[16,16,4096]{2,1,0:T(8,128)(2,1)} %dynamic-slice_bitcast_fusion), channel_id=1, source_target_pairs={{0,1},{1,0},{2,3},{3,2},{4,5},{5,4},{6,7},{7,6},{8,9},{9,8},{10,11... | collective-permute-start | bytes 6291464 | tf_op jit(solution)/shard_map/ppermute | solution.py:89
  764.8 24.9 %collective-permute-start.109 = (bf16[256,2048]{1,0:T(8,128)(2,1)S(1)}, bf16[256,2048]{1,0:T(8,128)(2,1)}, u32[]{:S(2)}, u32[]{:S(2)}) collective-permute-start(bf16[256,2048]{1,0:T(8,128)(2,1)S(1)} %copy-done.30), channel_id=1, source_target_pairs={{0,2},{2,0},{4,6},{6,4},{8,10},{10,8},{12,14},{14,12},{16,18},{18,... | collective-permute-start | bytes 3145736 | tf_op jit(solution)/shard_map/ppermute | solution.py:85
  779.5 27.8 %collective-permute-start.91 = (bf16[256,1536]{1,0:T(8,128)(2,1)}, bf16[256,1536]{1,0:T(8,128)(2,1)}, u32[]{:S(2)}, u32[]{:S(2)}) collective-permute-start(bf16[256,1536]{1,0:T(8,128)(2,1)} %pad_maximum_fusion.21), channel_id=1, source_target_pairs={{0,1},{1,0},{2,3},{3,2},{4,5},{5,4},{6,7},{7,6},{8,9},{9,8},{10,11... | collective-permute-start | bytes 2359304 | tf_op jit(solution)/shard_map/ppermute | solution.py:89
  780.1 34.0 %collective-permute-start.84 = (bf16[256,1536]{1,0:T(8,128)(2,1)}, bf16[256,1536]{1,0:T(8,128)(2,1)}, u32[]{:S(2)}, u32[]{:S(2)}) collective-permute-start(bf16[256,1536]{1,0:T(8,128)(2,1)} %pad_maximum_fusion.20), channel_id=1, source_target_pairs={{0,1},{1,0},{2,3},{3,2},{4,5},{5,4},{6,7},{7,6},{8,9},{9,8},{10,11... | collective-permute-start | bytes 2359304 | tf_op jit(solution)/shard_map/ppermute | solution.py:89
  795.1 57.0 %collective-permute-start.67 = (bf16[128,2048]{1,0:T(8,128)(2,1)}, bf16[128,2048]{1,0:T(8,128)(2,1)}, u32[]{:S(2)}, u32[]{:S(2)}) collective-permute-start(bf16[128,2048]{1,0:T(8,128)(2,1)} %fusion.32), channel_id=1, source_target_pairs={{0,16},{2,18},{4,20},{6,22},{8,24},{10,26},{12,28},{14,30},{16,0},... | collective-permute-start | bytes 1572872 | tf_op jit(solution)/shard_map/ppermute | solution.py:85
  807.3 43.5 %collective-permute-start.110 = (bf16[128,2048]{1,0:T(8,128)(2,1)}, bf16[128,2048]{1,0:T(8,128)(2,1)}, u32[]{:S(2)}, u32[]{:S(2)}) collective-permute-start(bf16[128,2048]{1,0:T(8,128)(2,1)} %add_convert_fusion.3), channel_id=1, source_target_pairs={{0,8},{2,10},{4,12},{6,14},{8,0},{10,2},{12,4},{14,6},{16,24},{18,... | collective-permute-start | bytes 1572872 | tf_op jit(solution)/shard_map/ppermute | solution.py:85
  849.9 26.9 %collective-permute-start.92 = (bf16[256,1536]{1,0:T(8,128)(2,1)S(1)}, bf16[256,1536]{1,0:T(8,128)(2,1)S(1)}, u32[]{:S(2)}, u32[]{:S(2)}) collective-permute-start(bf16[256,1536]{1,0:T(8,128)(2,1)S(1)} %copy-done.32), channel_id=1, source_target_pairs={{0,2},{2,0},{4,6},{6,4},{8,10},{10,8},{12,14},{14,12},{16,18},{18,... | collective-permute-start | bytes 2359304 | tf_op jit(solution)/shard_map/ppermute | solution.py:85
  856.7 22.3 %collective-permute-start.85 = (bf16[256,1536]{1,0:T(8,128)(2,1)S(1)}, bf16[256,1536]{1,0:T(8,128)(2,1)S(1)}, u32[]{:S(2)}, u32[]{:S(2)}) collective-permute-start(bf16[256,1536]{1,0:T(8,128)(2,1)S(1)} %get-tuple-element.181), channel_id=1, source_target_pairs={{0,4},{2,6},{4,0},{6,2},{8,12},{10,14},{12,8},{14,10},{16,20},{18,... | collective-permute-start | bytes 2359304 | tf_op jit(solution)/shard_map/ppermute | solution.py:85
  876.9 21.9 %collective-permute-start.93 = (bf16[128,1536]{1,0:T(8,128)(2,1)S(1)}, bf16[128,1536]{1,0:T(8,128)(2,1)S(1)}, u32[]{:S(2)}, u32[]{:S(2)}) collective-permute-start(bf16[128,1536]{1,0:T(8,128)(2,1)S(1)} %add_convert_fusion.4), channel_id=1, source_target_pairs={{0,8},{2,10},{4,12},{6,14},{8,0},{10,2},{12,4},{14,6},{16,24},{18,... | collective-permute-start | bytes 1179656 | tf_op jit(solution)/shard_map/ppermute | solution.py:85
  879.1 23.3 %collective-permute-start.86 = (bf16[128,1536]{1,0:T(8,128)(2,1)S(1)}, bf16[128,1536]{1,0:T(8,128)(2,1)S(1)}, u32[]{:S(2)}, u32[]{:S(2)}) collective-permute-start(bf16[128,1536]{1,0:T(8,128)(2,1)S(1)} %add_convert_fusion.5), channel_id=1, source_target_pairs={{0,8},{2,10},{4,12},{6,14},{8,0},{10,2},{12,4},{14,6},{16,24},{18,... | collective-permute-start | bytes 1179656 | tf_op jit(solution)/shard_map/ppermute | solution.py:85
  889.6 20.7 %collective-permute-start.101 = (bf16[128,4096]{1,0:T(8,128)(2,1)S(1)}, bf16[128,4096]{1,0:T(8,128)(2,1)S(1)}, u32[]{:S(2)}, u32[]{:S(2)}) collective-permute-start(bf16[128,4096]{1,0:T(8,128)(2,1)S(1)} %bitcast.361), channel_id=1, source_target_pairs={{0,2},{2,0},{4,6},{6,4},{8,10},{10,8},{12,14},{14,12},{16,18},{18,... | collective-permute-start | bytes 3145736 | tf_op jit(solution)/shard_map/ppermute | solution.py:85
  (195 other events, 2566.9 us)

commit v4 on v2

--- a/solution.py
+++ b/solution.py
@@ -132,13 +132,25 @@
     return values, places
 
 
-def fold(pieces, bits, rows):
-    count = rows << len(bits)
+def together(*values):
+    leaves, tree = jax.tree.flatten(values)
+    return jax.tree.unflatten(tree, lax.optimization_barrier(leaves))
+
+
+def fold_step(pieces, bit):
+    count = pieces[0].shape[0] // 2
+    sent = sum(p[count:].astype(F32) for p in pieces).astype(BF)
+    return [p[:count] for p in pieces] + [cross(sent, bit)]
+
+
+def fold_end(pieces):
+    return sum(p.astype(F32) for p in pieces)
+
+
+def fold(pieces, bits):
     for bit in bits:
-        count = count // 2
-        sent = sum(p[count:].astype(F32) for p in pieces).astype(BF)
-        pieces = [p[:count] for p in pieces] + [cross(sent, bit)]
-    return sum(p.astype(F32) for p in pieces)
+        pieces = fold_step(pieces, bit)
+    return fold_end(pieces)
 
 
 def fold_order(bits):
@@ -219,50 +231,70 @@
     )(jnp.stack(order).astype(jnp.int32), left, right)
 
 
-def group_left(left, bit):
+def cross_left(left, bit):
     experts, shards = lax.axis_size("expert"), lax.axis_size("shard")
-    tokens, columns = left.shape
     own = lax.axis_index("expert") // bit % 2
-    blocks = left.T.reshape(experts // (2 * bit), 2, bit, shards, -1, tokens)
+    blocks = left.T.reshape(experts // (2 * bit), 2, bit, shards, -1, left.shape[0])
     kept = lax.dynamic_index_in_dim(blocks, own, 1, keepdims=False)
     sent = lax.dynamic_index_in_dim(blocks, 1 - own, 1, keepdims=False)
-    blocks = jnp.concatenate([kept, cross(sent, bit)], -1).reshape(
-        experts // 2, shards, -1, 2 * tokens
-    )
+    return kept, cross(sent, bit)
+
+
+def pair_left(halves):
+    experts, shards = lax.axis_size("expert"), lax.axis_size("shard")
+    blocks = jnp.concatenate(halves, -1)
+    blocks = blocks.reshape(experts // 2, shards, *blocks.shape[-2:])
     if shards != 2:
         blocks = lax.all_to_all(blocks, "shard", split_axis=1, concat_axis=3, tiled=True)
-        return blocks.reshape(columns // (2 * shards), -1)
+        return blocks.reshape(-1, blocks.shape[-1])
     own = lax.axis_index("shard")
     kept = lax.dynamic_index_in_dim(blocks, own, 1, keepdims=False)
     sent = lax.dynamic_index_in_dim(blocks, 1 - own, 1, keepdims=False)
-    return jnp.concatenate([kept, swap(sent)], -1).reshape(columns // 4, -1)
-
-
-def group_right(right, bit):
-    right = jnp.concatenate([right, cross(right, bit)], 0)
+    blocks = jnp.concatenate([kept, swap(sent)], -1)
+    return blocks.reshape(-1, blocks.shape[-1])
+
+
+def pair_right(halves):
+    right = jnp.concatenate(halves, 0)
     if lax.axis_size("shard") != 2:
         return lax.all_gather(right, "shard", axis=0, tiled=True)
     return jnp.concatenate([right, swap(right)], 0)
 
 
-def reduce_product(left, right, bits):
-    kept, sent = gradient_halves(left, right, lax.axis_index("expert"), bits[1:])
-    rows = 2 * kept.shape[0] >> len(bits) - 1
-    arrived = cross(sent, bits[1])
-    return fold([kept, arrived], bits[2:], rows)
-
-
-def reduce_partial(partial, bits):
+def group_left(left, bit):
+    return pair_left(cross_left(left, bit))
+
+
+def group_right(right, bit):
+    return pair_right((right, cross(right, bit)))
+
+
+def product_group(left, right, bit):
+    return group_left(left, bit), group_right(right, bit)
+
+
+def product_halves(group, bits):
+    return gradient_halves(*group, lax.axis_index("expert"), bits)
+
+
+def product_sum(group, bits):
+    kept, sent = product_halves(group, bits[1:])
+    return fold([kept, cross(sent, bits[1])], bits[2:])
+
+
+def pair_partial(partial, bits):
     experts, shards = lax.axis_size("expert"), lax.axis_size("shard")
     rows = partial.shape[0] // (experts * shards)
     if shards != 2:
-        return lax.psum_scatter(partial, ("expert", "shard"), scatter_dimension=0, tiled=True)
-    own = lax.axis_index("shard")
-    blocks = partial.reshape(experts, 2, rows, partial.shape[1])
-    kept = lax.dynamic_index_in_dim(blocks, own, 1, keepdims=False)
-    sent = lax.dynamic_index_in_dim(blocks, 1 - own, 1, keepdims=False)
-    total = (kept.astype(F32) + swap(sent).astype(F32)).astype(partial.dtype)
-    return fold([differing(total, bits, lax.axis_index("expert")).reshape(experts * rows, -1)], bits, rows)
+        blocks = partial.reshape(experts, shards, rows, -1)
+        total = lax.psum_scatter(blocks, "shard", scatter_dimension=1, tiled=True)[:, 0]
+    else:
+        own = lax.axis_index("shard")
+        blocks = partial.reshape(experts, 2, rows, -1)
+        kept = lax.dynamic_index_in_dim(blocks, own, 1, keepdims=False)
+        sent = lax.dynamic_index_in_dim(blocks, 1 - own, 1, keepdims=False)
+        total = (kept.astype(F32) + swap(sent).astype(F32)).astype(partial.dtype)
+    return [differing(total, bits, lax.axis_index("expert")).reshape(experts * rows, -1)]
 
 
 def attend_kernel(
@@ -339,7 +371,7 @@
 
 def attend_back_kernel(
     grad_ref, expand_ref, keys_ref, weights_ref, queries_ref, mixed_ref, nope_ref, cosine_ref,
-    sine_ref, query_grad_ref, expand_grad_ref, key_grad_ref, latent_ref, scores_ref,
+    sine_ref, query_grad_ref, expand_grad_ref, key_out_ref, key_grad_ref, latent_ref, scores_ref,
 ):
     rows = grad_ref.shape[0]
     width = HEAD + ROPE
@@ -381,6 +413,10 @@
             mixed_ref[part, :], grad_ref[:, h * VHEAD : (h + 1) * VHEAD]
         ).astype(BF)
 
+    @pl.when(pl.program_id(0) == pl.num_programs(0) - 1)
+    def _():
+        key_out_ref[...] = key_grad_ref[...].T.astype(BF)
+
 
 def attend_back(grad_out, expand, keys, weights, queries, mixed, nope, cosine, sine):
     rows = grad_out.shape[0]
@@ -403,14 +439,18 @@
         out_specs=[
             pl.BlockSpec((rows, 2 * (HEAD + ROPE)), lambda i: (0, i)),
             pl.BlockSpec((RANK, 4 * HEAD), lambda i: (0, i)),
-            whole(RANK + ROPE, slot),
+            whole(slot, RANK + ROPE),
         ],
         out_shape=[
             jax.ShapeDtypeStruct((rows, HEADS * (HEAD + ROPE)), BF),
             jax.ShapeDtypeStruct((RANK, 2 * HEADS * HEAD), BF),
-            jax.ShapeDtypeStruct((RANK + ROPE, slot), F32),
-        ],
-        scratch_shapes=[pltpu.VMEM((2 * rows, RANK), BF), pltpu.VMEM((2 * rows, slot), BF)],
+            jax.ShapeDtypeStruct((slot, RANK + ROPE), BF),
+        ],
+        scratch_shapes=[
+            pltpu.VMEM((RANK + ROPE, slot), F32),
+            pltpu.VMEM((2 * rows, RANK), BF),
+            pltpu.VMEM((2 * rows, slot), BF),
+        ],
         compiler_params=pltpu.CompilerParams(vmem_limit_bytes=48 << 20),
         cost_estimate=pl.CostEstimate(
             flops=2 * HEADS * rows * slot * (3 * RANK + 2 * (RANK + ROPE)),
@@ -599,14 +639,16 @@
     grad_out_low = grad_out.astype(BF)
 
     expert_ids = jnp.arange(experts_all, dtype=jnp.int32)
-    member = jnp.any(routes[0][:, :, None] == expert_ids[None, None, :], 1)
+    member = jnp.any(routes[0].T[None] == expert_ids[:, None, None], 1)
     token_ids = jnp.arange(local_rows, dtype=jnp.int32)
-    earlier = (token_ids[None, :] < token_ids[:, None]).astype(BF)
-    rank = dot(earlier, member.astype(BF)).astype(jnp.int32)
+    earlier = (token_ids[:, None] < token_ids[None, :]).astype(BF)
+    rank = dot(member.astype(BF), earlier).astype(jnp.int32)
     place_ids = jnp.arange(capacity, dtype=jnp.int32)
     spread = (
-        member.T[:, None, :] & (rank.T[:, None, :] == place_ids[None, :, None])
-    ).reshape(experts_all * capacity, local_rows).astype(BF)
+        (member[:, None, :] & (rank[:, None, :] == place_ids[None, :, None]))
+        .reshape(experts_all * capacity, local_rows)
+        .astype(BF)
+    )
 
     def exchange(rows):
         return lax.all_to_all(
@@ -616,6 +658,8 @@
             concat_axis=0,
             tiled=True,
         ).reshape(owners * capacity, model_width)
+
+    received_grads = exchange(dot(spread, grad_out_low).astype(BF))
 
     inputs = tokens[0].astype(F32)
     inverse_attn = rms_scale(inputs)
@@ -644,9 +688,6 @@
     keys = jnp.concatenate(keys, 0)
     key_index = jnp.concatenate(key_index)
 
-    sent_grads, keys = lax.optimization_barrier((dot(spread, grad_out_low).astype(BF), keys))
-    received_grads = exchange(sent_grads)
-
     query_raw = times(attn_in, query_blocks)
     key_segment = layout(lengths[0], key_index)[0]
     allowed = (query_segment[:, None] == key_segment[None, :]) & (
@@ -656,25 +697,69 @@
     query_nope, queries, attention, mixed_latent, mixed_heads = attend(
         query_raw, cosine, sine_table, expand, keys, bias
     )
-    mixed_heads, received_grads = lax.optimization_barrier((mixed_heads, received_grads))
+    (
+        mixed_heads, received_grads, output_blocks, router, shared_in_blocks, shared_out_blocks,
+        expert_weights,
+    ) = together(
+        mixed_heads, received_grads, output_blocks, router, shared_in_blocks, shared_out_blocks,
+        expert_weights,
+    )
     hidden_state = inputs + times(mixed_heads, output_blocks)
     inverse_ffn = rms_scale(hidden_state)
     normed_ffn = hidden_state * inverse_ffn
     ffn_in = (normed_ffn * gain_ffn).astype(BF)
 
     received = exchange(dot(spread, ffn_in).astype(BF))
-    row_grads, hidden, hidden_grads, row_gate, row_grad_logits = expert_pass(
+    shared_both = times(ffn_in, shared_in_blocks)
+    shared_act, shared_slope = silu_parts(shared_both[:, :FF_S])
+    shared_up = shared_both[:, FF_S:]
+    shared_hidden = (shared_act * shared_up).astype(BF)
+    shared_result = times(shared_hidden, shared_out_blocks)
+    grad_shared_hidden = times_back(grad_out_low, shared_out_blocks)
+    grad_shared_gate = (grad_shared_hidden * shared_up * shared_slope).astype(BF)
+    grad_shared_up = (grad_shared_hidden * shared_act).astype(BF)
+    grad_ffn_in = times_back(
+        jnp.concatenate([grad_shared_gate, grad_shared_up], -1), shared_in_blocks
+    )
+    (
+        shared_hidden, grad_shared_gate, grad_shared_up, received, shared_result, grad_ffn_in,
+        shared_in, late_grad_out,
+    ) = together(
+        shared_hidden, grad_shared_gate, grad_shared_up, received, shared_result, grad_ffn_in,
+        ffn_in, grad_out_low,
+    )
+
+    shared_orders = ((4, 1, 2, 8), (4, 2, 1, 8), (4, 1, 2, 8))
+    shared_lefts = [
+        cross_left(left, order[0])
+        for left, order in zip((shared_hidden, shared_in, shared_in), shared_orders)
+    ]
+    shared_rights = [
+        (right, cross(right, order[0]))
+        for right, order in zip((late_grad_out, grad_shared_gate, grad_shared_up), shared_orders)
+    ]
+    expert_results = expert_pass(
         here[None], received, received_grads, router.T, expert_weights
     )
+    expert_results, shared_lefts, shared_rights = together(
+        expert_results, shared_lefts, shared_rights
+    )
+    shared_groups = [
+        (pair_left(left), pair_right(right)) for left, right in zip(shared_lefts, shared_rights)
+    ]
+    row_grads, hidden, hidden_grads, row_gate, row_grad_logits = expert_results
+
     returned_grads = exchange(row_grads)
+    halves = [
+        product_halves(group, order[1:]) for group, order in zip(shared_groups, shared_orders)
+    ]
+    shared_sums = [[kept, cross(sent, order[1])] for (kept, sent), order in zip(halves, shared_orders)]
     row_gate = row_gate.reshape(-1, 1)
     row_out = 0.0
     units = expert_weights[0][1].shape[0]
     for j, (_, weight) in enumerate(expert_weights):
         row_out = row_out + t_dot(hidden[j * units : (j + 1) * units], weight)
-    returned = exchange((row_gate * row_out).astype(BF))
-    routed = t_dot(spread, returned)
-    grad_routed = t_dot(spread, returned_grads)
+    row_out = (row_gate * row_out).astype(BF)
     weighted_grads = (row_gate * received_grads.astype(F32)).astype(BF)
     grad_expert_parts = [
         (
@@ -694,42 +779,27 @@
             ).astype(F32)
             for part in grad_expert_parts[0]
         ]
+    grad_router = dot(row_grad_logits, received)
+    returned_grads, row_out, grad_expert_in, grad_expert_out, grad_router, shared_sums = together(
+        returned_grads, row_out, grad_expert_in, grad_expert_out, grad_router, shared_sums
+    )
     grad_expert_in = grad_expert_in.transpose(2, 0, 1)[None]
     grad_expert_out = grad_expert_out[None]
-    grad_router = dot(row_grad_logits, received).T
-
-    shared_both = times(ffn_in, shared_in_blocks)
-    shared_act, shared_slope = silu_parts(shared_both[:, :FF_S])
-    shared_up = shared_both[:, FF_S:]
-    shared_hidden = (shared_act * shared_up).astype(BF)
-    shared_result = times(shared_hidden, shared_out_blocks)
-    block_result = hidden_state + shared_result + routed
-    grad_shared_hidden = times_back(grad_out_low, shared_out_blocks)
-    grad_shared_gate = (grad_shared_hidden * shared_up * shared_slope).astype(BF)
-    grad_shared_up = (grad_shared_hidden * shared_act).astype(BF)
-    grad_shared_both = jnp.concatenate([grad_shared_gate, grad_shared_up], -1)
-    grad_shared_out = reduce_product(
-        group_left(shared_hidden, first_x[0]), group_right(grad_out_low, first_x[0]), first_x
-    )
-    grad_shared_in = jnp.concatenate(
-        [
-            reduce_product(
-                group_left(ffn_in, order[0]), group_right(grads_in, order[0]), order
-            )
-            for order, grads_in in ((first_y, grad_shared_gate), (first_x, grad_shared_up))
-        ],
-        -1,
-    )
-    grad_ffn_in = times_back(grad_shared_both, shared_in_blocks) + grad_routed
+    returned = exchange(row_out)
+    grad_ffn_in = grad_ffn_in + t_dot(spread, returned_grads)
     grad_gain_ffn = jnp.sum(grad_ffn_in * normed_ffn, 0)
     grad_hidden_state = grad_out + norm_back(grad_ffn_in * gain_ffn, normed_ffn, inverse_ffn)
 
     grad_attn_out = grad_hidden_state.astype(BF)
-    grad_output = reduce_product(
-        group_left(mixed_heads, first_y[0]), group_right(grad_attn_out, first_y[0]), first_y
-    )
+    late_attn_in, late_heads, grad_attn_out = together(attn_in, mixed_heads, grad_attn_out)
     grad_mixed = times_back(grad_attn_out, output_blocks).astype(BF)
-    grad_query_raw, grad_expand, grad_keys = attend_back(
+    left_x, left_y = [group_left(late_attn_in, order[0]) for order in (first_x, first_y)]
+    output_group = product_group(late_heads, grad_attn_out, first_y[0])
+    grad_mixed, shared_sums = together(grad_mixed, shared_sums)
+    shared_sums = [
+        fold_step(pieces, order[2]) for pieces, order in zip(shared_sums, shared_orders)
+    ]
+    attention_grads = attend_back(
         grad_mixed,
         expand,
         keys,
@@ -740,68 +810,80 @@
         cosine,
         sine_table,
     )
-    grad_keys = grad_keys.T.astype(BF)
+    (grad_query_raw, grad_expand, grad_keys), shared_sums = together(attention_grads, shared_sums)
+    shared_sums = [
+        fold_step(pieces, order[3]) for pieces, order in zip(shared_sums, shared_orders)
+    ]
     slot_half = SLOT // 2
     grad_own_keys = jnp.concatenate(
         [
             fold(
                 [grad_keys[k * slot_half : (k + 1) * slot_half]],
                 tuple(reversed(collect_bits[k])),
-                part,
             )
             for k in range(2)
         ],
         0,
     )
-    grad_expand = reduce_partial(grad_expand, first_x).astype(F32)
+    query_half = grad_query_raw.shape[1] // 2
+    grad_query = jnp.concatenate(
+        [
+            product_sum(
+                (left_x, group_right(grad_query_raw[:, :query_half], first_x[0])), first_x
+            ),
+            product_sum(
+                (left_y, group_right(grad_query_raw[:, query_half:], first_y[0])), first_y
+            ),
+        ],
+        -1,
+    )
+    expand_sums = fold_step(pair_partial(grad_expand, first_x), first_x[0])
+    grad_own_keys, expand_sums = together(grad_own_keys, expand_sums)
+    grad_expand = fold(expand_sums, first_x[1:])
+    grad_output = product_sum(output_group, first_y)
     grad_latent_in = grad_own_keys[:, :RANK]
     grad_gain_latent = jnp.sum(grad_latent_in * normed_latent, 0)
     grad_latent = norm_back(grad_latent_in * gain_latent, normed_latent, inverse_latent)
     grad_latent_raw = jnp.concatenate(
         [grad_latent, rotate_back(grad_own_keys[:, RANK:], cosine, sine_table)], -1
     ).astype(BF)
-    left_x, left_y = group_left(attn_in, first_x[0]), group_left(attn_in, first_y[0])
-    query_half = grad_query_raw.shape[1] // 2
-    grad_query = jnp.concatenate(
-        [
-            reduce_product(
-                left_x, group_right(grad_query_raw[:, :query_half], first_x[0]), first_x
-            ),
-            reduce_product(
-                left_y, group_right(grad_query_raw[:, query_half:], first_y[0]), first_y
-            ),
-        ],
-        -1,
-    )
-    grad_latent_weight = reduce_product(
-        left_y, group_right(grad_latent_raw, first_y[0]), first_y
+    grad_latent_late, shared_sums = together(grad_latent_raw, shared_sums)
+    grad_shared_out, *grad_shared_in = [fold_end(pieces) for pieces in shared_sums]
+    grad_shared_in = jnp.concatenate(grad_shared_in, -1)
+    grad_latent_weight = product_sum(
+        (left_y, group_right(grad_latent_late, first_y[0])), first_y
     )
     grad_attn_in = times_back(grad_latent_raw, latent_blocks) + times_back(
         grad_query_raw, query_blocks
     )
     grad_gain_attn = jnp.sum(grad_attn_in * normed_attn, 0)
     tokens_grad = grad_hidden_state + norm_back(grad_attn_in * gain_attn, normed_attn, inverse_attn)
-
     devices = owners * shards
     rows = model_width // devices
-    latent_column = jnp.pad(
-        grad_gain_latent.reshape(devices, -1), ((0, 0), (0, rows - RANK // devices))
-    ).reshape(-1, 1)
     small = jnp.concatenate(
-        [grad_router, grad_gain_attn[:, None], grad_gain_ffn[:, None], latent_column], 1
-    )
-    small = reduce_partial(small, first_x).astype(F32)
+        [
+            vector.reshape(devices, -1)
+            for vector in (grad_router.T, grad_gain_attn, grad_gain_ffn, grad_gain_latent)
+        ],
+        1,
+    )
+    small, returned = together(small, returned)
+    small = lax.all_to_all(small, ("expert", "shard"), split_axis=0, concat_axis=0, tiled=True)
+    small = jnp.sum(small, 0)
+    routed = t_dot(spread, returned)
+    block_result = hidden_state + shared_result + routed
+    cuts = [rows * experts_all, rows * (experts_all + 1), rows * (experts_all + 2)]
     return (
         block_result.astype(BF)[None],
         tokens_grad.astype(BF)[None],
-        small[:, experts_all],
+        small[cuts[0] : cuts[1]],
         grad_query,
         grad_latent_weight,
-        small[: RANK // devices, experts_all + 2],
+        small[cuts[2] :],
         grad_expand,
         grad_output,
-        small[:, experts_all + 1],
-        small[:, :experts_all],
+        small[cuts[1] : cuts[2]],
+        small[: cuts[0]].reshape(rows, experts_all),
         grad_shared_in,
         grad_shared_out,
         grad_expert_in,

time: 860 us -> 918 us (1.067)
  waiting for transfers between devices: 277 us -> 328 us
  other arithmetic: 98.5 us -> 63.1 us
  starting transfers between devices: 112 us -> 146 us
  matrix products: 153 us -> 142 us
  Pallas kernels: 135 us -> 146 us
    all_to_all x4, waiting for transfers between devices: 0.01 us -> 30.9 us  [exchange(): lax.all_to_all(rows.reshape(owners, capacity, model_width), 'expert', spl...]
    ppermute x58 -> x53, starting transfers between devices: 84.4 us -> 103 us  [cross(): return lax.ppermute(values, 'expert', [(i, i ^ bit) for i in range(count)])]
    concatenate x28, other arithmetic: 29.9 us -> 13.9 us  [the longest x7 4.52 us: pair_right(): right = jnp.concatenate(halves, 0)]
    all_to_all x4, starting transfers between devices: 22.9 us -> 34.4 us  [exchange(): lax.all_to_all(rows.reshape(owners, capacity, model_width), 'expert', spl...]
    pallas_call x1, Pallas kernels: 46.6 us -> 57.8 us  [expert_pass(): pl.pallas_call(functools.partial(expert_kernel, sources), grid_spec=pltpu...]
    unnamed x217 -> x272, local copies, waits for them, and re-layouts: 16.2 us -> 24.8 us
    ppermute x58 -> x53, waiting for transfers between devices: 275 us -> 283 us  [cross(): return lax.ppermute(values, 'expert', [(i, i ^ bit) for i in range(count)])]
    convert_element_type x27 -> x22, other arithmetic: 25.4 us -> 21.4 us  [the longest x20 18 us: fold_step(): sent = sum((p[count:].astype(F32) for p in pieces)).astype(BF)]
  transfers between devices with their start and end apart: 89 -> 84, of which waited for: 38 -> 33; matrix products, arithmetic and copies ran while one was open for 37% -> 26% of each run, Pallas kernels for 16% -> 16%
where the time goes in v4:
time: 918 us; the launch traced here: 907 us
  waiting for transfers between devices  328 us (36%)
  starting transfers between devices  146 us (16%)
  Pallas kernels  146 us (16%)
  matrix products  142 us (15%)
  local copies, waits for them, and re-layouts  77.4 us (8%)
  other arithmetic  63.1 us (7%)
    ppermute x53, waiting for transfers between devices, cross(): return lax.ppermute(values, 'expert', [(i, i ^ bit) for i in range(count)])  283 us
    ppermute x53, starting transfers between devices, cross(): return lax.ppermute(values, 'expert', [(i, i ^ bit) for i in range(count)])  103 us
    dot_general x18, matrix products, dot(): return jnp.dot(left, right, preferred_element_type=F32)  79.7 us
    pallas_call x1, Pallas kernels, expert_pass(): pl.pallas_call(functools.partial(expert_kernel, sources), grid_spec=pltpu...  57.8 us
    dot_general x10, matrix products, dot_t(): lax.dot_general(left, right, (((1,), (1,)), ((), ())), preferred_element_...  42 us
    pallas_call x1, Pallas kernels, attend_back(): pl.pallas_call(attend_back_kernel, grid=(HEADS // 2,), in_specs=[pl.Block...  39.7 us
    all_to_all x4, starting transfers between devices, exchange(): lax.all_to_all(rows.reshape(owners, capacity, model_width), 'expert', spl...  34.4 us
    all_to_all x4, waiting for transfers between devices, exchange(): lax.all_to_all(rows.reshape(owners, capacity, model_width), 'expert', spl...  30.9 us
  transfers between devices with their start and end apart: 84, of which 33 were waited for; matrix products, arithmetic and copies ran while one was open for 26% of the time, Pallas kernels for 16%

profile of v4, /device:TPU:0, one launch (start us, length us, event | category | flops | bytes accessed | tf_op | source)
XLA Modules:
  0.0 907.2 jit_solution(8008344094690649797)
XLA Ops:
  6.6 4.1 convolution_convert_fusion.2
  10.7 8.1 all-to-all-start
  20.6 8.9 collective-permute-done.3
  32.7 4.0 collective-permute-start.4
  36.7 70.6 %collective-permute-done.4 = bf16[64,576]{1,0:T(8,128)(2,1)S(1)} collective-permute-done((bf16[64,576]{1,0:T(8,128)(2,1)S(1)}, bf16[64,576]{1,0:T(8,128)(2,1)S(1)}, u32[]{:S(2)}, u32[]{:S(2)}) %collective-permute-start.4) | collective-permute-done | bytes 73760 | tf_op jit(solution)/shard_map/ppermute | solution.py:85
  109.5 4.3 collective-permute-done.5
  115.5 4.3 collective-permute-start.6
  120.0 6.6 collective-permute-done.6
  131.5 13.9 %collective-permute-done.7 = bf16[512,576]{0,1:T(8,128)(2,1)} collective-permute-done((bf16[512,576]{0,1:T(8,128)(2,1)}, bf16[512,576]{0,1:T(8,128)(2,1)}, u32[]{:S(2)}, u32[]{:S(2)}) %collective-permute-start.7) | collective-permute-done | bytes 589856 | tf_op jit(solution)/shard_map/ppermute | solution.py:85
  148.8 11.8 %collective-permute-done.11 = bf16[512,576]{0,1:T(8,128)(2,1)S(1)} collective-permute-done((bf16[512,576]{0,1:T(8,128)(2,1)}, bf16[512,576]{0,1:T(8,128)(2,1)S(1)}, u32[]{:S(2)}, u32[]{:S(2)}) %collective-permute-start.11) | collective-permute-done | bytes 589856 | tf_op jit(solution)/shard_map/ppermute | solution.py:85
  161.7 5.1 fusion.68
  169.5 4.8 maximum_select_fusion.expand_ref
  185.2 3.9 convolution_add_fusion.1.raw_ref
  189.1 28.2 %shard_map.281 = (bf16[128,2048]{1,0:T(8,128)(2,1)S(1)}, bf16[2048,576]{1,0:T(8,128)(2,1)S(1)}, bf16[2048,2048]{1,0:T(8,128)(2,1)}, bf16[2048,512]{1,0:T(8,128)(2,1)S(1)}, bf16[128,2048]{1,0:T(8,128)(2,1)S(1)}) custom-call(f32[128,3072]{1,0:T(8,128)S(1)} %convolution_add_fusion.1.raw_ref, f32[128,32]{1,0:T(8,128)S(1)} %get-tuple-element.390.cosine_ref, ...), custom_call_target="tpu_custom_call" | custom-call | flops 9126805504 | bytes 8388608 | tf_op jit(solution)/shard_map/pallas_call | solution.py:338
  228.6 4.7 all-to-all-start.1
  233.9 4.6 fusion.115
  238.5 4.7 fusion.116
  243.3 6.1 fusion.58
  252.5 8.5 fusion.38
  261.0 3.8 fusion.39
  265.9 3.7 fusion.46
  269.6 4.8 convolution_add_fusion.4
  274.4 30.9 %all-to-all-done.1 = bf16[16,56,2048]{2,1,0:T(8,128)(2,1)} async-done(((bf16[16,56,2048]{2,1,0:T(8,128)(2,1)}), bf16[16,56,2048]{2,1,0:T(8,128)(2,1)}, u32[]{:S(2)}, u32[]{:S(2)}) %all-to-all-start.1) | async-done | bytes 3670048 | tf_op jit(solution)/shard_map/all_to_all | solution.py:654
  309.6 10.3 %collective-permute-start.18 = (bf16[2,4,2,88,128]{4,3,2,1,0:T(8,128)(2,1)}, bf16[2,4,2,88,128]{4,3,2,1,0:T(8,128)(2,1)}, u32[]{:S(2)}, u32[]{:S(2)}) collective-permute-start(bf16[2,4,2,88,128]{4,3,2,1,0:T(8,128)(2,1)} %get-tuple-element.354), channel_id=1, source_target_pairs={{0,8},{2,10},{4,12},{6,14},{8,0},{10,2},{12,4},{14,6},{16,24},{18,... | collective-permute-start | bytes 1081352 | tf_op jit(solution)/shard_map/ppermute | solution.py:85
  326.7 57.8 %shard_map.282 = (bf16[896,2048]{1,0:T(8,128)(2,1)}, bf16[1408,896]{1,0:T(8,128)(2,1)}, bf16[2,2,704,896]{3,2,1,0:T(8,128)(2,1)}, f32[1,896]{1,0:T(1,128)}, bf16[16,896]{1,0:T(8,128)(2,1)}) custom-call(s32[1]{0:T(128)} %bitcast.18.here_ref, bf16[896,2048]{1,0:T(8,128)(2,1)} %bitcast.17.rows_ref, bf16[896,2048]{1,0:T(8,128)(2,1)} %bitcast.8.grads_ref, ...), custom_call_target="tpu_custom_call" | custom-call | flops 25836912640 | bytes 28311552 | tf_op jit(solution)/shard_map/pallas_call | solution.py:531
  386.5 8.8 all-to-all-start.2
  395.3 10.2 %convolution_convert_fusion = bf16[2,704,2048]{2,1,0:T(8,128)(2,1)} fusion(bf16[896,2048]{1,0:T(8,128)(2,1)} %bitcast.17.rows_ref, bf16[2,2,704,896]{3,2,1,0:T(8,128)(2,1)} %get-tuple-element.171), kind=kOutput, calls=%fused_computation.5 | convolution fusion | flops 5170266112 | bytes 11960320 | tf_op jit(solution)/shard_map/dot_general | solution.py:72
  405.5 7.3 convolution_convert_fusion.3
  416.1 4.9 fusion.20
  421.1 7.0 multiply_convert_fusion.1
  430.1 3.3 fusion.117
  433.8 3.2 shard_map.283
  439.2 4.5 shard_map.284
  445.4 4.5 shard_map.285
  450.7 8.2 convert_add_fusion.1
  458.9 11.9 %convert_add_fusion = f32[2,704,2048]{2,1,0:T(8,128)} fusion(bf16[2,704,2048]{2,1,0:T(8,128)(2,1)} %collective-permute-done.23, bf16[896,2048]{1,0:T(8,128)(2,1)} %bitcast.17.rows_ref, bf16[2,2,704,896]{3,2,1,0:T(8,128)(2,1)S(1)} %bitcast.279), kind=kOutput, calls=%fused_computation | convolution fusion | flops 5173149696 | bytes 23494656 | tf_op jit(solution)/shard_map/dot_general | solution.py:72
  470.8 16.0 %collective-permute-done.27 = bf16[352,2048]{1,0:T(8,128)(2,1)S(1)} collective-permute-done((bf16[352,2048]{1,0:T(8,128)(2,1)S(1)}, bf16[352,2048]{1,0:T(8,128)(2,1)S(1)}, u32[]{:S(2)}, u32[]{:S(2)}) %collective-permute-start.27) | collective-permute-done | bytes 1441824 | tf_op jit(solution)/shard_map/ppermute | solution.py:85
  489.1 28.7 %collective-permute-done.33 = bf16[256,2816]{1,0:T(8,128)(2,1)} collective-permute-done((bf16[256,2816]{1,0:T(8,128)(2,1)S(1)}, bf16[256,2816]{1,0:T(8,128)(2,1)}, u32[]{:S(2)}, u32[]{:S(2)}) %collective-permute-start.33) | collective-permute-done | bytes 1441824 | tf_op jit(solution)/shard_map/ppermute | solution.py:85
  517.8 4.4 multiply_reduce_fusion
  523.7 4.0 fusion.119
  551.8 12.8 %all-to-all-start.3 = ((bf16[16,56,2048]{2,1,0:T(8,128)(2,1)}), bf16[16,56,2048]{2,1,0:T(8,128)(2,1)}, u32[]{:S(2)}, u32[]{:S(2)}) async-start(bf16[16,56,2048]{2,1,0:T(8,128)(2,1)} %bitcast.238), calls=%async_computation.3 | async-start | bytes 7340032 | tf_op jit(solution)/shard_map/all_to_all | solution.py:654
  574.4 39.7 %shard_map.286 = (bf16[128,3072]{1,0:T(8,128)(2,1)S(1)}, bf16[512,4096]{1,0:T(8,128)(2,1)}, bf16[2048,576]{1,0:T(8,128)(2,1)}) custom-call(bf16[128,2048]{1,0:T(8,128)(2,1)S(1)} %copy-done.2, bf16[512,4096]{1,0:T(8,128)(2,1)} %maximum_select_fusion.expand_ref, bf16[2048,576]{1,0:T(8,128)(2,1)} %constant_dynamic-update-slice_fusion.keys_ref, ...), custom_call_target="tpu_custom_call" | custom-call | flops 22548578304 | bytes 8388608 | tf_op jit(solution)/shard_map/pallas_call | solution.py:425
  623.8 18.7 %collective-permute-done.35 = bf16[128,2816]{1,0:T(8,128)(2,1)S(1)} collective-permute-done((bf16[128,2816]{1,0:T(8,128)(2,1)S(1)}, bf16[128,2816]{1,0:T(8,128)(2,1)S(1)}, u32[]{:S(2)}, u32[]{:S(2)}) %collective-permute-start.35) | collective-permute-done | bytes 720928 | tf_op jit(solution)/shard_map/ppermute | solution.py:85
  643.9 5.9 fusion.122
  657.0 3.3 dynamic-slice_bitcast_fusion
  666.5 5.8 fusion.123
  689.8 3.8 collective-permute-done.38
  695.0 4.2 collective-permute-start.39
  704.9 10.9 %collective-permute-start.40 = (bf16[64,576]{1,0:T(8,128)(2,1)S(1)}, bf16[64,576]{1,0:T(8,128)(2,1)S(1)}, u32[]{:S(2)}, u32[]{:S(2)}) collective-permute-start(bf16[64,576]{1,0:T(8,128)(2,1)S(1)} %add_convert_fusion.22), channel_id=1, source_target_pairs={{0,16},{2,18},{4,20},{6,22},{8,24},{10,26},{12,28},{14,30},{16,0},... | collective-permute-start | bytes 221192 | tf_op jit(solution)/shard_map/ppermute | solution.py:85
  731.2 24.7 %collective-permute-done.44 = bf16[64,576]{1,0:T(8,128)(2,1)S(1)} collective-permute-done((bf16[64,576]{1,0:T(8,128)(2,1)S(1)}, bf16[64,576]{1,0:T(8,128)(2,1)S(1)}, u32[]{:S(2)}, u32[]{:S(2)}) %collective-permute-start.44) | collective-permute-done | bytes 73760 | tf_op jit(solution)/shard_map/ppermute | solution.py:85
  757.9 16.4 %collective-permute-done.58 = bf16[256,1536]{1,0:T(8,128)(2,1)S(1)} collective-permute-done((bf16[256,1536]{1,0:T(8,128)(2,1)S(1)}, bf16[256,1536]{1,0:T(8,128)(2,1)S(1)}, u32[]{:S(2)}, u32[]{:S(2)}) %collective-permute-start.58) | collective-permute-done | bytes 786464 | tf_op jit(solution)/shard_map/ppermute | solution.py:85
  775.7 8.6 collective-permute-start.77
  789.0 14.3 %collective-permute-done.59 = bf16[128,1536]{1,0:T(8,128)(2,1)S(1)} collective-permute-done((bf16[128,1536]{1,0:T(8,128)(2,1)S(1)}, bf16[128,1536]{1,0:T(8,128)(2,1)S(1)}, u32[]{:S(2)}, u32[]{:S(2)}) %collective-permute-start.59) | collective-permute-done | bytes 393248 | tf_op jit(solution)/shard_map/ppermute | solution.py:85
  804.8 7.5 collective-permute-done.52
  812.9 9.7 %collective-permute-start.60 = (bf16[64,1536]{1,0:T(8,128)(2,1)S(1)}, bf16[64,1536]{1,0:T(8,128)(2,1)S(1)}, u32[]{:S(2)}, u32[]{:S(2)}) collective-permute-start(bf16[64,1536]{1,0:T(8,128)(2,1)S(1)} %add_convert_fusion.14), channel_id=1, source_target_pairs={{0,16},{2,18},{4,20},{6,22},{8,24},{10,26},{12,28},{14,30},{16,0},... | collective-permute-start | bytes 589832 | tf_op jit(solution)/shard_map/ppermute | solution.py:85
  822.8 7.6 collective-permute-done.60
  830.4 8.9 collective-permute-done.53
  840.4 9.2 %collective-permute-done.78 = bf16[64,2048]{1,0:T(8,128)(2,1)S(1)} collective-permute-done((bf16[64,2048]{1,0:T(8,128)(2,1)S(1)}, bf16[64,2048]{1,0:T(8,128)(2,1)S(1)}, u32[]{:S(2)}, u32[]{:S(2)}) %collective-permute-start.78) | collective-permute-done | bytes 262176 | tf_op jit(solution)/shard_map/ppermute | solution.py:85
  864.7 4.5 collective-permute-start.70
  872.1 4.4 collective-permute-start.67
  881.6 3.9 collective-permute-start.68
  892.2 4.0 all-to-all-start.4
  896.2 3.6 fusion.12
  899.8 4.9 all-to-all-done.4
  (608 shorter events, 219.7 us)
Async XLA Ops:
  0.6 220.3 %collective-permute-start.14 = (bf16[1024,5632]{1,0:T(8,128)(2,1)}, bf16[1024,5632]{1,0:T(8,128)(2,1)}, u32[]{:S(2)}, u32[]{:S(2)}) collective-permute-start(bf16[1024,5632]{1,0:T(8,128)(2,1)} %param.29), channel_id=1, source_target_pairs={{0,1},{1,0},{2,3},{3,2},{4,5},{5,4},{6,7},{7,6},{8,9},{9,8},{10,11... | collective-permute-start | bytes 34603016 | tf_op jit(solution)/shard_map/ppermute | solution.py:89
  1.9 17.8 %collective-permute-start = (bf16[1,2304]{1,0:T(2,128)(2,1)S(1)}, bf16[1,2304]{1,0:T(2,128)(2,1)S(1)}, u32[]{:S(2)}, u32[]{:S(2)}) collective-permute-start(bf16[1,2304]{1,0:T(2,128)(2,1)S(1)} %broadcast_in_dim.24), channel_id=1, source_target_pairs={{0,1},{1,0},{2,3},{3,2},{4,5},{5,4},{6,7},{7,6},{8,9},{9,8},{10,11... | collective-permute-start | bytes 13832 | tf_op jit(solution)/shard_map/ppermute | solution.py:89
  2.0 166.1 %collective-permute-start.1 = (bf16[1024,3072]{1,0:T(8,128)(2,1)}, bf16[1024,3072]{1,0:T(8,128)(2,1)}, u32[]{:S(2)}, u32[]{:S(2)}) collective-permute-start(bf16[1024,3072]{1,0:T(8,128)(2,1)} %param.22), channel_id=1, source_target_pairs={{0,1},{1,0},{2,3},{3,2},{4,5},{5,4},{6,7},{7,6},{8,9},{9,8},{10,11... | collective-permute-start | bytes 18874376 | tf_op jit(solution)/shard_map/ppermute | solution.py:89
  2.5 27.0 %collective-permute-start.3 = (bf16[1024,576]{0,1:T(8,128)(2,1)}, bf16[1024,576]{0,1:T(8,128)(2,1)}, u32[]{:S(2)}, u32[]{:S(2)}) collective-permute-start(bf16[1024,576]{0,1:T(8,128)(2,1)} %param.23), channel_id=1, source_target_pairs={{0,1},{1,0},{2,3},{3,2},{4,5},{5,4},{6,7},{7,6},{8,9},{9,8},{10,11... | collective-permute-start | bytes 3538952 | tf_op jit(solution)/shard_map/ppermute | solution.py:89
  2.5 126.8 %collective-permute-start.2 = (bf16[256,4096]{1,0:T(8,128)(2,1)}, bf16[256,4096]{1,0:T(8,128)(2,1)}, u32[]{:S(2)}, u32[]{:S(2)}) collective-permute-start(bf16[256,4096]{1,0:T(8,128)(2,1)} %param.25), channel_id=1, source_target_pairs={{0,1},{1,0},{2,3},{3,2},{4,5},{5,4},{6,7},{7,6},{8,9},{9,8},{10,11... | collective-permute-start | bytes 6291464 | tf_op jit(solution)/shard_map/ppermute | solution.py:89
  10.7 210.3 %all-to-all-start = ((bf16[16,56,2048]{2,1,0:T(8,128)(2,1)}), bf16[16,56,2048]{2,1,0:T(8,128)(2,1)}, u32[]{:S(2)}, u32[]{:S(2)}) async-start(bf16[16,56,2048]{2,1,0:T(8,128)(2,1)} %bitcast.225), calls=%async_computation | async-start | bytes 7340032 | tf_op jit(solution)/shard_map/all_to_all | solution.py:654
  32.7 74.6 %collective-permute-start.4 = (bf16[64,576]{1,0:T(8,128)(2,1)S(1)}, bf16[64,576]{1,0:T(8,128)(2,1)S(1)}, u32[]{:S(2)}, u32[]{:S(2)}) collective-permute-start(bf16[64,576]{1,0:T(8,128)(2,1)S(1)} %get-tuple-element.384), channel_id=1, source_target_pairs={{0,16},{2,18},{4,20},{6,22},{8,24},{10,26},{12,28},{14,30},{16,0},... | collective-permute-start | bytes 221192 | tf_op jit(solution)/shard_map/ppermute | solution.py:85
  36.7 71.6 %collective-permute-start.8 = (bf16[64,576]{1,0:T(8,128)(2,1)S(1)}, bf16[64,576]{1,0:T(8,128)(2,1)S(1)}, u32[]{:S(2)}, u32[]{:S(2)}) collective-permute-start(bf16[64,576]{1,0:T(8,128)(2,1)S(1)} %get-tuple-element.382), channel_id=1, source_target_pairs={{0,16},{2,18},{4,20},{6,22},{8,24},{10,26},{12,28},{14,30},{16,0},... | collective-permute-start | bytes 221192 | tf_op jit(solution)/shard_map/ppermute | solution.py:85
  115.5 11.1 %collective-permute-start.6 = (bf16[256,576]{1,0:T(8,128)(2,1)S(1)}, bf16[256,576]{1,0:T(8,128)(2,1)S(1)}, u32[]{:S(2)}, u32[]{:S(2)}) collective-permute-start(bf16[256,576]{1,0:T(8,128)(2,1)S(1)} %pad_maximum_fusion.28), channel_id=1, source_target_pairs={{0,4},{2,6},{4,0},{6,2},{8,12},{10,14},{12,8},{14,10},{16,20},{18,... | collective-permute-start | bytes 884744 | tf_op jit(solution)/shard_map/ppermute | solution.py:85
  126.6 94.3 %collective-permute-start.15 = (bf16[1408,2048]{1,0:T(8,128)(2,1)}, bf16[1408,2048]{1,0:T(8,128)(2,1)}, u32[]{:S(2)}, u32[]{:S(2)}) collective-permute-start(bf16[1408,2048]{1,0:T(8,128)(2,1)} %param.30), channel_id=1, source_target_pairs={{0,1},{1,0},{2,3},{3,2},{4,5},{5,4},{6,7},{7,6},{8,9},{9,8},{10,11... | collective-permute-start | bytes 17301512 | tf_op jit(solution)/shard_map/ppermute | solution.py:89
  128.2 92.7 %collective-permute-start.16 = (bf16[2,704,2048]{2,1,0:T(8,128)(2,1)}, bf16[2,704,2048]{2,1,0:T(8,128)(2,1)}, u32[]{:S(2)}, u32[]{:S(2)}) collective-permute-start(bf16[2,704,2048]{2,1,0:T(8,128)(2,1)} %bitcast.10.refs_0_), channel_id=1, source_target_pairs={{0,1},{1,0},{2,3},{3,2},{4,5},{5,4},{6,7},{7,6},{8,9},{9,8},{10,11... | collective-permute-start | bytes 17301512 | tf_op jit(solution)/shard_map/ppermute | solution.py:89
  129.4 16.1 %collective-permute-start.7 = (bf16[512,576]{0,1:T(8,128)(2,1)}, bf16[512,576]{0,1:T(8,128)(2,1)}, u32[]{:S(2)}, u32[]{:S(2)}) collective-permute-start(bf16[512,576]{0,1:T(8,128)(2,1)} %copy.127), channel_id=1, source_target_pairs={{0,2},{2,0},{4,6},{6,4},{8,10},{10,8},{12,14},{14,12},{16,18},{18,... | collective-permute-start | bytes 1769480 | tf_op jit(solution)/shard_map/ppermute | solution.py:85
  145.4 15.2 %collective-permute-start.11 = (bf16[512,576]{0,1:T(8,128)(2,1)}, bf16[512,576]{0,1:T(8,128)(2,1)S(1)}, u32[]{:S(2)}, u32[]{:S(2)}) collective-permute-start(bf16[512,576]{0,1:T(8,128)(2,1)} %copy.128), channel_id=1, source_target_pairs={{0,4},{2,6},{4,0},{6,2},{8,12},{10,14},{12,8},{14,10},{16,20},{18,... | collective-permute-start | bytes 1769480 | tf_op jit(solution)/shard_map/ppermute | solution.py:85
  160.6 60.3 %collective-permute-start.12 = (bf16[1024,2048]{1,0:T(8,128)(2,1)}, bf16[1024,2048]{1,0:T(8,128)(2,1)}, u32[]{:S(2)}, u32[]{:S(2)}) collective-permute-start(bf16[1024,2048]{1,0:T(8,128)(2,1)} %param.26), channel_id=1, source_target_pairs={{0,1},{1,0},{2,3},{3,2},{4,5},{5,4},{6,7},{7,6},{8,9},{9,8},{10,11... | collective-permute-start | bytes 12582920 | tf_op jit(solution)/shard_map/ppermute | solution.py:89
  168.1 52.8 %collective-permute-start.17 = (bf16[704,2048]{1,0:T(8,128)(2,1)}, bf16[704,2048]{1,0:T(8,128)(2,1)}, u32[]{:S(2)}, u32[]{:S(2)}) collective-permute-start(bf16[704,2048]{1,0:T(8,128)(2,1)} %bitcast.11.refs_1_), channel_id=1, source_target_pairs={{0,1},{1,0},{2,3},{3,2},{4,5},{5,4},{6,7},{7,6},{8,9},{9,8},{10,11... | collective-permute-start | bytes 8650760 | tf_op jit(solution)/shard_map/ppermute | solution.py:89
  228.6 76.7 %all-to-all-start.1 = ((bf16[16,56,2048]{2,1,0:T(8,128)(2,1)}), bf16[16,56,2048]{2,1,0:T(8,128)(2,1)}, u32[]{:S(2)}, u32[]{:S(2)}) async-start(bf16[16,56,2048]{2,1,0:T(8,128)(2,1)} %bitcast.224), calls=%async_computation.1 | async-start | bytes 7340032 | tf_op jit(solution)/shard_map/all_to_all | solution.py:654
  309.6 75.0 %collective-permute-start.18 = (bf16[2,4,2,88,128]{4,3,2,1,0:T(8,128)(2,1)}, bf16[2,4,2,88,128]{4,3,2,1,0:T(8,128)(2,1)}, u32[]{:S(2)}, u32[]{:S(2)}) collective-permute-start(bf16[2,4,2,88,128]{4,3,2,1,0:T(8,128)(2,1)} %get-tuple-element.354), channel_id=1, source_target_pairs={{0,8},{2,10},{4,12},{6,14},{8,0},{10,2},{12,4},{14,6},{16,24},{18,... | collective-permute-start | bytes 1081352 | tf_op jit(solution)/shard_map/ppermute | solution.py:85
  322.7 61.8 %collective-permute-start.19 = (bf16[2,4,2,64,128]{4,3,2,1,0:T(8,128)(2,1)S(1)}, bf16[2,4,2,64,128]{4,3,2,1,0:T(8,128)(2,1)S(1)}, u32[]{:S(2)}, u32[]{:S(2)}) collective-permute-start(bf16[2,4,2,64,128]{4,3,2,1,0:T(8,128)(2,1)S(1)} %get-tuple-element.376), channel_id=1, source_target_pairs={{0,8},{2,10},{4,12},{6,14},{8,0},{10,2},{12,4},{14,6},{16,24},{18,... | collective-permute-start | bytes 786440 | tf_op jit(solution)/shard_map/ppermute | solution.py:85
  322.7 61.9 %collective-permute-start.20 = (bf16[128,2048]{1,0:T(8,128)(2,1)S(1)}, bf16[128,2048]{1,0:T(8,128)(2,1)S(1)}, u32[]{:S(2)}, u32[]{:S(2)}) collective-permute-start(bf16[128,2048]{1,0:T(8,128)(2,1)S(1)} %fusion.27), channel_id=1, source_target_pairs={{0,8},{2,10},{4,12},{6,14},{8,0},{10,2},{12,4},{14,6},{16,24},{18,... | collective-permute-start | bytes 1572872 | tf_op jit(solution)/shard_map/ppermute | solution.py:85
  324.7 59.9 %collective-permute-start.21 = (bf16[128,2816]{1,0:T(8,128)(2,1)S(1)}, bf16[128,2816]{1,0:T(8,128)(2,1)S(1)}, u32[]{:S(2)}, u32[]{:S(2)}) collective-permute-start(bf16[128,2816]{1,0:T(8,128)(2,1)S(1)} %get-tuple-element.181), channel_id=1, source_target_pairs={{0,8},{2,10},{4,12},{6,14},{8,0},{10,2},{12,4},{14,6},{16,24},{18,... | collective-permute-start | bytes 2162696 | tf_op jit(solution)/shard_map/ppermute | solution.py:85
  324.8 59.8 %collective-permute-start.22 = (bf16[128,2816]{1,0:T(8,128)(2,1)S(1)}, bf16[128,2816]{1,0:T(8,128)(2,1)S(1)}, u32[]{:S(2)}, u32[]{:S(2)}) collective-permute-start(bf16[128,2816]{1,0:T(8,128)(2,1)S(1)} %get-tuple-element.187), channel_id=1, source_target_pairs={{0,8},{2,10},{4,12},{6,14},{8,0},{10,2},{12,4},{14,6},{16,24},{18,... | collective-permute-start | bytes 2162696 | tf_op jit(solution)/shard_map/ppermute | solution.py:85
  386.5 131.3 %all-to-all-start.2 = ((bf16[16,56,2048]{2,1,0:T(8,128)(2,1)}), bf16[16,56,2048]{2,1,0:T(8,128)(2,1)}, u32[]{:S(2)}, u32[]{:S(2)}) async-start(bf16[16,56,2048]{2,1,0:T(8,128)(2,1)} %bitcast.239), calls=%async_computation.2 | async-start | bytes 7340032 | tf_op jit(solution)/shard_map/all_to_all | solution.py:654
  405.5 53.4 %collective-permute-start.23 = (bf16[2,704,2048]{2,1,0:T(8,128)(2,1)}, bf16[2,704,2048]{2,1,0:T(8,128)(2,1)}, u32[]{:S(2)}, u32[]{:S(2)}) collective-permute-start(bf16[2,704,2048]{2,1,0:T(8,128)(2,1)} %convolution_convert_fusion), channel_id=1, source_target_pairs={{0,1},{1,0},{2,3},{3,2},{4,5},{5,4},{6,7},{7,6},{8,9},{9,8},{10,11... | collective-permute-start | bytes 17301512 | tf_op jit(solution)/shard_map/ppermute | solution.py:89
  412.8 37.8 %collective-permute-start.24 = (bf16[704,2048]{1,0:T(8,128)(2,1)}, bf16[704,2048]{1,0:T(8,128)(2,1)S(1)}, u32[]{:S(2)}, u32[]{:S(2)}) collective-permute-start(bf16[704,2048]{1,0:T(8,128)(2,1)} %convolution_convert_fusion.3), channel_id=1, source_target_pairs={{0,1},{1,0},{2,3},{3,2},{4,5},{5,4},{6,7},{7,6},{8,9},{9,8},{10,11... | collective-permute-start | bytes 8650760 | tf_op jit(solution)/shard_map/ppermute | solution.py:89
  414.5 15.4 %collective-permute-start.25 = (bf16[8,88,256]{2,1,0:T(8,128)(2,1)S(1)}, bf16[8,88,256]{2,1,0:T(8,128)(2,1)S(1)}, u32[]{:S(2)}, u32[]{:S(2)}) collective-permute-start(bf16[8,88,256]{2,1,0:T(8,128)(2,1)S(1)} %get-tuple-element.353), channel_id=1, source_target_pairs={{0,1},{1,0},{2,3},{3,2},{4,5},{5,4},{6,7},{7,6},{8,9},{9,8},{10,11... | collective-permute-start | bytes 1081352 | tf_op jit(solution)/shard_map/ppermute | solution.py:89
  414.8 14.4 %collective-permute-start.28 = (bf16[8,64,256]{2,1,0:T(8,128)(2,1)S(1)}, bf16[8,64,256]{2,1,0:T(8,128)(2,1)S(1)}, u32[]{:S(2)}, u32[]{:S(2)}) collective-permute-start(bf16[8,64,256]{2,1,0:T(8,128)(2,1)S(1)} %get-tuple-element.375), channel_id=1, source_target_pairs={{0,1},{1,0},{2,3},{3,2},{4,5},{5,4},{6,7},{7,6},{8,9},{9,8},{10,11... | collective-permute-start | bytes 786440 | tf_op jit(solution)/shard_map/ppermute | solution.py:89
  415.4 14.0 %collective-permute-start.31 = (bf16[8,64,256]{2,1,0:T(8,128)(2,1)S(1)}, bf16[8,64,256]{2,1,0:T(8,128)(2,1)S(1)}, u32[]{:S(2)}, u32[]{:S(2)}) collective-permute-start(bf16[8,64,256]{2,1,0:T(8,128)(2,1)S(1)} %get-tuple-element.373), channel_id=1, source_target_pairs={{0,1},{1,0},{2,3},{3,2},{4,5},{5,4},{6,7},{7,6},{8,9},{9,8},{10,11... | collective-permute-start | bytes 786440 | tf_op jit(solution)/shard_map/ppermute | solution.py:89
  429.9 15.3 %collective-permute-start.32 = (bf16[256,2816]{1,0:T(8,128)(2,1)S(1)}, bf16[256,2816]{1,0:T(8,128)(2,1)S(1)}, u32[]{:S(2)}, u32[]{:S(2)}) collective-permute-start(bf16[256,2816]{1,0:T(8,128)(2,1)S(1)} %pad_maximum_fusion.8), channel_id=1, source_target_pairs={{0,1},{1,0},{2,3},{3,2},{4,5},{5,4},{6,7},{7,6},{8,9},{9,8},{10,11... | collective-permute-start | bytes 4325384 | tf_op jit(solution)/shard_map/ppermute | solution.py:89
  437.0 49.8 %collective-permute-start.27 = (bf16[352,2048]{1,0:T(8,128)(2,1)S(1)}, bf16[352,2048]{1,0:T(8,128)(2,1)S(1)}, u32[]{:S(2)}, u32[]{:S(2)}) collective-permute-start(bf16[352,2048]{1,0:T(8,128)(2,1)S(1)} %get-tuple-element.178), channel_id=1, source_target_pairs={{0,2},{2,0},{4,6},{6,4},{8,10},{10,8},{12,14},{14,12},{16,18},{18,... | collective-permute-start | bytes 4325384 | tf_op jit(solution)/shard_map/ppermute | solution.py:85
  443.7 43.5 %collective-permute-start.30 = (bf16[256,2816]{1,0:T(8,128)(2,1)S(1)}, bf16[256,2816]{1,0:T(8,128)(2,1)S(1)}, u32[]{:S(2)}, u32[]{:S(2)}) collective-permute-start(bf16[256,2816]{1,0:T(8,128)(2,1)S(1)} %get-tuple-element.184), channel_id=1, source_target_pairs={{0,4},{2,6},{4,0},{6,2},{8,12},{10,14},{12,8},{14,10},{16,20},{18,... | collective-permute-start | bytes 4325384 | tf_op jit(solution)/shard_map/ppermute | solution.py:85
  450.0 67.7 %collective-permute-start.33 = (bf16[256,2816]{1,0:T(8,128)(2,1)S(1)}, bf16[256,2816]{1,0:T(8,128)(2,1)}, u32[]{:S(2)}, u32[]{:S(2)}) collective-permute-start(bf16[256,2816]{1,0:T(8,128)(2,1)S(1)} %get-tuple-element.190), channel_id=1, source_target_pairs={{0,2},{2,0},{4,6},{6,4},{8,10},{10,8},{12,14},{14,12},{16,18},{18,... | collective-permute-start | bytes 4325384 | tf_op jit(solution)/shard_map/ppermute | solution.py:85
  535.3 36.8 %collective-permute-start.54 = (bf16[4,2,2,64,128]{4,3,2,1,0:T(8,128)(2,1)}, bf16[4,2,2,64,128]{4,3,2,1,0:T(8,128)(2,1)}, u32[]{:S(2)}, u32[]{:S(2)}) collective-permute-start(bf16[4,2,2,64,128]{4,3,2,1,0:T(8,128)(2,1)} %get-tuple-element.370), channel_id=1, source_target_pairs={{0,4},{2,6},{4,0},{6,2},{8,12},{10,14},{12,8},{14,10},{16,20},{18,... | collective-permute-start | bytes 786440 | tf_op jit(solution)/shard_map/ppermute | solution.py:85
  547.4 73.3 %collective-permute-start.74 = (bf16[128,2048]{1,0:T(8,128)(2,1)}, bf16[128,2048]{1,0:T(8,128)(2,1)}, u32[]{:S(2)}, u32[]{:S(2)}) collective-permute-start(bf16[128,2048]{1,0:T(8,128)(2,1)} %get-tuple-element.194), channel_id=1, source_target_pairs={{0,4},{2,6},{4,0},{6,2},{8,12},{10,14},{12,8},{14,10},{16,20},{18,... | collective-permute-start | bytes 1572872 | tf_op jit(solution)/shard_map/ppermute | solution.py:85
  551.1 72.7 %collective-permute-start.34 = (bf16[176,2048]{1,0:T(8,128)(2,1)}, bf16[176,2048]{1,0:T(8,128)(2,1)}, u32[]{:S(2)}, u32[]{:S(2)}) collective-permute-start(bf16[176,2048]{1,0:T(8,128)(2,1)} %add_convert_fusion.2), channel_id=1, source_target_pairs={{0,4},{2,6},{4,0},{6,2},{8,12},{10,14},{12,8},{14,10},{16,20},{18,... | collective-permute-start | bytes 2162696 | tf_op jit(solution)/shard_map/ppermute | solution.py:85
  551.8 339.6 %all-to-all-start.3 = ((bf16[16,56,2048]{2,1,0:T(8,128)(2,1)}), bf16[16,56,2048]{2,1,0:T(8,128)(2,1)}, u32[]{:S(2)}, u32[]{:S(2)}) async-start(bf16[16,56,2048]{2,1,0:T(8,128)(2,1)} %bitcast.238), calls=%async_computation.3 | async-start | bytes 7340032 | tf_op jit(solution)/shard_map/all_to_all | solution.py:654
  566.7 50.4 %collective-permute-start.47 = (bf16[8,1,2,64,128]{4,3,2,0,1:T(8,128)(2,1)}, bf16[8,1,2,64,128]{4,3,2,0,1:T(8,128)(2,1)}, u32[]{:S(2)}, u32[]{:S(2)}) collective-permute-start(bf16[8,1,2,64,128]{4,3,2,0,1:T(8,128)(2,1)} %get-tuple-element.366), channel_id=1, source_target_pairs={{0,2},{2,0},{4,6},{6,4},{8,10},{10,8},{12,14},{14,12},{16,18},{18,... | collective-permute-start | bytes 786440 | tf_op jit(solution)/shard_map/ppermute | solution.py:85
  570.6 46.3 %collective-permute-start.72 = (bf16[4,2,2,64,128]{4,3,2,1,0:T(8,128)(2,1)S(1)}, bf16[4,2,2,64,128]{4,3,2,1,0:T(8,128)(2,1)S(1)}, u32[]{:S(2)}, u32[]{:S(2)}) collective-permute-start(bf16[4,2,2,64,128]{4,3,2,1,0:T(8,128)(2,1)S(1)} %get-tuple-element.362), channel_id=1, source_target_pairs={{0,4},{2,6},{4,0},{6,2},{8,12},{10,14},{12,8},{14,10},{16,20},{18,... | collective-permute-start | bytes 786440 | tf_op jit(solution)/shard_map/ppermute | solution.py:85
  573.2 47.4 %collective-permute-start.55 = (bf16[8,64,256]{2,1,0:T(8,128)(2,1)S(1)}, bf16[8,64,256]{2,1,0:T(8,128)(2,1)S(1)}, u32[]{:S(2)}, u32[]{:S(2)}) collective-permute-start(bf16[8,64,256]{2,1,0:T(8,128)(2,1)S(1)} %get-tuple-element.369), channel_id=1, source_target_pairs={{0,1},{1,0},{2,3},{3,2},{4,5},{5,4},{6,7},{7,6},{8,9},{9,8},{10,11... | collective-permute-start | bytes 786440 | tf_op jit(solution)/shard_map/ppermute | solution.py:89
  617.0 25.6 %collective-permute-start.35 = (bf16[128,2816]{1,0:T(8,128)(2,1)S(1)}, bf16[128,2816]{1,0:T(8,128)(2,1)S(1)}, u32[]{:S(2)}, u32[]{:S(2)}) collective-permute-start(bf16[128,2816]{1,0:T(8,128)(2,1)S(1)} %copy-done.77), channel_id=1, source_target_pairs={{0,2},{2,0},{4,6},{6,4},{8,10},{10,8},{12,14},{14,12},{16,18},{18,... | collective-permute-start | bytes 2162696 | tf_op jit(solution)/shard_map/ppermute | solution.py:85
  617.1 26.0 %collective-permute-start.36 = (bf16[128,2816]{1,0:T(8,128)(2,1)S(1)}, bf16[128,2816]{1,0:T(8,128)(2,1)S(1)}, u32[]{:S(2)}, u32[]{:S(2)}) collective-permute-start(bf16[128,2816]{1,0:T(8,128)(2,1)S(1)} %copy-done.76), channel_id=1, source_target_pairs={{0,4},{2,6},{4,0},{6,2},{8,12},{10,14},{12,8},{14,10},{16,20},{18,... | collective-permute-start | bytes 2162696 | tf_op jit(solution)/shard_map/ppermute | solution.py:85
  623.6 75.6 %collective-permute-start.75 = (bf16[256,2048]{1,0:T(8,128)(2,1)}, bf16[256,2048]{1,0:T(8,128)(2,1)}, u32[]{:S(2)}, u32[]{:S(2)}) collective-permute-start(bf16[256,2048]{1,0:T(8,128)(2,1)} %pad_maximum_fusion.11), channel_id=1, source_target_pairs={{0,1},{1,0},{2,3},{3,2},{4,5},{5,4},{6,7},{7,6},{8,9},{9,8},{10,11... | collective-permute-start | bytes 3145736 | tf_op jit(solution)/shard_map/ppermute | solution.py:89
  653.3 25.9 %collective-permute-start.37 = (bf16[512,576]{0,1:T(8,128)(2,1)}, bf16[512,576]{0,1:T(8,128)(2,1)}, u32[]{:S(2)}, u32[]{:S(2)}) collective-permute-start(bf16[512,576]{0,1:T(8,128)(2,1)} %copy.137), channel_id=1, source_target_pairs={{0,2},{2,0},{4,6},{6,4},{8,10},{10,8},{12,14},{14,12},{16,18},{18,... | collective-permute-start | bytes 1769480 | tf_op jit(solution)/shard_map/ppermute | solution.py:85
  656.9 23.5 %collective-permute-start.41 = (bf16[512,576]{0,1:T(8,128)(2,1)}, bf16[512,576]{0,1:T(8,128)(2,1)}, u32[]{:S(2)}, u32[]{:S(2)}) collective-permute-start(bf16[512,576]{0,1:T(8,128)(2,1)} %copy.142), channel_id=1, source_target_pairs={{0,4},{2,6},{4,0},{6,2},{8,12},{10,14},{12,8},{14,10},{16,20},{18,... | collective-permute-start | bytes 1769480 | tf_op jit(solution)/shard_map/ppermute | solution.py:85
  660.3 16.5 %collective-permute-start.56 = (bf16[128,1536]{1,0:T(8,128)(2,1)S(1)}, bf16[128,1536]{1,0:T(8,128)(2,1)S(1)}, u32[]{:S(2)}, u32[]{:S(2)}) collective-permute-start(bf16[128,1536]{1,0:T(8,128)(2,1)S(1)} %get-tuple-element.351), channel_id=1, source_target_pairs={{0,4},{2,6},{4,0},{6,2},{8,12},{10,14},{12,8},{14,10},{16,20},{18,... | collective-permute-start | bytes 1179656 | tf_op jit(solution)/shard_map/ppermute | solution.py:85
  662.3 15.6 %collective-permute-start.49 = (bf16[128,1536]{1,0:T(8,128)(2,1)S(1)}, bf16[128,1536]{1,0:T(8,128)(2,1)S(1)}, u32[]{:S(2)}, u32[]{:S(2)}) collective-permute-start(bf16[128,1536]{1,0:T(8,128)(2,1)S(1)} %get-tuple-element.350), channel_id=1, source_target_pairs={{0,2},{2,0},{4,6},{6,4},{8,10},{10,8},{12,14},{14,12},{16,18},{18,... | collective-permute-start | bytes 1179656 | tf_op jit(solution)/shard_map/ppermute | solution.py:85
  676.8 107.6 %collective-permute-start.45 = (bf16[16,16,4096]{2,1,0:T(8,128)(2,1)}, bf16[16,16,4096]{2,1,0:T(8,128)(2,1)}, u32[]{:S(2)}, u32[]{:S(2)}) collective-permute-start(bf16[16,16,4096]{2,1,0:T(8,128)(2,1)} %dynamic-slice_bitcast_fusion), channel_id=1, source_target_pairs={{0,1},{1,0},{2,3},{3,2},{4,5},{5,4},{6,7},{7,6},{8,9},{9,8},{10,11... | collective-permute-start | bytes 6291464 | tf_op jit(solution)/shard_map/ppermute | solution.py:89
  677.8 44.8 %collective-permute-start.57 = (bf16[256,1536]{1,0:T(8,128)(2,1)}, bf16[256,1536]{1,0:T(8,128)(2,1)}, u32[]{:S(2)}, u32[]{:S(2)}) collective-permute-start(bf16[256,1536]{1,0:T(8,128)(2,1)} %pad_maximum_fusion.15), channel_id=1, source_target_pairs={{0,1},{1,0},{2,3},{3,2},{4,5},{5,4},{6,7},{7,6},{8,9},{9,8},{10,11... | collective-permute-start | bytes 2359304 | tf_op jit(solution)/shard_map/ppermute | solution.py:89
  693.6 33.5 %collective-permute-start.50 = (bf16[256,1536]{1,0:T(8,128)(2,1)}, bf16[256,1536]{1,0:T(8,128)(2,1)S(1)}, u32[]{:S(2)}, u32[]{:S(2)}) collective-permute-start(bf16[256,1536]{1,0:T(8,128)(2,1)} %pad_maximum_fusion.14), channel_id=1, source_target_pairs={{0,1},{1,0},{2,3},{3,2},{4,5},{5,4},{6,7},{7,6},{8,9},{9,8},{10,11... | collective-permute-start | bytes 2359304 | tf_op jit(solution)/shard_map/ppermute | solution.py:89
  701.0 17.5 %collective-permute-start.43 = (bf16[128,576]{1,0:T(8,128)(2,1)S(1)}, bf16[128,576]{1,0:T(8,128)(2,1)S(1)}, u32[]{:S(2)}, u32[]{:S(2)}) collective-permute-start(bf16[128,576]{1,0:T(8,128)(2,1)S(1)} %get-tuple-element.343), channel_id=1, source_target_pairs={{0,8},{2,10},{4,12},{6,14},{8,0},{10,2},{12,4},{14,6},{16,24},{18,... | collective-permute-start | bytes 442376 | tf_op jit(solution)/shard_map/ppermute | solution.py:85
  704.9 15.1 %collective-permute-start.40 = (bf16[64,576]{1,0:T(8,128)(2,1)S(1)}, bf16[64,576]{1,0:T(8,128)(2,1)S(1)}, u32[]{:S(2)}, u32[]{:S(2)}) collective-permute-start(bf16[64,576]{1,0:T(8,128)(2,1)S(1)} %add_convert_fusion.22), channel_id=1, source_target_pairs={{0,16},{2,18},{4,20},{6,22},{8,24},{10,26},{12,28},{14,30},{16,0},... | collective-permute-start | bytes 221192 | tf_op jit(solution)/shard_map/ppermute | solution.py:85
  718.5 133.2 %collective-permute-start.61 = (bf16[88,2048]{1,0:T(8,128)(2,1)S(1)}, bf16[88,2048]{1,0:T(8,128)(2,1)S(1)}, u32[]{:S(2)}, u32[]{:S(2)}) collective-permute-start(bf16[88,2048]{1,0:T(8,128)(2,1)S(1)} %copy-done.84), channel_id=1, source_target_pairs={{0,16},{2,18},{4,20},{6,22},{8,24},{10,26},{12,28},{14,30},{16,0},... | collective-permute-start | bytes 1081352 | tf_op jit(solution)/shard_map/ppermute | solution.py:85
  720.0 131.7 %collective-permute-start.62 = (bf16[64,2816]{1,0:T(8,128)(2,1)S(1)}, bf16[64,2816]{1,0:T(8,128)(2,1)S(1)}, u32[]{:S(2)}, u32[]{:S(2)}) collective-permute-start(bf16[64,2816]{1,0:T(8,128)(2,1)S(1)} %copy-done.83), channel_id=1, source_target_pairs={{0,16},{2,18},{4,20},{6,22},{8,24},{10,26},{12,28},{14,30},{16,0},... | collective-permute-start | bytes 1081352 | tf_op jit(solution)/shard_map/ppermute | solution.py:85
  722.6 35.1 %collective-permute-start.76 = (bf16[256,2048]{1,0:T(8,128)(2,1)S(1)}, bf16[256,2048]{1,0:T(8,128)(2,1)S(1)}, u32[]{:S(2)}, u32[]{:S(2)}) collective-permute-start(bf16[256,2048]{1,0:T(8,128)(2,1)S(1)} %get-tuple-element.243), channel_id=1, source_target_pairs={{0,2},{2,0},{4,6},{6,4},{8,10},{10,8},{12,14},{14,12},{16,18},{18,... | collective-permute-start | bytes 3145736 | tf_op jit(solution)/shard_map/ppermute | solution.py:85
  727.2 28.8 %collective-permute-start.44 = (bf16[64,576]{1,0:T(8,128)(2,1)S(1)}, bf16[64,576]{1,0:T(8,128)(2,1)S(1)}, u32[]{:S(2)}, u32[]{:S(2)}) collective-permute-start(bf16[64,576]{1,0:T(8,128)(2,1)S(1)} %get-tuple-element.341), channel_id=1, source_target_pairs={{0,16},{2,18},{4,20},{6,22},{8,24},{10,26},{12,28},{14,30},{16,0},... | collective-permute-start | bytes 221192 | tf_op jit(solution)/shard_map/ppermute | solution.py:85
  755.9 18.5 %collective-permute-start.58 = (bf16[256,1536]{1,0:T(8,128)(2,1)S(1)}, bf16[256,1536]{1,0:T(8,128)(2,1)S(1)}, u32[]{:S(2)}, u32[]{:S(2)}) collective-permute-start(bf16[256,1536]{1,0:T(8,128)(2,1)S(1)} %get-tuple-element.226), channel_id=1, source_target_pairs={{0,2},{2,0},{4,6},{6,4},{8,10},{10,8},{12,14},{14,12},{16,18},{18,... | collective-permute-start | bytes 2359304 | tf_op jit(solution)/shard_map/ppermute | solution.py:85
  757.7 18.0 %collective-permute-start.51 = (bf16[256,1536]{1,0:T(8,128)(2,1)S(1)}, bf16[256,1536]{1,0:T(8,128)(2,1)S(1)}, u32[]{:S(2)}, u32[]{:S(2)}) collective-permute-start(bf16[256,1536]{1,0:T(8,128)(2,1)S(1)} %get-tuple-element.224), channel_id=1, source_target_pairs={{0,4},{2,6},{4,0},{6,2},{8,12},{10,14},{12,8},{14,10},{16,20},{18,... | collective-permute-start | bytes 2359304 | tf_op jit(solution)/shard_map/ppermute | solution.py:85
  774.4 77.4 %collective-permute-start.63 = (bf16[64,2816]{1,0:T(8,128)(2,1)S(1)}, bf16[64,2816]{1,0:T(8,128)(2,1)S(1)}, u32[]{:S(2)}, u32[]{:S(2)}) collective-permute-start(bf16[64,2816]{1,0:T(8,128)(2,1)S(1)} %copy-done.82), channel_id=1, source_target_pairs={{0,16},{2,18},{4,20},{6,22},{8,24},{10,26},{12,28},{14,30},{16,0},... | collective-permute-start | bytes 1081352 | tf_op jit(solution)/shard_map/ppermute | solution.py:85
  775.7 37.2 %collective-permute-start.77 = (bf16[128,2048]{1,0:T(8,128)(2,1)S(1)}, bf16[128,2048]{1,0:T(8,128)(2,1)S(1)}, u32[]{:S(2)}, u32[]{:S(2)}) collective-permute-start(bf16[128,2048]{1,0:T(8,128)(2,1)S(1)} %add_convert_fusion.3), channel_id=1, source_target_pairs={{0,8},{2,10},{4,12},{6,14},{8,0},{10,2},{12,4},{14,6},{16,24},{18,... | collective-permute-start | bytes 1572872 | tf_op jit(solution)/shard_map/ppermute | solution.py:85
  784.4 18.9 %collective-permute-start.59 = (bf16[128,1536]{1,0:T(8,128)(2,1)S(1)}, bf16[128,1536]{1,0:T(8,128)(2,1)S(1)}, u32[]{:S(2)}, u32[]{:S(2)}) collective-permute-start(bf16[128,1536]{1,0:T(8,128)(2,1)S(1)} %add_convert_fusion.5), channel_id=1, source_target_pairs={{0,8},{2,10},{4,12},{6,14},{8,0},{10,2},{12,4},{14,6},{16,24},{18,... | collective-permute-start | bytes 1179656 | tf_op jit(solution)/shard_map/ppermute | solution.py:85
  812.3 38.2 %collective-permute-start.46 = (bf16[128,4096]{1,0:T(8,128)(2,1)S(1)}, bf16[128,4096]{1,0:T(8,128)(2,1)S(1)}, u32[]{:S(2)}, u32[]{:S(2)}) collective-permute-start(bf16[128,4096]{1,0:T(8,128)(2,1)S(1)} %bitcast.254), channel_id=1, source_target_pairs={{0,2},{2,0},{4,6},{6,4},{8,10},{10,8},{12,14},{14,12},{16,18},{18,... | collective-permute-start | bytes 3145736 | tf_op jit(solution)/shard_map/ppermute | solution.py:85
  812.9 17.4 %collective-permute-start.60 = (bf16[64,1536]{1,0:T(8,128)(2,1)S(1)}, bf16[64,1536]{1,0:T(8,128)(2,1)S(1)}, u32[]{:S(2)}, u32[]{:S(2)}) collective-permute-start(bf16[64,1536]{1,0:T(8,128)(2,1)S(1)} %add_convert_fusion.14), channel_id=1, source_target_pairs={{0,16},{2,18},{4,20},{6,22},{8,24},{10,26},{12,28},{14,30},{16,0},... | collective-permute-start | bytes 589832 | tf_op jit(solution)/shard_map/ppermute | solution.py:85
  839.3 10.2 %collective-permute-start.78 = (bf16[64,2048]{1,0:T(8,128)(2,1)S(1)}, bf16[64,2048]{1,0:T(8,128)(2,1)S(1)}, u32[]{:S(2)}, u32[]{:S(2)}) collective-permute-start(bf16[64,2048]{1,0:T(8,128)(2,1)S(1)} %add_convert_fusion.12), channel_id=1, source_target_pairs={{0,16},{2,18},{4,20},{6,22},{8,24},{10,26},{12,28},{14,30},{16,0},... | collective-permute-start | bytes 786440 | tf_op jit(solution)/shard_map/ppermute | solution.py:85
  864.7 11.8 %collective-permute-start.70 = (bf16[32,4096]{1,0:T(8,128)(2,1)}, bf16[32,4096]{1,0:T(8,128)(2,1)}, u32[]{:S(2)}, u32[]{:S(2)}) collective-permute-start(bf16[32,4096]{1,0:T(8,128)(2,1)} %add_convert_fusion.13), channel_id=1, source_target_pairs={{0,8},{2,10},{4,12},{6,14},{8,0},{10,2},{12,4},{14,6},{16,24},{18,... | collective-permute-start | bytes 786440 | tf_op jit(solution)/shard_map/ppermute | solution.py:85
  892.2 12.6 %all-to-all-start.4 = ((f32[32,1,1168]{2,1,0:T(1,128)}), f32[32,1,1168]{2,1,0:T(1,128)S(1)}, u32[]{:S(2)}, u32[]{:S(2)}) async-start(f32[32,1,1168]{2,1,0:T(1,128)} %copy.149), calls=%async_computation.4 | async-start | bytes 327680 | tf_op jit(solution)/shard_map/all_to_all | solution.py:871
  (152 other events, 2332.2 us)

commit v5 on v4

--- a/solution.py
+++ b/solution.py
@@ -124,33 +124,9 @@
     return jnp.where(first, jnp.concatenate(pieces, 1), jnp.concatenate(pieces[::-1], 1))
 
 
-def collect(values, bits):
-    places = [0]
-    for bit in bits:
-        values = jnp.concatenate([values, cross(values, bit)], 0)
-        places = places + [place ^ bit for place in places]
-    return values, places
-
-
 def together(*values):
     leaves, tree = jax.tree.flatten(values)
     return jax.tree.unflatten(tree, lax.optimization_barrier(leaves))
-
-
-def fold_step(pieces, bit):
-    count = pieces[0].shape[0] // 2
-    sent = sum(p[count:].astype(F32) for p in pieces).astype(BF)
-    return [p[:count] for p in pieces] + [cross(sent, bit)]
-
-
-def fold_end(pieces):
-    return sum(p.astype(F32) for p in pieces)
-
-
-def fold(pieces, bits):
-    for bit in bits:
-        pieces = fold_step(pieces, bit)
-    return fold_end(pieces)
 
 
 def fold_order(bits):
@@ -171,115 +147,99 @@
     return blocks.reshape((1 << count,) + blocks.shape[count:])
 
 
-def gradient_kernel(rows, order_ref, left_ref, right_ref, kept_ref, sent_ref, picked_ref):
-    count = picked_ref.shape[0] // rows
+def group_messages(own, crossed):
+    if lax.axis_size("shard") != 2:
+        both = lax.all_gather(jnp.concatenate([own, crossed], 0), "shard", axis=0, tiled=True)
+        return [both]
+    return [own, crossed, swap(own), swap(crossed)]
+
+
+def product_kernel(rows, sources, order_ref, *refs):
+    lefts, rights = refs[:sources], refs[sources : 2 * sources]
+    kept_ref, sent_ref, picked_ref, turned_ref = refs[2 * sources :]
+    count = order_ref.shape[0]
+    padded = picked_ref.shape[0] // count
 
     @pl.when(pl.program_id(0) == 0)
     def _():
+        start = 0
+        for left_ref in lefts:
+            tokens = left_ref.shape[0]
+            turned_ref[:, start : start + tokens] = left_ref[...].astype(F32).T
+            start += tokens
+        if padded > rows:
+            picked_ref[...] = jnp.zeros_like(picked_ref)
         for j in range(count):
             start = pl.multiple_of(order_ref[j] * rows, rows)
-            picked_ref[j * rows : (j + 1) * rows, :] = left_ref[pl.ds(start, rows), :]
+            picked_ref[j * padded : j * padded + rows, :] = turned_ref[
+                pl.ds(start, rows), :
+            ].astype(picked_ref.dtype)
 
     half = kept_ref.shape[0]
-    right = right_ref[...]
+    right = jnp.concatenate([right_ref[...] for right_ref in rights], 0)
     kept_ref[...] = dot(picked_ref[:half, :].astype(BF), right).astype(kept_ref.dtype)
     sent_ref[...] = dot(picked_ref[half:, :].astype(BF), right).astype(sent_ref.dtype)
 
 
-def gradient_halves(left, right, blocks, bits):
+def product_halves(lefts, left_part, rights, right_part, bits):
+    (left_start, left_columns), (start, columns) = left_part, right_part
+    shards = lax.axis_size("shard")
+    rows = left_columns // (lax.axis_size("expert") * shards)
+    padded = -(-rows // 16) * 16
+    order = (
+        lax.axis_index("expert") ^ jnp.array(fold_order(bits), jnp.int32)
+    ) * shards + lax.axis_index("shard")
     count = 1 << len(bits)
-    rows_all, tokens = left.shape
-    columns = right.shape[1]
-    rows = rows_all // count
-    half = rows_all // 2
+    half = count * padded // 2
+    tokens = sum(left.shape[0] for left in lefts)
     if rows % 8:
-        picked = differing(left.reshape(count, rows, tokens), bits, blocks).reshape(-1, tokens)
+        left = jnp.concatenate(
+            [left[:, left_start : left_start + left_columns] for left in lefts], 0
+        )
+        right = jnp.concatenate([right[:, start : start + columns] for right in rights], 0)
+        blocks = left.T.reshape(-1, shards, rows, tokens)
+        blocks = lax.dynamic_index_in_dim(blocks, lax.axis_index("shard"), 1, keepdims=False)
+        others = [bit for bit in (1, 2, 4, 8) if bit not in bits]
+        picked = differing(blocks, (*others, *bits), lax.axis_index("expert"))[:count]
+        picked = jnp.pad(picked, ((0, 0), (0, padded - rows), (0, 0))).reshape(-1, tokens)
         product = dot(picked, right).astype(BF)
-        return product[:half], product[half:]
-    order = []
-    for place in fold_order(bits):
-        block = 0
-        for k, bit in enumerate(sorted(bits)):
-            flipped = (blocks >> bit.bit_length() - 1) & 1
-            block = block + ((flipped ^ (place // bit & 1)) << k)
-        order.append(block)
-    if rows % 16:
-        left = left.astype(F32)
-    tile = next(t for t in (512, 384, 256, 128, columns) if columns % t == 0)
+        return product[:half], product[half:], picked
+    tile = next(t for t in (512, 384, 256, 128) if columns % t == 0 and start % t == 0)
     return pl.pallas_call(
-        functools.partial(gradient_kernel, rows),
+        functools.partial(product_kernel, rows, len(lefts)),
         grid_spec=pltpu.PrefetchScalarGridSpec(
             num_scalar_prefetch=1,
             grid=(columns // tile,),
             in_specs=[
-                pl.BlockSpec((rows_all, tokens), lambda i, order: (0, 0)),
-                pl.BlockSpec((tokens, tile), lambda i, order: (0, i)),
+                pl.BlockSpec(
+                    (left.shape[0], left_columns),
+                    lambda i, order: (0, left_start // left_columns),
+                )
+                for left in lefts
+            ]
+            + [
+                pl.BlockSpec((right.shape[0], tile), lambda i, order: (0, i + start // tile))
+                for right in rights
             ],
             out_specs=[
                 pl.BlockSpec((half, tile), lambda i, order: (0, i)),
                 pl.BlockSpec((half, tile), lambda i, order: (0, i)),
+                pl.BlockSpec((count * padded, tokens), lambda i, order: (0, 0)),
             ],
-            scratch_shapes=[pltpu.VMEM((rows_all, tokens), left.dtype)],
-        ),
-        out_shape=[jax.ShapeDtypeStruct((half, columns), BF)] * 2,
-        compiler_params=pltpu.CompilerParams(vmem_limit_bytes=40 << 20),
+            scratch_shapes=[pltpu.VMEM((left_columns, tokens), F32)],
+        ),
+        out_shape=[
+            jax.ShapeDtypeStruct((half, columns), BF),
+            jax.ShapeDtypeStruct((half, columns), BF),
+            jax.ShapeDtypeStruct((count * padded, tokens), F32 if rows % 16 else BF),
+        ],
+        compiler_params=pltpu.CompilerParams(vmem_limit_bytes=56 << 20),
         cost_estimate=pl.CostEstimate(
             flops=4 * half * tokens * columns,
-            bytes_accessed=4 * half * columns + 2 * tokens * (rows_all + columns),
+            bytes_accessed=4 * half * columns + 2 * tokens * (left_columns + columns),
             transcendentals=0,
         ),
-    )(jnp.stack(order).astype(jnp.int32), left, right)
-
-
-def cross_left(left, bit):
-    experts, shards = lax.axis_size("expert"), lax.axis_size("shard")
-    own = lax.axis_index("expert") // bit % 2
-    blocks = left.T.reshape(experts // (2 * bit), 2, bit, shards, -1, left.shape[0])
-    kept = lax.dynamic_index_in_dim(blocks, own, 1, keepdims=False)
-    sent = lax.dynamic_index_in_dim(blocks, 1 - own, 1, keepdims=False)
-    return kept, cross(sent, bit)
-
-
-def pair_left(halves):
-    experts, shards = lax.axis_size("expert"), lax.axis_size("shard")
-    blocks = jnp.concatenate(halves, -1)
-    blocks = blocks.reshape(experts // 2, shards, *blocks.shape[-2:])
-    if shards != 2:
-        blocks = lax.all_to_all(blocks, "shard", split_axis=1, concat_axis=3, tiled=True)
-        return blocks.reshape(-1, blocks.shape[-1])
-    own = lax.axis_index("shard")
-    kept = lax.dynamic_index_in_dim(blocks, own, 1, keepdims=False)
-    sent = lax.dynamic_index_in_dim(blocks, 1 - own, 1, keepdims=False)
-    blocks = jnp.concatenate([kept, swap(sent)], -1)
-    return blocks.reshape(-1, blocks.shape[-1])
-
-
-def pair_right(halves):
-    right = jnp.concatenate(halves, 0)
-    if lax.axis_size("shard") != 2:
-        return lax.all_gather(right, "shard", axis=0, tiled=True)
-    return jnp.concatenate([right, swap(right)], 0)
-
-
-def group_left(left, bit):
-    return pair_left(cross_left(left, bit))
-
-
-def group_right(right, bit):
-    return pair_right((right, cross(right, bit)))
-
-
-def product_group(left, right, bit):
-    return group_left(left, bit), group_right(right, bit)
-
-
-def product_halves(group, bits):
-    return gradient_halves(*group, lax.axis_index("expert"), bits)
-
-
-def product_sum(group, bits):
-    kept, sent = product_halves(group, bits[1:])
-    return fold([kept, cross(sent, bits[1])], bits[2:])
+    )(order.astype(jnp.int32), *lefts, *rights)
 
 
 def pair_partial(partial, bits):
@@ -295,6 +255,271 @@
         sent = lax.dynamic_index_in_dim(blocks, 1 - own, 1, keepdims=False)
         total = (kept.astype(F32) + swap(sent).astype(F32)).astype(partial.dtype)
     return [differing(total, bits, lax.axis_index("expert")).reshape(experts * rows, -1)]
+
+
+def line_places():
+    return range(4, lax.axis_size("expert"), 4)
+
+
+def partner(place):
+    here = lax.axis_index("expert")
+    there = here
+    bit = 1
+    while bit <= place:
+        if place & bit:
+            there = there + bit * (1 - 2 * (here // bit % 2))
+        bit *= 2
+    return there, lax.axis_index("shard")
+
+
+def greet(places):
+    barrier = pltpu.get_barrier_semaphore()
+    for place in places:
+        pl.semaphore_signal(
+            barrier, inc=1, device_id=partner(place), device_id_type=pl.DeviceIdType.MESH
+        )
+    pl.semaphore_wait(barrier, len(places))
+
+
+def slot_parts(rows):
+    plane, line = (1, 2, 3), tuple(line_places())
+    cut = rows // 4
+    return (pl.ds(cut, rows - cut), line, plane), (pl.ds(0, cut), plane, line)
+
+
+def gather_kernel(own_ref, out_ref, send_sems, recv_sems):
+    parts = slot_parts(own_ref.shape[0])
+
+    def send(k, rows, block, place):
+        copy = pltpu.make_async_remote_copy(
+            src_ref=out_ref.at[block, rows],
+            dst_ref=out_ref.at[block ^ place, rows],
+            send_sem=send_sems.at[k, block ^ place],
+            recv_sem=recv_sems.at[k, block ^ place],
+            device_id=partner(place),
+            device_id_type=pl.DeviceIdType.MESH,
+        )
+        copy.start()
+        return copy
+
+    greet((1, 2, 3, *line_places()))
+    out_ref[0] = own_ref[...]
+    copies = {}
+    for k, (rows, first, _) in enumerate(parts):
+        for place in first:
+            copies[k, place] = send(k, rows, 0, place)
+    for k, (rows, _, second) in enumerate(parts):
+        for place in second:
+            copies[k, place] = send(k, rows, 0, place)
+    arrived = set()
+    for k in (1, 0):
+        rows, first, second = parts[k]
+        for block in first:
+            copies[k, block].wait_recv()
+            arrived.add((k, block))
+            for place in second:
+                copies[k, block ^ place] = send(k, rows, block, place)
+    for key, copy in copies.items():
+        copy.wait_send()
+        if key not in arrived:
+            copy.wait_recv()
+
+
+def gather_slot(own):
+    count = lax.axis_size("expert")
+    return pl.pallas_call(
+        gather_kernel,
+        in_specs=[pl.BlockSpec(memory_space=pltpu.VMEM)],
+        out_specs=pl.BlockSpec(memory_space=pltpu.VMEM),
+        out_shape=jax.ShapeDtypeStruct((count, *own.shape), own.dtype),
+        scratch_shapes=[pltpu.SemaphoreType.DMA((2, count)), pltpu.SemaphoreType.DMA((2, count))],
+        compiler_params=pltpu.CompilerParams(
+            collective_id=0, has_side_effects=True, vmem_limit_bytes=16 << 20
+        ),
+        cost_estimate=pl.CostEstimate(
+            flops=5 * 10**10, bytes_accessed=4 * count * own.size, transcendentals=0
+        ),
+    )(own)
+
+
+def scatter_kernel(part_ref, out_ref, *refs):
+    parts = slot_parts(out_ref.shape[0])
+    buffers = [refs[7 * k : 7 * k + 7] for k in range(2)]
+    greet((1, 2, 3, *line_places()))
+    copies = []
+
+    def send(source, target, sems, index, place):
+        copy = pltpu.make_async_remote_copy(
+            src_ref=source,
+            dst_ref=target,
+            send_sem=sems[0].at[index],
+            recv_sem=sems[1].at[index],
+            device_id=partner(place),
+            device_id_type=pl.DeviceIdType.MESH,
+        )
+        copy.start()
+        copies.append(copy)
+        return copy
+
+    firsts = []
+    for (rows, second, first), (first_ref, _, _, *sems) in zip(parts, buffers):
+        firsts.append(
+            [
+                [
+                    send(
+                        part_ref.at[block ^ place, rows],
+                        first_ref.at[k, i],
+                        sems[:2],
+                        (k, i),
+                        place,
+                    )
+                    for i, place in enumerate(first)
+                ]
+                for k, block in enumerate((*second, 0))
+            ]
+        )
+    lasts = {}
+    for p in (1, 0):
+        rows, second, _ = parts[p]
+        first_ref, sum_ref, last_ref, *sems = buffers[p]
+        for k, block in enumerate((*second, 0)):
+            total = part_ref[block, rows, :].astype(F32)
+            for i, copy in enumerate(firsts[p][k]):
+                copy.wait_recv()
+                total = total + first_ref[k, i].astype(F32)
+            if block:
+                sum_ref[k] = total.astype(sum_ref.dtype)
+                lasts[p, k] = send(sum_ref.at[k], last_ref.at[k], sems[2:], k, block)
+            else:
+                out_ref[rows, :] = total
+    for (p, k), copy in lasts.items():
+        copy.wait_recv()
+        out_ref[parts[p][0], :] += buffers[p][2][k].astype(F32)
+    for copy in copies:
+        copy.wait_send()
+
+
+def scatter_slot(part):
+    count, rows, columns = part.shape
+    lines = count // 4
+    cut = rows // 4
+    scratch = []
+    for height, groups, firsts in ((rows - cut, lines, 3), (cut, 4, lines - 1)):
+        scratch += [
+            pltpu.VMEM((groups, firsts, height, columns), part.dtype),
+            pltpu.VMEM((groups - 1, height, columns), part.dtype),
+            pltpu.VMEM((groups - 1, height, columns), part.dtype),
+            pltpu.SemaphoreType.DMA((groups, firsts)),
+            pltpu.SemaphoreType.DMA((groups, firsts)),
+            pltpu.SemaphoreType.DMA((groups - 1,)),
+            pltpu.SemaphoreType.DMA((groups - 1,)),
+        ]
+    return pl.pallas_call(
+        scatter_kernel,
+        in_specs=[pl.BlockSpec(memory_space=pltpu.VMEM)],
+        out_specs=pl.BlockSpec(memory_space=pltpu.VMEM),
+        out_shape=jax.ShapeDtypeStruct((rows, columns), F32),
+        scratch_shapes=scratch,
+        compiler_params=pltpu.CompilerParams(
+            collective_id=1, has_side_effects=True, vmem_limit_bytes=24 << 20
+        ),
+        cost_estimate=pl.CostEstimate(
+            flops=5 * 10**10, bytes_accessed=4 * part.size, transcendentals=0
+        ),
+    )(part)
+
+
+REDUCE_STEPS = (1, 5, 3, 0, 7, 7, 4, 4, 3, 6, 2, 6, 0, 5, 7, 2,
+                5, 2, 6, 7, 0, 3, 0, 4, 1, 2, 5, 3, 7, 1, 2)
+
+
+def reduce_kernel(plans, steps, *refs):
+    refs = list(refs)
+    take = lambda count: [refs.pop(0) for _ in range(count)]
+    pieces = [take(count) for _, count, _ in plans]
+    firsts = [take(1)[0] if split else None for _, _, split in plans]
+    outs = take(len(plans))
+    sends = [[None if split and t == 0 else take(1)[0] for t in range(len(bits))] for bits, _, split in plans]
+    arrivals = [take(len(bits)) for bits, _, _ in plans]
+    send_sems, recv_sems = refs
+    greet(sorted({bit for bits, _, _ in plans for bit in bits}))
+    copies = []
+
+    def add(target, parts, start, count):
+        @pl.loop(0, count // 16)
+        def _(k):
+            here = pl.multiple_of(k * 16, 16)
+            total = sum(part[pl.ds(start + here, 16), :].astype(F32) for part in parts)
+            target[pl.ds(here, 16), :] = total.astype(target.dtype)
+
+    latest = [None] * len(plans)
+    done = [0] * len(plans)
+    for g in steps:
+        bits, _, split = plans[g]
+        t = done[g]
+        done[g] += 1
+        if t:
+            latest[g].wait_recv()
+            pieces[g].append(arrivals[g][t - 1])
+        if t == len(bits):
+            add(outs[g], pieces[g], 0, outs[g].shape[0])
+            continue
+        count = arrivals[g][t].shape[0]
+        source = firsts[g]
+        if t or not split:
+            source = sends[g][t]
+            add(source, pieces[g], count, count)
+        copy = pltpu.make_async_remote_copy(
+            src_ref=source,
+            dst_ref=arrivals[g][t],
+            send_sem=send_sems.at[g, t],
+            recv_sem=recv_sems.at[g, t],
+            device_id=partner(bits[t]),
+            device_id_type=pl.DeviceIdType.MESH,
+        )
+        copy.start()
+        copies.append(copy)
+        latest[g] = copy
+    for copy in copies:
+        copy.wait_send()
+
+
+def reduce_all(groups, steps):
+    plans = tuple((bits, len(pieces), first is not None) for bits, pieces, first in groups)
+    outs, sends, arrivals = [], [], []
+    for bits, pieces, first in groups:
+        count, columns = pieces[0].shape
+        count = count * (1 if first is None else 2)
+        for t in range(len(bits)):
+            count = count // 2
+            arrivals.append(pltpu.VMEM((count, columns), BF))
+            if t or first is None:
+                sends.append(pltpu.VMEM((count, columns), BF))
+        outs.append(jax.ShapeDtypeStruct((count, columns), F32))
+    operands = [piece for _, pieces, _ in groups for piece in pieces]
+    operands += [first for _, _, first in groups if first is not None]
+    most = max(len(bits) for bits, _, _ in groups)
+    in_vmem = pl.BlockSpec(memory_space=pltpu.VMEM)
+    return pl.pallas_call(
+        functools.partial(reduce_kernel, plans, steps),
+        in_specs=[in_vmem] * len(operands),
+        out_specs=[in_vmem] * len(outs),
+        out_shape=outs,
+        scratch_shapes=[
+            *sends,
+            *arrivals,
+            pltpu.SemaphoreType.DMA((len(groups), most)),
+            pltpu.SemaphoreType.DMA((len(groups), most)),
+        ],
+        compiler_params=pltpu.CompilerParams(
+            collective_id=2, has_side_effects=True, vmem_limit_bytes=58 << 20
+        ),
+        cost_estimate=pl.CostEstimate(
+            flops=10**11,
+            bytes_accessed=4 * sum(operand.size for operand in operands),
+            transcendentals=0,
+        ),
+    )(*operands)
 
 
 def attend_kernel(
@@ -370,7 +595,7 @@
 
 
 def attend_back_kernel(
-    grad_ref, expand_ref, keys_ref, weights_ref, queries_ref, mixed_ref, nope_ref, cosine_ref,
+    order_ref, grad_ref, expand_ref, keys_ref, weights_ref, queries_ref, mixed_ref, nope_ref, cosine_ref,
     sine_ref, query_grad_ref, expand_grad_ref, key_out_ref, key_grad_ref, latent_ref, scores_ref,
 ):
     rows = grad_ref.shape[0]
@@ -406,50 +631,58 @@
         query_grad_ref[:, h * width : (h + 1) * width] = jnp.concatenate(
             [nope, first * cosine + second * sine, second * cosine - first * sine], -1
         ).astype(BF)
-        expand_grad_ref[:, key_part] = t_dot(
-            latent, nope_ref[:, h * HEAD : (h + 1) * HEAD]
-        ).astype(BF)
-        expand_grad_ref[:, value_part] = t_dot(
+        key_grad = t_dot(latent, nope_ref[:, h * HEAD : (h + 1) * HEAD]).astype(BF)
+        value_grad = t_dot(
             mixed_ref[part, :], grad_ref[:, h * VHEAD : (h + 1) * VHEAD]
         ).astype(BF)
+        count = order_ref.shape[0]
+        height = RANK // count
+        for j in range(count):
+            target = pl.ds(pl.multiple_of(order_ref[j] * height, height), height)
+            source = slice(j * height, (j + 1) * height)
+            expand_grad_ref[target, key_part] = key_grad[source, :]
+            expand_grad_ref[target, value_part] = value_grad[source, :]
 
     @pl.when(pl.program_id(0) == pl.num_programs(0) - 1)
     def _():
         key_out_ref[...] = key_grad_ref[...].T.astype(BF)
 
 
-def attend_back(grad_out, expand, keys, weights, queries, mixed, nope, cosine, sine):
+def attend_back(grad_out, expand, keys, weights, queries, mixed, nope, cosine, sine, order):
     rows = grad_out.shape[0]
     slot = keys.shape[0]
-    whole = lambda *shape: pl.BlockSpec(shape, lambda i: (0,) * len(shape))
+    whole = lambda *shape: pl.BlockSpec(shape, lambda i, order: (0,) * len(shape))
     return pl.pallas_call(
         attend_back_kernel,
-        grid=(HEADS // 2,),
-        in_specs=[
-            pl.BlockSpec((rows, 2 * VHEAD), lambda i: (0, i)),
-            pl.BlockSpec((RANK, 4 * HEAD), lambda i: (0, i)),
+        grid_spec=pltpu.PrefetchScalarGridSpec(
+            num_scalar_prefetch=1,
+            grid=(HEADS // 2,),
+            in_specs=[
+            pl.BlockSpec((rows, 2 * VHEAD), lambda i, order: (0, i)),
+            pl.BlockSpec((RANK, 4 * HEAD), lambda i, order: (0, i)),
             whole(slot, RANK + ROPE),
-            pl.BlockSpec((2 * rows, slot), lambda i: (i, 0)),
-            pl.BlockSpec((2 * rows, RANK + ROPE), lambda i: (i, 0)),
-            pl.BlockSpec((2 * rows, RANK), lambda i: (i, 0)),
-            pl.BlockSpec((rows, 2 * HEAD), lambda i: (0, i)),
+            pl.BlockSpec((2 * rows, slot), lambda i, order: (i, 0)),
+            pl.BlockSpec((2 * rows, RANK + ROPE), lambda i, order: (i, 0)),
+            pl.BlockSpec((2 * rows, RANK), lambda i, order: (i, 0)),
+            pl.BlockSpec((rows, 2 * HEAD), lambda i, order: (0, i)),
             whole(rows, ROPE // 2),
             whole(rows, ROPE // 2),
         ],
         out_specs=[
-            pl.BlockSpec((rows, 2 * (HEAD + ROPE)), lambda i: (0, i)),
-            pl.BlockSpec((RANK, 4 * HEAD), lambda i: (0, i)),
+            pl.BlockSpec((rows, 2 * (HEAD + ROPE)), lambda i, order: (0, i)),
+            pl.BlockSpec((RANK, 4 * HEAD), lambda i, order: (0, i)),
             whole(slot, RANK + ROPE),
         ],
+        scratch_shapes=[
+            pltpu.VMEM((RANK + ROPE, slot), F32),
+            pltpu.VMEM((2 * rows, RANK), BF),
+            pltpu.VMEM((2 * rows, slot), BF),
+        ],
+        ),
         out_shape=[
             jax.ShapeDtypeStruct((rows, HEADS * (HEAD + ROPE)), BF),
             jax.ShapeDtypeStruct((RANK, 2 * HEADS * HEAD), BF),
             jax.ShapeDtypeStruct((slot, RANK + ROPE), BF),
-        ],
-        scratch_shapes=[
-            pltpu.VMEM((RANK + ROPE, slot), F32),
-            pltpu.VMEM((2 * rows, RANK), BF),
-            pltpu.VMEM((2 * rows, slot), BF),
         ],
         compiler_params=pltpu.CompilerParams(vmem_limit_bytes=48 << 20),
         cost_estimate=pl.CostEstimate(
@@ -457,7 +690,7 @@
             bytes_accessed=2 * HEADS * rows * slot,
             transcendentals=0,
         ),
-    )(grad_out, expand, keys, weights, queries, mixed, nope, cosine, sine)
+    )(order, grad_out, expand, keys, weights, queries, mixed, nope, cosine, sine)
 
 
 def expert_kernel(sources, here_ref, rows_ref, grads_ref, router_ref, *refs):
@@ -592,9 +825,6 @@
     capacity = max(2, 9 * local_rows * topk_count // (8 * experts_all))
     capacity = -(-capacity // 8) * 8
     here = lax.axis_index("expert")
-    bits = [1 << k for k in range(owners.bit_length() - 1)]
-    first_x = tuple(bits)
-    first_y = tuple(bits[1:2] + bits[:1] + bits[2:])
 
     query_blocks = row_blocks(query_weight)
     latent_blocks = row_blocks(latent_weight)
@@ -613,24 +843,6 @@
     gain_ffn = gains[:, cut : 2 * cut].reshape(-1)
     gain_latent = gains[:, 2 * cut :].reshape(-1)
     expand = whole_rows(expand_weight)
-    output_blocks = row_blocks(output_weight)
-    router = whole_rows(router_weight)
-    shared_out_blocks = row_blocks(shared_out)
-    shared_in_blocks = row_blocks(shared_in)
-    expert_in_rows = expert_in[0].transpose(1, 2, 0)
-    if shards == 2:
-        expert_weights = [
-            (expert_in_rows, expert_out[0]),
-            (swap(expert_in_rows), swap(expert_out[0])),
-        ]
-    else:
-        expert_weights = [
-            (
-                lax.all_gather(expert_in_rows, "shard", axis=1, tiled=True),
-                lax.all_gather(expert_out[0], "shard", axis=0, tiled=True),
-            )
-        ]
-
     here_index = here * local_rows + jnp.arange(local_rows, dtype=jnp.int32)
     query_segment, query_position, query_valid = layout(lengths[0], here_index)
     cosine, sine_table = rope_tables(query_position)
@@ -659,7 +871,6 @@
             tiled=True,
         ).reshape(owners * capacity, model_width)
 
-    received_grads = exchange(dot(spread, grad_out_low).astype(BF))
 
     inputs = tokens[0].astype(F32)
     inverse_attn = rms_scale(inputs)
@@ -672,21 +883,37 @@
     latent_in = (normed_latent * gain_latent).astype(BF)
     key_rope = rotate(latent_raw[:, RANK:], cosine, sine_table).astype(BF)
     own_keys = jnp.concatenate([latent_in, key_rope], -1)
-    part = local_rows // 2
-    collect_bits = (tuple(reversed(first_x)), tuple(reversed(first_y)))
-    keys, key_index = [], []
-    for k in range(2):
-        gathered, places = collect(own_keys[k * part : (k + 1) * part], collect_bits[k])
-        keys.append(gathered)
-        key_index.append(
+    expert_in_rows, expert_out_rows = expert_in[0].transpose(1, 2, 0), expert_out[0]
+    (
+        own_keys, output_weight, router_weight, shared_in, shared_out, expert_in_rows, expert_out_rows,
+    ) = together(
+        own_keys, output_weight, router_weight, shared_in, shared_out, expert_in_rows, expert_out_rows,
+    )
+    output_blocks = row_blocks(output_weight)
+    router = whole_rows(router_weight)
+    shared_out_blocks = row_blocks(shared_out)
+    shared_in_blocks = row_blocks(shared_in)
+    if shards == 2:
+        expert_weights = [
+            (expert_in_rows, expert_out_rows),
+            (swap(expert_in_rows), swap(expert_out_rows)),
+        ]
+    else:
+        expert_weights = [
             (
-                (here ^ jnp.array(places, jnp.int32))[:, None] * local_rows
-                + k * part
-                + jnp.arange(part, dtype=jnp.int32)[None, :]
-            ).reshape(-1)
-        )
-    keys = jnp.concatenate(keys, 0)
-    key_index = jnp.concatenate(key_index)
+                lax.all_gather(expert_in_rows, "shard", axis=1, tiled=True),
+                lax.all_gather(expert_out_rows, "shard", axis=0, tiled=True),
+            )
+        ]
+
+    sent_grads = dot(spread, grad_out_low).astype(BF)
+    keys, sent_grads = together(gather_slot(own_keys), sent_grads)
+    received_grads = exchange(sent_grads)
+    keys = keys.reshape(-1, RANK + ROPE)
+    key_index = (
+        (here ^ jnp.arange(owners, dtype=jnp.int32))[:, None] * local_rows
+        + jnp.arange(local_rows, dtype=jnp.int32)[None, :]
+    ).reshape(-1)
 
     query_raw = times(attn_in, query_blocks)
     key_segment = layout(lengths[0], key_index)[0]
@@ -721,67 +948,70 @@
     grad_ffn_in = times_back(
         jnp.concatenate([grad_shared_gate, grad_shared_up], -1), shared_in_blocks
     )
-    (
-        shared_hidden, grad_shared_gate, grad_shared_up, received, shared_result, grad_ffn_in,
-        shared_in, late_grad_out,
-    ) = together(
-        shared_hidden, grad_shared_gate, grad_shared_up, received, shared_result, grad_ffn_in,
-        ffn_in, grad_out_low,
-    )
-
-    shared_orders = ((4, 1, 2, 8), (4, 2, 1, 8), (4, 1, 2, 8))
-    shared_lefts = [
-        cross_left(left, order[0])
-        for left, order in zip((shared_hidden, shared_in, shared_in), shared_orders)
-    ]
-    shared_rights = [
-        (right, cross(right, order[0]))
-        for right, order in zip((late_grad_out, grad_shared_gate, grad_shared_up), shared_orders)
-    ]
+    out_message = jnp.concatenate([shared_hidden, grad_out_low], 1)
+    in_message = jnp.concatenate([ffn_in, grad_shared_gate, grad_shared_up], 1)
+    received, shared_result, grad_ffn_in, out_message, in_message = together(
+        received, shared_result, grad_ffn_in, out_message, in_message
+    )
+
+    early_message = jnp.concatenate([attn_in, mixed_heads], 1)
+    received, early_message = together(received, early_message)
+    arrived = cross(out_message, 1), cross(in_message, 4), cross(early_message, 2)
     expert_results = expert_pass(
         here[None], received, received_grads, router.T, expert_weights
     )
-    expert_results, shared_lefts, shared_rights = together(
-        expert_results, shared_lefts, shared_rights
-    )
-    shared_groups = [
-        (pair_left(left), pair_right(right)) for left, right in zip(shared_lefts, shared_rights)
+    row_grads, hidden, hidden_grads, row_gate, row_grad_logits = expert_results
+
+    returned_grads = exchange(row_grads)
+    units = expert_weights[0][1].shape[0]
+    row_gate = row_gate.reshape(-1, 1)
+    weighted_grads = (row_gate * received_grads.astype(F32)).astype(BF)
+
+    def expert_grads(j):
+        return (
+            dot(hidden_grads[j].reshape(2 * units, -1), received).reshape(2, units, -1),
+            dot(hidden[j * units : (j + 1) * units], weighted_grads),
+        )
+
+    other_parts = [part.astype(BF) for part in expert_grads(len(expert_weights) - 1)]
+    other_parts, arrived = together(other_parts, arrived)
+    out_messages = group_messages(out_message, arrived[0])
+    in_messages = group_messages(in_message, arrived[1])
+    early_messages = group_messages(early_message, arrived[2])
+    cut = 4096
+    shared_halves = [
+        product_halves(messages, left_part, messages, right_part, order)[:2]
+        for messages, left_part, right_part, order in (
+            (out_messages, (0, FF_S), (FF_S, model_width), (2, 8, 4)),
+            (in_messages, (0, model_width), (model_width, cut), (1, 2, 8)),
+            (in_messages, (0, model_width), (model_width + cut, 2 * FF_S - cut), (2, 1, 8)),
+        )
     ]
-    row_grads, hidden, hidden_grads, row_gate, row_grad_logits = expert_results
-
-    returned_grads = exchange(row_grads)
-    halves = [
-        product_halves(group, order[1:]) for group, order in zip(shared_groups, shared_orders)
+    hidden, hidden_grads, shared_halves, early_messages = together(
+        hidden, hidden_grads, shared_halves, early_messages
+    )
+    shared_sums = [
+        [kept, cross(sent, bit)] for (kept, sent), bit in zip(shared_halves, (2, 1, 2))
     ]
-    shared_sums = [[kept, cross(sent, order[1])] for (kept, sent), order in zip(halves, shared_orders)]
-    row_gate = row_gate.reshape(-1, 1)
     row_out = 0.0
-    units = expert_weights[0][1].shape[0]
     for j, (_, weight) in enumerate(expert_weights):
         row_out = row_out + t_dot(hidden[j * units : (j + 1) * units], weight)
     row_out = (row_gate * row_out).astype(BF)
-    weighted_grads = (row_gate * received_grads.astype(F32)).astype(BF)
-    grad_expert_parts = [
-        (
-            dot(hidden_grads[j].reshape(2 * units, -1), received).reshape(2, units, -1),
-            dot(hidden[j * units : (j + 1) * units], weighted_grads),
+    if shards == 2:
+        hidden, hidden_grads, other_parts = together(
+            hidden, hidden_grads, [swap(part) for part in other_parts]
         )
-        for j in range(len(expert_weights))
-    ]
-    if shards == 2:
         grad_expert_in, grad_expert_out = [
-            own + swap(other.astype(BF)).astype(F32) for own, other in zip(*grad_expert_parts)
+            own + other.astype(F32) for own, other in zip(expert_grads(0), other_parts)
         ]
     else:
         grad_expert_in, grad_expert_out = [
-            lax.psum_scatter(
-                part.astype(BF), "shard", scatter_dimension=part.ndim - 2, tiled=True
-            ).astype(F32)
-            for part in grad_expert_parts[0]
+            lax.psum_scatter(part, "shard", scatter_dimension=part.ndim - 2, tiled=True).astype(F32)
+            for part in other_parts
         ]
     grad_router = dot(row_grad_logits, received)
-    returned_grads, row_out, grad_expert_in, grad_expert_out, grad_router, shared_sums = together(
-        returned_grads, row_out, grad_expert_in, grad_expert_out, grad_router, shared_sums
+    returned_grads, row_out, grad_expert_in, grad_expert_out, grad_router = together(
+        returned_grads, row_out, grad_expert_in, grad_expert_out, grad_router
     )
     grad_expert_in = grad_expert_in.transpose(2, 0, 1)[None]
     grad_expert_out = grad_expert_out[None]
@@ -791,14 +1021,17 @@
     grad_hidden_state = grad_out + norm_back(grad_ffn_in * gain_ffn, normed_ffn, inverse_ffn)
 
     grad_attn_out = grad_hidden_state.astype(BF)
-    late_attn_in, late_heads, grad_attn_out = together(attn_in, mixed_heads, grad_attn_out)
     grad_mixed = times_back(grad_attn_out, output_blocks).astype(BF)
-    left_x, left_y = [group_left(late_attn_in, order[0]) for order in (first_x, first_y)]
-    output_group = product_group(late_heads, grad_attn_out, first_y[0])
-    grad_mixed, shared_sums = together(grad_mixed, shared_sums)
-    shared_sums = [
-        fold_step(pieces, order[2]) for pieces, order in zip(shared_sums, shared_orders)
-    ]
+    grad_mixed, grad_attn_out = together(grad_mixed, grad_attn_out)
+    out_arrived = cross(grad_attn_out, 2)
+    expand_order = (2, 1, 4, 8)
+    if shards == 2:
+        differs = here ^ jnp.arange(owners, dtype=jnp.int32)
+        place = sum((differs // bit % 2) << (3 - k) for k, bit in enumerate(expand_order))
+        other = lax.axis_index("shard") ^ jnp.arange(2, dtype=jnp.int32)
+        block_order = (other[None, :] * owners + place[:, None]).reshape(-1).astype(jnp.int32)
+    else:
+        block_order = jnp.zeros((1,), jnp.int32)
     attention_grads = attend_back(
         grad_mixed,
         expand,
@@ -809,50 +1042,47 @@
         query_nope,
         cosine,
         sine_table,
-    )
-    (grad_query_raw, grad_expand, grad_keys), shared_sums = together(attention_grads, shared_sums)
-    shared_sums = [
-        fold_step(pieces, order[3]) for pieces, order in zip(shared_sums, shared_orders)
-    ]
-    slot_half = SLOT // 2
-    grad_own_keys = jnp.concatenate(
-        [
-            fold(
-                [grad_keys[k * slot_half : (k + 1) * slot_half]],
-                tuple(reversed(collect_bits[k])),
-            )
-            for k in range(2)
-        ],
-        0,
-    )
-    query_half = grad_query_raw.shape[1] // 2
-    grad_query = jnp.concatenate(
-        [
-            product_sum(
-                (left_x, group_right(grad_query_raw[:, :query_half], first_x[0])), first_x
-            ),
-            product_sum(
-                (left_y, group_right(grad_query_raw[:, query_half:], first_y[0])), first_y
-            ),
-        ],
-        -1,
-    )
-    expand_sums = fold_step(pair_partial(grad_expand, first_x), first_x[0])
-    grad_own_keys, expand_sums = together(grad_own_keys, expand_sums)
-    grad_expand = fold(expand_sums, first_x[1:])
-    grad_output = product_sum(output_group, first_y)
+        block_order,
+    )
+    attention_grads, shared_sums, out_arrived = together(
+        attention_grads, shared_sums, out_arrived
+    )
+    grad_query_raw, grad_expand, grad_keys = attention_grads
+
+    query_arrived = cross(grad_query_raw, 2)
+    own_query = grad_query_raw
+    if shards == 2:
+        half_rank = RANK // 2
+        expand_pair = [grad_expand[:half_rank], swap(grad_expand[half_rank:])]
+    else:
+        expand_pair = pair_partial(grad_expand, expand_order)
+    grad_own_keys, returned, query_arrived, grad_query_raw, expand_pair = together(
+        scatter_slot(grad_keys.reshape(owners, local_rows, -1)),
+        returned,
+        query_arrived,
+        grad_query_raw,
+        expand_pair,
+    )
     grad_latent_in = grad_own_keys[:, :RANK]
     grad_gain_latent = jnp.sum(grad_latent_in * normed_latent, 0)
     grad_latent = norm_back(grad_latent_in * gain_latent, normed_latent, inverse_latent)
     grad_latent_raw = jnp.concatenate(
         [grad_latent, rotate_back(grad_own_keys[:, RANK:], cosine, sine_table)], -1
     ).astype(BF)
-    grad_latent_late, shared_sums = together(grad_latent_raw, shared_sums)
-    grad_shared_out, *grad_shared_in = [fold_end(pieces) for pieces in shared_sums]
-    grad_shared_in = jnp.concatenate(grad_shared_in, -1)
-    grad_latent_weight = product_sum(
-        (left_y, group_right(grad_latent_late, first_y[0])), first_y
-    )
+    latent_message = jnp.pad(grad_latent_raw, ((0, 0), (0, -grad_latent_raw.shape[1] % 128)))
+    latent_messages = group_messages(latent_message, cross(latent_message, 2))
+    query_messages = group_messages(own_query, query_arrived)
+    out_messages = group_messages(grad_attn_out, out_arrived)
+    in_part, heads_part = (0, model_width), (model_width, HEADS * VHEAD)
+    whole_part = lambda array: (0, array.shape[1])
+    *query_halves, picked = product_halves(
+        early_messages, in_part, query_messages, whole_part(grad_query_raw), (1, 4, 8)
+    )
+    output_halves = product_halves(
+        early_messages, heads_part, out_messages, whole_part(grad_attn_out), (4, 1, 8)
+    )[:2]
+    latent_product = dot(picked, jnp.concatenate(latent_messages, 0)).astype(BF)
+    latent_halves = jnp.split(latent_product, 2, 0)
     grad_attn_in = times_back(grad_latent_raw, latent_blocks) + times_back(
         grad_query_raw, query_blocks
     )
@@ -867,19 +1097,37 @@
         ],
         1,
     )
-    small, returned = together(small, returned)
-    small = lax.all_to_all(small, ("expert", "shard"), split_axis=0, concat_axis=0, tiled=True)
-    small = jnp.sum(small, 0)
+    cuts = [rows * experts_all, rows * (experts_all + 1), rows * (experts_all + 2)]
+    small = jnp.pad(small, ((0, 0), (0, -small.shape[1] % 2048))).reshape(devices * 16, -1)
+    small_pair = pair_partial(small.astype(BF), expand_order)
+    sums = reduce_all(
+        [
+            ((1, 4, 8), [latent_halves[0]], latent_halves[1]),
+            ((8, 4), shared_sums[0], None),
+            (expand_order, expand_pair, None),
+            ((1, 4, 8), [query_halves[0]], query_halves[1]),
+            ((2, 8), shared_sums[1], None),
+            ((4, 1, 8), [output_halves[0]], output_halves[1]),
+            ((1, 8), shared_sums[2], None),
+            (expand_order, small_pair, None),
+        ],
+        REDUCE_STEPS,
+    )
+    grad_latent_weight = sums[0][:, : RANK + ROPE]
+    grad_shared_out = sums[1][: FF_S // devices]
+    grad_expand, grad_query = sums[2:4]
+    grad_shared_in = jnp.concatenate([sums[4], sums[6]], 1)
+    grad_output = sums[5]
+    small = sums[7].reshape(-1)
     routed = t_dot(spread, returned)
     block_result = hidden_state + shared_result + routed
-    cuts = [rows * experts_all, rows * (experts_all + 1), rows * (experts_all + 2)]
     return (
         block_result.astype(BF)[None],
         tokens_grad.astype(BF)[None],
         small[cuts[0] : cuts[1]],
         grad_query,
         grad_latent_weight,
-        small[cuts[2] :],
+        small[cuts[2] : cuts[2] + RANK // devices],
         grad_expand,
         grad_output,
         small[cuts[1] : cuts[2]],

time: 918 us -> 705 us (0.77)
  waiting for transfers between devices: 328 us -> 49.3 us
  Pallas kernels: 146 us -> 369 us
  starting transfers between devices: 146 us -> 73.3 us
  local copies, waits for them, and re-layouts: 77.4 us -> 31.8 us
  other arithmetic: 63.1 us -> 30.7 us
    ppermute x53 -> x9, waiting for transfers between devices: 283 us -> 0.02 us  [cross(): return lax.ppermute(values, 'expert', [(i, i ^ bit) for i in range(count)])]
    pallas_call x8 -> x9, Pallas kernels: 60.3 us -> 296 us  [the longest x1 123 us: reduce_all(): pl.pallas_call(functools.partial(reduce_kernel, plans, steps), in_specs=[...]
    ppermute x53 -> x9, starting transfers between devices: 103 us -> 27.2 us  [cross(): return lax.ppermute(values, 'expert', [(i, i ^ bit) for i in range(count)])]
    convert_element_type x22 -> x1, other arithmetic: 19.2 us -> 1.79 us  [per_device(): (grad_shared_hidden * shared_up * shared_slope).astype(BF)]
    slice x36 -> x3, local copies, waits for them, and re-layouts: 21.4 us -> 7.37 us  [the longest x1 4.11 us: per_device(): expand_pair = [grad_expand[:half_rank], swap(grad_expand[half_rank:])]]
    pallas_call x1, Pallas kernels: 57.8 us -> 46.6 us  [expert_pass(): pl.pallas_call(functools.partial(expert_kernel, sources), grid_spec=pltpu...]
    unnamed x272 -> x163, local copies, waits for them, and re-layouts: 24.8 us -> 17 us
    dot_general x18 -> x19, matrix products: 79.7 us -> 81.5 us  [dot(): return jnp.dot(left, right, preferred_element_type=F32)]
  transfers between devices with their start and end apart: 84 -> 39, of which waited for: 33 -> 6; matrix products, arithmetic and copies ran while one was open for 26% -> 24% of each run, Pallas kernels for 16% -> 35%
where the time goes in v5:
time: 705 us; the launch traced here: 699 us
  Pallas kernels  369 us (52%)
  matrix products  141 us (20%)
  starting transfers between devices  73.3 us (10%)
  waiting for transfers between devices  49.3 us (7%)
  local copies, waits for them, and re-layouts  31.8 us (5%)
  other arithmetic  30.7 us (4%)
    pallas_call x1, Pallas kernels, reduce_all(): pl.pallas_call(functools.partial(reduce_kernel, plans, steps), in_specs=[...  123 us
    dot_general x19, matrix products, dot(): return jnp.dot(left, right, preferred_element_type=F32)  81.5 us
    pallas_call x1, Pallas kernels, scatter_slot(): pl.pallas_call(scatter_kernel, in_specs=[pl.BlockSpec(memory_space=pltpu....  58.1 us
    pallas_call x1, Pallas kernels, expert_pass(): pl.pallas_call(functools.partial(expert_kernel, sources), grid_spec=pltpu...  46.6 us
    dot_general x10, matrix products, dot_t(): lax.dot_general(left, right, (((1,), (1,)), ((), ())), preferred_element_...  42.3 us
    pallas_call x5, Pallas kernels, product_halves(): pl.pallas_call(functools.partial(product_kernel, rows, len(lefts)), grid_...  42.1 us
    pallas_call x1, Pallas kernels, attend_back(): pl.pallas_call(attend_back_kernel, grid_spec=pltpu.PrefetchScalarGridSpec...  39.9 us
    all_to_all x4, starting transfers between devices, exchange(): lax.all_to_all(rows.reshape(owners, capacity, model_width), 'expert', spl...  39.9 us
  transfers between devices with their start and end apart: 39, of which 6 were waited for; matrix products, arithmetic and copies ran while one was open for 24% of the time, Pallas kernels for 35%

profile of v5, /device:TPU:0, one launch (start us, length us, event | category | flops | bytes accessed | tf_op | source)
XLA Modules:
  0.0 699.3 jit_solution(8546898546204632852)
XLA Ops:
  8.1 4.1 convolution_convert_fusion.2
  13.1 1.8 convolution_add_fusion.6
  15.8 31.9 %shard_map.308 = bf16[16,128,576]{2,1,0:T(8,128)(2,1)S(1)} custom-call(bf16[128,576]{1,0:T(8,128)(2,1)S(1)} %pad_maximum_fusion.7.own_ref), custom_call_target="tpu_custom_call" | custom-call | flops 49999998976 | bytes 4718592 | tf_op jit(solution)/shard_map/pallas_call | solution.py:330
  47.7 1.6 copy-done.1
  49.3 5.1 all-to-all-start
  55.1 3.3 collective-permute-done.5
  62.6 3.9 fusion.66
  67.2 4.9 maximum_select_fusion.expand_ref
  72.1 3.9 convolution_add_fusion.1.raw_ref
  76.1 27.0 %shard_map.309 = (bf16[128,2048]{1,0:T(8,128)(2,1)S(1)}, bf16[2048,576]{1,0:T(8,128)(2,1)S(1)}, bf16[2048,2048]{1,0:T(8,128)(2,1)}, bf16[2048,512]{1,0:T(8,128)(2,1)S(1)}, bf16[128,2048]{1,0:T(8,128)(2,1)S(1)}) custom-call(f32[128,3072]{1,0:T(8,128)S(1)} %convolution_add_fusion.1.raw_ref, f32[128,32]{1,0:T(8,128)S(1)} %get-tuple-element.317.cosine_ref, ...), custom_call_target="tpu_custom_call" | custom-call | flops 9126805504 | bytes 8388608 | tf_op jit(solution)/shard_map/pallas_call | solution.py:563
  103.1 1.5 copy-done.4
  105.5 18.5 %all-to-all-done = bf16[16,56,2048]{2,1,0:T(8,128)(2,1)} async-done(((bf16[16,56,2048]{2,1,0:T(8,128)(2,1)}), bf16[16,56,2048]{2,1,0:T(8,128)(2,1)}, u32[]{:S(2)}, u32[]{:S(2)}) %all-to-all-start) | async-done | bytes 3670048 | tf_op jit(solution)/shard_map/all_to_all | solution.py:866
  124.0 3.1 fusion.59
  129.6 2.9 convolution_convert_fusion.1
  132.6 17.4 %all-to-all-start.1 = ((bf16[16,56,2048]{2,1,0:T(8,128)(2,1)}), bf16[16,56,2048]{2,1,0:T(8,128)(2,1)}, u32[]{:S(2)}, u32[]{:S(2)}) async-start(bf16[16,56,2048]{2,1,0:T(8,128)(2,1)} %bitcast.156), calls=%async_computation.1 | async-start | bytes 7340032 | tf_op jit(solution)/shard_map/all_to_all | solution.py:866
  150.0 5.7 fusion.124
  155.7 5.5 fusion.125
  161.2 6.1 fusion.56
  167.3 6.3 convolution_add_fusion
  173.6 1.8 multiply_convert_fusion.5
  175.5 4.6 fusion.39
  180.0 8.2 %fusion.38 = f32[128,1024]{1,0:T(8,128)S(1)} fusion(bf16[1024,5632]{1,0:T(8,128)(2,1)} %collective-permute-done.6, bf16[128,2816]{1,0:T(8,128)(2,1)S(1)} %get-tuple-element.302, bf16[128,2816]{1,0:T(8,128)(2,1)S(1)} %get-tuple-element.301), kind=kOutput, calls=%fused_computation.75 | convolution fusion | flops 1479278592 | bytes 13500416 | tf_op jit(solution)/shard_map/dot_general | solution.py:76
  189.4 3.7 fusion.53
  193.1 2.0 convolution_add_fusion.4
  198.8 20.5 %all-to-all-done.1 = bf16[16,56,2048]{2,1,0:T(8,128)(2,1)} async-done(((bf16[16,56,2048]{2,1,0:T(8,128)(2,1)}), bf16[16,56,2048]{2,1,0:T(8,128)(2,1)}, u32[]{:S(2)}, u32[]{:S(2)}) %all-to-all-start.1) | async-done | bytes 3670048 | tf_op jit(solution)/shard_map/all_to_all | solution.py:866
  219.3 5.4 collective-permute-start.12
  224.7 9.3 %collective-permute-start.11 = (bf16[128,7680]{1,0:T(8,128)(2,1)}, bf16[128,7680]{1,0:T(8,128)(2,1)}, u32[]{:S(2)}, u32[]{:S(2)}) collective-permute-start(bf16[128,7680]{1,0:T(8,128)(2,1)} %pad_maximum_fusion.refs_0_.refs_4_), channel_id=1, source_target_pairs={{0,8},{2,10},{4,12},{6,14},{8,0},{10,2},{12,4},{14,6},{16,24},{18,... | collective-permute-start | bytes 5898248 | tf_op jit(solution)/shard_map/ppermute | solution.py:85
  234.0 1.5 collective-permute-start.10
  235.5 46.6 %shard_map.310 = (bf16[896,2048]{1,0:T(8,128)(2,1)}, bf16[1408,896]{1,0:T(8,128)(2,1)}, bf16[2,2,704,896]{3,2,1,0:T(8,128)(2,1)}, f32[1,896]{1,0:T(1,128)}, bf16[16,896]{1,0:T(8,128)(2,1)}) custom-call(s32[1]{0:T(128)} %bitcast.19.here_ref, bf16[896,2048]{1,0:T(8,128)(2,1)} %bitcast.17.rows_ref, bf16[896,2048]{1,0:T(8,128)(2,1)} %bitcast.13.grads_ref, ...), custom_call_target="tpu_custom_call" | custom-call | flops 25836912640 | bytes 28311552 | tf_op jit(solution)/shard_map/pallas_call | solution.py:764
  282.8 7.4 %convolution_convert_fusion.3 = bf16[704,2048]{1,0:T(8,128)(2,1)} fusion(bf16[896,2048]{1,0:T(8,128)(2,1)} %bitcast.13.grads_ref, f32[896]{0:T(1024)S(1)} %reduce, bf16[1408,896]{1,0:T(8,128)(2,1)} %get-tuple-element.180), kind=kOutput, calls=%fused_computation.13 | convolution fusion | flops 2590638080 | bytes 7818752 | tf_op jit(solution)/shard_map/dot_general | solution.py:72
  290.2 10.0 %convolution_convert_fusion = bf16[2,704,2048]{2,1,0:T(8,128)(2,1)} fusion(bf16[896,2048]{1,0:T(8,128)(2,1)} %bitcast.17.rows_ref, bf16[2,2,704,896]{3,2,1,0:T(8,128)(2,1)S(1)} %copy-done.67), kind=kOutput, calls=%fused_computation.5 | convolution fusion | flops 5170266112 | bytes 11960320 | tf_op jit(solution)/shard_map/dot_general | solution.py:72
  301.3 4.7 all-to-all-start.2
  307.6 5.6 collective-permute-done.13.refs_2_.refs_6_
  317.7 3.3 fusion.126
  321.0 10.2 %shard_map.311 = (bf16[384,2048]{1,0:T(8,128)(2,1)}, bf16[384,2048]{1,0:T(8,128)(2,1)}, f32[768,512]{1,0:T(8,128)}) custom-call(s32[8]{0:T(128)} %multiply_add_fusion.4.order_ref, bf16[128,4864]{1,0:T(8,128)(2,1)} %pad_maximum_fusion.3.refs_0_.refs_4_, bf16[128,4864]{1,0:T(8,128)(2,1)} %copy-done.24, bf16[128,4864]{1,0:T(8,128)(2,1)} %copy-done.25, ...), custom_call_target="tpu_custom_call" | custom-call | flops 1610612736 | bytes 8126464 | tf_op jit(solution)/shard_map/pallas_call | solution.py:208
  331.1 6.2 shard_map.313
  337.4 10.2 %shard_map.312 = (bf16[256,4096]{1,0:T(8,128)(2,1)}, bf16[256,4096]{1,0:T(8,128)(2,1)}, bf16[512,512]{1,0:T(8,128)(2,1)}) custom-call(s32[8]{0:T(128)} %get-tuple-element.326.order_ref, bf16[128,7680]{1,0:T(8,128)(2,1)} %pad_maximum_fusion.refs_0_.refs_4_, bf16[128,7680]{1,0:T(8,128)(2,1)} %collective-permute-done.11.refs_1_.refs_5_, ...), custom_call_target="tpu_custom_call" | custom-call | flops 2147483648 | bytes 10485760 | tf_op jit(solution)/shard_map/pallas_call | solution.py:208
  348.3 1.8 collective-permute-start.21
  350.3 5.0 fusion.20
  355.4 4.9 multiply_convert_fusion
  360.3 7.7 %convert_add_fusion.1 = f32[704,2048]{1,0:T(8,128)} fusion(bf16[704,2048]{1,0:T(8,128)(2,1)} %collective-permute-done.20, bf16[896,2048]{1,0:T(8,128)(2,1)} %bitcast.13.grads_ref, f32[896]{0:T(1024)S(1)} %reduce, bf16[1408,896]{1,0:T(8,128)(2,1)S(1)} %copy-done.66), kind=kOutput, calls=%fused_computation.4 | convolution fusion | flops 2592079872 | bytes 13586432 | tf_op jit(solution)/shard_map/dot_general | solution.py:72
  367.9 12.0 %convert_add_fusion = f32[2,704,2048]{2,1,0:T(8,128)} fusion(bf16[2,704,2048]{2,1,0:T(8,128)(2,1)} %collective-permute-done.19, bf16[896,2048]{1,0:T(8,128)(2,1)} %bitcast.17.rows_ref, bf16[2,2,704,896]{3,2,1,0:T(8,128)(2,1)S(1)} %bitcast.190), kind=kOutput, calls=%fused_computation | convolution fusion | flops 5173149696 | bytes 23494656 | tf_op jit(solution)/shard_map/dot_general | solution.py:72
  380.0 3.7 multiply_reduce_fusion
  383.8 1.5 fusion.118
  386.5 2.6 fusion.127
  389.0 3.9 fusion.128
  393.1 2.4 collective-permute-start.24
  395.4 12.7 %all-to-all-start.3 = ((bf16[16,56,2048]{2,1,0:T(8,128)(2,1)}), bf16[16,56,2048]{2,1,0:T(8,128)(2,1)}, u32[]{:S(2)}, u32[]{:S(2)}) async-start(bf16[16,56,2048]{2,1,0:T(8,128)(2,1)} %bitcast.161), calls=%async_computation.3 | async-start | bytes 7340032 | tf_op jit(solution)/shard_map/all_to_all | solution.py:866
  409.2 39.9 %shard_map.314 = (bf16[128,3072]{1,0:T(8,128)(2,1)S(1)}, bf16[512,4096]{1,0:T(8,128)(2,1)}, bf16[2048,576]{1,0:T(8,128)(2,1)}) custom-call(s32[32]{0:T(128)S(1)} %add.354.order_ref, bf16[128,2048]{1,0:T(8,128)(2,1)S(1)} %fusion.36.grad_ref, bf16[512,4096]{1,0:T(8,128)(2,1)} %maximum_select_fusion.expand_ref, bf16[2048,576]{1,0:T(8,128)(2,1)} %bitcast.151, ...), custom_call_target="tpu_custom_call" | custom-call | flops 22548578304 | bytes 8388608 | tf_op jit(solution)/shard_map/pallas_call | solution.py:655
  451.3 2.1 collective-permute-start.25
  453.3 4.1 fusion.120
  458.0 58.1 %shard_map.315 = f32[128,576]{1,0:T(8,128)S(1)} custom-call(bf16[16,128,576]{2,1,0:T(8,128)(2,1)S(1)} %bitcast.153), custom_call_target="tpu_custom_call" | custom-call | flops 49999998976 | bytes 4718592 | tf_op jit(solution)/shard_map/pallas_call | solution.py:417
  517.0 7.0 %shard_map.317 = (bf16[256,2048]{1,0:T(8,128)(2,1)}, bf16[256,2048]{1,0:T(8,128)(2,1)}, bf16[512,512]{1,0:T(8,128)(2,1)}) custom-call(s32[8]{0:T(128)} %multiply_add_fusion.order_ref, bf16[128,4096]{1,0:T(8,128)(2,1)} %pad_maximum_fusion.4.refs_0_, bf16[128,4096]{1,0:T(8,128)(2,1)} %collective-permute-done.12.refs_1_, ...), custom_call_target="tpu_custom_call" | custom-call | flops 1073741824 | bytes 6291456 | tf_op jit(solution)/shard_map/pallas_call | solution.py:208
  526.1 3.9 collective-permute-start.29
  530.0 5.0 fusion.131
  535.0 1.6 fusion.130
  536.7 5.0 fusion.132
  544.1 2.7 fusion.47
  546.8 3.9 fusion.13
  552.8 8.4 %shard_map.316 = (bf16[256,3072]{1,0:T(8,128)(2,1)}, bf16[256,3072]{1,0:T(8,128)(2,1)}, bf16[512,512]{1,0:T(8,128)(2,1)}) custom-call(s32[8]{0:T(128)} %multiply_add_fusion.1.order_ref, bf16[128,4096]{1,0:T(8,128)(2,1)} %pad_maximum_fusion.4.refs_0_, bf16[128,4096]{1,0:T(8,128)(2,1)} %collective-permute-done.12.refs_1_, ...), custom_call_target="tpu_custom_call" | custom-call | flops 1610612736 | bytes 8388608 | tf_op jit(solution)/shard_map/pallas_call | solution.py:208
  561.3 1.6 convolution_convert_fusion.4
  563.8 123.5 %shard_map.318 = (f32[64,640]{1,0:T(8,128)}, f32[96,2048]{1,0:T(8,128)}, f32[16,4096]{1,0:T(8,128)}, f32[64,3072]{1,0:T(8,128)}, f32[64,4096]{1,0:T(8,128)}, /*i...) custom-call(bf16[256,640]{1,0:T(8,128)(2,1)} %get-tuple-element.307.refs_0_, ...), custom_call_target="tpu_custom_call" | custom-call | flops 99999997952 | bytes 38141952 | tf_op jit(solution)/shard_map/pallas_call | solution.py:503
  690.6 2.1 slice.118
  693.4 2.6 pad_maximum_fusion.2
  (300 shorter events, 50.2 us)
Async XLA Ops:
  0.6 11.6 %copy-start.12 = (bf16[1,128,2048]{2,1,0:T(8,128)(2,1)S(1)}, bf16[1,128,2048]{2,1,0:T(8,128)(2,1)}, u32[]{:S(2)}) copy-start(bf16[1,128,2048]{2,1,0:T(8,128)(2,1)} %param.21) | copy-start | bytes 1572868
  1.4 10.7 %collective-permute-start = (bf16[1,2304]{1,0:T(2,128)(2,1)S(1)}, bf16[1,2304]{1,0:T(2,128)(2,1)S(1)}, u32[]{:S(2)}, u32[]{:S(2)}) collective-permute-start(bf16[1,2304]{1,0:T(2,128)(2,1)S(1)} %broadcast_in_dim.24), channel_id=1, source_target_pairs={{0,1},{1,0},{2,3},{3,2},{4,5},{5,4},{6,7},{7,6},{8,9},{9,8},{10,11... | collective-permute-start | bytes 13832 | tf_op jit(solution)/shard_map/ppermute | solution.py:89
  2.0 11.1 %collective-permute-start.3 = (bf16[1024,576]{0,1:T(8,128)(2,1)}, bf16[1024,576]{0,1:T(8,128)(2,1)}, u32[]{:S(2)}, u32[]{:S(2)}) collective-permute-start(bf16[1024,576]{0,1:T(8,128)(2,1)} %param.26), channel_id=1, source_target_pairs={{0,1},{1,0},{2,3},{3,2},{4,5},{5,4},{6,7},{7,6},{8,9},{9,8},{10,11... | collective-permute-start | bytes 3538952 | tf_op jit(solution)/shard_map/ppermute | solution.py:89
  2.0 59.2 %collective-permute-start.1 = (bf16[1024,3072]{1,0:T(8,128)(2,1)}, bf16[1024,3072]{1,0:T(8,128)(2,1)}, u32[]{:S(2)}, u32[]{:S(2)}) collective-permute-start(bf16[1024,3072]{1,0:T(8,128)(2,1)} %param.25), channel_id=1, source_target_pairs={{0,1},{1,0},{2,3},{3,2},{4,5},{5,4},{6,7},{7,6},{8,9},{9,8},{10,11... | collective-permute-start | bytes 18874376 | tf_op jit(solution)/shard_map/ppermute | solution.py:89
  5.7 9.4 %copy-start.54 = (f32[128]{0:T(128)}, f32[128]{0:T(128)S(1)}, u32[]{:S(2)}) copy-start(f32[128]{0:T(128)S(1)} %fusion.113) | copy-start | bytes 1540
  5.8 55.9 %copy-start.52 = (f32[128]{0:T(128)}, f32[128]{0:T(128)S(1)}, u32[]{:S(2)}) copy-start(f32[128]{0:T(128)S(1)} %compare_convert_fusion) | copy-start | bytes 1540
  12.5 59.6 %copy-start.17 = (bf16[128,2048]{1,0:T(8,128)(2,1)}, bf16[128,2048]{1,0:T(8,128)(2,1)S(1)}, u32[]{:S(2)}) copy-start(bf16[128,2048]{1,0:T(8,128)(2,1)S(1)} %fusion.28) | copy-start | bytes 1572868
  14.9 32.8 %copy-start.21 = (f32[128,576]{1,0:T(8,128)}, f32[128,576]{1,0:T(8,128)S(1)}, u32[]{:S(2)}) copy-start(f32[128,576]{1,0:T(8,128)S(1)} %convolution_add_fusion.6) | copy-start | bytes 884740
  15.0 32.6 %copy-start.56 = (f32[128]{0:T(128)}, f32[128]{0:T(128)S(1)}, u32[]{:S(2)}) copy-start(f32[128]{0:T(128)S(1)} %add_rsqrt_fusion.1) | copy-start | bytes 1540
  15.6 108.4 %collective-permute-start.6 = (bf16[1024,5632]{1,0:T(8,128)(2,1)}, bf16[1024,5632]{1,0:T(8,128)(2,1)}, u32[]{:S(2)}, u32[]{:S(2)}) collective-permute-start(bf16[1024,5632]{1,0:T(8,128)(2,1)} %param.32), channel_id=1, source_target_pairs={{0,1},{1,0},{2,3},{3,2},{4,5},{5,4},{6,7},{7,6},{8,9},{9,8},{10,11... | collective-permute-start | bytes 34603016 | tf_op jit(solution)/shard_map/ppermute | solution.py:89
  49.3 12.4 %copy-start.28 = (bf16[1,128,2048]{2,1,0:T(8,128)(2,1)S(1)}, bf16[1,128,2048]{2,1,0:T(8,128)(2,1)}, u32[]{:S(2)}) copy-start(bf16[1,128,2048]{2,1,0:T(8,128)(2,1)} %param.36) | copy-start | bytes 1572868
  49.3 74.7 %all-to-all-start = ((bf16[16,56,2048]{2,1,0:T(8,128)(2,1)}), bf16[16,56,2048]{2,1,0:T(8,128)(2,1)}, u32[]{:S(2)}, u32[]{:S(2)}) async-start(bf16[16,56,2048]{2,1,0:T(8,128)(2,1)} %bitcast.159), calls=%async_computation | async-start | bytes 7340032 | tf_op jit(solution)/shard_map/all_to_all | solution.py:866
  54.4 4.6 collective-permute-start.2
  54.5 3.9 collective-permute-start.5
  55.0 50.5 %collective-permute-start.7 = (bf16[1408,2048]{1,0:T(8,128)(2,1)}, bf16[1408,2048]{1,0:T(8,128)(2,1)}, u32[]{:S(2)}, u32[]{:S(2)}) collective-permute-start(bf16[1408,2048]{1,0:T(8,128)(2,1)} %param.33), channel_id=1, source_target_pairs={{0,1},{1,0},{2,3},{3,2},{4,5},{5,4},{6,7},{7,6},{8,9},{9,8},{10,11... | collective-permute-start | bytes 17301512 | tf_op jit(solution)/shard_map/ppermute | solution.py:89
  58.4 47.1 %collective-permute-start.8 = (bf16[2,704,2048]{2,1,0:T(8,128)(2,1)}, bf16[2,704,2048]{2,1,0:T(8,128)(2,1)}, u32[]{:S(2)}, u32[]{:S(2)}) collective-permute-start(bf16[2,704,2048]{2,1,0:T(8,128)(2,1)} %bitcast.182), channel_id=1, source_target_pairs={{0,1},{1,0},{2,3},{3,2},{4,5},{5,4},{6,7},{7,6},{8,9},{9,8},{10,11... | collective-permute-start | bytes 17301512 | tf_op jit(solution)/shard_map/ppermute | solution.py:89
  59.0 46.4 %collective-permute-start.4 = (bf16[1024,2048]{1,0:T(8,128)(2,1)}, bf16[1024,2048]{1,0:T(8,128)(2,1)}, u32[]{:S(2)}, u32[]{:S(2)}) collective-permute-start(bf16[1024,2048]{1,0:T(8,128)(2,1)} %param.29), channel_id=1, source_target_pairs={{0,1},{1,0},{2,3},{3,2},{4,5},{5,4},{6,7},{7,6},{8,9},{9,8},{10,11... | collective-permute-start | bytes 12582920 | tf_op jit(solution)/shard_map/ppermute | solution.py:89
  59.5 70.2 %copy-start.34 = (pred[896,128]{1,0:T(32,128)(4,1)}, pred[896,128]{1,0:T(32,128)(4,1)S(1)}, u32[]{:S(2)}) copy-start(pred[896,128]{1,0:T(32,128)(4,1)S(1)} %fusion.52) | copy-start | bytes 344068
  61.2 44.2 %collective-permute-start.9 = (bf16[704,2048]{1,0:T(8,128)(2,1)}, bf16[704,2048]{1,0:T(8,128)(2,1)}, u32[]{:S(2)}, u32[]{:S(2)}) collective-permute-start(bf16[704,2048]{1,0:T(8,128)(2,1)} %bitcast.184), channel_id=1, source_target_pairs={{0,1},{1,0},{2,3},{3,2},{4,5},{5,4},{6,7},{7,6},{8,9},{9,8},{10,11... | collective-permute-start | bytes 8650760 | tf_op jit(solution)/shard_map/ppermute | solution.py:89
  129.6 37.7 %copy-start.15 = (bf16[128,2048]{1,0:T(8,128)(2,1)}, bf16[128,2048]{1,0:T(8,128)(2,1)S(1)}, u32[]{:S(2)}) copy-start(bf16[128,2048]{1,0:T(8,128)(2,1)S(1)} %multiply_convert_fusion.7) | copy-start | bytes 1572868
  132.6 86.7 %all-to-all-start.1 = ((bf16[16,56,2048]{2,1,0:T(8,128)(2,1)}), bf16[16,56,2048]{2,1,0:T(8,128)(2,1)}, u32[]{:S(2)}, u32[]{:S(2)}) async-start(bf16[16,56,2048]{2,1,0:T(8,128)(2,1)} %bitcast.156), calls=%async_computation.1 | async-start | bytes 7340032 | tf_op jit(solution)/shard_map/all_to_all | solution.py:866
  161.2 14.3 %slice-start = ((s8[11534336]{0:T(1024)(128)(4,1)}), s8[4194304]{0:T(1024)(128)(4,1)S(1)}, s32[]{:S(2)}) async-start(s8[11534336]{0:T(1024)(128)(4,1)} %bitcast.154), calls=%async_computation.4 | async-start | bytes 8388608
  161.2 14.3 %slice-start.1 = ((s8[11534336]{0:T(1024)(128)(4,1)}), s8[4194304]{0:T(1024)(128)(4,1)S(1)}, s32[]{:S(2)}) async-start(s8[11534336]{0:T(1024)(128)(4,1)} %bitcast.154), calls=%async_computation.5 | async-start | bytes 8388608
  175.4 17.7 %slice-start.3 = ((s8[5767168]{0:T(1024)(128)(4,1)}), s8[1572864]{0:T(1024)(128)(4,1)S(1)}, s32[]{:S(2)}) async-start(s8[5767168]{0:T(1024)(128)(4,1)} %bitcast.157), calls=%async_computation.7 | async-start | bytes 3145728
  180.0 9.4 %copy-start.23 = (bf16[128,2816]{1,0:T(8,128)(2,1)S(1)}, bf16[128,2816]{1,0:T(8,128)(2,1)}, u32[]{:S(2)}) copy-start(bf16[128,2816]{1,0:T(8,128)(2,1)} %get-tuple-element.305) | copy-start | bytes 2162692
  180.0 13.1 %slice-start.4 = ((s8[5767168]{0:T(1024)(128)(4,1)}), s8[4194304]{0:T(1024)(128)(4,1)S(1)}, s32[]{:S(2)}) async-start(s8[5767168]{0:T(1024)(128)(4,1)} %bitcast.157), calls=%async_computation.8 | async-start | bytes 8388608
  219.3 80.8 %collective-permute-start.12 = (bf16[128,4096]{1,0:T(8,128)(2,1)}, bf16[128,4096]{1,0:T(8,128)(2,1)}, u32[]{:S(2)}, u32[]{:S(2)}) collective-permute-start(bf16[128,4096]{1,0:T(8,128)(2,1)} %pad_maximum_fusion.4.refs_0_), channel_id=1, source_target_pairs={{0,4},{2,6},{4,0},{6,2},{8,12},{10,14},{12,8},{14,10},{16,20},{18,... | collective-permute-start | bytes 3145736 | tf_op jit(solution)/shard_map/ppermute | solution.py:85
  224.7 75.5 %collective-permute-start.11 = (bf16[128,7680]{1,0:T(8,128)(2,1)}, bf16[128,7680]{1,0:T(8,128)(2,1)}, u32[]{:S(2)}, u32[]{:S(2)}) collective-permute-start(bf16[128,7680]{1,0:T(8,128)(2,1)} %pad_maximum_fusion.refs_0_.refs_4_), channel_id=1, source_target_pairs={{0,8},{2,10},{4,12},{6,14},{8,0},{10,2},{12,4},{14,6},{16,24},{18,... | collective-permute-start | bytes 5898248 | tf_op jit(solution)/shard_map/ppermute | solution.py:85
  234.0 66.1 %collective-permute-start.10 = (bf16[128,4864]{1,0:T(8,128)(2,1)}, bf16[128,4864]{1,0:T(8,128)(2,1)S(1)}, u32[]{:S(2)}, u32[]{:S(2)}) collective-permute-start(bf16[128,4864]{1,0:T(8,128)(2,1)} %pad_maximum_fusion.3.refs_0_.refs_4_), channel_id=1, source_target_pairs={{0,2},{2,0},{4,6},{6,4},{8,10},{10,8},{12,14},{14,12},{16,18},{18,... | collective-permute-start | bytes 3735560 | tf_op jit(solution)/shard_map/ppermute | solution.py:85
  300.2 60.1 %collective-permute-start.19 = (bf16[2,704,2048]{2,1,0:T(8,128)(2,1)}, bf16[2,704,2048]{2,1,0:T(8,128)(2,1)}, u32[]{:S(2)}, u32[]{:S(2)}) collective-permute-start(bf16[2,704,2048]{2,1,0:T(8,128)(2,1)} %convolution_convert_fusion), channel_id=1, source_target_pairs={{0,1},{1,0},{2,3},{3,2},{4,5},{5,4},{6,7},{7,6},{8,9},{9,8},{10,11... | collective-permute-start | bytes 17301512 | tf_op jit(solution)/shard_map/ppermute | solution.py:89
  301.2 13.3 %copy-start.63 = (s32[8]{0:T(128)S(1)}, s32[8]{0:T(128)}, u32[]{:S(2)}) copy-start(s32[8]{0:T(128)} %constant.197.clone) | copy-start | bytes 100
  301.2 15.3 %copy-start.62 = (s32[8]{0:T(128)S(1)}, s32[8]{0:T(128)}, u32[]{:S(2)}) copy-start(s32[8]{0:T(128)} %constant.196.clone) | copy-start | bytes 100
  301.2 15.9 %copy-start.60 = (s32[8]{0:T(128)S(1)}, s32[8]{0:T(128)}, u32[]{:S(2)}) copy-start(s32[8]{0:T(128)} %constant.194.clone) | copy-start | bytes 100
  301.2 15.9 %copy-start.61 = (s32[8]{0:T(128)S(1)}, s32[8]{0:T(128)}, u32[]{:S(2)}) copy-start(s32[8]{0:T(128)} %constant.195.clone) | copy-start | bytes 100
  301.3 16.4 %copy-start.49 = (bf16[16,896]{1,0:T(8,128)(2,1)S(1)}, bf16[16,896]{1,0:T(8,128)(2,1)}, u32[]{:S(2)}) copy-start(bf16[16,896]{1,0:T(8,128)(2,1)} %get-tuple-element.182) | copy-start | bytes 86020
  301.3 78.7 %all-to-all-start.2 = ((bf16[16,56,2048]{2,1,0:T(8,128)(2,1)}), bf16[16,56,2048]{2,1,0:T(8,128)(2,1)}, u32[]{:S(2)}, u32[]{:S(2)}) async-start(bf16[16,56,2048]{2,1,0:T(8,128)(2,1)} %bitcast.160), calls=%async_computation.2 | async-start | bytes 7340032 | tf_op jit(solution)/shard_map/all_to_all | solution.py:866
  305.9 9.1 %collective-permute-start.15 = (bf16[128,7680]{1,0:T(8,128)(2,1)}, bf16[128,7680]{1,0:T(8,128)(2,1)}, u32[]{:S(2)}, u32[]{:S(2)}) collective-permute-start(bf16[128,7680]{1,0:T(8,128)(2,1)} %pad_maximum_fusion.refs_0_.refs_4_), channel_id=1, source_target_pairs={{0,1},{1,0},{2,3},{3,2},{4,5},{5,4},{6,7},{7,6},{8,9},{9,8},{10,11... | collective-permute-start | bytes 5898248 | tf_op jit(solution)/shard_map/ppermute | solution.py:89
  306.0 7.2 %collective-permute-start.13 = (bf16[128,4864]{1,0:T(8,128)(2,1)S(1)}, bf16[128,4864]{1,0:T(8,128)(2,1)S(1)}, u32[]{:S(2)}, u32[]{:S(2)}) collective-permute-start(bf16[128,4864]{1,0:T(8,128)(2,1)S(1)} %copy-done.14), channel_id=1, source_target_pairs={{0,1},{1,0},{2,3},{3,2},{4,5},{5,4},{6,7},{7,6},{8,9},{9,8},{10,11... | collective-permute-start | bytes 3735560 | tf_op jit(solution)/shard_map/ppermute | solution.py:89
  306.5 9.9 %collective-permute-start.14 = (bf16[128,4864]{1,0:T(8,128)(2,1)}, bf16[128,4864]{1,0:T(8,128)(2,1)}, u32[]{:S(2)}, u32[]{:S(2)}) collective-permute-start(bf16[128,4864]{1,0:T(8,128)(2,1)} %copy-done.24), channel_id=1, source_target_pairs={{0,1},{1,0},{2,3},{3,2},{4,5},{5,4},{6,7},{7,6},{8,9},{9,8},{10,11... | collective-permute-start | bytes 3735560 | tf_op jit(solution)/shard_map/ppermute | solution.py:89
  306.6 24.5 %collective-permute-start.16 = (bf16[128,7680]{1,0:T(8,128)(2,1)}, bf16[128,7680]{1,0:T(8,128)(2,1)}, u32[]{:S(2)}, u32[]{:S(2)}) collective-permute-start(bf16[128,7680]{1,0:T(8,128)(2,1)} %collective-permute-done.11.refs_1_.refs_5_), channel_id=1, source_target_pairs={{0,1},{1,0},{2,3},{3,2},{4,5},{5,4},{6,7},{7,6},{8,9},{9,8},{10,11... | collective-permute-start | bytes 5898248 | tf_op jit(solution)/shard_map/ppermute | solution.py:89
  314.3 45.9 %collective-permute-start.20 = (bf16[704,2048]{1,0:T(8,128)(2,1)}, bf16[704,2048]{1,0:T(8,128)(2,1)}, u32[]{:S(2)}, u32[]{:S(2)}) collective-permute-start(bf16[704,2048]{1,0:T(8,128)(2,1)} %convolution_convert_fusion.3), channel_id=1, source_target_pairs={{0,1},{1,0},{2,3},{3,2},{4,5},{5,4},{6,7},{7,6},{8,9},{9,8},{10,11... | collective-permute-start | bytes 8650760 | tf_op jit(solution)/shard_map/ppermute | solution.py:89
  315.0 32.6 %collective-permute-start.17 = (bf16[128,4096]{1,0:T(8,128)(2,1)}, bf16[128,4096]{1,0:T(8,128)(2,1)}, u32[]{:S(2)}, u32[]{:S(2)}) collective-permute-start(bf16[128,4096]{1,0:T(8,128)(2,1)} %pad_maximum_fusion.4.refs_0_), channel_id=1, source_target_pairs={{0,1},{1,0},{2,3},{3,2},{4,5},{5,4},{6,7},{7,6},{8,9},{9,8},{10,11... | collective-permute-start | bytes 3145736 | tf_op jit(solution)/shard_map/ppermute | solution.py:89
  316.4 31.2 %collective-permute-start.18 = (bf16[128,4096]{1,0:T(8,128)(2,1)}, bf16[128,4096]{1,0:T(8,128)(2,1)}, u32[]{:S(2)}, u32[]{:S(2)}) collective-permute-start(bf16[128,4096]{1,0:T(8,128)(2,1)} %collective-permute-done.12.refs_1_), channel_id=1, source_target_pairs={{0,1},{1,0},{2,3},{3,2},{4,5},{5,4},{6,7},{7,6},{8,9},{9,8},{10,11... | collective-permute-start | bytes 3145736 | tf_op jit(solution)/shard_map/ppermute | solution.py:89
  337.4 12.9 %copy-start.66 = (bf16[1408,896]{1,0:T(8,128)(2,1)S(1)}, bf16[1408,896]{1,0:T(8,128)(2,1)}, u32[]{:S(2)}) copy-start(bf16[1408,896]{1,0:T(8,128)(2,1)} %get-tuple-element.180) | copy-start | bytes 7569412
  347.6 103.6 %collective-permute-start.22 = (bf16[256,4096]{1,0:T(8,128)(2,1)}, bf16[256,4096]{1,0:T(8,128)(2,1)}, u32[]{:S(2)}, u32[]{:S(2)}) collective-permute-start(bf16[256,4096]{1,0:T(8,128)(2,1)} %get-tuple-element.195), channel_id=1, source_target_pairs={{0,2},{2,0},{4,6},{6,4},{8,10},{10,8},{12,14},{14,12},{16,18},{18,... | collective-permute-start | bytes 6291464 | tf_op jit(solution)/shard_map/ppermute | solution.py:85
  348.3 103.0 %collective-permute-start.21 = (bf16[384,2048]{1,0:T(8,128)(2,1)}, bf16[384,2048]{1,0:T(8,128)(2,1)}, u32[]{:S(2)}, u32[]{:S(2)}) collective-permute-start(bf16[384,2048]{1,0:T(8,128)(2,1)} %get-tuple-element.193), channel_id=1, source_target_pairs={{0,4},{2,6},{4,0},{6,2},{8,12},{10,14},{12,8},{14,10},{16,20},{18,... | collective-permute-start | bytes 4718600 | tf_op jit(solution)/shard_map/ppermute | solution.py:85
  350.1 101.1 %collective-permute-start.23 = (bf16[256,1536]{1,0:T(8,128)(2,1)}, bf16[256,1536]{1,0:T(8,128)(2,1)}, u32[]{:S(2)}, u32[]{:S(2)}) collective-permute-start(bf16[256,1536]{1,0:T(8,128)(2,1)} %get-tuple-element.197), channel_id=1, source_target_pairs={{0,4},{2,6},{4,0},{6,2},{8,12},{10,14},{12,8},{14,10},{16,20},{18,... | collective-permute-start | bytes 2359304 | tf_op jit(solution)/shard_map/ppermute | solution.py:85
  350.3 17.6 %slice-start.5 = ((s8[5046272]{0:T(1024)(128)(4,1)}), s8[4194304]{0:T(1024)(128)(4,1)S(1)}, s32[]{:S(2)}) async-start(s8[5046272]{0:T(1024)(128)(4,1)} %bitcast.189), calls=%async_computation.9 | async-start | bytes 8388608
  355.3 12.6 %slice-start.6 = ((s8[5046272]{0:T(1024)(128)(4,1)}), s8[851968]{0:T(1024)(128)(4,1)S(1)}, s32[]{:S(2)}) async-start(s8[5046272]{0:T(1024)(128)(4,1)} %bitcast.189), calls=%async_computation.10 | async-start | bytes 1703936
  367.9 12.0 %copy-start.35 = (pred[896,128]{1,0:T(32,128)(4,1)S(1)}, pred[896,128]{1,0:T(32,128)(4,1)}, u32[]{:S(2)}) copy-start(pred[896,128]{1,0:T(32,128)(4,1)} %copy-done.34) | copy-start | bytes 344068
  393.1 58.2 %collective-permute-start.24 = (bf16[128,2048]{1,0:T(8,128)(2,1)}, bf16[128,2048]{1,0:T(8,128)(2,1)}, u32[]{:S(2)}, u32[]{:S(2)}) collective-permute-start(bf16[128,2048]{1,0:T(8,128)(2,1)} %get-tuple-element.198.refs_4_), channel_id=1, source_target_pairs={{0,4},{2,6},{4,0},{6,2},{8,12},{10,14},{12,8},{14,10},{16,20},{18,... | collective-permute-start | bytes 1572872 | tf_op jit(solution)/shard_map/ppermute | solution.py:85
  395.4 120.7 %collective-permute-start.32 = (bf16[128,2048]{1,0:T(8,128)(2,1)}, bf16[128,2048]{1,0:T(8,128)(2,1)}, u32[]{:S(2)}, u32[]{:S(2)}) collective-permute-start(bf16[128,2048]{1,0:T(8,128)(2,1)} %get-tuple-element.198.refs_4_), channel_id=1, source_target_pairs={{0,1},{1,0},{2,3},{3,2},{4,5},{5,4},{6,7},{7,6},{8,9},{9,8},{10,11... | collective-permute-start | bytes 1572872 | tf_op jit(solution)/shard_map/ppermute | solution.py:89
  395.4 129.5 %all-to-all-start.3 = ((bf16[16,56,2048]{2,1,0:T(8,128)(2,1)}), bf16[16,56,2048]{2,1,0:T(8,128)(2,1)}, u32[]{:S(2)}, u32[]{:S(2)}) async-start(bf16[16,56,2048]{2,1,0:T(8,128)(2,1)} %bitcast.161), calls=%async_computation.3 | async-start | bytes 7340032 | tf_op jit(solution)/shard_map/all_to_all | solution.py:866
  449.2 87.5 %copy-start = (bf16[128,3072]{1,0:T(8,128)(2,1)}, bf16[128,3072]{1,0:T(8,128)(2,1)S(1)}, u32[]{:S(2)}) copy-start(bf16[128,3072]{1,0:T(8,128)(2,1)S(1)} %get-tuple-element.205.refs_4_) | copy-start | bytes 2359300
  451.3 72.7 %collective-permute-start.25 = (bf16[128,3072]{1,0:T(8,128)(2,1)S(1)}, bf16[128,3072]{1,0:T(8,128)(2,1)S(1)}, u32[]{:S(2)}, u32[]{:S(2)}) collective-permute-start(bf16[128,3072]{1,0:T(8,128)(2,1)S(1)} %get-tuple-element.205.refs_4_), channel_id=1, source_target_pairs={{0,4},{2,6},{4,0},{6,2},{8,12},{10,14},{12,8},{14,10},{16,20},{18,... | collective-permute-start | bytes 2359304 | tf_op jit(solution)/shard_map/ppermute | solution.py:85
  453.3 98.6 %collective-permute-start.27 = (bf16[128,3072]{1,0:T(8,128)(2,1)S(1)}, bf16[128,3072]{1,0:T(8,128)(2,1)}, u32[]{:S(2)}, u32[]{:S(2)}) collective-permute-start(bf16[128,3072]{1,0:T(8,128)(2,1)S(1)} %get-tuple-element.205.refs_4_), channel_id=1, source_target_pairs={{0,1},{1,0},{2,3},{3,2},{4,5},{5,4},{6,7},{7,6},{8,9},{9,8},{10,11... | collective-permute-start | bytes 2359304 | tf_op jit(solution)/shard_map/ppermute | solution.py:89
  457.5 67.4 %collective-permute-start.26 = (bf16[256,4096]{1,0:T(8,128)(2,1)S(1)}, bf16[256,4096]{1,0:T(8,128)(2,1)}, u32[]{:S(2)}, u32[]{:S(2)}) collective-permute-start(bf16[256,4096]{1,0:T(8,128)(2,1)S(1)} %get-tuple-element.303), channel_id=1, source_target_pairs={{0,1},{1,0},{2,3},{3,2},{4,5},{5,4},{6,7},{7,6},{8,9},{9,8},{10,11... | collective-permute-start | bytes 6291464 | tf_op jit(solution)/shard_map/ppermute | solution.py:89
  458.0 58.2 %collective-permute-start.33 = (bf16[128,2048]{1,0:T(8,128)(2,1)}, bf16[128,2048]{1,0:T(8,128)(2,1)S(1)}, u32[]{:S(2)}, u32[]{:S(2)}) collective-permute-start(bf16[128,2048]{1,0:T(8,128)(2,1)} %collective-permute-done.24.refs_5_), channel_id=1, source_target_pairs={{0,1},{1,0},{2,3},{3,2},{4,5},{5,4},{6,7},{7,6},{8,9},{9,8},{10,11... | collective-permute-start | bytes 1572872 | tf_op jit(solution)/shard_map/ppermute | solution.py:89
  516.1 9.6 %copy-start.27 = (bf16[1024,576]{0,1:T(8,128)(2,1)S(1)}, bf16[1024,576]{0,1:T(8,128)(2,1)}, u32[]{:S(2)}) copy-start(bf16[1024,576]{0,1:T(8,128)(2,1)} %param.26) | copy-start | bytes 3538948
  526.1 24.7 %collective-permute-start.29 = (bf16[128,640]{1,0:T(8,128)(2,1)S(1)}, bf16[128,640]{1,0:T(8,128)(2,1)S(1)}, u32[]{:S(2)}, u32[]{:S(2)}) collective-permute-start(bf16[128,640]{1,0:T(8,128)(2,1)S(1)} %pad.9), channel_id=1, source_target_pairs={{0,4},{2,6},{4,0},{6,2},{8,12},{10,14},{12,8},{14,10},{16,20},{18,... | collective-permute-start | bytes 491528 | tf_op jit(solution)/shard_map/ppermute | solution.py:85
  530.0 31.3 %collective-permute-start.30 = (bf16[128,640]{1,0:T(8,128)(2,1)S(1)}, bf16[128,640]{1,0:T(8,128)(2,1)}, u32[]{:S(2)}, u32[]{:S(2)}) collective-permute-start(bf16[128,640]{1,0:T(8,128)(2,1)S(1)} %pad.9), channel_id=1, source_target_pairs={{0,1},{1,0},{2,3},{3,2},{4,5},{5,4},{6,7},{7,6},{8,9},{9,8},{10,11... | collective-permute-start | bytes 491528 | tf_op jit(solution)/shard_map/ppermute | solution.py:89
  543.4 7.2 %collective-permute-start.34 = (bf16[16,16,128]{2,1,0:T(8,128)(2,1)S(1)}, bf16[16,16,128]{2,1,0:T(8,128)(2,1)S(1)}, u32[]{:S(2)}, u32[]{:S(2)}) collective-permute-start(bf16[16,16,128]{2,1,0:T(8,128)(2,1)S(1)} %dynamic-slice_bitcast_fusion), channel_id=1, source_target_pairs={{0,1},{1,0},{2,3},{3,2},{4,5},{5,4},{6,7},{7,6},{8,9},{9,8},{10,11... | collective-permute-start | bytes 196616 | tf_op jit(solution)/shard_map/ppermute | solution.py:89
  544.0 7.9 %collective-permute-start.28 = (bf16[128,3072]{1,0:T(8,128)(2,1)}, bf16[128,3072]{1,0:T(8,128)(2,1)S(1)}, u32[]{:S(2)}, u32[]{:S(2)}) collective-permute-start(bf16[128,3072]{1,0:T(8,128)(2,1)} %copy-done.38), channel_id=1, source_target_pairs={{0,1},{1,0},{2,3},{3,2},{4,5},{5,4},{6,7},{7,6},{8,9},{9,8},{10,11... | collective-permute-start | bytes 2359304 | tf_op jit(solution)/shard_map/ppermute | solution.py:89
  550.8 10.5 %collective-permute-start.31 = (bf16[128,640]{1,0:T(8,128)(2,1)S(1)}, bf16[128,640]{1,0:T(8,128)(2,1)S(1)}, u32[]{:S(2)}, u32[]{:S(2)}) collective-permute-start(bf16[128,640]{1,0:T(8,128)(2,1)S(1)} %collective-permute-done.29), channel_id=1, source_target_pairs={{0,1},{1,0},{2,3},{3,2},{4,5},{5,4},{6,7},{7,6},{8,9},{9,8},{10,11... | collective-permute-start | bytes 491528 | tf_op jit(solution)/shard_map/ppermute | solution.py:89
  (50 other events, 231.4 us)

commit v6 on v5

--- a/solution.py
+++ b/solution.py
@@ -693,7 +693,7 @@
     )(order, grad_out, expand, keys, weights, queries, mixed, nope, cosine, sine)
 
 
-def expert_kernel(sources, here_ref, rows_ref, grads_ref, router_ref, *refs):
+def expert_kernel(sources, here_ref, rows_ref, router_ref, *refs):
     weights = refs[: 2 * sources]
     (
         row_grad_ref, units_ref, back_ref, gate_ref, logit_grad_ref, total_ref, probs_ref, share_ref,
@@ -712,10 +712,10 @@
         share_ref[...] = jnp.zeros_like(share_ref)
         total_ref[...] = jnp.zeros_like(total_ref)
 
-    def work(in_ref, out_ref):
+    def work(in_ref, slopes_ref):
         gate = dot_t(in_ref[0], rows_ref[...])
         up = dot_t(in_ref[1], rows_ref[...])
-        back = dot_t(out_ref[...], grads_ref[...])
+        back = slopes_ref[...]
         sigma = 1.0 / (1.0 + jnp.exp(-gate))
         act = gate * sigma
         units = (act * up).astype(BF)
@@ -744,7 +744,7 @@
         ).astype(BF)
 
 
-def expert_pass(here, rows, grads, router, weights):
+def expert_pass(here, rows, router, weights):
     count, width = rows.shape
     experts = router.shape[0]
     sources = len(weights)
@@ -754,13 +754,12 @@
     once = pl.Buffered(1)
     in_specs = [
         pl.BlockSpec((count, width), lambda i, h: (0, 0), pipeline_mode=once),
-        pl.BlockSpec((count, width), lambda i, h: (0, 0), pipeline_mode=once),
         pl.BlockSpec((experts, width), lambda i, h: (0, 0)),
     ]
     for k in range(sources):
         at = lambda i, k=k: jnp.clip(i - k * chunks, 0, chunks - 1)
         in_specs.append(pl.BlockSpec((2, tile, width), lambda i, h, at=at: (0, at(i), 0)))
-        in_specs.append(pl.BlockSpec((tile, width), lambda i, h, at=at: (at(i), 0)))
+        in_specs.append(pl.BlockSpec((tile, count), lambda i, h, at=at: (at(i), 0)))
     return pl.pallas_call(
         functools.partial(expert_kernel, sources),
         grid_spec=pltpu.PrefetchScalarGridSpec(
@@ -791,11 +790,11 @@
         ],
         compiler_params=pltpu.CompilerParams(vmem_limit_bytes=58 << 20),
         cost_estimate=pl.CostEstimate(
-            flops=10 * count * width * sources * units,
-            bytes_accessed=6 * (count + sources * units) * width,
+            flops=8 * count * width * sources * units,
+            bytes_accessed=4 * (count + sources * units) * width,
             transcendentals=count * sources * units,
         ),
-    )(here, rows, grads, router, *[piece for pair in weights for piece in pair])
+    )(here, rows, router, *[piece for pair in weights for piece in pair])
 
 
 def per_device(
@@ -948,17 +947,21 @@
     grad_ffn_in = times_back(
         jnp.concatenate([grad_shared_gate, grad_shared_up], -1), shared_in_blocks
     )
+    out_slopes = [dot_t(weight_out, received_grads) for _, weight_out in expert_weights]
     out_message = jnp.concatenate([shared_hidden, grad_out_low], 1)
     in_message = jnp.concatenate([ffn_in, grad_shared_gate, grad_shared_up], 1)
-    received, shared_result, grad_ffn_in, out_message, in_message = together(
-        received, shared_result, grad_ffn_in, out_message, in_message
+    received, shared_result, grad_ffn_in, out_slopes, out_message, in_message = together(
+        received, shared_result, grad_ffn_in, out_slopes, out_message, in_message
     )
 
     early_message = jnp.concatenate([attn_in, mixed_heads], 1)
     received, early_message = together(received, early_message)
     arrived = cross(out_message, 1), cross(in_message, 4), cross(early_message, 2)
     expert_results = expert_pass(
-        here[None], received, received_grads, router.T, expert_weights
+        here[None],
+        received,
+        router.T,
+        [(weight_in, slopes) for (weight_in, _), slopes in zip(expert_weights, out_slopes)],
     )
     row_grads, hidden, hidden_grads, row_gate, row_grad_logits = expert_results
 

time: 705 us -> 699 us (level)
  matrix products: 141 us -> 161 us
  waiting for transfers between devices: 49.3 us -> 29.8 us
    all_to_all x4, waiting for transfers between devices: 39.1 us -> 18.7 us  [exchange(): lax.all_to_all(rows.reshape(owners, capacity, model_width), 'expert', spl...]
    dot_general x10 -> x12, matrix products: 42.3 us -> 60.6 us  [dot_t(): lax.dot_general(left, right, (((1,), (1,)), ((), ())), preferred_element_...]
    all_to_all x4, starting transfers between devices: 39.9 us -> 53.3 us  [exchange(): lax.all_to_all(rows.reshape(owners, capacity, model_width), 'expert', spl...]
    ppermute x9, starting transfers between devices: 27.2 us -> 16.4 us  [cross(): return lax.ppermute(values, 'expert', [(i, i ^ bit) for i in range(count)])]
    pallas_call x1, Pallas kernels: 46.6 us -> 39 us  [expert_pass(): pl.pallas_call(functools.partial(expert_kernel, sources), grid_spec=pltpu...]
    unnamed x163 -> x151, local copies, waits for them, and re-layouts: 17 us -> 15.8 us
  transfers between devices with their start and end apart: 39 -> 39, of which waited for: 6 -> 5; matrix products, arithmetic and copies ran while one was open for 24% -> 27% of each run, Pallas kernels for 35% -> 34%
where the time goes in v6:
time: 699 us; the launch traced here: 694 us
  Pallas kernels  362 us (52%)
  matrix products  161 us (23%)
  starting transfers between devices  76 us (11%)
  other arithmetic  30.9 us (4%)
  local copies, waits for them, and re-layouts  30.6 us (4%)
  waiting for transfers between devices  29.8 us (4%)
    pallas_call x1, Pallas kernels, reduce_all(): pl.pallas_call(functools.partial(reduce_kernel, plans, steps), in_specs=[...  124 us
    dot_general x19, matrix products, dot(): return jnp.dot(left, right, preferred_element_type=F32)  82.9 us
    dot_general x12, matrix products, dot_t(): lax.dot_general(left, right, (((1,), (1,)), ((), ())), preferred_element_...  60.6 us
    pallas_call x1, Pallas kernels, scatter_slot(): pl.pallas_call(scatter_kernel, in_specs=[pl.BlockSpec(memory_space=pltpu....  57.9 us
    all_to_all x4, starting transfers between devices, exchange(): lax.all_to_all(rows.reshape(owners, capacity, model_width), 'expert', spl...  53.3 us
    pallas_call x5, Pallas kernels, product_halves(): pl.pallas_call(functools.partial(product_kernel, rows, len(lefts)), grid_...  42 us
    pallas_call x1, Pallas kernels, attend_back(): pl.pallas_call(attend_back_kernel, grid_spec=pltpu.PrefetchScalarGridSpec...  40 us
    pallas_call x1, Pallas kernels, expert_pass(): pl.pallas_call(functools.partial(expert_kernel, sources), grid_spec=pltpu...  39 us
  transfers between devices with their start and end apart: 39, of which 5 were waited for; matrix products, arithmetic and copies ran while one was open for 27% of the time, Pallas kernels for 34%

profile of v6, /device:TPU:0, one launch (start us, length us, event | category | flops | bytes accessed | tf_op | source)
XLA Modules:
  0.0 693.6 jit_solution(17074633222053366686)
XLA Ops:
  8.1 4.1 convolution_convert_fusion.2
  13.1 1.8 convolution_add_fusion.6
  15.8 31.9 %shard_map.308 = bf16[16,128,576]{2,1,0:T(8,128)(2,1)S(1)} custom-call(bf16[128,576]{1,0:T(8,128)(2,1)S(1)} %pad_maximum_fusion.7.own_ref), custom_call_target="tpu_custom_call" | custom-call | flops 49999998976 | bytes 4718592 | tf_op jit(solution)/shard_map/pallas_call | solution.py:330
  47.7 1.5 copy-done.1
  49.2 5.3 all-to-all-start
  55.2 3.3 collective-permute-done.5
  62.7 3.9 fusion.66
  67.3 4.8 maximum_select_fusion.expand_ref
  72.1 3.9 convolution_add_fusion.1.raw_ref
  76.1 27.1 %shard_map.309 = (bf16[128,2048]{1,0:T(8,128)(2,1)S(1)}, bf16[2048,576]{1,0:T(8,128)(2,1)S(1)}, bf16[2048,2048]{1,0:T(8,128)(2,1)}, bf16[2048,512]{1,0:T(8,128)(2,1)S(1)}, bf16[128,2048]{1,0:T(8,128)(2,1)S(1)}) custom-call(f32[128,3072]{1,0:T(8,128)S(1)} %convolution_add_fusion.1.raw_ref, f32[128,32]{1,0:T(8,128)S(1)} %get-tuple-element.321.cosine_ref, ...), custom_call_target="tpu_custom_call" | custom-call | flops 9126805504 | bytes 8388608 | tf_op jit(solution)/shard_map/pallas_call | solution.py:563
  103.2 1.5 copy-done.4
  105.4 18.7 %all-to-all-done = bf16[16,56,2048]{2,1,0:T(8,128)(2,1)} async-done(((bf16[16,56,2048]{2,1,0:T(8,128)(2,1)}), bf16[16,56,2048]{2,1,0:T(8,128)(2,1)}, u32[]{:S(2)}, u32[]{:S(2)}) %all-to-all-start) | async-done | bytes 3670048 | tf_op jit(solution)/shard_map/all_to_all | solution.py:865
  124.1 3.0 fusion.59
  129.7 2.9 convolution_convert_fusion.1
  132.7 29.2 %all-to-all-start.1 = ((bf16[16,56,2048]{2,1,0:T(8,128)(2,1)}), bf16[16,56,2048]{2,1,0:T(8,128)(2,1)}, u32[]{:S(2)}, u32[]{:S(2)}) async-start(bf16[16,56,2048]{2,1,0:T(8,128)(2,1)} %bitcast.158), calls=%async_computation.1 | async-start | bytes 7340032 | tf_op jit(solution)/shard_map/all_to_all | solution.py:865
  161.9 6.0 fusion.56
  167.9 5.5 fusion.124
  173.4 7.7 %convolution_add_fusion = f32[128,5632]{1,0:T(8,128)} fusion(f32[128,5632]{1,0:T(8,128)S(1)} %fusion.56, bf16[1024,5632]{1,0:T(8,128)(2,1)} %param.32, bf16[128,2048]{1,0:T(8,128)(2,1)S(1)} %multiply_convert_fusion.7, s32[]{:T(128)S(6)} %select_n.233), kind=kOutput, calls=%fused_computation.3 | convolution fusion | flops 1477115904 | bytes 17563652 | tf_op jit(solution)/shard_map/dot_general | solution.py:72
  181.1 5.5 fusion.125
  186.7 3.0 multiply_convert_fusion.5
  189.7 8.2 %fusion.39 = f32[128,1024]{1,0:T(8,128)S(1)} fusion(bf16[1024,5632]{1,0:T(8,128)(2,1)} %param.32, bf16[128,2816]{1,0:T(8,128)(2,1)S(1)} %get-tuple-element.306, bf16[128,2816]{1,0:T(8,128)(2,1)S(1)} %get-tuple-element.305), kind=kOutput, calls=%fused_computation.76 | convolution fusion | flops 1479278592 | bytes 13500416 | tf_op jit(solution)/shard_map/dot_general | solution.py:76
  197.9 8.1 %fusion.38 = f32[128,1024]{1,0:T(8,128)S(1)} fusion(bf16[1024,5632]{1,0:T(8,128)(2,1)} %collective-permute-done.6, bf16[128,2816]{1,0:T(8,128)(2,1)S(1)} %get-tuple-element.306, bf16[128,2816]{1,0:T(8,128)(2,1)S(1)} %get-tuple-element.305), kind=kOutput, calls=%fused_computation.75 | convolution fusion | flops 1479278592 | bytes 13500416 | tf_op jit(solution)/shard_map/dot_general | solution.py:76
  207.2 3.7 fusion.53
  210.9 2.0 convolution_add_fusion.4
  214.1 8.0 %fusion.127.refs_3_ = f32[704,896]{1,0:T(8,128)} fusion(bf16[704,2048]{1,0:T(8,128)(2,1)} %collective-permute-done.9, bf16[896,2048]{1,0:T(8,128)(2,1)} %bitcast.13), kind=kOutput, calls=%fused_computation.235 | convolution fusion | flops 2583691264 | bytes 9076736 | tf_op jit(solution)/shard_map/dot_general | solution.py:76
  222.1 6.8 fusion.126.refs_1_
  230.5 1.6 collective-permute-start.12
  232.0 2.1 collective-permute-start.11
  235.6 39.0 %shard_map.310 = (bf16[896,2048]{1,0:T(8,128)(2,1)}, bf16[1408,896]{1,0:T(8,128)(2,1)}, bf16[2,2,704,896]{3,2,1,0:T(8,128)(2,1)}, f32[1,896]{1,0:T(1,128)}, bf16[16,896]{1,0:T(8,128)(2,1)}) custom-call(s32[1]{0:T(128)} %bitcast.19.here_ref, bf16[896,2048]{1,0:T(8,128)(2,1)} %bitcast.17.rows_ref, bf16[16,2048]{1,0:T(8,128)(2,1)} %bitcast.176, ...), custom_call_target="tpu_custom_call" | custom-call | flops 20669530112 | bytes 18874368 | tf_op jit(solution)/shard_map/pallas_call | solution.py:763
  275.3 7.4 %convolution_convert_fusion.3 = bf16[704,2048]{1,0:T(8,128)(2,1)} fusion(bf16[896,2048]{1,0:T(8,128)(2,1)} %bitcast.13, f32[896]{0:T(1024)S(1)} %reduce, bf16[1408,896]{1,0:T(8,128)(2,1)} %get-tuple-element.184), kind=kOutput, calls=%fused_computation.13 | convolution fusion | flops 2590638080 | bytes 7818752 | tf_op jit(solution)/shard_map/dot_general | solution.py:72
  282.8 10.0 %convolution_convert_fusion = bf16[2,704,2048]{2,1,0:T(8,128)(2,1)} fusion(bf16[896,2048]{1,0:T(8,128)(2,1)} %bitcast.17.rows_ref, bf16[2,2,704,896]{3,2,1,0:T(8,128)(2,1)S(1)} %copy-done.64), kind=kOutput, calls=%fused_computation.5 | convolution fusion | flops 5170266112 | bytes 11960320 | tf_op jit(solution)/shard_map/dot_general | solution.py:72
  292.9 4.7 all-to-all-start.2
  299.3 6.5 collective-permute-done.13.refs_2_.refs_6_
  310.3 3.3 fusion.128
  313.5 10.1 %shard_map.311 = (bf16[384,2048]{1,0:T(8,128)(2,1)}, bf16[384,2048]{1,0:T(8,128)(2,1)}, f32[768,512]{1,0:T(8,128)}) custom-call(s32[8]{0:T(128)} %multiply_add_fusion.4.order_ref, bf16[128,4864]{1,0:T(8,128)(2,1)} %copy-done.14, bf16[128,4864]{1,0:T(8,128)(2,1)} %collective-permute-done.10.refs_1_.refs_5_, bf16[128,4864]{1,0:T(8,128)(2,1)} %copy-done.23, ...), custom_call_target="tpu_custom_call" | custom-call | flops 1610612736 | bytes 8126464 | tf_op jit(solution)/shard_map/pallas_call | solution.py:208
  323.7 6.2 shard_map.313
  329.9 10.2 %shard_map.312 = (bf16[256,4096]{1,0:T(8,128)(2,1)}, bf16[256,4096]{1,0:T(8,128)(2,1)}, bf16[512,512]{1,0:T(8,128)(2,1)}) custom-call(s32[8]{0:T(128)} %get-tuple-element.330.order_ref, bf16[128,7680]{1,0:T(8,128)(2,1)} %pad_maximum_fusion.refs_0_.refs_4_, bf16[128,7680]{1,0:T(8,128)(2,1)} %collective-permute-done.11.refs_1_.refs_5_, ...), custom_call_target="tpu_custom_call" | custom-call | flops 2147483648 | bytes 10485760 | tf_op jit(solution)/shard_map/pallas_call | solution.py:208
  340.8 2.0 collective-permute-start.23
  342.8 5.0 fusion.20
  347.9 4.9 multiply_convert_fusion
  352.8 7.6 %convert_add_fusion.1 = f32[704,2048]{1,0:T(8,128)} fusion(bf16[704,2048]{1,0:T(8,128)(2,1)} %collective-permute-done.20, bf16[896,2048]{1,0:T(8,128)(2,1)} %bitcast.13, f32[896]{0:T(1024)S(1)} %reduce, bf16[1408,896]{1,0:T(8,128)(2,1)S(1)} %copy-done.63), kind=kOutput, calls=%fused_computation.4 | convolution fusion | flops 2592079872 | bytes 13586432 | tf_op jit(solution)/shard_map/dot_general | solution.py:72
  360.5 12.0 %convert_add_fusion = f32[2,704,2048]{2,1,0:T(8,128)} fusion(bf16[2,704,2048]{2,1,0:T(8,128)(2,1)} %collective-permute-done.19, bf16[896,2048]{1,0:T(8,128)(2,1)} %bitcast.17.rows_ref, bf16[2,2,704,896]{3,2,1,0:T(8,128)(2,1)S(1)} %bitcast.192), kind=kOutput, calls=%fused_computation | convolution fusion | flops 5173149696 | bytes 23494656 | tf_op jit(solution)/shard_map/dot_general | solution.py:72
  372.6 3.7 multiply_reduce_fusion
  376.3 1.5 fusion.118
  379.0 2.6 fusion.129
  381.6 3.9 fusion.130
  385.6 2.8 collective-permute-start.24
  388.5 14.2 %all-to-all-start.3 = ((bf16[16,56,2048]{2,1,0:T(8,128)(2,1)}), bf16[16,56,2048]{2,1,0:T(8,128)(2,1)}, u32[]{:S(2)}, u32[]{:S(2)}) async-start(bf16[16,56,2048]{2,1,0:T(8,128)(2,1)} %bitcast.163), calls=%async_computation.3 | async-start | bytes 7340032 | tf_op jit(solution)/shard_map/all_to_all | solution.py:865
  403.7 40.0 %shard_map.314 = (bf16[128,3072]{1,0:T(8,128)(2,1)S(1)}, bf16[512,4096]{1,0:T(8,128)(2,1)}, bf16[2048,576]{1,0:T(8,128)(2,1)}) custom-call(s32[32]{0:T(128)S(1)} %add.354.order_ref, bf16[128,2048]{1,0:T(8,128)(2,1)S(1)} %fusion.36.grad_ref, bf16[512,4096]{1,0:T(8,128)(2,1)} %maximum_select_fusion.expand_ref, bf16[2048,576]{1,0:T(8,128)(2,1)} %bitcast.155, ...), custom_call_target="tpu_custom_call" | custom-call | flops 22548578304 | bytes 8388608 | tf_op jit(solution)/shard_map/pallas_call | solution.py:655
  445.8 2.1 collective-permute-start.25
  447.8 4.1 fusion.120
  452.4 57.9 %shard_map.315 = f32[128,576]{1,0:T(8,128)S(1)} custom-call(bf16[16,128,576]{2,1,0:T(8,128)(2,1)S(1)} %bitcast.157), custom_call_target="tpu_custom_call" | custom-call | flops 49999998976 | bytes 4718592 | tf_op jit(solution)/shard_map/pallas_call | solution.py:417
  511.2 6.9 shard_map.317
  520.3 3.7 collective-permute-start.29
  524.0 5.0 fusion.133
  529.0 1.6 fusion.132
  530.7 5.0 fusion.134
  538.2 2.7 fusion.47
  540.9 3.9 fusion.13
  546.9 8.5 %shard_map.316 = (bf16[256,3072]{1,0:T(8,128)(2,1)}, bf16[256,3072]{1,0:T(8,128)(2,1)}, bf16[512,512]{1,0:T(8,128)(2,1)}) custom-call(s32[8]{0:T(128)} %multiply_add_fusion.1.order_ref, bf16[128,4096]{1,0:T(8,128)(2,1)} %pad_maximum_fusion.4.refs_0_, bf16[128,4096]{1,0:T(8,128)(2,1)} %collective-permute-done.12.refs_1_, ...), custom_call_target="tpu_custom_call" | custom-call | flops 1610612736 | bytes 8388608 | tf_op jit(solution)/shard_map/pallas_call | solution.py:208
  555.4 1.6 convolution_convert_fusion.4
  557.9 123.8 %shard_map.318 = (f32[64,640]{1,0:T(8,128)}, f32[96,2048]{1,0:T(8,128)}, f32[16,4096]{1,0:T(8,128)}, f32[64,3072]{1,0:T(8,128)}, f32[64,4096]{1,0:T(8,128)}, /*i...) custom-call(bf16[256,640]{1,0:T(8,128)(2,1)} %get-tuple-element.311.refs_0_, ...), custom_call_target="tpu_custom_call" | custom-call | flops 99999997952 | bytes 38141952 | tf_op jit(solution)/shard_map/pallas_call | solution.py:503
  685.0 2.1 slice.118
  687.8 2.6 pad_maximum_fusion.2
  (289 shorter events, 49.6 us)
Async XLA Ops:
  0.6 11.6 %copy-start.12 = (bf16[1,128,2048]{2,1,0:T(8,128)(2,1)S(1)}, bf16[1,128,2048]{2,1,0:T(8,128)(2,1)}, u32[]{:S(2)}) copy-start(bf16[1,128,2048]{2,1,0:T(8,128)(2,1)} %param.21) | copy-start | bytes 1572868
  1.4 10.7 %collective-permute-start = (bf16[1,2304]{1,0:T(2,128)(2,1)S(1)}, bf16[1,2304]{1,0:T(2,128)(2,1)S(1)}, u32[]{:S(2)}, u32[]{:S(2)}) collective-permute-start(bf16[1,2304]{1,0:T(2,128)(2,1)S(1)} %broadcast_in_dim.24), channel_id=1, source_target_pairs={{0,1},{1,0},{2,3},{3,2},{4,5},{5,4},{6,7},{7,6},{8,9},{9,8},{10,11... | collective-permute-start | bytes 13832 | tf_op jit(solution)/shard_map/ppermute | solution.py:89
  2.0 11.1 %collective-permute-start.3 = (bf16[1024,576]{0,1:T(8,128)(2,1)}, bf16[1024,576]{0,1:T(8,128)(2,1)}, u32[]{:S(2)}, u32[]{:S(2)}) collective-permute-start(bf16[1024,576]{0,1:T(8,128)(2,1)} %param.26), channel_id=1, source_target_pairs={{0,1},{1,0},{2,3},{3,2},{4,5},{5,4},{6,7},{7,6},{8,9},{9,8},{10,11... | collective-permute-start | bytes 3538952 | tf_op jit(solution)/shard_map/ppermute | solution.py:89
  2.0 59.3 %collective-permute-start.1 = (bf16[1024,3072]{1,0:T(8,128)(2,1)}, bf16[1024,3072]{1,0:T(8,128)(2,1)}, u32[]{:S(2)}, u32[]{:S(2)}) collective-permute-start(bf16[1024,3072]{1,0:T(8,128)(2,1)} %param.25), channel_id=1, source_target_pairs={{0,1},{1,0},{2,3},{3,2},{4,5},{5,4},{6,7},{7,6},{8,9},{9,8},{10,11... | collective-permute-start | bytes 18874376 | tf_op jit(solution)/shard_map/ppermute | solution.py:89
  5.7 9.4 %copy-start.50 = (f32[128]{0:T(128)}, f32[128]{0:T(128)S(1)}, u32[]{:S(2)}) copy-start(f32[128]{0:T(128)S(1)} %fusion.113) | copy-start | bytes 1540
  5.8 56.0 %copy-start.48 = (f32[128]{0:T(128)}, f32[128]{0:T(128)S(1)}, u32[]{:S(2)}) copy-start(f32[128]{0:T(128)S(1)} %compare_convert_fusion) | copy-start | bytes 1540
  12.5 59.6 %copy-start.17 = (bf16[128,2048]{1,0:T(8,128)(2,1)}, bf16[128,2048]{1,0:T(8,128)(2,1)S(1)}, u32[]{:S(2)}) copy-start(bf16[128,2048]{1,0:T(8,128)(2,1)S(1)} %fusion.28) | copy-start | bytes 1572868
  14.9 32.8 %copy-start.21 = (f32[128,576]{1,0:T(8,128)}, f32[128,576]{1,0:T(8,128)S(1)}, u32[]{:S(2)}) copy-start(f32[128,576]{1,0:T(8,128)S(1)} %convolution_add_fusion.6) | copy-start | bytes 884740
  15.1 32.6 %copy-start.52 = (f32[128]{0:T(128)}, f32[128]{0:T(128)S(1)}, u32[]{:S(2)}) copy-start(f32[128]{0:T(128)S(1)} %add_rsqrt_fusion.1) | copy-start | bytes 1540
  15.6 108.5 %collective-permute-start.6 = (bf16[1024,5632]{1,0:T(8,128)(2,1)}, bf16[1024,5632]{1,0:T(8,128)(2,1)}, u32[]{:S(2)}, u32[]{:S(2)}) collective-permute-start(bf16[1024,5632]{1,0:T(8,128)(2,1)} %param.32), channel_id=1, source_target_pairs={{0,1},{1,0},{2,3},{3,2},{4,5},{5,4},{6,7},{7,6},{8,9},{9,8},{10,11... | collective-permute-start | bytes 34603016 | tf_op jit(solution)/shard_map/ppermute | solution.py:89
  49.2 12.6 %copy-start.26 = (bf16[1,128,2048]{2,1,0:T(8,128)(2,1)S(1)}, bf16[1,128,2048]{2,1,0:T(8,128)(2,1)}, u32[]{:S(2)}) copy-start(bf16[1,128,2048]{2,1,0:T(8,128)(2,1)} %param.36) | copy-start | bytes 1572868
  49.2 74.9 %all-to-all-start = ((bf16[16,56,2048]{2,1,0:T(8,128)(2,1)}), bf16[16,56,2048]{2,1,0:T(8,128)(2,1)}, u32[]{:S(2)}, u32[]{:S(2)}) async-start(bf16[16,56,2048]{2,1,0:T(8,128)(2,1)} %bitcast.161), calls=%async_computation | async-start | bytes 7340032 | tf_op jit(solution)/shard_map/all_to_all | solution.py:865
  54.5 4.6 collective-permute-start.2
  54.6 3.9 collective-permute-start.5
  55.1 50.3 %collective-permute-start.7 = (bf16[1408,2048]{1,0:T(8,128)(2,1)}, bf16[1408,2048]{1,0:T(8,128)(2,1)}, u32[]{:S(2)}, u32[]{:S(2)}) collective-permute-start(bf16[1408,2048]{1,0:T(8,128)(2,1)} %param.33), channel_id=1, source_target_pairs={{0,1},{1,0},{2,3},{3,2},{4,5},{5,4},{6,7},{7,6},{8,9},{9,8},{10,11... | collective-permute-start | bytes 17301512 | tf_op jit(solution)/shard_map/ppermute | solution.py:89
  58.5 46.9 %collective-permute-start.8 = (bf16[2,704,2048]{2,1,0:T(8,128)(2,1)}, bf16[2,704,2048]{2,1,0:T(8,128)(2,1)}, u32[]{:S(2)}, u32[]{:S(2)}) collective-permute-start(bf16[2,704,2048]{2,1,0:T(8,128)(2,1)} %bitcast.184), channel_id=1, source_target_pairs={{0,1},{1,0},{2,3},{3,2},{4,5},{5,4},{6,7},{7,6},{8,9},{9,8},{10,11... | collective-permute-start | bytes 17301512 | tf_op jit(solution)/shard_map/ppermute | solution.py:89
  59.2 46.3 %collective-permute-start.4 = (bf16[1024,2048]{1,0:T(8,128)(2,1)}, bf16[1024,2048]{1,0:T(8,128)(2,1)}, u32[]{:S(2)}, u32[]{:S(2)}) collective-permute-start(bf16[1024,2048]{1,0:T(8,128)(2,1)} %param.29), channel_id=1, source_target_pairs={{0,1},{1,0},{2,3},{3,2},{4,5},{5,4},{6,7},{7,6},{8,9},{9,8},{10,11... | collective-permute-start | bytes 12582920 | tf_op jit(solution)/shard_map/ppermute | solution.py:89
  59.6 70.1 %copy-start.30 = (pred[896,128]{1,0:T(32,128)(4,1)}, pred[896,128]{1,0:T(32,128)(4,1)S(1)}, u32[]{:S(2)}) copy-start(pred[896,128]{1,0:T(32,128)(4,1)S(1)} %fusion.52) | copy-start | bytes 344068
  61.4 44.1 %collective-permute-start.9 = (bf16[704,2048]{1,0:T(8,128)(2,1)}, bf16[704,2048]{1,0:T(8,128)(2,1)}, u32[]{:S(2)}, u32[]{:S(2)}) collective-permute-start(bf16[704,2048]{1,0:T(8,128)(2,1)} %bitcast.186), channel_id=1, source_target_pairs={{0,1},{1,0},{2,3},{3,2},{4,5},{5,4},{6,7},{7,6},{8,9},{9,8},{10,11... | collective-permute-start | bytes 8650760 | tf_op jit(solution)/shard_map/ppermute | solution.py:89
  129.7 43.7 %copy-start.15 = (bf16[128,2048]{1,0:T(8,128)(2,1)}, bf16[128,2048]{1,0:T(8,128)(2,1)S(1)}, u32[]{:S(2)}) copy-start(bf16[128,2048]{1,0:T(8,128)(2,1)S(1)} %multiply_convert_fusion.7) | copy-start | bytes 1572868
  132.7 97.8 %all-to-all-start.1 = ((bf16[16,56,2048]{2,1,0:T(8,128)(2,1)}), bf16[16,56,2048]{2,1,0:T(8,128)(2,1)}, u32[]{:S(2)}, u32[]{:S(2)}) async-start(bf16[16,56,2048]{2,1,0:T(8,128)(2,1)} %bitcast.158), calls=%async_computation.1 | async-start | bytes 7340032 | tf_op jit(solution)/shard_map/all_to_all | solution.py:865
  189.7 21.2 %slice-start = ((s8[5767168]{0:T(1024)(128)(4,1)}), s8[4194304]{0:T(1024)(128)(4,1)S(1)}, s32[]{:S(2)}) async-start(s8[5767168]{0:T(1024)(128)(4,1)} %bitcast.159), calls=%async_computation.4 | async-start | bytes 8388608
  197.9 13.0 %slice-start.1 = ((s8[5767168]{0:T(1024)(128)(4,1)}), s8[1572864]{0:T(1024)(128)(4,1)S(1)}, s32[]{:S(2)}) async-start(s8[5767168]{0:T(1024)(128)(4,1)} %bitcast.159), calls=%async_computation.5 | async-start | bytes 3145728
  214.1 84.0 %copy-start.14 = (bf16[128,4864]{1,0:T(8,128)(2,1)}, bf16[128,4864]{1,0:T(8,128)(2,1)S(1)}, u32[]{:S(2)}) copy-start(bf16[128,4864]{1,0:T(8,128)(2,1)S(1)} %pad_maximum_fusion.3.refs_0_.refs_4_) | copy-start | bytes 3735556
  230.5 62.3 %collective-permute-start.12 = (bf16[128,4096]{1,0:T(8,128)(2,1)}, bf16[128,4096]{1,0:T(8,128)(2,1)}, u32[]{:S(2)}, u32[]{:S(2)}) collective-permute-start(bf16[128,4096]{1,0:T(8,128)(2,1)} %pad_maximum_fusion.4.refs_0_), channel_id=1, source_target_pairs={{0,4},{2,6},{4,0},{6,2},{8,12},{10,14},{12,8},{14,10},{16,20},{18,... | collective-permute-start | bytes 3145736 | tf_op jit(solution)/shard_map/ppermute | solution.py:85
  232.0 60.8 %collective-permute-start.11 = (bf16[128,7680]{1,0:T(8,128)(2,1)}, bf16[128,7680]{1,0:T(8,128)(2,1)}, u32[]{:S(2)}, u32[]{:S(2)}) collective-permute-start(bf16[128,7680]{1,0:T(8,128)(2,1)} %pad_maximum_fusion.refs_0_.refs_4_), channel_id=1, source_target_pairs={{0,8},{2,10},{4,12},{6,14},{8,0},{10,2},{12,4},{14,6},{16,24},{18,... | collective-permute-start | bytes 5898248 | tf_op jit(solution)/shard_map/ppermute | solution.py:85
  234.1 58.7 %collective-permute-start.10 = (bf16[128,4864]{1,0:T(8,128)(2,1)S(1)}, bf16[128,4864]{1,0:T(8,128)(2,1)}, u32[]{:S(2)}, u32[]{:S(2)}) collective-permute-start(bf16[128,4864]{1,0:T(8,128)(2,1)S(1)} %pad_maximum_fusion.3.refs_0_.refs_4_), channel_id=1, source_target_pairs={{0,2},{2,0},{4,6},{6,4},{8,10},{10,8},{12,14},{14,12},{16,18},{18,... | collective-permute-start | bytes 3735560 | tf_op jit(solution)/shard_map/ppermute | solution.py:85
  292.8 60.0 %collective-permute-start.19 = (bf16[2,704,2048]{2,1,0:T(8,128)(2,1)}, bf16[2,704,2048]{2,1,0:T(8,128)(2,1)}, u32[]{:S(2)}, u32[]{:S(2)}) collective-permute-start(bf16[2,704,2048]{2,1,0:T(8,128)(2,1)} %convolution_convert_fusion), channel_id=1, source_target_pairs={{0,1},{1,0},{2,3},{3,2},{4,5},{5,4},{6,7},{7,6},{8,9},{9,8},{10,11... | collective-permute-start | bytes 17301512 | tf_op jit(solution)/shard_map/ppermute | solution.py:89
  292.9 14.1 %copy-start.59 = (s32[8]{0:T(128)S(1)}, s32[8]{0:T(128)}, u32[]{:S(2)}) copy-start(s32[8]{0:T(128)} %constant.197.clone) | copy-start | bytes 100
  292.9 16.2 %copy-start.58 = (s32[8]{0:T(128)S(1)}, s32[8]{0:T(128)}, u32[]{:S(2)}) copy-start(s32[8]{0:T(128)} %constant.196.clone) | copy-start | bytes 100
  292.9 16.9 %copy-start.56 = (s32[8]{0:T(128)S(1)}, s32[8]{0:T(128)}, u32[]{:S(2)}) copy-start(s32[8]{0:T(128)} %constant.194.clone) | copy-start | bytes 100
  292.9 16.9 %copy-start.57 = (s32[8]{0:T(128)S(1)}, s32[8]{0:T(128)}, u32[]{:S(2)}) copy-start(s32[8]{0:T(128)} %constant.195.clone) | copy-start | bytes 100
  292.9 17.4 %copy-start.45 = (bf16[16,896]{1,0:T(8,128)(2,1)S(1)}, bf16[16,896]{1,0:T(8,128)(2,1)}, u32[]{:S(2)}) copy-start(bf16[16,896]{1,0:T(8,128)(2,1)} %get-tuple-element.186) | copy-start | bytes 86020
  292.9 79.6 %all-to-all-start.2 = ((bf16[16,56,2048]{2,1,0:T(8,128)(2,1)}), bf16[16,56,2048]{2,1,0:T(8,128)(2,1)}, u32[]{:S(2)}, u32[]{:S(2)}) async-start(bf16[16,56,2048]{2,1,0:T(8,128)(2,1)} %bitcast.162), calls=%async_computation.2 | async-start | bytes 7340032 | tf_op jit(solution)/shard_map/all_to_all | solution.py:865
  297.6 10.0 %collective-permute-start.15 = (bf16[128,7680]{1,0:T(8,128)(2,1)}, bf16[128,7680]{1,0:T(8,128)(2,1)}, u32[]{:S(2)}, u32[]{:S(2)}) collective-permute-start(bf16[128,7680]{1,0:T(8,128)(2,1)} %pad_maximum_fusion.refs_0_.refs_4_), channel_id=1, source_target_pairs={{0,1},{1,0},{2,3},{3,2},{4,5},{5,4},{6,7},{7,6},{8,9},{9,8},{10,11... | collective-permute-start | bytes 5898248 | tf_op jit(solution)/shard_map/ppermute | solution.py:89
  298.1 7.7 %collective-permute-start.13 = (bf16[128,4864]{1,0:T(8,128)(2,1)S(1)}, bf16[128,4864]{1,0:T(8,128)(2,1)S(1)}, u32[]{:S(2)}, u32[]{:S(2)}) collective-permute-start(bf16[128,4864]{1,0:T(8,128)(2,1)S(1)} %pad_maximum_fusion.3.refs_0_.refs_4_), channel_id=1, source_target_pairs={{0,1},{1,0},{2,3},{3,2},{4,5},{5,4},{6,7},{7,6},{8,9},{9,8},{10,11... | collective-permute-start | bytes 3735560 | tf_op jit(solution)/shard_map/ppermute | solution.py:89
  298.2 10.7 %collective-permute-start.14 = (bf16[128,4864]{1,0:T(8,128)(2,1)}, bf16[128,4864]{1,0:T(8,128)(2,1)}, u32[]{:S(2)}, u32[]{:S(2)}) collective-permute-start(bf16[128,4864]{1,0:T(8,128)(2,1)} %collective-permute-done.10.refs_1_.refs_5_), channel_id=1, source_target_pairs={{0,1},{1,0},{2,3},{3,2},{4,5},{5,4},{6,7},{7,6},{8,9},{9,8},{10,11... | collective-permute-start | bytes 3735560 | tf_op jit(solution)/shard_map/ppermute | solution.py:89
  298.6 25.0 %collective-permute-start.16 = (bf16[128,7680]{1,0:T(8,128)(2,1)}, bf16[128,7680]{1,0:T(8,128)(2,1)}, u32[]{:S(2)}, u32[]{:S(2)}) collective-permute-start(bf16[128,7680]{1,0:T(8,128)(2,1)} %collective-permute-done.11.refs_1_.refs_5_), channel_id=1, source_target_pairs={{0,1},{1,0},{2,3},{3,2},{4,5},{5,4},{6,7},{7,6},{8,9},{9,8},{10,11... | collective-permute-start | bytes 5898248 | tf_op jit(solution)/shard_map/ppermute | solution.py:89
  306.8 46.0 %collective-permute-start.20 = (bf16[704,2048]{1,0:T(8,128)(2,1)}, bf16[704,2048]{1,0:T(8,128)(2,1)}, u32[]{:S(2)}, u32[]{:S(2)}) collective-permute-start(bf16[704,2048]{1,0:T(8,128)(2,1)} %convolution_convert_fusion.3), channel_id=1, source_target_pairs={{0,1},{1,0},{2,3},{3,2},{4,5},{5,4},{6,7},{7,6},{8,9},{9,8},{10,11... | collective-permute-start | bytes 8650760 | tf_op jit(solution)/shard_map/ppermute | solution.py:89
  307.6 32.6 %collective-permute-start.17 = (bf16[128,4096]{1,0:T(8,128)(2,1)}, bf16[128,4096]{1,0:T(8,128)(2,1)}, u32[]{:S(2)}, u32[]{:S(2)}) collective-permute-start(bf16[128,4096]{1,0:T(8,128)(2,1)} %pad_maximum_fusion.4.refs_0_), channel_id=1, source_target_pairs={{0,1},{1,0},{2,3},{3,2},{4,5},{5,4},{6,7},{7,6},{8,9},{9,8},{10,11... | collective-permute-start | bytes 3145736 | tf_op jit(solution)/shard_map/ppermute | solution.py:89
  309.0 31.2 %collective-permute-start.18 = (bf16[128,4096]{1,0:T(8,128)(2,1)}, bf16[128,4096]{1,0:T(8,128)(2,1)}, u32[]{:S(2)}, u32[]{:S(2)}) collective-permute-start(bf16[128,4096]{1,0:T(8,128)(2,1)} %collective-permute-done.12.refs_1_), channel_id=1, source_target_pairs={{0,1},{1,0},{2,3},{3,2},{4,5},{5,4},{6,7},{7,6},{8,9},{9,8},{10,11... | collective-permute-start | bytes 3145736 | tf_op jit(solution)/shard_map/ppermute | solution.py:89
  329.9 12.9 %copy-start.63 = (bf16[1408,896]{1,0:T(8,128)(2,1)S(1)}, bf16[1408,896]{1,0:T(8,128)(2,1)}, u32[]{:S(2)}) copy-start(bf16[1408,896]{1,0:T(8,128)(2,1)} %get-tuple-element.184) | copy-start | bytes 7569412
  340.2 105.6 %collective-permute-start.22 = (bf16[256,4096]{1,0:T(8,128)(2,1)}, bf16[256,4096]{1,0:T(8,128)(2,1)}, u32[]{:S(2)}, u32[]{:S(2)}) collective-permute-start(bf16[256,4096]{1,0:T(8,128)(2,1)} %get-tuple-element.199), channel_id=1, source_target_pairs={{0,2},{2,0},{4,6},{6,4},{8,10},{10,8},{12,14},{14,12},{16,18},{18,... | collective-permute-start | bytes 6291464 | tf_op jit(solution)/shard_map/ppermute | solution.py:85
  340.8 104.9 %collective-permute-start.21 = (bf16[384,2048]{1,0:T(8,128)(2,1)}, bf16[384,2048]{1,0:T(8,128)(2,1)}, u32[]{:S(2)}, u32[]{:S(2)}) collective-permute-start(bf16[384,2048]{1,0:T(8,128)(2,1)} %get-tuple-element.197), channel_id=1, source_target_pairs={{0,4},{2,6},{4,0},{6,2},{8,12},{10,14},{12,8},{14,10},{16,20},{18,... | collective-permute-start | bytes 4718600 | tf_op jit(solution)/shard_map/ppermute | solution.py:85
  340.8 104.9 %collective-permute-start.23 = (bf16[256,1536]{1,0:T(8,128)(2,1)}, bf16[256,1536]{1,0:T(8,128)(2,1)}, u32[]{:S(2)}, u32[]{:S(2)}) collective-permute-start(bf16[256,1536]{1,0:T(8,128)(2,1)} %get-tuple-element.201), channel_id=1, source_target_pairs={{0,4},{2,6},{4,0},{6,2},{8,12},{10,14},{12,8},{14,10},{16,20},{18,... | collective-permute-start | bytes 2359304 | tf_op jit(solution)/shard_map/ppermute | solution.py:85
  342.8 17.6 %slice-start.2 = ((s8[5046272]{0:T(1024)(128)(4,1)}), s8[4194304]{0:T(1024)(128)(4,1)S(1)}, s32[]{:S(2)}) async-start(s8[5046272]{0:T(1024)(128)(4,1)} %bitcast.191), calls=%async_computation.6 | async-start | bytes 8388608
  347.9 12.6 %slice-start.3 = ((s8[5046272]{0:T(1024)(128)(4,1)}), s8[851968]{0:T(1024)(128)(4,1)S(1)}, s32[]{:S(2)}) async-start(s8[5046272]{0:T(1024)(128)(4,1)} %bitcast.191), calls=%async_computation.7 | async-start | bytes 1703936
  360.5 12.1 %copy-start.31 = (pred[896,128]{1,0:T(32,128)(4,1)S(1)}, pred[896,128]{1,0:T(32,128)(4,1)}, u32[]{:S(2)}) copy-start(pred[896,128]{1,0:T(32,128)(4,1)} %copy-done.30) | copy-start | bytes 344068
  385.6 60.1 %collective-permute-start.24 = (bf16[128,2048]{1,0:T(8,128)(2,1)}, bf16[128,2048]{1,0:T(8,128)(2,1)}, u32[]{:S(2)}, u32[]{:S(2)}) collective-permute-start(bf16[128,2048]{1,0:T(8,128)(2,1)} %get-tuple-element.202.refs_4_), channel_id=1, source_target_pairs={{0,4},{2,6},{4,0},{6,2},{8,12},{10,14},{12,8},{14,10},{16,20},{18,... | collective-permute-start | bytes 1572872 | tf_op jit(solution)/shard_map/ppermute | solution.py:85
  388.5 121.9 %collective-permute-start.32 = (bf16[128,2048]{1,0:T(8,128)(2,1)}, bf16[128,2048]{1,0:T(8,128)(2,1)}, u32[]{:S(2)}, u32[]{:S(2)}) collective-permute-start(bf16[128,2048]{1,0:T(8,128)(2,1)} %get-tuple-element.202.refs_4_), channel_id=1, source_target_pairs={{0,1},{1,0},{2,3},{3,2},{4,5},{5,4},{6,7},{7,6},{8,9},{9,8},{10,11... | collective-permute-start | bytes 1572872 | tf_op jit(solution)/shard_map/ppermute | solution.py:89
  388.5 130.6 %all-to-all-start.3 = ((bf16[16,56,2048]{2,1,0:T(8,128)(2,1)}), bf16[16,56,2048]{2,1,0:T(8,128)(2,1)}, u32[]{:S(2)}, u32[]{:S(2)}) async-start(bf16[16,56,2048]{2,1,0:T(8,128)(2,1)} %bitcast.163), calls=%async_computation.3 | async-start | bytes 7340032 | tf_op jit(solution)/shard_map/all_to_all | solution.py:865
  443.7 86.9 %copy-start = (bf16[128,3072]{1,0:T(8,128)(2,1)}, bf16[128,3072]{1,0:T(8,128)(2,1)S(1)}, u32[]{:S(2)}) copy-start(bf16[128,3072]{1,0:T(8,128)(2,1)S(1)} %get-tuple-element.209.refs_4_) | copy-start | bytes 2359300
  445.8 72.4 %collective-permute-start.25 = (bf16[128,3072]{1,0:T(8,128)(2,1)S(1)}, bf16[128,3072]{1,0:T(8,128)(2,1)S(1)}, u32[]{:S(2)}, u32[]{:S(2)}) collective-permute-start(bf16[128,3072]{1,0:T(8,128)(2,1)S(1)} %get-tuple-element.209.refs_4_), channel_id=1, source_target_pairs={{0,4},{2,6},{4,0},{6,2},{8,12},{10,14},{12,8},{14,10},{16,20},{18,... | collective-permute-start | bytes 2359304 | tf_op jit(solution)/shard_map/ppermute | solution.py:85
  447.8 98.2 %collective-permute-start.27 = (bf16[128,3072]{1,0:T(8,128)(2,1)S(1)}, bf16[128,3072]{1,0:T(8,128)(2,1)}, u32[]{:S(2)}, u32[]{:S(2)}) collective-permute-start(bf16[128,3072]{1,0:T(8,128)(2,1)S(1)} %get-tuple-element.209.refs_4_), channel_id=1, source_target_pairs={{0,1},{1,0},{2,3},{3,2},{4,5},{5,4},{6,7},{7,6},{8,9},{9,8},{10,11... | collective-permute-start | bytes 2359304 | tf_op jit(solution)/shard_map/ppermute | solution.py:89
  451.9 67.1 %collective-permute-start.26 = (bf16[256,4096]{1,0:T(8,128)(2,1)S(1)}, bf16[256,4096]{1,0:T(8,128)(2,1)}, u32[]{:S(2)}, u32[]{:S(2)}) collective-permute-start(bf16[256,4096]{1,0:T(8,128)(2,1)S(1)} %get-tuple-element.307), channel_id=1, source_target_pairs={{0,1},{1,0},{2,3},{3,2},{4,5},{5,4},{6,7},{7,6},{8,9},{9,8},{10,11... | collective-permute-start | bytes 6291464 | tf_op jit(solution)/shard_map/ppermute | solution.py:89
  452.4 58.0 %collective-permute-start.33 = (bf16[128,2048]{1,0:T(8,128)(2,1)}, bf16[128,2048]{1,0:T(8,128)(2,1)S(1)}, u32[]{:S(2)}, u32[]{:S(2)}) collective-permute-start(bf16[128,2048]{1,0:T(8,128)(2,1)} %collective-permute-done.24.refs_5_), channel_id=1, source_target_pairs={{0,1},{1,0},{2,3},{3,2},{4,5},{5,4},{6,7},{7,6},{8,9},{9,8},{10,11... | collective-permute-start | bytes 1572872 | tf_op jit(solution)/shard_map/ppermute | solution.py:89
  510.4 8.9 %copy-start.51 = (f32[128]{0:T(128)S(1)}, f32[128]{0:T(128)}, u32[]{:S(2)}) copy-start(f32[128]{0:T(128)} %copy-done.50) | copy-start | bytes 1540
  510.4 8.9 %copy-start.55 = (f32[32]{0:T(128)S(1)}, f32[32]{0:T(128)}, u32[]{:S(2)}) copy-start(f32[32]{0:T(128)} %copy-done.54) | copy-start | bytes 388
  510.4 9.5 %copy-start.25 = (bf16[1024,576]{0,1:T(8,128)(2,1)S(1)}, bf16[1024,576]{0,1:T(8,128)(2,1)}, u32[]{:S(2)}) copy-start(bf16[1024,576]{0,1:T(8,128)(2,1)} %param.26) | copy-start | bytes 3538948
  520.3 24.6 %collective-permute-start.29 = (bf16[128,640]{1,0:T(8,128)(2,1)S(1)}, bf16[128,640]{1,0:T(8,128)(2,1)S(1)}, u32[]{:S(2)}, u32[]{:S(2)}) collective-permute-start(bf16[128,640]{1,0:T(8,128)(2,1)S(1)} %pad.9), channel_id=1, source_target_pairs={{0,4},{2,6},{4,0},{6,2},{8,12},{10,14},{12,8},{14,10},{16,20},{18,... | collective-permute-start | bytes 491528 | tf_op jit(solution)/shard_map/ppermute | solution.py:85
  524.0 31.4 %collective-permute-start.30 = (bf16[128,640]{1,0:T(8,128)(2,1)S(1)}, bf16[128,640]{1,0:T(8,128)(2,1)}, u32[]{:S(2)}, u32[]{:S(2)}) collective-permute-start(bf16[128,640]{1,0:T(8,128)(2,1)S(1)} %pad.9), channel_id=1, source_target_pairs={{0,1},{1,0},{2,3},{3,2},{4,5},{5,4},{6,7},{7,6},{8,9},{9,8},{10,11... | collective-permute-start | bytes 491528 | tf_op jit(solution)/shard_map/ppermute | solution.py:89
  537.5 7.2 %collective-permute-start.34 = (bf16[16,16,128]{2,1,0:T(8,128)(2,1)S(1)}, bf16[16,16,128]{2,1,0:T(8,128)(2,1)S(1)}, u32[]{:S(2)}, u32[]{:S(2)}) collective-permute-start(bf16[16,16,128]{2,1,0:T(8,128)(2,1)S(1)} %dynamic-slice_bitcast_fusion), channel_id=1, source_target_pairs={{0,1},{1,0},{2,3},{3,2},{4,5},{5,4},{6,7},{7,6},{8,9},{9,8},{10,11... | collective-permute-start | bytes 196616 | tf_op jit(solution)/shard_map/ppermute | solution.py:89
  538.1 7.9 %collective-permute-start.28 = (bf16[128,3072]{1,0:T(8,128)(2,1)}, bf16[128,3072]{1,0:T(8,128)(2,1)S(1)}, u32[]{:S(2)}, u32[]{:S(2)}) collective-permute-start(bf16[128,3072]{1,0:T(8,128)(2,1)} %copy-done.34), channel_id=1, source_target_pairs={{0,1},{1,0},{2,3},{3,2},{4,5},{5,4},{6,7},{7,6},{8,9},{9,8},{10,11... | collective-permute-start | bytes 2359304 | tf_op jit(solution)/shard_map/ppermute | solution.py:89
  544.9 10.5 %collective-permute-start.31 = (bf16[128,640]{1,0:T(8,128)(2,1)S(1)}, bf16[128,640]{1,0:T(8,128)(2,1)S(1)}, u32[]{:S(2)}, u32[]{:S(2)}) collective-permute-start(bf16[128,640]{1,0:T(8,128)(2,1)S(1)} %collective-permute-done.29), channel_id=1, source_target_pairs={{0,1},{1,0},{2,3},{3,2},{4,5},{5,4},{6,7},{7,6},{8,9},{9,8},{10,11... | collective-permute-start | bytes 491528 | tf_op jit(solution)/shard_map/ppermute | solution.py:89
  (44 other events, 196.9 us)

commit v7 on v6

--- a/solution.py
+++ b/solution.py
@@ -154,23 +154,35 @@
     return [own, crossed, swap(own), swap(crossed)]
 
 
-def product_kernel(rows, sources, order_ref, *refs):
+def product_kernel(rows, group, sources, order_ref, *refs):
     lefts, rights = refs[:sources], refs[sources : 2 * sources]
     kept_ref, sent_ref, picked_ref, turned_ref = refs[2 * sources :]
     count = order_ref.shape[0]
     padded = picked_ref.shape[0] // count
+    left_columns = lefts[0].shape[1]
+
+    def turn(block, place):
+        start = 0
+        columns = pl.ds(pl.multiple_of(block * group, group), group) if group < left_columns else slice(None)
+        for left_ref in lefts:
+            tokens = left_ref.shape[0]
+            turned_ref[place * group : (place + 1) * group, start : start + tokens] = (
+                left_ref[:, columns].astype(F32).T
+            )
+            start += tokens
 
     @pl.when(pl.program_id(0) == 0)
     def _():
-        start = 0
-        for left_ref in lefts:
-            tokens = left_ref.shape[0]
-            turned_ref[:, start : start + tokens] = left_ref[...].astype(F32).T
-            start += tokens
         if padded > rows:
             picked_ref[...] = jnp.zeros_like(picked_ref)
+        if group == left_columns:
+            turn(0, 0)
         for j in range(count):
-            start = pl.multiple_of(order_ref[j] * rows, rows)
+            if group < left_columns:
+                turn(order_ref[j] * rows // group, j)
+                start = pl.multiple_of(j * group + order_ref[j] * rows % group, rows)
+            else:
+                start = pl.multiple_of(order_ref[j] * rows, rows)
             picked_ref[j * padded : j * padded + rows, :] = turned_ref[
                 pl.ds(start, rows), :
             ].astype(picked_ref.dtype)
@@ -204,9 +216,11 @@
         picked = jnp.pad(picked, ((0, 0), (0, padded - rows), (0, 0))).reshape(-1, tokens)
         product = dot(picked, right).astype(BF)
         return product[:half], product[half:], picked
-    tile = next(t for t in (512, 384, 256, 128) if columns % t == 0 and start % t == 0)
+    tile = next(t for t in (2048, 1536, 1024, 512, 384, 256, 128) if columns % t == 0 and start % t == 0)
+    group = rows * shards if rows * shards % 128 == 0 else left_columns
+    turned = left_columns if group == left_columns else count * group
     return pl.pallas_call(
-        functools.partial(product_kernel, rows, len(lefts)),
+        functools.partial(product_kernel, rows, group, len(lefts)),
         grid_spec=pltpu.PrefetchScalarGridSpec(
             num_scalar_prefetch=1,
             grid=(columns // tile,),
@@ -226,7 +240,7 @@
                 pl.BlockSpec((half, tile), lambda i, order: (0, i)),
                 pl.BlockSpec((count * padded, tokens), lambda i, order: (0, 0)),
             ],
-            scratch_shapes=[pltpu.VMEM((left_columns, tokens), F32)],
+            scratch_shapes=[pltpu.VMEM((turned, tokens), F32)],
         ),
         out_shape=[
             jax.ShapeDtypeStruct((half, columns), BF),

time: 699 us -> 694 us (level)
  Pallas kernels: 362 us -> 354 us
    all_to_all x4, starting transfers between devices: 53.3 us -> 41 us  [exchange(): lax.all_to_all(rows.reshape(owners, capacity, model_width), 'expert', spl...]
    ppermute x9, starting transfers between devices: 16.4 us -> 28.4 us  [cross(): return lax.ppermute(values, 'expert', [(i, i ^ bit) for i in range(count)])]
    pallas_call x5, Pallas kernels: 42 us -> 34 us  [product_halves(): pl.pallas_call(functools.partial(product_kernel, rows, group, len(lefts))...]
  transfers between devices with their start and end apart: 39 -> 39, of which waited for: 5 -> 7; matrix products, arithmetic and copies ran while one was open for 27% -> 27% of each run, Pallas kernels for 34% -> 34%
where the time goes in v7:
time: 694 us; the launch traced here: 689 us
  Pallas kernels  354 us (51%)
  matrix products  161 us (23%)
  starting transfers between devices  75.7 us (11%)
  waiting for transfers between devices  32.4 us (5%)
  other arithmetic  30.9 us (4%)
  local copies, waits for them, and re-layouts  30.6 us (4%)
    pallas_call x1, Pallas kernels, reduce_all(): pl.pallas_call(functools.partial(reduce_kernel, plans, steps), in_specs=[...  123 us
    dot_general x19, matrix products, dot(): return jnp.dot(left, right, preferred_element_type=F32)  82.9 us
    dot_general x12, matrix products, dot_t(): lax.dot_general(left, right, (((1,), (1,)), ((), ())), preferred_element_...  60.6 us
    pallas_call x1, Pallas kernels, scatter_slot(): pl.pallas_call(scatter_kernel, in_specs=[pl.BlockSpec(memory_space=pltpu....  59.4 us
    all_to_all x4, starting transfers between devices, exchange(): lax.all_to_all(rows.reshape(owners, capacity, model_width), 'expert', spl...  41 us
    pallas_call x1, Pallas kernels, attend_back(): pl.pallas_call(attend_back_kernel, grid_spec=pltpu.PrefetchScalarGridSpec...  40.2 us
    pallas_call x1, Pallas kernels, expert_pass(): pl.pallas_call(functools.partial(expert_kernel, sources), grid_spec=pltpu...  39 us
    pallas_call x5, Pallas kernels, product_halves(): pl.pallas_call(functools.partial(product_kernel, rows, group, len(lefts))...  34 us
  transfers between devices with their start and end apart: 39, of which 7 were waited for; matrix products, arithmetic and copies ran while one was open for 27% of the time, Pallas kernels for 34%

profile of v7, /device:TPU:0, one launch (start us, length us, event | category | flops | bytes accessed | tf_op | source)
XLA Modules:
  0.0 688.7 jit_solution(2501639729325451756)
XLA Ops:
  8.1 4.1 convolution_convert_fusion.2
  13.1 1.8 convolution_add_fusion.6
  15.8 31.9 %shard_map.308 = bf16[16,128,576]{2,1,0:T(8,128)(2,1)S(1)} custom-call(bf16[128,576]{1,0:T(8,128)(2,1)S(1)} %pad_maximum_fusion.7.own_ref), custom_call_target="tpu_custom_call" | custom-call | flops 49999998976 | bytes 4718592 | tf_op jit(solution)/shard_map/pallas_call | solution.py:344
  47.7 1.5 copy-done.1
  49.2 5.1 all-to-all-start
  55.0 3.3 collective-permute-done.5
  62.5 3.9 fusion.66
  67.1 4.8 maximum_select_fusion.expand_ref
  71.9 3.9 convolution_add_fusion.1.raw_ref
  75.9 27.0 %shard_map.309 = (bf16[128,2048]{1,0:T(8,128)(2,1)S(1)}, bf16[2048,576]{1,0:T(8,128)(2,1)S(1)}, bf16[2048,2048]{1,0:T(8,128)(2,1)}, bf16[2048,512]{1,0:T(8,128)(2,1)S(1)}, bf16[128,2048]{1,0:T(8,128)(2,1)S(1)}) custom-call(f32[128,3072]{1,0:T(8,128)S(1)} %convolution_add_fusion.1.raw_ref, f32[128,32]{1,0:T(8,128)S(1)} %get-tuple-element.321.cosine_ref, ...), custom_call_target="tpu_custom_call" | custom-call | flops 9126805504 | bytes 8388608 | tf_op jit(solution)/shard_map/pallas_call | solution.py:577
  105.2 18.7 %all-to-all-done = bf16[16,56,2048]{2,1,0:T(8,128)(2,1)} async-done(((bf16[16,56,2048]{2,1,0:T(8,128)(2,1)}), bf16[16,56,2048]{2,1,0:T(8,128)(2,1)}, u32[]{:S(2)}, u32[]{:S(2)}) %all-to-all-start) | async-done | bytes 3670048 | tf_op jit(solution)/shard_map/all_to_all | solution.py:879
  123.9 3.0 fusion.59
  129.6 2.9 convolution_convert_fusion.1
  132.5 17.4 %all-to-all-start.1 = ((bf16[16,56,2048]{2,1,0:T(8,128)(2,1)}), bf16[16,56,2048]{2,1,0:T(8,128)(2,1)}, u32[]{:S(2)}, u32[]{:S(2)}) async-start(bf16[16,56,2048]{2,1,0:T(8,128)(2,1)} %bitcast.158), calls=%async_computation.1 | async-start | bytes 7340032 | tf_op jit(solution)/shard_map/all_to_all | solution.py:879
  150.0 6.0 fusion.56
  156.0 5.5 fusion.124
  161.5 7.7 %convolution_add_fusion = f32[128,5632]{1,0:T(8,128)} fusion(f32[128,5632]{1,0:T(8,128)S(1)} %fusion.56, bf16[1024,5632]{1,0:T(8,128)(2,1)} %param.32, bf16[128,2048]{1,0:T(8,128)(2,1)S(1)} %multiply_convert_fusion.7, s32[]{:T(128)S(6)} %select_n.233), kind=kOutput, calls=%fused_computation.3 | convolution fusion | flops 1477115904 | bytes 17563652 | tf_op jit(solution)/shard_map/dot_general | solution.py:72
  169.2 5.5 fusion.125
  174.7 3.0 multiply_convert_fusion.5
  177.8 8.2 %fusion.39 = f32[128,1024]{1,0:T(8,128)S(1)} fusion(bf16[1024,5632]{1,0:T(8,128)(2,1)} %param.32, bf16[128,2816]{1,0:T(8,128)(2,1)S(1)} %get-tuple-element.306, bf16[128,2816]{1,0:T(8,128)(2,1)S(1)} %get-tuple-element.305), kind=kOutput, calls=%fused_computation.76 | convolution fusion | flops 1479278592 | bytes 13500416 | tf_op jit(solution)/shard_map/dot_general | solution.py:76
  186.0 8.1 %fusion.38 = f32[128,1024]{1,0:T(8,128)S(1)} fusion(bf16[1024,5632]{1,0:T(8,128)(2,1)} %collective-permute-done.6, bf16[128,2816]{1,0:T(8,128)(2,1)S(1)} %get-tuple-element.306, bf16[128,2816]{1,0:T(8,128)(2,1)S(1)} %get-tuple-element.305), kind=kOutput, calls=%fused_computation.75 | convolution fusion | flops 1479278592 | bytes 13500416 | tf_op jit(solution)/shard_map/dot_general | solution.py:76
  195.3 3.7 fusion.53
  199.0 2.0 convolution_add_fusion.4
  202.2 8.0 %fusion.127.refs_3_ = f32[704,896]{1,0:T(8,128)} fusion(bf16[704,2048]{1,0:T(8,128)(2,1)} %collective-permute-done.9, bf16[896,2048]{1,0:T(8,128)(2,1)} %bitcast.13), kind=kOutput, calls=%fused_computation.235 | convolution fusion | flops 2583691264 | bytes 9076736 | tf_op jit(solution)/shard_map/dot_general | solution.py:76
  210.2 6.8 fusion.126.refs_1_
  219.3 5.4 collective-permute-start.12
  224.6 9.3 %collective-permute-start.11 = (bf16[128,7680]{1,0:T(8,128)(2,1)}, bf16[128,7680]{1,0:T(8,128)(2,1)}, u32[]{:S(2)}, u32[]{:S(2)}) collective-permute-start(bf16[128,7680]{1,0:T(8,128)(2,1)} %pad_maximum_fusion.refs_0_.refs_4_), channel_id=1, source_target_pairs={{0,8},{2,10},{4,12},{6,14},{8,0},{10,2},{12,4},{14,6},{16,24},{18,... | collective-permute-start | bytes 5898248 | tf_op jit(solution)/shard_map/ppermute | solution.py:85
  235.4 39.0 %shard_map.310 = (bf16[896,2048]{1,0:T(8,128)(2,1)}, bf16[1408,896]{1,0:T(8,128)(2,1)}, bf16[2,2,704,896]{3,2,1,0:T(8,128)(2,1)}, f32[1,896]{1,0:T(1,128)}, bf16[16,896]{1,0:T(8,128)(2,1)}) custom-call(s32[1]{0:T(128)} %bitcast.19.here_ref, bf16[896,2048]{1,0:T(8,128)(2,1)} %bitcast.17.rows_ref, bf16[16,2048]{1,0:T(8,128)(2,1)} %bitcast.176, ...), custom_call_target="tpu_custom_call" | custom-call | flops 20669530112 | bytes 18874368 | tf_op jit(solution)/shard_map/pallas_call | solution.py:777
  275.2 7.4 %convolution_convert_fusion.3 = bf16[704,2048]{1,0:T(8,128)(2,1)} fusion(bf16[896,2048]{1,0:T(8,128)(2,1)} %bitcast.13, f32[896]{0:T(1024)S(1)} %reduce, bf16[1408,896]{1,0:T(8,128)(2,1)} %get-tuple-element.184), kind=kOutput, calls=%fused_computation.13 | convolution fusion | flops 2590638080 | bytes 7818752 | tf_op jit(solution)/shard_map/dot_general | solution.py:72
  282.6 10.0 %convolution_convert_fusion = bf16[2,704,2048]{2,1,0:T(8,128)(2,1)} fusion(bf16[896,2048]{1,0:T(8,128)(2,1)} %bitcast.17.rows_ref, bf16[2,2,704,896]{3,2,1,0:T(8,128)(2,1)S(1)} %copy-done.64), kind=kOutput, calls=%fused_computation.5 | convolution fusion | flops 5170266112 | bytes 11960320 | tf_op jit(solution)/shard_map/dot_general | solution.py:72
  292.8 4.7 all-to-all-start.2
  299.2 6.5 collective-permute-done.13.refs_2_.refs_6_
  310.2 3.3 fusion.128
  313.4 10.1 %shard_map.311 = (bf16[384,2048]{1,0:T(8,128)(2,1)}, bf16[384,2048]{1,0:T(8,128)(2,1)}, f32[768,512]{1,0:T(8,128)}) custom-call(s32[8]{0:T(128)} %multiply_add_fusion.4.order_ref, bf16[128,4864]{1,0:T(8,128)(2,1)} %copy-done.14, bf16[128,4864]{1,0:T(8,128)(2,1)} %collective-permute-done.10.refs_1_.refs_5_, bf16[128,4864]{1,0:T(8,128)(2,1)} %copy-done.23, ...), custom_call_target="tpu_custom_call" | custom-call | flops 1610612736 | bytes 8126464 | tf_op jit(solution)/shard_map/pallas_call | solution.py:222
  323.6 5.0 shard_map.313
  328.5 7.0 %shard_map.312 = (bf16[256,4096]{1,0:T(8,128)(2,1)}, bf16[256,4096]{1,0:T(8,128)(2,1)}, bf16[512,512]{1,0:T(8,128)(2,1)}) custom-call(s32[8]{0:T(128)} %get-tuple-element.330.order_ref, bf16[128,7680]{1,0:T(8,128)(2,1)} %pad_maximum_fusion.refs_0_.refs_4_, bf16[128,7680]{1,0:T(8,128)(2,1)} %collective-permute-done.11.refs_1_.refs_5_, ...), custom_call_target="tpu_custom_call" | custom-call | flops 2147483648 | bytes 10485760 | tf_op jit(solution)/shard_map/pallas_call | solution.py:222
  336.2 2.0 collective-permute-start.23
  338.2 5.0 fusion.20
  343.3 4.9 multiply_convert_fusion
  348.2 7.6 %convert_add_fusion.1 = f32[704,2048]{1,0:T(8,128)} fusion(bf16[704,2048]{1,0:T(8,128)(2,1)} %collective-permute-done.20, bf16[896,2048]{1,0:T(8,128)(2,1)} %bitcast.13, f32[896]{0:T(1024)S(1)} %reduce, bf16[1408,896]{1,0:T(8,128)(2,1)S(1)} %copy-done.63), kind=kOutput, calls=%fused_computation.4 | convolution fusion | flops 2592079872 | bytes 13586432 | tf_op jit(solution)/shard_map/dot_general | solution.py:72
  355.9 12.0 %convert_add_fusion = f32[2,704,2048]{2,1,0:T(8,128)} fusion(bf16[2,704,2048]{2,1,0:T(8,128)(2,1)} %collective-permute-done.19, bf16[896,2048]{1,0:T(8,128)(2,1)} %bitcast.17.rows_ref, bf16[2,2,704,896]{3,2,1,0:T(8,128)(2,1)S(1)} %bitcast.192), kind=kOutput, calls=%fused_computation | convolution fusion | flops 5173149696 | bytes 23494656 | tf_op jit(solution)/shard_map/dot_general | solution.py:72
  367.9 1.8 all-to-all-done.2
  369.7 3.7 multiply_reduce_fusion
  373.5 1.5 fusion.118
  376.2 2.6 fusion.129
  378.7 3.9 fusion.130
  382.8 5.6 collective-permute-start.24
  388.3 13.8 %all-to-all-start.3 = ((bf16[16,56,2048]{2,1,0:T(8,128)(2,1)}), bf16[16,56,2048]{2,1,0:T(8,128)(2,1)}, u32[]{:S(2)}, u32[]{:S(2)}) async-start(bf16[16,56,2048]{2,1,0:T(8,128)(2,1)} %bitcast.163), calls=%async_computation.3 | async-start | bytes 7340032 | tf_op jit(solution)/shard_map/all_to_all | solution.py:879
  403.2 40.2 %shard_map.314 = (bf16[128,3072]{1,0:T(8,128)(2,1)S(1)}, bf16[512,4096]{1,0:T(8,128)(2,1)}, bf16[2048,576]{1,0:T(8,128)(2,1)}) custom-call(s32[32]{0:T(128)S(1)} %add.354.order_ref, bf16[128,2048]{1,0:T(8,128)(2,1)S(1)} %fusion.36.grad_ref, bf16[512,4096]{1,0:T(8,128)(2,1)} %maximum_select_fusion.expand_ref, bf16[2048,576]{1,0:T(8,128)(2,1)} %bitcast.155, ...), custom_call_target="tpu_custom_call" | custom-call | flops 22548578304 | bytes 8388608 | tf_op jit(solution)/shard_map/pallas_call | solution.py:669
  445.5 1.9 collective-permute-start.25
  447.4 4.1 fusion.120
  452.0 59.4 %shard_map.315 = f32[128,576]{1,0:T(8,128)S(1)} custom-call(bf16[16,128,576]{2,1,0:T(8,128)(2,1)S(1)} %bitcast.157), custom_call_target="tpu_custom_call" | custom-call | flops 49999998976 | bytes 4718592 | tf_op jit(solution)/shard_map/pallas_call | solution.py:431
  512.3 5.6 shard_map.317
  520.0 2.0 collective-permute-start.29
  522.0 5.0 fusion.133
  527.0 1.6 fusion.132
  528.7 5.0 fusion.134
  536.2 2.7 fusion.47
  538.9 3.9 fusion.13
  544.9 6.3 shard_map.316
  551.3 1.6 convolution_convert_fusion.4
  553.8 123.0 %shard_map.318 = (f32[64,640]{1,0:T(8,128)}, f32[96,2048]{1,0:T(8,128)}, f32[16,4096]{1,0:T(8,128)}, f32[64,3072]{1,0:T(8,128)}, f32[64,4096]{1,0:T(8,128)}, /*i...) custom-call(bf16[256,640]{1,0:T(8,128)(2,1)} %get-tuple-element.311.refs_0_, ...), custom_call_target="tpu_custom_call" | custom-call | flops 99999997952 | bytes 38141952 | tf_op jit(solution)/shard_map/pallas_call | solution.py:517
  680.1 2.1 slice.118
  682.9 2.6 pad_maximum_fusion.2
  (289 shorter events, 51.8 us)
Async XLA Ops:
  0.6 11.6 %copy-start.12 = (bf16[1,128,2048]{2,1,0:T(8,128)(2,1)S(1)}, bf16[1,128,2048]{2,1,0:T(8,128)(2,1)}, u32[]{:S(2)}) copy-start(bf16[1,128,2048]{2,1,0:T(8,128)(2,1)} %param.21) | copy-start | bytes 1572868
  1.4 10.7 %collective-permute-start = (bf16[1,2304]{1,0:T(2,128)(2,1)S(1)}, bf16[1,2304]{1,0:T(2,128)(2,1)S(1)}, u32[]{:S(2)}, u32[]{:S(2)}) collective-permute-start(bf16[1,2304]{1,0:T(2,128)(2,1)S(1)} %broadcast_in_dim.24), channel_id=1, source_target_pairs={{0,1},{1,0},{2,3},{3,2},{4,5},{5,4},{6,7},{7,6},{8,9},{9,8},{10,11... | collective-permute-start | bytes 13832 | tf_op jit(solution)/shard_map/ppermute | solution.py:89
  2.0 11.1 %collective-permute-start.3 = (bf16[1024,576]{0,1:T(8,128)(2,1)}, bf16[1024,576]{0,1:T(8,128)(2,1)}, u32[]{:S(2)}, u32[]{:S(2)}) collective-permute-start(bf16[1024,576]{0,1:T(8,128)(2,1)} %param.26), channel_id=1, source_target_pairs={{0,1},{1,0},{2,3},{3,2},{4,5},{5,4},{6,7},{7,6},{8,9},{9,8},{10,11... | collective-permute-start | bytes 3538952 | tf_op jit(solution)/shard_map/ppermute | solution.py:89
  2.0 59.1 %collective-permute-start.1 = (bf16[1024,3072]{1,0:T(8,128)(2,1)}, bf16[1024,3072]{1,0:T(8,128)(2,1)}, u32[]{:S(2)}, u32[]{:S(2)}) collective-permute-start(bf16[1024,3072]{1,0:T(8,128)(2,1)} %param.25), channel_id=1, source_target_pairs={{0,1},{1,0},{2,3},{3,2},{4,5},{5,4},{6,7},{7,6},{8,9},{9,8},{10,11... | collective-permute-start | bytes 18874376 | tf_op jit(solution)/shard_map/ppermute | solution.py:89
  5.7 9.4 %copy-start.50 = (f32[128]{0:T(128)}, f32[128]{0:T(128)S(1)}, u32[]{:S(2)}) copy-start(f32[128]{0:T(128)S(1)} %fusion.113) | copy-start | bytes 1540
  5.8 55.8 %copy-start.48 = (f32[128]{0:T(128)}, f32[128]{0:T(128)S(1)}, u32[]{:S(2)}) copy-start(f32[128]{0:T(128)S(1)} %compare_convert_fusion) | copy-start | bytes 1540
  12.5 59.4 %copy-start.17 = (bf16[128,2048]{1,0:T(8,128)(2,1)}, bf16[128,2048]{1,0:T(8,128)(2,1)S(1)}, u32[]{:S(2)}) copy-start(bf16[128,2048]{1,0:T(8,128)(2,1)S(1)} %fusion.28) | copy-start | bytes 1572868
  14.9 32.8 %copy-start.21 = (f32[128,576]{1,0:T(8,128)}, f32[128,576]{1,0:T(8,128)S(1)}, u32[]{:S(2)}) copy-start(f32[128,576]{1,0:T(8,128)S(1)} %convolution_add_fusion.6) | copy-start | bytes 884740
  15.0 32.6 %copy-start.52 = (f32[128]{0:T(128)}, f32[128]{0:T(128)S(1)}, u32[]{:S(2)}) copy-start(f32[128]{0:T(128)S(1)} %add_rsqrt_fusion.1) | copy-start | bytes 1540
  15.6 108.3 %collective-permute-start.6 = (bf16[1024,5632]{1,0:T(8,128)(2,1)}, bf16[1024,5632]{1,0:T(8,128)(2,1)}, u32[]{:S(2)}, u32[]{:S(2)}) collective-permute-start(bf16[1024,5632]{1,0:T(8,128)(2,1)} %param.32), channel_id=1, source_target_pairs={{0,1},{1,0},{2,3},{3,2},{4,5},{5,4},{6,7},{7,6},{8,9},{9,8},{10,11... | collective-permute-start | bytes 34603016 | tf_op jit(solution)/shard_map/ppermute | solution.py:89
  49.2 12.4 %copy-start.26 = (bf16[1,128,2048]{2,1,0:T(8,128)(2,1)S(1)}, bf16[1,128,2048]{2,1,0:T(8,128)(2,1)}, u32[]{:S(2)}) copy-start(bf16[1,128,2048]{2,1,0:T(8,128)(2,1)} %param.36) | copy-start | bytes 1572868
  49.2 74.7 %all-to-all-start = ((bf16[16,56,2048]{2,1,0:T(8,128)(2,1)}), bf16[16,56,2048]{2,1,0:T(8,128)(2,1)}, u32[]{:S(2)}, u32[]{:S(2)}) async-start(bf16[16,56,2048]{2,1,0:T(8,128)(2,1)} %bitcast.161), calls=%async_computation | async-start | bytes 7340032 | tf_op jit(solution)/shard_map/all_to_all | solution.py:879
  54.3 4.6 collective-permute-start.2
  54.4 3.9 collective-permute-start.5
  54.9 50.3 %collective-permute-start.7 = (bf16[1408,2048]{1,0:T(8,128)(2,1)}, bf16[1408,2048]{1,0:T(8,128)(2,1)}, u32[]{:S(2)}, u32[]{:S(2)}) collective-permute-start(bf16[1408,2048]{1,0:T(8,128)(2,1)} %param.33), channel_id=1, source_target_pairs={{0,1},{1,0},{2,3},{3,2},{4,5},{5,4},{6,7},{7,6},{8,9},{9,8},{10,11... | collective-permute-start | bytes 17301512 | tf_op jit(solution)/shard_map/ppermute | solution.py:89
  58.3 46.9 %collective-permute-start.8 = (bf16[2,704,2048]{2,1,0:T(8,128)(2,1)}, bf16[2,704,2048]{2,1,0:T(8,128)(2,1)}, u32[]{:S(2)}, u32[]{:S(2)}) collective-permute-start(bf16[2,704,2048]{2,1,0:T(8,128)(2,1)} %bitcast.184), channel_id=1, source_target_pairs={{0,1},{1,0},{2,3},{3,2},{4,5},{5,4},{6,7},{7,6},{8,9},{9,8},{10,11... | collective-permute-start | bytes 17301512 | tf_op jit(solution)/shard_map/ppermute | solution.py:89
  59.0 46.2 %collective-permute-start.4 = (bf16[1024,2048]{1,0:T(8,128)(2,1)}, bf16[1024,2048]{1,0:T(8,128)(2,1)}, u32[]{:S(2)}, u32[]{:S(2)}) collective-permute-start(bf16[1024,2048]{1,0:T(8,128)(2,1)} %param.29), channel_id=1, source_target_pairs={{0,1},{1,0},{2,3},{3,2},{4,5},{5,4},{6,7},{7,6},{8,9},{9,8},{10,11... | collective-permute-start | bytes 12582920 | tf_op jit(solution)/shard_map/ppermute | solution.py:89
  59.4 70.2 %copy-start.30 = (pred[896,128]{1,0:T(32,128)(4,1)}, pred[896,128]{1,0:T(32,128)(4,1)S(1)}, u32[]{:S(2)}) copy-start(pred[896,128]{1,0:T(32,128)(4,1)S(1)} %fusion.52) | copy-start | bytes 344068
  61.2 44.1 %collective-permute-start.9 = (bf16[704,2048]{1,0:T(8,128)(2,1)}, bf16[704,2048]{1,0:T(8,128)(2,1)}, u32[]{:S(2)}, u32[]{:S(2)}) collective-permute-start(bf16[704,2048]{1,0:T(8,128)(2,1)} %bitcast.186), channel_id=1, source_target_pairs={{0,1},{1,0},{2,3},{3,2},{4,5},{5,4},{6,7},{7,6},{8,9},{9,8},{10,11... | collective-permute-start | bytes 8650760 | tf_op jit(solution)/shard_map/ppermute | solution.py:89
  129.6 31.9 %copy-start.15 = (bf16[128,2048]{1,0:T(8,128)(2,1)}, bf16[128,2048]{1,0:T(8,128)(2,1)S(1)}, u32[]{:S(2)}) copy-start(bf16[128,2048]{1,0:T(8,128)(2,1)S(1)} %multiply_convert_fusion.7) | copy-start | bytes 1572868
  132.5 86.8 %all-to-all-start.1 = ((bf16[16,56,2048]{2,1,0:T(8,128)(2,1)}), bf16[16,56,2048]{2,1,0:T(8,128)(2,1)}, u32[]{:S(2)}, u32[]{:S(2)}) async-start(bf16[16,56,2048]{2,1,0:T(8,128)(2,1)} %bitcast.158), calls=%async_computation.1 | async-start | bytes 7340032 | tf_op jit(solution)/shard_map/all_to_all | solution.py:879
  177.8 21.2 %slice-start = ((s8[5767168]{0:T(1024)(128)(4,1)}), s8[4194304]{0:T(1024)(128)(4,1)S(1)}, s32[]{:S(2)}) async-start(s8[5767168]{0:T(1024)(128)(4,1)} %bitcast.159), calls=%async_computation.4 | async-start | bytes 8388608
  186.0 13.0 %slice-start.1 = ((s8[5767168]{0:T(1024)(128)(4,1)}), s8[1572864]{0:T(1024)(128)(4,1)S(1)}, s32[]{:S(2)}) async-start(s8[5767168]{0:T(1024)(128)(4,1)} %bitcast.159), calls=%async_computation.5 | async-start | bytes 3145728
  202.2 95.8 %copy-start.14 = (bf16[128,4864]{1,0:T(8,128)(2,1)}, bf16[128,4864]{1,0:T(8,128)(2,1)S(1)}, u32[]{:S(2)}) copy-start(bf16[128,4864]{1,0:T(8,128)(2,1)S(1)} %pad_maximum_fusion.3.refs_0_.refs_4_) | copy-start | bytes 3735556
  202.2 8.0 %copy-start.61 = (bf16[1,704,2048]{2,1,0:T(8,128)(2,1)S(1)}, bf16[1,704,2048]{2,1,0:T(8,128)(2,1)}, u32[]{:S(2)}) copy-start(bf16[1,704,2048]{2,1,0:T(8,128)(2,1)} %param.35) | copy-start | bytes 8650756
  219.3 73.4 %collective-permute-start.12 = (bf16[128,4096]{1,0:T(8,128)(2,1)}, bf16[128,4096]{1,0:T(8,128)(2,1)}, u32[]{:S(2)}, u32[]{:S(2)}) collective-permute-start(bf16[128,4096]{1,0:T(8,128)(2,1)} %pad_maximum_fusion.4.refs_0_), channel_id=1, source_target_pairs={{0,4},{2,6},{4,0},{6,2},{8,12},{10,14},{12,8},{14,10},{16,20},{18,... | collective-permute-start | bytes 3145736 | tf_op jit(solution)/shard_map/ppermute | solution.py:85
  224.6 68.0 %collective-permute-start.11 = (bf16[128,7680]{1,0:T(8,128)(2,1)}, bf16[128,7680]{1,0:T(8,128)(2,1)}, u32[]{:S(2)}, u32[]{:S(2)}) collective-permute-start(bf16[128,7680]{1,0:T(8,128)(2,1)} %pad_maximum_fusion.refs_0_.refs_4_), channel_id=1, source_target_pairs={{0,8},{2,10},{4,12},{6,14},{8,0},{10,2},{12,4},{14,6},{16,24},{18,... | collective-permute-start | bytes 5898248 | tf_op jit(solution)/shard_map/ppermute | solution.py:85
  234.0 58.7 %collective-permute-start.10 = (bf16[128,4864]{1,0:T(8,128)(2,1)S(1)}, bf16[128,4864]{1,0:T(8,128)(2,1)}, u32[]{:S(2)}, u32[]{:S(2)}) collective-permute-start(bf16[128,4864]{1,0:T(8,128)(2,1)S(1)} %pad_maximum_fusion.3.refs_0_.refs_4_), channel_id=1, source_target_pairs={{0,2},{2,0},{4,6},{6,4},{8,10},{10,8},{12,14},{14,12},{16,18},{18,... | collective-permute-start | bytes 3735560 | tf_op jit(solution)/shard_map/ppermute | solution.py:85
  292.6 55.6 %collective-permute-start.19 = (bf16[2,704,2048]{2,1,0:T(8,128)(2,1)}, bf16[2,704,2048]{2,1,0:T(8,128)(2,1)}, u32[]{:S(2)}, u32[]{:S(2)}) collective-permute-start(bf16[2,704,2048]{2,1,0:T(8,128)(2,1)} %convolution_convert_fusion), channel_id=1, source_target_pairs={{0,1},{1,0},{2,3},{3,2},{4,5},{5,4},{6,7},{7,6},{8,9},{9,8},{10,11... | collective-permute-start | bytes 17301512 | tf_op jit(solution)/shard_map/ppermute | solution.py:89
  292.7 14.1 %copy-start.59 = (s32[8]{0:T(128)S(1)}, s32[8]{0:T(128)}, u32[]{:S(2)}) copy-start(s32[8]{0:T(128)} %constant.197.clone) | copy-start | bytes 100
  292.7 16.2 %copy-start.58 = (s32[8]{0:T(128)S(1)}, s32[8]{0:T(128)}, u32[]{:S(2)}) copy-start(s32[8]{0:T(128)} %constant.196.clone) | copy-start | bytes 100
  292.8 16.9 %copy-start.56 = (s32[8]{0:T(128)S(1)}, s32[8]{0:T(128)}, u32[]{:S(2)}) copy-start(s32[8]{0:T(128)} %constant.194.clone) | copy-start | bytes 100
  292.8 16.9 %copy-start.57 = (s32[8]{0:T(128)S(1)}, s32[8]{0:T(128)}, u32[]{:S(2)}) copy-start(s32[8]{0:T(128)} %constant.195.clone) | copy-start | bytes 100
  292.8 17.4 %copy-start.45 = (bf16[16,896]{1,0:T(8,128)(2,1)S(1)}, bf16[16,896]{1,0:T(8,128)(2,1)}, u32[]{:S(2)}) copy-start(bf16[16,896]{1,0:T(8,128)(2,1)} %get-tuple-element.186) | copy-start | bytes 86020
  292.8 76.9 %all-to-all-start.2 = ((bf16[16,56,2048]{2,1,0:T(8,128)(2,1)}), bf16[16,56,2048]{2,1,0:T(8,128)(2,1)}, u32[]{:S(2)}, u32[]{:S(2)}) async-start(bf16[16,56,2048]{2,1,0:T(8,128)(2,1)} %bitcast.162), calls=%async_computation.2 | async-start | bytes 7340032 | tf_op jit(solution)/shard_map/all_to_all | solution.py:879
  297.5 10.0 %collective-permute-start.15 = (bf16[128,7680]{1,0:T(8,128)(2,1)}, bf16[128,7680]{1,0:T(8,128)(2,1)}, u32[]{:S(2)}, u32[]{:S(2)}) collective-permute-start(bf16[128,7680]{1,0:T(8,128)(2,1)} %pad_maximum_fusion.refs_0_.refs_4_), channel_id=1, source_target_pairs={{0,1},{1,0},{2,3},{3,2},{4,5},{5,4},{6,7},{7,6},{8,9},{9,8},{10,11... | collective-permute-start | bytes 5898248 | tf_op jit(solution)/shard_map/ppermute | solution.py:89
  298.0 7.7 %collective-permute-start.13 = (bf16[128,4864]{1,0:T(8,128)(2,1)S(1)}, bf16[128,4864]{1,0:T(8,128)(2,1)S(1)}, u32[]{:S(2)}, u32[]{:S(2)}) collective-permute-start(bf16[128,4864]{1,0:T(8,128)(2,1)S(1)} %pad_maximum_fusion.3.refs_0_.refs_4_), channel_id=1, source_target_pairs={{0,1},{1,0},{2,3},{3,2},{4,5},{5,4},{6,7},{7,6},{8,9},{9,8},{10,11... | collective-permute-start | bytes 3735560 | tf_op jit(solution)/shard_map/ppermute | solution.py:89
  298.1 10.7 %collective-permute-start.14 = (bf16[128,4864]{1,0:T(8,128)(2,1)}, bf16[128,4864]{1,0:T(8,128)(2,1)}, u32[]{:S(2)}, u32[]{:S(2)}) collective-permute-start(bf16[128,4864]{1,0:T(8,128)(2,1)} %collective-permute-done.10.refs_1_.refs_5_), channel_id=1, source_target_pairs={{0,1},{1,0},{2,3},{3,2},{4,5},{5,4},{6,7},{7,6},{8,9},{9,8},{10,11... | collective-permute-start | bytes 3735560 | tf_op jit(solution)/shard_map/ppermute | solution.py:89
  298.5 25.0 %collective-permute-start.16 = (bf16[128,7680]{1,0:T(8,128)(2,1)}, bf16[128,7680]{1,0:T(8,128)(2,1)}, u32[]{:S(2)}, u32[]{:S(2)}) collective-permute-start(bf16[128,7680]{1,0:T(8,128)(2,1)} %collective-permute-done.11.refs_1_.refs_5_), channel_id=1, source_target_pairs={{0,1},{1,0},{2,3},{3,2},{4,5},{5,4},{6,7},{7,6},{8,9},{9,8},{10,11... | collective-permute-start | bytes 5898248 | tf_op jit(solution)/shard_map/ppermute | solution.py:89
  306.7 41.5 %collective-permute-start.20 = (bf16[704,2048]{1,0:T(8,128)(2,1)}, bf16[704,2048]{1,0:T(8,128)(2,1)}, u32[]{:S(2)}, u32[]{:S(2)}) collective-permute-start(bf16[704,2048]{1,0:T(8,128)(2,1)} %convolution_convert_fusion.3), channel_id=1, source_target_pairs={{0,1},{1,0},{2,3},{3,2},{4,5},{5,4},{6,7},{7,6},{8,9},{9,8},{10,11... | collective-permute-start | bytes 8650760 | tf_op jit(solution)/shard_map/ppermute | solution.py:89
  307.4 28.1 %collective-permute-start.17 = (bf16[128,4096]{1,0:T(8,128)(2,1)}, bf16[128,4096]{1,0:T(8,128)(2,1)}, u32[]{:S(2)}, u32[]{:S(2)}) collective-permute-start(bf16[128,4096]{1,0:T(8,128)(2,1)} %pad_maximum_fusion.4.refs_0_), channel_id=1, source_target_pairs={{0,1},{1,0},{2,3},{3,2},{4,5},{5,4},{6,7},{7,6},{8,9},{9,8},{10,11... | collective-permute-start | bytes 3145736 | tf_op jit(solution)/shard_map/ppermute | solution.py:89
  308.8 26.7 %collective-permute-start.18 = (bf16[128,4096]{1,0:T(8,128)(2,1)}, bf16[128,4096]{1,0:T(8,128)(2,1)}, u32[]{:S(2)}, u32[]{:S(2)}) collective-permute-start(bf16[128,4096]{1,0:T(8,128)(2,1)} %collective-permute-done.12.refs_1_), channel_id=1, source_target_pairs={{0,1},{1,0},{2,3},{3,2},{4,5},{5,4},{6,7},{7,6},{8,9},{9,8},{10,11... | collective-permute-start | bytes 3145736 | tf_op jit(solution)/shard_map/ppermute | solution.py:89
  328.5 9.7 %copy-start.63 = (bf16[1408,896]{1,0:T(8,128)(2,1)S(1)}, bf16[1408,896]{1,0:T(8,128)(2,1)}, u32[]{:S(2)}) copy-start(bf16[1408,896]{1,0:T(8,128)(2,1)} %get-tuple-element.184) | copy-start | bytes 7569412
  335.6 109.9 %collective-permute-start.22 = (bf16[256,4096]{1,0:T(8,128)(2,1)}, bf16[256,4096]{1,0:T(8,128)(2,1)}, u32[]{:S(2)}, u32[]{:S(2)}) collective-permute-start(bf16[256,4096]{1,0:T(8,128)(2,1)} %get-tuple-element.199), channel_id=1, source_target_pairs={{0,2},{2,0},{4,6},{6,4},{8,10},{10,8},{12,14},{14,12},{16,18},{18,... | collective-permute-start | bytes 6291464 | tf_op jit(solution)/shard_map/ppermute | solution.py:85
  336.2 109.2 %collective-permute-start.21 = (bf16[384,2048]{1,0:T(8,128)(2,1)}, bf16[384,2048]{1,0:T(8,128)(2,1)}, u32[]{:S(2)}, u32[]{:S(2)}) collective-permute-start(bf16[384,2048]{1,0:T(8,128)(2,1)} %get-tuple-element.197), channel_id=1, source_target_pairs={{0,4},{2,6},{4,0},{6,2},{8,12},{10,14},{12,8},{14,10},{16,20},{18,... | collective-permute-start | bytes 4718600 | tf_op jit(solution)/shard_map/ppermute | solution.py:85
  336.2 109.2 %collective-permute-start.23 = (bf16[256,1536]{1,0:T(8,128)(2,1)}, bf16[256,1536]{1,0:T(8,128)(2,1)}, u32[]{:S(2)}, u32[]{:S(2)}) collective-permute-start(bf16[256,1536]{1,0:T(8,128)(2,1)} %get-tuple-element.201), channel_id=1, source_target_pairs={{0,4},{2,6},{4,0},{6,2},{8,12},{10,14},{12,8},{14,10},{16,20},{18,... | collective-permute-start | bytes 2359304 | tf_op jit(solution)/shard_map/ppermute | solution.py:85
  338.2 17.6 %slice-start.2 = ((s8[5046272]{0:T(1024)(128)(4,1)}), s8[4194304]{0:T(1024)(128)(4,1)S(1)}, s32[]{:S(2)}) async-start(s8[5046272]{0:T(1024)(128)(4,1)} %bitcast.191), calls=%async_computation.6 | async-start | bytes 8388608
  343.3 12.6 %slice-start.3 = ((s8[5046272]{0:T(1024)(128)(4,1)}), s8[851968]{0:T(1024)(128)(4,1)S(1)}, s32[]{:S(2)}) async-start(s8[5046272]{0:T(1024)(128)(4,1)} %bitcast.191), calls=%async_computation.7 | async-start | bytes 1703936
  355.9 13.8 %copy-start.31 = (pred[896,128]{1,0:T(32,128)(4,1)S(1)}, pred[896,128]{1,0:T(32,128)(4,1)}, u32[]{:S(2)}) copy-start(pred[896,128]{1,0:T(32,128)(4,1)} %copy-done.30) | copy-start | bytes 344068
  382.8 62.7 %collective-permute-start.24 = (bf16[128,2048]{1,0:T(8,128)(2,1)}, bf16[128,2048]{1,0:T(8,128)(2,1)}, u32[]{:S(2)}, u32[]{:S(2)}) collective-permute-start(bf16[128,2048]{1,0:T(8,128)(2,1)} %get-tuple-element.202.refs_4_), channel_id=1, source_target_pairs={{0,4},{2,6},{4,0},{6,2},{8,12},{10,14},{12,8},{14,10},{16,20},{18,... | collective-permute-start | bytes 1572872 | tf_op jit(solution)/shard_map/ppermute | solution.py:85
  388.3 123.1 %collective-permute-start.32 = (bf16[128,2048]{1,0:T(8,128)(2,1)}, bf16[128,2048]{1,0:T(8,128)(2,1)}, u32[]{:S(2)}, u32[]{:S(2)}) collective-permute-start(bf16[128,2048]{1,0:T(8,128)(2,1)} %get-tuple-element.202.refs_4_), channel_id=1, source_target_pairs={{0,1},{1,0},{2,3},{3,2},{4,5},{5,4},{6,7},{7,6},{8,9},{9,8},{10,11... | collective-permute-start | bytes 1572872 | tf_op jit(solution)/shard_map/ppermute | solution.py:89
  388.3 130.4 %all-to-all-start.3 = ((bf16[16,56,2048]{2,1,0:T(8,128)(2,1)}), bf16[16,56,2048]{2,1,0:T(8,128)(2,1)}, u32[]{:S(2)}, u32[]{:S(2)}) async-start(bf16[16,56,2048]{2,1,0:T(8,128)(2,1)} %bitcast.163), calls=%async_computation.3 | async-start | bytes 7340032 | tf_op jit(solution)/shard_map/all_to_all | solution.py:879
  443.4 85.3 %copy-start = (bf16[128,3072]{1,0:T(8,128)(2,1)}, bf16[128,3072]{1,0:T(8,128)(2,1)S(1)}, u32[]{:S(2)}) copy-start(bf16[128,3072]{1,0:T(8,128)(2,1)S(1)} %get-tuple-element.209.refs_4_) | copy-start | bytes 2359300
  445.5 72.4 %collective-permute-start.25 = (bf16[128,3072]{1,0:T(8,128)(2,1)S(1)}, bf16[128,3072]{1,0:T(8,128)(2,1)S(1)}, u32[]{:S(2)}, u32[]{:S(2)}) collective-permute-start(bf16[128,3072]{1,0:T(8,128)(2,1)S(1)} %get-tuple-element.209.refs_4_), channel_id=1, source_target_pairs={{0,4},{2,6},{4,0},{6,2},{8,12},{10,14},{12,8},{14,10},{16,20},{18,... | collective-permute-start | bytes 2359304 | tf_op jit(solution)/shard_map/ppermute | solution.py:85
  447.4 96.6 %collective-permute-start.27 = (bf16[128,3072]{1,0:T(8,128)(2,1)S(1)}, bf16[128,3072]{1,0:T(8,128)(2,1)}, u32[]{:S(2)}, u32[]{:S(2)}) collective-permute-start(bf16[128,3072]{1,0:T(8,128)(2,1)S(1)} %get-tuple-element.209.refs_4_), channel_id=1, source_target_pairs={{0,1},{1,0},{2,3},{3,2},{4,5},{5,4},{6,7},{7,6},{8,9},{9,8},{10,11... | collective-permute-start | bytes 2359304 | tf_op jit(solution)/shard_map/ppermute | solution.py:89
  451.5 67.2 %collective-permute-start.26 = (bf16[256,4096]{1,0:T(8,128)(2,1)S(1)}, bf16[256,4096]{1,0:T(8,128)(2,1)}, u32[]{:S(2)}, u32[]{:S(2)}) collective-permute-start(bf16[256,4096]{1,0:T(8,128)(2,1)S(1)} %get-tuple-element.307), channel_id=1, source_target_pairs={{0,1},{1,0},{2,3},{3,2},{4,5},{5,4},{6,7},{7,6},{8,9},{9,8},{10,11... | collective-permute-start | bytes 6291464 | tf_op jit(solution)/shard_map/ppermute | solution.py:89
  452.0 59.5 %collective-permute-start.33 = (bf16[128,2048]{1,0:T(8,128)(2,1)}, bf16[128,2048]{1,0:T(8,128)(2,1)S(1)}, u32[]{:S(2)}, u32[]{:S(2)}) collective-permute-start(bf16[128,2048]{1,0:T(8,128)(2,1)} %collective-permute-done.24.refs_5_), channel_id=1, source_target_pairs={{0,1},{1,0},{2,3},{3,2},{4,5},{5,4},{6,7},{7,6},{8,9},{9,8},{10,11... | collective-permute-start | bytes 1572872 | tf_op jit(solution)/shard_map/ppermute | solution.py:89
  511.5 8.1 %copy-start.25 = (bf16[1024,576]{0,1:T(8,128)(2,1)S(1)}, bf16[1024,576]{0,1:T(8,128)(2,1)}, u32[]{:S(2)}) copy-start(bf16[1024,576]{0,1:T(8,128)(2,1)} %param.26) | copy-start | bytes 3538948
  520.0 22.9 %collective-permute-start.29 = (bf16[128,640]{1,0:T(8,128)(2,1)S(1)}, bf16[128,640]{1,0:T(8,128)(2,1)S(1)}, u32[]{:S(2)}, u32[]{:S(2)}) collective-permute-start(bf16[128,640]{1,0:T(8,128)(2,1)S(1)} %pad.9), channel_id=1, source_target_pairs={{0,4},{2,6},{4,0},{6,2},{8,12},{10,14},{12,8},{14,10},{16,20},{18,... | collective-permute-start | bytes 491528 | tf_op jit(solution)/shard_map/ppermute | solution.py:85
  522.0 29.2 %collective-permute-start.30 = (bf16[128,640]{1,0:T(8,128)(2,1)S(1)}, bf16[128,640]{1,0:T(8,128)(2,1)}, u32[]{:S(2)}, u32[]{:S(2)}) collective-permute-start(bf16[128,640]{1,0:T(8,128)(2,1)S(1)} %pad.9), channel_id=1, source_target_pairs={{0,1},{1,0},{2,3},{3,2},{4,5},{5,4},{6,7},{7,6},{8,9},{9,8},{10,11... | collective-permute-start | bytes 491528 | tf_op jit(solution)/shard_map/ppermute | solution.py:89
  535.5 7.3 %collective-permute-start.34 = (bf16[16,16,128]{2,1,0:T(8,128)(2,1)S(1)}, bf16[16,16,128]{2,1,0:T(8,128)(2,1)S(1)}, u32[]{:S(2)}, u32[]{:S(2)}) collective-permute-start(bf16[16,16,128]{2,1,0:T(8,128)(2,1)S(1)} %dynamic-slice_bitcast_fusion), channel_id=1, source_target_pairs={{0,1},{1,0},{2,3},{3,2},{4,5},{5,4},{6,7},{7,6},{8,9},{9,8},{10,11... | collective-permute-start | bytes 196616 | tf_op jit(solution)/shard_map/ppermute | solution.py:89
  536.1 7.9 %collective-permute-start.28 = (bf16[128,3072]{1,0:T(8,128)(2,1)}, bf16[128,3072]{1,0:T(8,128)(2,1)S(1)}, u32[]{:S(2)}, u32[]{:S(2)}) collective-permute-start(bf16[128,3072]{1,0:T(8,128)(2,1)} %copy-done.34), channel_id=1, source_target_pairs={{0,1},{1,0},{2,3},{3,2},{4,5},{5,4},{6,7},{7,6},{8,9},{9,8},{10,11... | collective-permute-start | bytes 2359304 | tf_op jit(solution)/shard_map/ppermute | solution.py:89
  542.9 8.3 %collective-permute-start.31 = (bf16[128,640]{1,0:T(8,128)(2,1)S(1)}, bf16[128,640]{1,0:T(8,128)(2,1)S(1)}, u32[]{:S(2)}, u32[]{:S(2)}) collective-permute-start(bf16[128,640]{1,0:T(8,128)(2,1)S(1)} %collective-permute-done.29), channel_id=1, source_target_pairs={{0,1},{1,0},{2,3},{3,2},{4,5},{5,4},{6,7},{7,6},{8,9},{9,8},{10,11... | collective-permute-start | bytes 491528 | tf_op jit(solution)/shard_map/ppermute | solution.py:89
  676.8 8.7 %copy-start.33 = (f32[64,3072]{1,0:T(8,128)S(1)}, f32[64,3072]{1,0:T(8,128)}, u32[]{:S(2)}) copy-start(f32[64,3072]{1,0:T(8,128)} %get-tuple-element.350) | copy-start | bytes 2359300
  (44 other events, 190.9 us)

commit v8 on v7

--- a/solution.py
+++ b/solution.py
@@ -1070,7 +1070,7 @@
     own_query = grad_query_raw
     if shards == 2:
         half_rank = RANK // 2
-        expand_pair = [grad_expand[:half_rank], swap(grad_expand[half_rank:])]
+        expand_pair = [swap(grad_expand[half_rank:]), grad_expand]
     else:
         expand_pair = pair_partial(grad_expand, expand_order)
     grad_own_keys, returned, query_arrived, grad_query_raw, expand_pair = together(

time: 694 us -> 695 us (level)
  no operation moved by 1% of the time
where the time goes in v8:
time: 695 us; the launch traced here: 689 us
  Pallas kernels  358 us (52%)
  matrix products  161 us (23%)
  starting transfers between devices  75.7 us (11%)
  waiting for transfers between devices  32.2 us (5%)
  other arithmetic  30.9 us (4%)
  local copies, waits for them, and re-layouts  28.4 us (4%)
    pallas_call x1, Pallas kernels, reduce_all(): pl.pallas_call(functools.partial(reduce_kernel, plans, steps), in_specs=[...  124 us
    dot_general x19, matrix products, dot(): return jnp.dot(left, right, preferred_element_type=F32)  82.8 us
    pallas_call x1, Pallas kernels, scatter_slot(): pl.pallas_call(scatter_kernel, in_specs=[pl.BlockSpec(memory_space=pltpu....  61.4 us
    dot_general x12, matrix products, dot_t(): lax.dot_general(left, right, (((1,), (1,)), ((), ())), preferred_element_...  60.6 us
    all_to_all x4, starting transfers between devices, exchange(): lax.all_to_all(rows.reshape(owners, capacity, model_width), 'expert', spl...  41 us
    pallas_call x1, Pallas kernels, attend_back(): pl.pallas_call(attend_back_kernel, grid_spec=pltpu.PrefetchScalarGridSpec...  40.1 us
    pallas_call x1, Pallas kernels, expert_pass(): pl.pallas_call(functools.partial(expert_kernel, sources), grid_spec=pltpu...  39 us
    pallas_call x5, Pallas kernels, product_halves(): pl.pallas_call(functools.partial(product_kernel, rows, group, len(lefts))...  34.1 us
  transfers between devices with their start and end apart: 39, of which 7 were waited for; matrix products, arithmetic and copies ran while one was open for 27% of the time, Pallas kernels for 34%

profile of v8, /device:TPU:0, one launch (start us, length us, event | category | flops | bytes accessed | tf_op | source)
XLA Modules:
  0.0 689.5 jit_solution(11421094104064763218)
XLA Ops:
  8.1 4.1 convolution_convert_fusion.2
  13.1 1.8 convolution_add_fusion.6
  15.8 31.9 %shard_map.308 = bf16[16,128,576]{2,1,0:T(8,128)(2,1)S(1)} custom-call(bf16[128,576]{1,0:T(8,128)(2,1)S(1)} %pad_maximum_fusion.7.own_ref), custom_call_target="tpu_custom_call" | custom-call | flops 49999998976 | bytes 4718592 | tf_op jit(solution)/shard_map/pallas_call | solution.py:344
  49.2 5.1 all-to-all-start
  55.0 3.3 collective-permute-done.5
  62.5 3.9 fusion.66
  67.1 4.9 maximum_select_fusion.expand_ref
  72.0 3.9 convolution_add_fusion.1.raw_ref
  76.0 27.0 %shard_map.309 = (bf16[128,2048]{1,0:T(8,128)(2,1)S(1)}, bf16[2048,576]{1,0:T(8,128)(2,1)S(1)}, bf16[2048,2048]{1,0:T(8,128)(2,1)}, bf16[2048,512]{1,0:T(8,128)(2,1)S(1)}, bf16[128,2048]{1,0:T(8,128)(2,1)S(1)}) custom-call(f32[128,3072]{1,0:T(8,128)S(1)} %convolution_add_fusion.1.raw_ref, f32[128,32]{1,0:T(8,128)S(1)} %get-tuple-element.319.cosine_ref, ...), custom_call_target="tpu_custom_call" | custom-call | flops 9126805504 | bytes 8388608 | tf_op jit(solution)/shard_map/pallas_call | solution.py:577
  103.0 1.5 copy-done.4
  105.3 18.6 %all-to-all-done = bf16[16,56,2048]{2,1,0:T(8,128)(2,1)} async-done(((bf16[16,56,2048]{2,1,0:T(8,128)(2,1)}), bf16[16,56,2048]{2,1,0:T(8,128)(2,1)}, u32[]{:S(2)}, u32[]{:S(2)}) %all-to-all-start) | async-done | bytes 3670048 | tf_op jit(solution)/shard_map/all_to_all | solution.py:879
  123.9 3.0 fusion.59
  129.5 2.9 convolution_convert_fusion.1
  132.4 17.4 %all-to-all-start.1 = ((bf16[16,56,2048]{2,1,0:T(8,128)(2,1)}), bf16[16,56,2048]{2,1,0:T(8,128)(2,1)}, u32[]{:S(2)}, u32[]{:S(2)}) async-start(bf16[16,56,2048]{2,1,0:T(8,128)(2,1)} %bitcast.158), calls=%async_computation.1 | async-start | bytes 7340032 | tf_op jit(solution)/shard_map/all_to_all | solution.py:879
  149.9 6.0 fusion.56
  155.9 5.5 fusion.123
  161.4 7.7 %convolution_add_fusion = f32[128,5632]{1,0:T(8,128)} fusion(f32[128,5632]{1,0:T(8,128)S(1)} %fusion.56, bf16[1024,5632]{1,0:T(8,128)(2,1)} %param.32, bf16[128,2048]{1,0:T(8,128)(2,1)S(1)} %multiply_convert_fusion.7, s32[]{:T(128)S(6)} %select_n.233), kind=kOutput, calls=%fused_computation.3 | convolution fusion | flops 1477115904 | bytes 17563652 | tf_op jit(solution)/shard_map/dot_general | solution.py:72
  169.1 5.5 fusion.124
  174.7 3.0 multiply_convert_fusion.5
  177.7 8.2 %fusion.39 = f32[128,1024]{1,0:T(8,128)S(1)} fusion(bf16[1024,5632]{1,0:T(8,128)(2,1)} %param.32, bf16[128,2816]{1,0:T(8,128)(2,1)S(1)} %get-tuple-element.306, bf16[128,2816]{1,0:T(8,128)(2,1)S(1)} %get-tuple-element.305), kind=kOutput, calls=%fused_computation.76 | convolution fusion | flops 1479278592 | bytes 13500416 | tf_op jit(solution)/shard_map/dot_general | solution.py:76
  185.9 8.1 %fusion.38 = f32[128,1024]{1,0:T(8,128)S(1)} fusion(bf16[1024,5632]{1,0:T(8,128)(2,1)} %collective-permute-done.6, bf16[128,2816]{1,0:T(8,128)(2,1)S(1)} %get-tuple-element.306, bf16[128,2816]{1,0:T(8,128)(2,1)S(1)} %get-tuple-element.305), kind=kOutput, calls=%fused_computation.75 | convolution fusion | flops 1479278592 | bytes 13500416 | tf_op jit(solution)/shard_map/dot_general | solution.py:76
  195.2 3.7 fusion.53
  199.0 2.0 convolution_add_fusion.4
  202.2 8.1 %fusion.126.refs_3_ = f32[704,896]{1,0:T(8,128)} fusion(bf16[704,2048]{1,0:T(8,128)(2,1)} %collective-permute-done.9, bf16[896,2048]{1,0:T(8,128)(2,1)} %bitcast.13), kind=kOutput, calls=%fused_computation.234 | convolution fusion | flops 2583691264 | bytes 9076736 | tf_op jit(solution)/shard_map/dot_general | solution.py:76
  210.2 6.8 fusion.125.refs_1_
  219.2 5.4 collective-permute-start.12
  224.6 9.3 %collective-permute-start.11 = (bf16[128,7680]{1,0:T(8,128)(2,1)}, bf16[128,7680]{1,0:T(8,128)(2,1)}, u32[]{:S(2)}, u32[]{:S(2)}) collective-permute-start(bf16[128,7680]{1,0:T(8,128)(2,1)} %pad_maximum_fusion.refs_0_.refs_4_), channel_id=1, source_target_pairs={{0,8},{2,10},{4,12},{6,14},{8,0},{10,2},{12,4},{14,6},{16,24},{18,... | collective-permute-start | bytes 5898248 | tf_op jit(solution)/shard_map/ppermute | solution.py:85
  235.4 39.0 %shard_map.310 = (bf16[896,2048]{1,0:T(8,128)(2,1)}, bf16[1408,896]{1,0:T(8,128)(2,1)}, bf16[2,2,704,896]{3,2,1,0:T(8,128)(2,1)}, f32[1,896]{1,0:T(1,128)}, bf16[16,896]{1,0:T(8,128)(2,1)}) custom-call(s32[1]{0:T(128)} %bitcast.19.here_ref, bf16[896,2048]{1,0:T(8,128)(2,1)} %bitcast.17.rows_ref, bf16[16,2048]{1,0:T(8,128)(2,1)} %bitcast.176, ...), custom_call_target="tpu_custom_call" | custom-call | flops 20669530112 | bytes 18874368 | tf_op jit(solution)/shard_map/pallas_call | solution.py:777
  275.1 7.4 %convolution_convert_fusion.3 = bf16[704,2048]{1,0:T(8,128)(2,1)} fusion(bf16[896,2048]{1,0:T(8,128)(2,1)} %bitcast.13, f32[896]{0:T(1024)S(1)} %reduce, bf16[1408,896]{1,0:T(8,128)(2,1)} %get-tuple-element.184), kind=kOutput, calls=%fused_computation.13 | convolution fusion | flops 2590638080 | bytes 7818752 | tf_op jit(solution)/shard_map/dot_general | solution.py:72
  282.5 10.0 %convolution_convert_fusion = bf16[2,704,2048]{2,1,0:T(8,128)(2,1)} fusion(bf16[896,2048]{1,0:T(8,128)(2,1)} %bitcast.17.rows_ref, bf16[2,2,704,896]{3,2,1,0:T(8,128)(2,1)S(1)} %copy-done.64), kind=kOutput, calls=%fused_computation.5 | convolution fusion | flops 5170266112 | bytes 11960320 | tf_op jit(solution)/shard_map/dot_general | solution.py:72
  292.7 4.7 all-to-all-start.2
  299.1 6.5 collective-permute-done.13.refs_2_.refs_6_
  310.1 3.3 fusion.127
  313.3 10.2 %shard_map.311 = (bf16[384,2048]{1,0:T(8,128)(2,1)}, bf16[384,2048]{1,0:T(8,128)(2,1)}, f32[768,512]{1,0:T(8,128)}) custom-call(s32[8]{0:T(128)} %multiply_add_fusion.4.order_ref, bf16[128,4864]{1,0:T(8,128)(2,1)} %copy-done.14, bf16[128,4864]{1,0:T(8,128)(2,1)} %collective-permute-done.10.refs_1_.refs_5_, bf16[128,4864]{1,0:T(8,128)(2,1)} %copy-done.23, ...), custom_call_target="tpu_custom_call" | custom-call | flops 1610612736 | bytes 8126464 | tf_op jit(solution)/shard_map/pallas_call | solution.py:222
  323.5 5.0 shard_map.313
  328.5 7.0 %shard_map.312 = (bf16[256,4096]{1,0:T(8,128)(2,1)}, bf16[256,4096]{1,0:T(8,128)(2,1)}, bf16[512,512]{1,0:T(8,128)(2,1)}) custom-call(s32[8]{0:T(128)} %get-tuple-element.328.order_ref, bf16[128,7680]{1,0:T(8,128)(2,1)} %pad_maximum_fusion.refs_0_.refs_4_, bf16[128,7680]{1,0:T(8,128)(2,1)} %collective-permute-done.11.refs_1_.refs_5_, ...), custom_call_target="tpu_custom_call" | custom-call | flops 2147483648 | bytes 10485760 | tf_op jit(solution)/shard_map/pallas_call | solution.py:222
  336.2 2.0 collective-permute-start.23
  338.2 5.0 fusion.20
  343.3 4.9 multiply_convert_fusion
  348.2 7.7 %convert_add_fusion.1 = f32[704,2048]{1,0:T(8,128)} fusion(bf16[704,2048]{1,0:T(8,128)(2,1)} %collective-permute-done.20, bf16[896,2048]{1,0:T(8,128)(2,1)} %bitcast.13, f32[896]{0:T(1024)S(1)} %reduce, bf16[1408,896]{1,0:T(8,128)(2,1)S(1)} %copy-done.63), kind=kOutput, calls=%fused_computation.4 | convolution fusion | flops 2592079872 | bytes 13586432 | tf_op jit(solution)/shard_map/dot_general | solution.py:72
  355.9 12.0 %convert_add_fusion = f32[2,704,2048]{2,1,0:T(8,128)} fusion(bf16[2,704,2048]{2,1,0:T(8,128)(2,1)} %collective-permute-done.19, bf16[896,2048]{1,0:T(8,128)(2,1)} %bitcast.17.rows_ref, bf16[2,2,704,896]{3,2,1,0:T(8,128)(2,1)S(1)} %bitcast.192), kind=kOutput, calls=%fused_computation | convolution fusion | flops 5173149696 | bytes 23494656 | tf_op jit(solution)/shard_map/dot_general | solution.py:72
  367.9 1.7 all-to-all-done.2
  369.6 3.7 multiply_reduce_fusion
  373.4 1.5 fusion.118
  376.1 2.6 fusion.128
  378.6 3.9 fusion.129
  382.7 5.6 collective-permute-start.24
  388.2 13.8 %all-to-all-start.3 = ((bf16[16,56,2048]{2,1,0:T(8,128)(2,1)}), bf16[16,56,2048]{2,1,0:T(8,128)(2,1)}, u32[]{:S(2)}, u32[]{:S(2)}) async-start(bf16[16,56,2048]{2,1,0:T(8,128)(2,1)} %bitcast.163), calls=%async_computation.3 | async-start | bytes 7340032 | tf_op jit(solution)/shard_map/all_to_all | solution.py:879
  403.1 40.1 %shard_map.314 = (bf16[128,3072]{1,0:T(8,128)(2,1)S(1)}, bf16[512,4096]{1,0:T(8,128)(2,1)}, bf16[2048,576]{1,0:T(8,128)(2,1)}) custom-call(s32[32]{0:T(128)S(1)} %add.354.order_ref, bf16[128,2048]{1,0:T(8,128)(2,1)S(1)} %fusion.36.grad_ref, bf16[512,4096]{1,0:T(8,128)(2,1)} %maximum_select_fusion.expand_ref, bf16[2048,576]{1,0:T(8,128)(2,1)} %bitcast.155, ...), custom_call_target="tpu_custom_call" | custom-call | flops 22548578304 | bytes 8388608 | tf_op jit(solution)/shard_map/pallas_call | solution.py:669
  445.4 1.9 collective-permute-start.25
  447.3 1.8 slice.105
  449.8 61.4 %shard_map.315 = f32[128,576]{1,0:T(8,128)S(1)} custom-call(bf16[16,128,576]{2,1,0:T(8,128)(2,1)S(1)} %bitcast.157), custom_call_target="tpu_custom_call" | custom-call | flops 49999998976 | bytes 4718592 | tf_op jit(solution)/shard_map/pallas_call | solution.py:431
  512.0 5.6 shard_map.317
  519.7 1.9 collective-permute-start.29
  521.6 5.0 fusion.132
  526.6 1.6 fusion.131
  528.3 5.0 fusion.133
  535.7 2.7 fusion.47
  538.4 3.9 fusion.13
  544.4 6.3 shard_map.316
  550.8 1.6 convolution_convert_fusion.4
  553.3 124.2 %shard_map.318 = (f32[64,640]{1,0:T(8,128)}, f32[96,2048]{1,0:T(8,128)}, f32[16,4096]{1,0:T(8,128)}, f32[64,3072]{1,0:T(8,128)}, f32[64,4096]{1,0:T(8,128)}, /*i...) custom-call(bf16[256,640]{1,0:T(8,128)(2,1)} %get-tuple-element.309.refs_0_, ...), custom_call_target="tpu_custom_call" | custom-call | flops 99999997952 | bytes 42336256 | tf_op jit(solution)/shard_map/pallas_call | solution.py:517
  680.8 2.1 slice.114
  683.6 2.6 pad_maximum_fusion.2
  (289 shorter events, 51.9 us)
Async XLA Ops:
  0.6 11.6 %copy-start.12 = (bf16[1,128,2048]{2,1,0:T(8,128)(2,1)S(1)}, bf16[1,128,2048]{2,1,0:T(8,128)(2,1)}, u32[]{:S(2)}) copy-start(bf16[1,128,2048]{2,1,0:T(8,128)(2,1)} %param.21) | copy-start | bytes 1572868
  1.4 10.7 %collective-permute-start = (bf16[1,2304]{1,0:T(2,128)(2,1)S(1)}, bf16[1,2304]{1,0:T(2,128)(2,1)S(1)}, u32[]{:S(2)}, u32[]{:S(2)}) collective-permute-start(bf16[1,2304]{1,0:T(2,128)(2,1)S(1)} %broadcast_in_dim.24), channel_id=1, source_target_pairs={{0,1},{1,0},{2,3},{3,2},{4,5},{5,4},{6,7},{7,6},{8,9},{9,8},{10,11... | collective-permute-start | bytes 13832 | tf_op jit(solution)/shard_map/ppermute | solution.py:89
  2.0 11.1 %collective-permute-start.3 = (bf16[1024,576]{0,1:T(8,128)(2,1)}, bf16[1024,576]{0,1:T(8,128)(2,1)}, u32[]{:S(2)}, u32[]{:S(2)}) collective-permute-start(bf16[1024,576]{0,1:T(8,128)(2,1)} %param.26), channel_id=1, source_target_pairs={{0,1},{1,0},{2,3},{3,2},{4,5},{5,4},{6,7},{7,6},{8,9},{9,8},{10,11... | collective-permute-start | bytes 3538952 | tf_op jit(solution)/shard_map/ppermute | solution.py:89
  2.0 59.1 %collective-permute-start.1 = (bf16[1024,3072]{1,0:T(8,128)(2,1)}, bf16[1024,3072]{1,0:T(8,128)(2,1)}, u32[]{:S(2)}, u32[]{:S(2)}) collective-permute-start(bf16[1024,3072]{1,0:T(8,128)(2,1)} %param.25), channel_id=1, source_target_pairs={{0,1},{1,0},{2,3},{3,2},{4,5},{5,4},{6,7},{7,6},{8,9},{9,8},{10,11... | collective-permute-start | bytes 18874376 | tf_op jit(solution)/shard_map/ppermute | solution.py:89
  5.7 9.4 %copy-start.50 = (f32[128]{0:T(128)}, f32[128]{0:T(128)S(1)}, u32[]{:S(2)}) copy-start(f32[128]{0:T(128)S(1)} %fusion.113) | copy-start | bytes 1540
  5.8 55.8 %copy-start.48 = (f32[128]{0:T(128)}, f32[128]{0:T(128)S(1)}, u32[]{:S(2)}) copy-start(f32[128]{0:T(128)S(1)} %compare_convert_fusion) | copy-start | bytes 1540
  12.5 59.5 %copy-start.17 = (bf16[128,2048]{1,0:T(8,128)(2,1)}, bf16[128,2048]{1,0:T(8,128)(2,1)S(1)}, u32[]{:S(2)}) copy-start(bf16[128,2048]{1,0:T(8,128)(2,1)S(1)} %fusion.28) | copy-start | bytes 1572868
  14.9 32.8 %copy-start.21 = (f32[128,576]{1,0:T(8,128)}, f32[128,576]{1,0:T(8,128)S(1)}, u32[]{:S(2)}) copy-start(f32[128,576]{1,0:T(8,128)S(1)} %convolution_add_fusion.6) | copy-start | bytes 884740
  15.0 32.6 %copy-start.52 = (f32[128]{0:T(128)}, f32[128]{0:T(128)S(1)}, u32[]{:S(2)}) copy-start(f32[128]{0:T(128)S(1)} %add_rsqrt_fusion.1) | copy-start | bytes 1540
  15.6 108.3 %collective-permute-start.6 = (bf16[1024,5632]{1,0:T(8,128)(2,1)}, bf16[1024,5632]{1,0:T(8,128)(2,1)}, u32[]{:S(2)}, u32[]{:S(2)}) collective-permute-start(bf16[1024,5632]{1,0:T(8,128)(2,1)} %param.32), channel_id=1, source_target_pairs={{0,1},{1,0},{2,3},{3,2},{4,5},{5,4},{6,7},{7,6},{8,9},{9,8},{10,11... | collective-permute-start | bytes 34603016 | tf_op jit(solution)/shard_map/ppermute | solution.py:89
  49.2 12.4 %copy-start.26 = (bf16[1,128,2048]{2,1,0:T(8,128)(2,1)S(1)}, bf16[1,128,2048]{2,1,0:T(8,128)(2,1)}, u32[]{:S(2)}) copy-start(bf16[1,128,2048]{2,1,0:T(8,128)(2,1)} %param.36) | copy-start | bytes 1572868
  49.2 74.7 %all-to-all-start = ((bf16[16,56,2048]{2,1,0:T(8,128)(2,1)}), bf16[16,56,2048]{2,1,0:T(8,128)(2,1)}, u32[]{:S(2)}, u32[]{:S(2)}) async-start(bf16[16,56,2048]{2,1,0:T(8,128)(2,1)} %bitcast.161), calls=%async_computation | async-start | bytes 7340032 | tf_op jit(solution)/shard_map/all_to_all | solution.py:879
  54.3 4.6 collective-permute-start.2
  54.4 3.9 collective-permute-start.5
  54.9 50.4 %collective-permute-start.7 = (bf16[1408,2048]{1,0:T(8,128)(2,1)}, bf16[1408,2048]{1,0:T(8,128)(2,1)}, u32[]{:S(2)}, u32[]{:S(2)}) collective-permute-start(bf16[1408,2048]{1,0:T(8,128)(2,1)} %param.33), channel_id=1, source_target_pairs={{0,1},{1,0},{2,3},{3,2},{4,5},{5,4},{6,7},{7,6},{8,9},{9,8},{10,11... | collective-permute-start | bytes 17301512 | tf_op jit(solution)/shard_map/ppermute | solution.py:89
  58.3 47.0 %collective-permute-start.8 = (bf16[2,704,2048]{2,1,0:T(8,128)(2,1)}, bf16[2,704,2048]{2,1,0:T(8,128)(2,1)}, u32[]{:S(2)}, u32[]{:S(2)}) collective-permute-start(bf16[2,704,2048]{2,1,0:T(8,128)(2,1)} %bitcast.184), channel_id=1, source_target_pairs={{0,1},{1,0},{2,3},{3,2},{4,5},{5,4},{6,7},{7,6},{8,9},{9,8},{10,11... | collective-permute-start | bytes 17301512 | tf_op jit(solution)/shard_map/ppermute | solution.py:89
  58.9 46.4 %collective-permute-start.4 = (bf16[1024,2048]{1,0:T(8,128)(2,1)}, bf16[1024,2048]{1,0:T(8,128)(2,1)}, u32[]{:S(2)}, u32[]{:S(2)}) collective-permute-start(bf16[1024,2048]{1,0:T(8,128)(2,1)} %param.29), channel_id=1, source_target_pairs={{0,1},{1,0},{2,3},{3,2},{4,5},{5,4},{6,7},{7,6},{8,9},{9,8},{10,11... | collective-permute-start | bytes 12582920 | tf_op jit(solution)/shard_map/ppermute | solution.py:89
  59.3 70.1 %copy-start.30 = (pred[896,128]{1,0:T(32,128)(4,1)}, pred[896,128]{1,0:T(32,128)(4,1)S(1)}, u32[]{:S(2)}) copy-start(pred[896,128]{1,0:T(32,128)(4,1)S(1)} %fusion.52) | copy-start | bytes 344068
  61.1 44.2 %collective-permute-start.9 = (bf16[704,2048]{1,0:T(8,128)(2,1)}, bf16[704,2048]{1,0:T(8,128)(2,1)}, u32[]{:S(2)}, u32[]{:S(2)}) collective-permute-start(bf16[704,2048]{1,0:T(8,128)(2,1)} %bitcast.186), channel_id=1, source_target_pairs={{0,1},{1,0},{2,3},{3,2},{4,5},{5,4},{6,7},{7,6},{8,9},{9,8},{10,11... | collective-permute-start | bytes 8650760 | tf_op jit(solution)/shard_map/ppermute | solution.py:89
  129.5 31.9 %copy-start.15 = (bf16[128,2048]{1,0:T(8,128)(2,1)}, bf16[128,2048]{1,0:T(8,128)(2,1)S(1)}, u32[]{:S(2)}) copy-start(bf16[128,2048]{1,0:T(8,128)(2,1)S(1)} %multiply_convert_fusion.7) | copy-start | bytes 1572868
  132.4 86.7 %all-to-all-start.1 = ((bf16[16,56,2048]{2,1,0:T(8,128)(2,1)}), bf16[16,56,2048]{2,1,0:T(8,128)(2,1)}, u32[]{:S(2)}, u32[]{:S(2)}) async-start(bf16[16,56,2048]{2,1,0:T(8,128)(2,1)} %bitcast.158), calls=%async_computation.1 | async-start | bytes 7340032 | tf_op jit(solution)/shard_map/all_to_all | solution.py:879
  177.7 21.2 %slice-start = ((s8[5767168]{0:T(1024)(128)(4,1)}), s8[4194304]{0:T(1024)(128)(4,1)S(1)}, s32[]{:S(2)}) async-start(s8[5767168]{0:T(1024)(128)(4,1)} %bitcast.159), calls=%async_computation.4 | async-start | bytes 8388608
  185.9 13.0 %slice-start.1 = ((s8[5767168]{0:T(1024)(128)(4,1)}), s8[1572864]{0:T(1024)(128)(4,1)S(1)}, s32[]{:S(2)}) async-start(s8[5767168]{0:T(1024)(128)(4,1)} %bitcast.159), calls=%async_computation.5 | async-start | bytes 3145728
  202.1 95.8 %copy-start.14 = (bf16[128,4864]{1,0:T(8,128)(2,1)}, bf16[128,4864]{1,0:T(8,128)(2,1)S(1)}, u32[]{:S(2)}) copy-start(bf16[128,4864]{1,0:T(8,128)(2,1)S(1)} %pad_maximum_fusion.3.refs_0_.refs_4_) | copy-start | bytes 3735556
  202.1 8.1 %copy-start.61 = (bf16[1,704,2048]{2,1,0:T(8,128)(2,1)S(1)}, bf16[1,704,2048]{2,1,0:T(8,128)(2,1)}, u32[]{:S(2)}) copy-start(bf16[1,704,2048]{2,1,0:T(8,128)(2,1)} %param.35) | copy-start | bytes 8650756
  219.2 73.3 %collective-permute-start.12 = (bf16[128,4096]{1,0:T(8,128)(2,1)}, bf16[128,4096]{1,0:T(8,128)(2,1)}, u32[]{:S(2)}, u32[]{:S(2)}) collective-permute-start(bf16[128,4096]{1,0:T(8,128)(2,1)} %pad_maximum_fusion.4.refs_0_), channel_id=1, source_target_pairs={{0,4},{2,6},{4,0},{6,2},{8,12},{10,14},{12,8},{14,10},{16,20},{18,... | collective-permute-start | bytes 3145736 | tf_op jit(solution)/shard_map/ppermute | solution.py:85
  224.6 68.0 %collective-permute-start.11 = (bf16[128,7680]{1,0:T(8,128)(2,1)}, bf16[128,7680]{1,0:T(8,128)(2,1)}, u32[]{:S(2)}, u32[]{:S(2)}) collective-permute-start(bf16[128,7680]{1,0:T(8,128)(2,1)} %pad_maximum_fusion.refs_0_.refs_4_), channel_id=1, source_target_pairs={{0,8},{2,10},{4,12},{6,14},{8,0},{10,2},{12,4},{14,6},{16,24},{18,... | collective-permute-start | bytes 5898248 | tf_op jit(solution)/shard_map/ppermute | solution.py:85
  233.9 58.6 %collective-permute-start.10 = (bf16[128,4864]{1,0:T(8,128)(2,1)S(1)}, bf16[128,4864]{1,0:T(8,128)(2,1)}, u32[]{:S(2)}, u32[]{:S(2)}) collective-permute-start(bf16[128,4864]{1,0:T(8,128)(2,1)S(1)} %pad_maximum_fusion.3.refs_0_.refs_4_), channel_id=1, source_target_pairs={{0,2},{2,0},{4,6},{6,4},{8,10},{10,8},{12,14},{14,12},{16,18},{18,... | collective-permute-start | bytes 3735560 | tf_op jit(solution)/shard_map/ppermute | solution.py:85
  292.5 55.6 %collective-permute-start.19 = (bf16[2,704,2048]{2,1,0:T(8,128)(2,1)}, bf16[2,704,2048]{2,1,0:T(8,128)(2,1)}, u32[]{:S(2)}, u32[]{:S(2)}) collective-permute-start(bf16[2,704,2048]{2,1,0:T(8,128)(2,1)} %convolution_convert_fusion), channel_id=1, source_target_pairs={{0,1},{1,0},{2,3},{3,2},{4,5},{5,4},{6,7},{7,6},{8,9},{9,8},{10,11... | collective-permute-start | bytes 17301512 | tf_op jit(solution)/shard_map/ppermute | solution.py:89
  292.6 14.1 %copy-start.59 = (s32[8]{0:T(128)S(1)}, s32[8]{0:T(128)}, u32[]{:S(2)}) copy-start(s32[8]{0:T(128)} %constant.197.clone) | copy-start | bytes 100
  292.6 16.2 %copy-start.58 = (s32[8]{0:T(128)S(1)}, s32[8]{0:T(128)}, u32[]{:S(2)}) copy-start(s32[8]{0:T(128)} %constant.196.clone) | copy-start | bytes 100
  292.7 16.9 %copy-start.56 = (s32[8]{0:T(128)S(1)}, s32[8]{0:T(128)}, u32[]{:S(2)}) copy-start(s32[8]{0:T(128)} %constant.194.clone) | copy-start | bytes 100
  292.7 16.9 %copy-start.57 = (s32[8]{0:T(128)S(1)}, s32[8]{0:T(128)}, u32[]{:S(2)}) copy-start(s32[8]{0:T(128)} %constant.195.clone) | copy-start | bytes 100
  292.7 17.4 %copy-start.45 = (bf16[16,896]{1,0:T(8,128)(2,1)S(1)}, bf16[16,896]{1,0:T(8,128)(2,1)}, u32[]{:S(2)}) copy-start(bf16[16,896]{1,0:T(8,128)(2,1)} %get-tuple-element.186) | copy-start | bytes 86020
  292.7 76.9 %all-to-all-start.2 = ((bf16[16,56,2048]{2,1,0:T(8,128)(2,1)}), bf16[16,56,2048]{2,1,0:T(8,128)(2,1)}, u32[]{:S(2)}, u32[]{:S(2)}) async-start(bf16[16,56,2048]{2,1,0:T(8,128)(2,1)} %bitcast.162), calls=%async_computation.2 | async-start | bytes 7340032 | tf_op jit(solution)/shard_map/all_to_all | solution.py:879
  297.4 9.9 %collective-permute-start.15 = (bf16[128,7680]{1,0:T(8,128)(2,1)}, bf16[128,7680]{1,0:T(8,128)(2,1)}, u32[]{:S(2)}, u32[]{:S(2)}) collective-permute-start(bf16[128,7680]{1,0:T(8,128)(2,1)} %pad_maximum_fusion.refs_0_.refs_4_), channel_id=1, source_target_pairs={{0,1},{1,0},{2,3},{3,2},{4,5},{5,4},{6,7},{7,6},{8,9},{9,8},{10,11... | collective-permute-start | bytes 5898248 | tf_op jit(solution)/shard_map/ppermute | solution.py:89
  297.9 7.7 %collective-permute-start.13 = (bf16[128,4864]{1,0:T(8,128)(2,1)S(1)}, bf16[128,4864]{1,0:T(8,128)(2,1)S(1)}, u32[]{:S(2)}, u32[]{:S(2)}) collective-permute-start(bf16[128,4864]{1,0:T(8,128)(2,1)S(1)} %pad_maximum_fusion.3.refs_0_.refs_4_), channel_id=1, source_target_pairs={{0,1},{1,0},{2,3},{3,2},{4,5},{5,4},{6,7},{7,6},{8,9},{9,8},{10,11... | collective-permute-start | bytes 3735560 | tf_op jit(solution)/shard_map/ppermute | solution.py:89
  298.0 10.8 %collective-permute-start.14 = (bf16[128,4864]{1,0:T(8,128)(2,1)}, bf16[128,4864]{1,0:T(8,128)(2,1)}, u32[]{:S(2)}, u32[]{:S(2)}) collective-permute-start(bf16[128,4864]{1,0:T(8,128)(2,1)} %collective-permute-done.10.refs_1_.refs_5_), channel_id=1, source_target_pairs={{0,1},{1,0},{2,3},{3,2},{4,5},{5,4},{6,7},{7,6},{8,9},{9,8},{10,11... | collective-permute-start | bytes 3735560 | tf_op jit(solution)/shard_map/ppermute | solution.py:89
  298.4 25.1 %collective-permute-start.16 = (bf16[128,7680]{1,0:T(8,128)(2,1)}, bf16[128,7680]{1,0:T(8,128)(2,1)}, u32[]{:S(2)}, u32[]{:S(2)}) collective-permute-start(bf16[128,7680]{1,0:T(8,128)(2,1)} %collective-permute-done.11.refs_1_.refs_5_), channel_id=1, source_target_pairs={{0,1},{1,0},{2,3},{3,2},{4,5},{5,4},{6,7},{7,6},{8,9},{9,8},{10,11... | collective-permute-start | bytes 5898248 | tf_op jit(solution)/shard_map/ppermute | solution.py:89
  306.6 41.6 %collective-permute-start.20 = (bf16[704,2048]{1,0:T(8,128)(2,1)}, bf16[704,2048]{1,0:T(8,128)(2,1)}, u32[]{:S(2)}, u32[]{:S(2)}) collective-permute-start(bf16[704,2048]{1,0:T(8,128)(2,1)} %convolution_convert_fusion.3), channel_id=1, source_target_pairs={{0,1},{1,0},{2,3},{3,2},{4,5},{5,4},{6,7},{7,6},{8,9},{9,8},{10,11... | collective-permute-start | bytes 8650760 | tf_op jit(solution)/shard_map/ppermute | solution.py:89
  307.3 28.2 %collective-permute-start.17 = (bf16[128,4096]{1,0:T(8,128)(2,1)}, bf16[128,4096]{1,0:T(8,128)(2,1)}, u32[]{:S(2)}, u32[]{:S(2)}) collective-permute-start(bf16[128,4096]{1,0:T(8,128)(2,1)} %pad_maximum_fusion.4.refs_0_), channel_id=1, source_target_pairs={{0,1},{1,0},{2,3},{3,2},{4,5},{5,4},{6,7},{7,6},{8,9},{9,8},{10,11... | collective-permute-start | bytes 3145736 | tf_op jit(solution)/shard_map/ppermute | solution.py:89
  308.7 26.8 %collective-permute-start.18 = (bf16[128,4096]{1,0:T(8,128)(2,1)}, bf16[128,4096]{1,0:T(8,128)(2,1)}, u32[]{:S(2)}, u32[]{:S(2)}) collective-permute-start(bf16[128,4096]{1,0:T(8,128)(2,1)} %collective-permute-done.12.refs_1_), channel_id=1, source_target_pairs={{0,1},{1,0},{2,3},{3,2},{4,5},{5,4},{6,7},{7,6},{8,9},{9,8},{10,11... | collective-permute-start | bytes 3145736 | tf_op jit(solution)/shard_map/ppermute | solution.py:89
  328.5 9.7 %copy-start.63 = (bf16[1408,896]{1,0:T(8,128)(2,1)S(1)}, bf16[1408,896]{1,0:T(8,128)(2,1)}, u32[]{:S(2)}) copy-start(bf16[1408,896]{1,0:T(8,128)(2,1)} %get-tuple-element.184) | copy-start | bytes 7569412
  335.6 109.8 %collective-permute-start.22 = (bf16[256,4096]{1,0:T(8,128)(2,1)}, bf16[256,4096]{1,0:T(8,128)(2,1)}, u32[]{:S(2)}, u32[]{:S(2)}) collective-permute-start(bf16[256,4096]{1,0:T(8,128)(2,1)} %get-tuple-element.199), channel_id=1, source_target_pairs={{0,2},{2,0},{4,6},{6,4},{8,10},{10,8},{12,14},{14,12},{16,18},{18,... | collective-permute-start | bytes 6291464 | tf_op jit(solution)/shard_map/ppermute | solution.py:85
  336.2 109.1 %collective-permute-start.21 = (bf16[384,2048]{1,0:T(8,128)(2,1)}, bf16[384,2048]{1,0:T(8,128)(2,1)}, u32[]{:S(2)}, u32[]{:S(2)}) collective-permute-start(bf16[384,2048]{1,0:T(8,128)(2,1)} %get-tuple-element.197), channel_id=1, source_target_pairs={{0,4},{2,6},{4,0},{6,2},{8,12},{10,14},{12,8},{14,10},{16,20},{18,... | collective-permute-start | bytes 4718600 | tf_op jit(solution)/shard_map/ppermute | solution.py:85
  336.2 109.1 %collective-permute-start.23 = (bf16[256,1536]{1,0:T(8,128)(2,1)}, bf16[256,1536]{1,0:T(8,128)(2,1)}, u32[]{:S(2)}, u32[]{:S(2)}) collective-permute-start(bf16[256,1536]{1,0:T(8,128)(2,1)} %get-tuple-element.201), channel_id=1, source_target_pairs={{0,4},{2,6},{4,0},{6,2},{8,12},{10,14},{12,8},{14,10},{16,20},{18,... | collective-permute-start | bytes 2359304 | tf_op jit(solution)/shard_map/ppermute | solution.py:85
  338.2 17.6 %slice-start.2 = ((s8[5046272]{0:T(1024)(128)(4,1)}), s8[4194304]{0:T(1024)(128)(4,1)S(1)}, s32[]{:S(2)}) async-start(s8[5046272]{0:T(1024)(128)(4,1)} %bitcast.191), calls=%async_computation.6 | async-start | bytes 8388608
  343.3 12.6 %slice-start.3 = ((s8[5046272]{0:T(1024)(128)(4,1)}), s8[851968]{0:T(1024)(128)(4,1)S(1)}, s32[]{:S(2)}) async-start(s8[5046272]{0:T(1024)(128)(4,1)} %bitcast.191), calls=%async_computation.7 | async-start | bytes 1703936
  355.8 13.7 %copy-start.31 = (pred[896,128]{1,0:T(32,128)(4,1)S(1)}, pred[896,128]{1,0:T(32,128)(4,1)}, u32[]{:S(2)}) copy-start(pred[896,128]{1,0:T(32,128)(4,1)} %copy-done.30) | copy-start | bytes 344068
  382.7 62.7 %collective-permute-start.24 = (bf16[128,2048]{1,0:T(8,128)(2,1)}, bf16[128,2048]{1,0:T(8,128)(2,1)}, u32[]{:S(2)}, u32[]{:S(2)}) collective-permute-start(bf16[128,2048]{1,0:T(8,128)(2,1)} %get-tuple-element.202.refs_4_), channel_id=1, source_target_pairs={{0,4},{2,6},{4,0},{6,2},{8,12},{10,14},{12,8},{14,10},{16,20},{18,... | collective-permute-start | bytes 1572872 | tf_op jit(solution)/shard_map/ppermute | solution.py:85
  388.2 123.0 %collective-permute-start.32 = (bf16[128,2048]{1,0:T(8,128)(2,1)}, bf16[128,2048]{1,0:T(8,128)(2,1)}, u32[]{:S(2)}, u32[]{:S(2)}) collective-permute-start(bf16[128,2048]{1,0:T(8,128)(2,1)} %get-tuple-element.202.refs_4_), channel_id=1, source_target_pairs={{0,1},{1,0},{2,3},{3,2},{4,5},{5,4},{6,7},{7,6},{8,9},{9,8},{10,11... | collective-permute-start | bytes 1572872 | tf_op jit(solution)/shard_map/ppermute | solution.py:89
  388.2 130.3 %all-to-all-start.3 = ((bf16[16,56,2048]{2,1,0:T(8,128)(2,1)}), bf16[16,56,2048]{2,1,0:T(8,128)(2,1)}, u32[]{:S(2)}, u32[]{:S(2)}) async-start(bf16[16,56,2048]{2,1,0:T(8,128)(2,1)} %bitcast.163), calls=%async_computation.3 | async-start | bytes 7340032 | tf_op jit(solution)/shard_map/all_to_all | solution.py:879
  443.2 85.0 %copy-start = (bf16[128,3072]{1,0:T(8,128)(2,1)}, bf16[128,3072]{1,0:T(8,128)(2,1)S(1)}, u32[]{:S(2)}) copy-start(bf16[128,3072]{1,0:T(8,128)(2,1)S(1)} %get-tuple-element.209.refs_4_) | copy-start | bytes 2359300
  445.4 72.3 %collective-permute-start.25 = (bf16[128,3072]{1,0:T(8,128)(2,1)S(1)}, bf16[128,3072]{1,0:T(8,128)(2,1)S(1)}, u32[]{:S(2)}, u32[]{:S(2)}) collective-permute-start(bf16[128,3072]{1,0:T(8,128)(2,1)S(1)} %get-tuple-element.209.refs_4_), channel_id=1, source_target_pairs={{0,4},{2,6},{4,0},{6,2},{8,12},{10,14},{12,8},{14,10},{16,20},{18,... | collective-permute-start | bytes 2359304 | tf_op jit(solution)/shard_map/ppermute | solution.py:85
  447.3 96.3 %collective-permute-start.27 = (bf16[128,3072]{1,0:T(8,128)(2,1)S(1)}, bf16[128,3072]{1,0:T(8,128)(2,1)}, u32[]{:S(2)}, u32[]{:S(2)}) collective-permute-start(bf16[128,3072]{1,0:T(8,128)(2,1)S(1)} %get-tuple-element.209.refs_4_), channel_id=1, source_target_pairs={{0,1},{1,0},{2,3},{3,2},{4,5},{5,4},{6,7},{7,6},{8,9},{9,8},{10,11... | collective-permute-start | bytes 2359304 | tf_op jit(solution)/shard_map/ppermute | solution.py:89
  449.1 69.4 %collective-permute-start.26 = (bf16[256,4096]{1,0:T(8,128)(2,1)S(1)}, bf16[256,4096]{1,0:T(8,128)(2,1)}, u32[]{:S(2)}, u32[]{:S(2)}) collective-permute-start(bf16[256,4096]{1,0:T(8,128)(2,1)S(1)} %slice.105), channel_id=1, source_target_pairs={{0,1},{1,0},{2,3},{3,2},{4,5},{5,4},{6,7},{7,6},{8,9},{9,8},{10,11... | collective-permute-start | bytes 6291464 | tf_op jit(solution)/shard_map/ppermute | solution.py:89
  449.7 61.6 %collective-permute-start.33 = (bf16[128,2048]{1,0:T(8,128)(2,1)}, bf16[128,2048]{1,0:T(8,128)(2,1)S(1)}, u32[]{:S(2)}, u32[]{:S(2)}) collective-permute-start(bf16[128,2048]{1,0:T(8,128)(2,1)} %collective-permute-done.24.refs_5_), channel_id=1, source_target_pairs={{0,1},{1,0},{2,3},{3,2},{4,5},{5,4},{6,7},{7,6},{8,9},{9,8},{10,11... | collective-permute-start | bytes 1572872 | tf_op jit(solution)/shard_map/ppermute | solution.py:89
  511.2 8.1 %copy-start.25 = (bf16[1024,576]{0,1:T(8,128)(2,1)S(1)}, bf16[1024,576]{0,1:T(8,128)(2,1)}, u32[]{:S(2)}) copy-start(bf16[1024,576]{0,1:T(8,128)(2,1)} %param.26) | copy-start | bytes 3538948
  519.7 22.7 %collective-permute-start.29 = (bf16[128,640]{1,0:T(8,128)(2,1)S(1)}, bf16[128,640]{1,0:T(8,128)(2,1)S(1)}, u32[]{:S(2)}, u32[]{:S(2)}) collective-permute-start(bf16[128,640]{1,0:T(8,128)(2,1)S(1)} %pad.9), channel_id=1, source_target_pairs={{0,4},{2,6},{4,0},{6,2},{8,12},{10,14},{12,8},{14,10},{16,20},{18,... | collective-permute-start | bytes 491528 | tf_op jit(solution)/shard_map/ppermute | solution.py:85
  521.6 29.1 %collective-permute-start.30 = (bf16[128,640]{1,0:T(8,128)(2,1)S(1)}, bf16[128,640]{1,0:T(8,128)(2,1)}, u32[]{:S(2)}, u32[]{:S(2)}) collective-permute-start(bf16[128,640]{1,0:T(8,128)(2,1)S(1)} %pad.9), channel_id=1, source_target_pairs={{0,1},{1,0},{2,3},{3,2},{4,5},{5,4},{6,7},{7,6},{8,9},{9,8},{10,11... | collective-permute-start | bytes 491528 | tf_op jit(solution)/shard_map/ppermute | solution.py:89
  535.1 7.2 %collective-permute-start.34 = (bf16[16,16,128]{2,1,0:T(8,128)(2,1)S(1)}, bf16[16,16,128]{2,1,0:T(8,128)(2,1)S(1)}, u32[]{:S(2)}, u32[]{:S(2)}) collective-permute-start(bf16[16,16,128]{2,1,0:T(8,128)(2,1)S(1)} %dynamic-slice_bitcast_fusion), channel_id=1, source_target_pairs={{0,1},{1,0},{2,3},{3,2},{4,5},{5,4},{6,7},{7,6},{8,9},{9,8},{10,11... | collective-permute-start | bytes 196616 | tf_op jit(solution)/shard_map/ppermute | solution.py:89
  535.6 7.9 %collective-permute-start.28 = (bf16[128,3072]{1,0:T(8,128)(2,1)}, bf16[128,3072]{1,0:T(8,128)(2,1)S(1)}, u32[]{:S(2)}, u32[]{:S(2)}) collective-permute-start(bf16[128,3072]{1,0:T(8,128)(2,1)} %copy-done.34), channel_id=1, source_target_pairs={{0,1},{1,0},{2,3},{3,2},{4,5},{5,4},{6,7},{7,6},{8,9},{9,8},{10,11... | collective-permute-start | bytes 2359304 | tf_op jit(solution)/shard_map/ppermute | solution.py:89
  542.4 8.4 %collective-permute-start.31 = (bf16[128,640]{1,0:T(8,128)(2,1)S(1)}, bf16[128,640]{1,0:T(8,128)(2,1)S(1)}, u32[]{:S(2)}, u32[]{:S(2)}) collective-permute-start(bf16[128,640]{1,0:T(8,128)(2,1)S(1)} %collective-permute-done.29), channel_id=1, source_target_pairs={{0,1},{1,0},{2,3},{3,2},{4,5},{5,4},{6,7},{7,6},{8,9},{9,8},{10,11... | collective-permute-start | bytes 491528 | tf_op jit(solution)/shard_map/ppermute | solution.py:89
  677.5 8.7 %copy-start.33 = (f32[64,3072]{1,0:T(8,128)S(1)}, f32[64,3072]{1,0:T(8,128)}, u32[]{:S(2)}) copy-start(f32[64,3072]{1,0:T(8,128)} %get-tuple-element.348) | copy-start | bytes 2359300
  (44 other events, 188.8 us)
